TPU v7x, 32 devices: a whole 2x2x4 slice. The times are simulated.
32 devices in a mesh: dp: 2 (over y), seq: 4 (over x, core), shard: 4 (over z).
Axes of the slice: x: 2, y: 2, z: 4, core: 2. Of those that a mesh axis runs over, the one named last changes fastest.
Arguments:
- tokens: int32 [8, 1024], P(('dp', 'shard'), 'seq'), may hold values from 0 to 50277
- block_ids: int32 [8, 1024], P(('dp', 'shard')), may hold values from 0 to 7, never falling along the last dimension, each value on 1 to 256 neighbouring positions
- completion: int32 [8, 1024], P(('dp', 'seq')), may hold values from 0 to 1, as said below
- regroup: int32 [8, 256], P(('dp', 'seq')), may hold values from 0 to 255, each once within a row
- targets: int32 [2048], replicated, may hold values from 0 to 50277
- step_count: int32 [1], replicated, may hold values from 1 to 20
- layer_mats: float32 [2, 3, 4352, 1088], P(None, None, ('dp', 'seq', 'shard'))
- mats_moment: float32 [2, 3, 4352, 1088], P(None, None, ('dp', 'seq', 'shard')), may hold values from -3.8146973e-06 to 3.8146973e-06
- mats_square: float32 [2, 3, 4352, 1088], P(None, None, ('dp', 'seq', 'shard')), may hold values from 1.2343522e-13 to 1.9939536e-12
- embed_table: float32 [51328, 1088], P(('dp', 'seq', 'shard'))
- table_moment: float32 [51328, 1088], P(('dp', 'seq', 'shard')), may hold values from -3.8146973e-06 to 3.8146973e-06
- table_square: float32 [51328, 1088], P(('dp', 'seq', 'shard')), may hold values from 1.2343522e-13 to 1.9939536e-12
Outputs:
- loss_value: float32 [1], replicated
- grad_norm: float32 [1], replicated
- updated_mats: float32 [2, 3, 4352, 1088], P(None, None, ('dp', 'seq', 'shard'))
- moment_mats: float32 [2, 3, 4352, 1088], P(None, None, ('dp', 'seq', 'shard'))
- square_mats: float32 [2, 3, 4352, 1088], P(None, None, ('dp', 'seq', 'shard'))
- updated_table: float32 [51328, 1088], P(('dp', 'seq', 'shard'))
- moment_table: float32 [51328, 1088], P(('dp', 'seq', 'shard'))
- square_table: float32 [51328, 1088], P(('dp', 'seq', 'shard'))
Inputs may be any that keep to these rules, and one draw needn't show every extreme that they name: `completion`: each row holds exactly 256 ones; their split among the 4 column blocks of 256 varies. `regroup`: each row is a permutation. `block_ids`: along a sequence the numbers never fall; a block has at most 256 positions.
All inputs are finite; a program needn't handle non-finite values.
Results may differ from a plain program's by a relative error of at most 0.007.
The roundings to bfloat16 on the way count: a program that leaves them out, or rounds other values in their place, can miss the bound.
Values may be sent and summed in bfloat16 or wider, within the bound.
A program may use at most 896 MiB of HBM per device.

v0:
```python
from functools import partial

import jax
import jax.numpy as jnp
from jax import lax
from jax.sharding import PartitionSpec as P

HEADS = 17
HEAD = 64
VOCAB = 50278


NORM_EPS = 1e-05
CLIP_NORM = 0.02
BETA_ONE = 0.9
BETA_TWO = 0.95
ADAM_EPS = 1e-08
DECAY_RATE = 0.1
RATE_MATS = 0.05
RATE_TABLE = 0.1
RATE_SMALL = 0.5
MASK_FILL = -1e30


def joined_2(x, axis, combine):
    everything = jax.tree.map(
        lambda part, kind: lax.all_gather(part.astype(kind), axis),
        x,
        (jnp.bfloat16, jnp.bfloat16, jnp.bfloat16),
    )

    def take(k):
        return jax.tree.map(lambda part, own: part[k].astype(own.dtype), everything, x)

    return lax.fori_loop(
        1, lax.axis_size(axis), lambda k, so_far: combine(so_far, take(k)), take(0)
    )


def dot_rows(left_op, right_op):
    return lax.dot_general(
        left_op, right_op, (((1,), (1,)), ((), ())), preferred_element_type=jnp.float32
    )


def dot_cols(left_op, right_op):
    return lax.dot_general(
        left_op, right_op, (((0,), (0,)), ((), ())), preferred_element_type=jnp.float32
    )


def dot_plain(left_op, right_op):
    return jnp.dot(left_op, right_op, preferred_element_type=jnp.float32)


def column_sums(values):
    return jnp.sum(values.astype(jnp.float32), 0)


def layer_norm(values, gain, shift):
    center = values - jnp.mean(values, -1, keepdims=True)
    spread = jnp.mean(center * center, -1, keepdims=True)
    return center * lax.rsqrt(spread + NORM_EPS) * gain + shift


def norm_back(values, gain, shift, grad):
    unused, pull = jax.vjp(layer_norm, values, gain, shift)
    return pull(grad)


def to_sequences(rows_in, seqs, groups):
    tok_count = rows_in.shape[0] // (seqs * groups)
    split = rows_in.reshape(groups, seqs, tok_count, HEADS, HEAD)
    return jnp.swapaxes(split, 0, 1).reshape(seqs, groups * tok_count, HEADS, HEAD)


def from_sequences(seq_rows, groups):
    seqs = seq_rows.shape[0]
    tok_count = seq_rows.shape[1] // groups
    split = seq_rows.reshape(seqs, groups, tok_count, HEADS * HEAD)
    return jnp.swapaxes(split, 0, 1).reshape(groups * seqs * tok_count, HEADS * HEAD)


def gather_layer(mats_one):
    return lax.all_gather(mats_one, ("dp", "seq", "shard"), axis=1, tiled=True)


def layer_forward(state, weights, params, query_ids, key_ids):
    seqs, tok_count = query_ids.shape
    groups = lax.axis_size("seq")
    width = state.shape[1]
    scale = HEAD ** (-0.5)
    hidden = layer_norm(state, params[0], params[1]).astype(jnp.bfloat16)
    joined = dot_rows(hidden, weights[0, : 3 * width])
    queries = (joined[:, :width] + params[2]).astype(jnp.bfloat16)
    key_rows = joined[:, width : 2 * width].astype(jnp.bfloat16)
    val_rows = (joined[:, 2 * width :] + params[3]).astype(jnp.bfloat16)
    key_all, val_all = (
        lax.all_gather(key_rows, "seq", axis=0, tiled=True),
        lax.all_gather(val_rows, "seq", axis=0, tiled=True),
    )
    key_seq = to_sequences(key_all, seqs, groups)
    val_seq = to_sequences(val_all, seqs, groups)
    query_seq = queries.reshape(seqs, tok_count, HEADS, HEAD)
    scores = (
        jnp.einsum("sqhd,skhd->shqk", query_seq, key_seq, preferred_element_type=jnp.float32)
        * scale
    )
    allowed = key_ids[:, None, None, :] <= query_ids[:, None, :, None]
    scores = jnp.where(allowed, scores, MASK_FILL)
    raised = jnp.exp(scores - jnp.max(scores, -1, keepdims=True))
    probs = raised / jnp.sum(raised, -1, keepdims=True)
    attended = jnp.einsum(
        "shqk,skhd->sqhd", probs.astype(jnp.bfloat16), val_seq, preferred_element_type=jnp.float32
    )
    attended = attended.reshape(-1, width).astype(jnp.bfloat16)
    mid_state = state + dot_plain(attended, weights[0, 3 * width :]) + params[4]
    normed = layer_norm(mid_state, params[5], params[6]).astype(jnp.bfloat16)
    upward = dot_rows(normed, weights[1]) + params[8:12].reshape(-1)
    active = jax.nn.gelu(upward, approximate=True).astype(jnp.bfloat16)
    output = mid_state + dot_plain(active, weights[2]) + params[7]
    return (
        output,
        (hidden, query_seq, key_seq, val_seq, probs, attended, mid_state, normed, upward, active),
    )


def layer_backward(state, weights, params, query_ids, key_ids, grad_in):
    groups = lax.axis_size("seq")
    width = state.shape[1]
    scale = HEAD ** (-0.5)
    unused, saved = layer_forward(state, weights, params, query_ids, key_ids)
    hidden, query_seq, key_seq, val_seq, probs, attended, mid_state, normed, upward, active = saved
    down_grad = grad_in.astype(jnp.bfloat16)
    grad_down = dot_cols(active, down_grad)
    act_grad = dot_rows(down_grad, weights[2])
    unused_gelu, gelu_pull = jax.vjp(partial(jax.nn.gelu, approximate=True), upward)
    up_grad = gelu_pull(act_grad)[0].astype(jnp.bfloat16)
    grad_up = dot_cols(up_grad, normed)
    mid_back, gain_two, shift_two = norm_back(
        mid_state, params[5], params[6], dot_plain(up_grad, weights[1])
    )
    mid_grad = grad_in + mid_back
    out_grad = mid_grad.astype(jnp.bfloat16)
    grad_proj = dot_cols(attended, out_grad)
    att_grad = dot_rows(out_grad, weights[0, 3 * width :]).astype(jnp.bfloat16)
    att_seq = att_grad.reshape(query_seq.shape)
    prob_grad = jnp.einsum("sqhd,skhd->shqk", att_seq, val_seq, preferred_element_type=jnp.float32)
    val_part = jnp.einsum(
        "shqk,sqhd->skhd", probs.astype(jnp.bfloat16), att_seq, preferred_element_type=jnp.float32
    )
    score_grad = (probs * (prob_grad - jnp.sum(probs * prob_grad, -1, keepdims=True))).astype(
        jnp.bfloat16
    )
    query_grad = (
        jnp.einsum("shqk,skhd->sqhd", score_grad, key_seq, preferred_element_type=jnp.float32)
        * scale
    )
    query_grad = query_grad.reshape(-1, width).astype(jnp.bfloat16)
    key_part = (
        jnp.einsum("shqk,sqhd->skhd", score_grad, query_seq, preferred_element_type=jnp.float32)
        * scale
    )
    key_grad, val_grad = (
        lax.psum_scatter(
            from_sequences(key_part, groups).astype(jnp.bfloat16),
            "seq",
            scatter_dimension=0,
            tiled=True,
        ).astype(jnp.float32),
        lax.psum_scatter(
            from_sequences(val_part, groups).astype(jnp.bfloat16),
            "seq",
            scatter_dimension=0,
            tiled=True,
        ).astype(jnp.float32),
    )
    key_grad = key_grad.astype(jnp.bfloat16)
    val_grad = val_grad.astype(jnp.bfloat16)
    joined_grad = jnp.concatenate([query_grad, key_grad, val_grad], 1)
    grad_joined = dot_cols(joined_grad, hidden)
    state_back, gain_one, shift_one = norm_back(
        state, params[0], params[1], dot_plain(joined_grad, weights[0, : 3 * width])
    )
    small_grad = jnp.concatenate(
        [
            jnp.stack(
                [
                    gain_one,
                    shift_one,
                    column_sums(query_grad),
                    column_sums(val_grad),
                    column_sums(out_grad),
                    gain_two,
                    shift_two,
                    column_sums(down_grad),
                ]
            ),
            column_sums(up_grad).reshape(4, width),
        ],
        0,
    )
    mats_grad = jnp.stack([jnp.concatenate([grad_joined, grad_proj], 0), grad_up, grad_down])
    return (mid_grad + state_back, mats_grad, small_grad)


def merge_soft(first, second):
    top_first, total_first, pick_first = first
    top_second, total_second, pick_second = second
    highest = jnp.maximum(top_first, top_second)
    total = total_first * jnp.exp(top_first - highest) + total_second * jnp.exp(
        top_second - highest
    )
    return (highest, total, pick_first + pick_second)


def adam_step(weights, moment, square, grad, rate, decay, step):
    moment = BETA_ONE * moment + (1 - BETA_ONE) * grad
    square = BETA_TWO * square + (1 - BETA_TWO) * grad * grad
    moment_hat = moment / (1 - BETA_ONE**step)
    square_hat = square / (1 - BETA_TWO**step)
    weights = weights - rate * (moment_hat / (jnp.sqrt(square_hat) + ADAM_EPS) + decay * weights)
    return (weights, moment, square)


def on_device(
    tokens,
    block_ids,
    completion,
    regroup,
    targets,
    step_count,
    layer_mats,
    mats_moment,
    mats_square,
    embed_table,
    table_moment,
    table_square,
):
    seqs, tok_count = tokens.shape
    seq_length = block_ids.shape[1]
    width = embed_table.shape[1]
    table_local = embed_table.shape[0]
    layers = layer_mats.shape[0]
    shards = lax.axis_size("shard")
    seq_at = lax.axis_index("seq")
    shard_at = lax.axis_index("shard")
    device_at = lax.axis_index(("dp", "seq", "shard"))
    bf_zero = jnp.zeros((), jnp.bfloat16)
    first_row = device_at * table_local
    table_own = embed_table.astype(jnp.bfloat16)
    token_ids = tokens.reshape(-1)
    place_ids = jnp.broadcast_to(
        VOCAB + seq_at * tok_count + jnp.arange(tok_count, dtype=jnp.int32), (seqs, tok_count)
    ).reshape(-1)
    small_ids = VOCAB + seq_length + jnp.arange(12 * layers + 2, dtype=jnp.int32)
    local_rows = seqs * tok_count
    table_all = lax.all_gather(table_own, ("dp", "seq", "shard"), axis=0, tiled=True)
    state = table_all[token_ids].astype(jnp.float32) + table_all[place_ids].astype(jnp.float32)
    small = table_all[VOCAB + seq_length :].astype(jnp.float32)
    query_ids = lax.dynamic_slice_in_dim(block_ids, seq_at * tok_count, tok_count, 1)
    mats_low = layer_mats.astype(jnp.bfloat16)
    inputs = []
    kept = []
    for layer_at in range(layers):
        weights = gather_layer(mats_low[layer_at])
        inputs.append(state)
        kept.append(weights)
        state = layer_forward(
            state, weights, small[12 * layer_at : 12 * layer_at + 12], query_ids, block_ids
        )[0]
    final_gain = small[12 * layers]
    final_shift = small[12 * layers + 1]
    final = layer_norm(state, final_gain, final_shift).astype(jnp.bfloat16)
    group_mask = completion[0]
    slot_of = regroup[0]
    comp_rows = slot_of.shape[0] // shards
    counts = jnp.sum(group_mask.reshape(shards, local_rows), 1)
    starts = jnp.cumsum(counts) - counts
    base = starts[shard_at]
    mine = lax.dynamic_slice_in_dim(group_mask, shard_at * local_rows, local_rows)
    ones_first = jnp.argsort(1 - mine, stable=True)
    rank_of = jnp.zeros_like(slot_of).at[slot_of].set(jnp.arange(slot_of.shape[0], dtype=jnp.int32))
    offset = rank_of - base
    owned = (offset >= 0) & (offset < counts[shard_at])
    source = ones_first[jnp.clip(offset, 0, local_rows - 1)]
    outgoing = jnp.where(owned[:, None], final[source], bf_zero).reshape(shards, comp_rows, width)
    incoming = lax.all_to_all(outgoing, "shard", split_axis=0, concat_axis=0, tiled=True)
    regrouped = jnp.sum(incoming.astype(jnp.float32), 0).astype(jnp.bfloat16)
    rows_all = targets.shape[0]
    head_in = lax.all_gather(regrouped, ("dp", "seq", "shard"), axis=0, tiled=True)
    columns = first_row + jnp.arange(table_local, dtype=jnp.int32)
    live = (columns < VOCAB)[None, :]
    logits = dot_rows(head_in, table_own)
    masked = jnp.where(live, logits, MASK_FILL)
    top_local = jnp.max(masked, 1)
    total_local = jnp.sum(jnp.where(live, jnp.exp(masked - top_local[:, None]), 0.0), 1)
    target_hit = columns[None, :] == targets[:, None]
    pick_local = jnp.sum(jnp.where(target_hit, logits, 0.0), 1)
    highest, total, picked = joined_2(
        (top_local, total_local, pick_local), ("dp", "seq", "shard"), merge_soft
    )
    log_total = highest + jnp.log(total)
    loss_value = jnp.sum(log_total - picked) / rows_all
    probs = jnp.where(live, jnp.exp(masked - log_total[:, None]), 0.0)
    logit_grad = ((probs - target_hit.astype(jnp.float32)) / rows_all).astype(jnp.bfloat16)
    head_grad = dot_cols(logit_grad, head_in)
    head_back = lax.psum_scatter(
        dot_plain(logit_grad, table_own), ("dp", "seq", "shard"), scatter_dimension=0, tiled=True
    ).astype(jnp.bfloat16)
    my_ranks = lax.dynamic_slice_in_dim(rank_of, shard_at * comp_rows, comp_rows)
    owner = jnp.sum((my_ranks[:, None] >= starts[None, :]).astype(jnp.int32), 1) - 1
    sendback = jnp.where(
        owner[None, :, None] == jnp.arange(shards)[:, None, None], head_back[None], bf_zero
    )
    returned = lax.all_to_all(sendback, "shard", split_axis=0, concat_axis=0, tiled=True).reshape(
        shards * comp_rows, width
    )
    local_rank = base + jnp.cumsum(mine) - 1
    local_slot = slot_of[jnp.clip(local_rank, 0, slot_of.shape[0] - 1)]
    final_grad = jnp.where(mine[:, None] == 1, returned[local_slot], bf_zero).astype(jnp.float32)
    state_grad, gain_final, shift_final = norm_back(state, final_gain, final_shift, final_grad)
    mats_grads = [None] * layers
    small_grads = [None] * layers
    for layer_at in reversed(range(layers)):
        weights = gather_layer(mats_low[layer_at])
        state_grad, mats_part, small_part = layer_backward(
            inputs[layer_at],
            weights,
            small[12 * layer_at : 12 * layer_at + 12],
            query_ids,
            block_ids,
            state_grad,
        )
        mats_grads[layer_at] = lax.psum_scatter(
            mats_part, ("dp", "seq", "shard"), scatter_dimension=1, tiled=True
        )
        small_grads[layer_at] = small_part
    small_grad = jnp.concatenate(small_grads + [jnp.stack([gain_final, shift_final])], 0)
    value_all = jnp.concatenate([state_grad, small_grad], 0)
    index_pair = jnp.stack(
        [
            jnp.concatenate([token_ids, small_ids]),
            jnp.concatenate([place_ids, jnp.full(small_ids.shape, -1, jnp.int32)]),
        ],
        1,
    )
    gathered_vals = lax.all_gather(
        value_all.astype(jnp.bfloat16), ("dp", "seq", "shard"), axis=0, tiled=True
    ).astype(value_all.dtype)
    gathered_ids = lax.all_gather(index_pair, ("dp", "seq", "shard"), axis=0, tiled=True)
    table_grad = jnp.zeros((table_local, width), jnp.float32)
    for column in range(2):
        relative = gathered_ids[:, column] - first_row
        relative = jnp.where((relative >= 0) & (relative < table_local), relative, table_local)
        table_grad = table_grad.at[relative].add(gathered_vals, mode="drop")
    table_grad = table_grad + head_grad
    mats_grad = jnp.stack(mats_grads)
    local_squares = jnp.sum(mats_grad * mats_grad) + jnp.sum(table_grad * table_grad)
    grad_norm = jnp.sqrt(lax.psum(local_squares, ("dp", "seq", "shard")))
    factor = CLIP_NORM / grad_norm
    step = step_count[0].astype(jnp.float32)
    new_mats = adam_step(
        layer_mats, mats_moment, mats_square, factor * mats_grad, RATE_MATS, DECAY_RATE, step
    )
    plain_rows = (columns < VOCAB + seq_length)[:, None]
    rate = jnp.where(plain_rows, RATE_TABLE, RATE_SMALL)
    decay = jnp.where(plain_rows, DECAY_RATE, 0.0)
    new_table = adam_step(
        embed_table, table_moment, table_square, factor * table_grad, rate, decay, step
    )
    return (
        loss_value.reshape(1),
        grad_norm.reshape(1),
        new_mats[0],
        new_mats[1],
        new_mats[2],
        new_table[0],
        new_table[1],
        new_table[2],
    )


def solution(mesh):
    in_specs = (
        P(("dp", "shard"), "seq"),
        P(("dp", "shard"), None),
        P(("dp", "seq"), None),
        P(("dp", "seq"), None),
        P(),
        P(),
        P(None, None, ("dp", "seq", "shard"), None),
        P(None, None, ("dp", "seq", "shard"), None),
        P(None, None, ("dp", "seq", "shard"), None),
        P(("dp", "seq", "shard"), None),
        P(("dp", "seq", "shard"), None),
        P(("dp", "seq", "shard"), None),
    )
    out_specs = (
        P(),
        P(),
        P(None, None, ("dp", "seq", "shard"), None),
        P(None, None, ("dp", "seq", "shard"), None),
        P(None, None, ("dp", "seq", "shard"), None),
        P(("dp", "seq", "shard"), None),
        P(("dp", "seq", "shard"), None),
        P(("dp", "seq", "shard"), None),
    )
    return jax.shard_map(
        on_device, mesh=mesh, in_specs=in_specs, out_specs=out_specs, check_vma=False
    )
```

profile of v0, /device:TPU:0, one launch (start us, length us, event | category | flops | bytes accessed | tf_op | source)
XLA Modules:
  0.0 4965.6 jit_solution(11051250431661519673)
XLA Ops:
  17.5 587.7 %all-gather.32.cloned.1.call-done = bf16[32,1604,1088]{1,2,0:T(8,128)(2,1)} async-done(((bf16[1,1604,1088]{1,2,0:T(8,128)(2,1)}), bf16[32,1604,1088]{1,2,0:T(8,128)(2,1)}) %all-gather.32.cloned.1.call-update) | async-done | bytes 111689744 | tf_op jit(solution)/shard_map/all_gather | solution.py:258
  605.2 123.5 %copy.218 = bf16[32,1604,1088]{1,0,2:T(8,128)(2,1)} copy(bf16[32,1604,1088]{1,2,0:T(8,128)(2,1)} %all-gather.32.cloned.1.call-done) | data formatting | bytes 223379456 | tf_op jit(solution)/shard_map/all_gather | solution.py:258
  728.8 189.4 %reshape.846 = bf16[51328,1088]{0,1:T(8,128)(2,1)} reshape(bf16[32,1604,1088]{1,0,2:T(8,128)(2,1)} %copy.218) | data formatting | bytes 223379456
  918.2 134.3 %copy.219 = bf16[51328,1088]{1,0:T(8,128)(2,1)} copy(bf16[51328,1088]{0,1:T(8,128)(2,1)} %reshape.846) | data formatting | bytes 223379456
  1081.2 16.6 all-gather.20.cloned.1.call-done
  1097.8 14.3 fusion.136
  1153.0 152.0 %all-gather.30.cloned.1.call-done = bf16[1,3,4352,1088]{3,2,1,0:T(8,128)(2,1)} async-done(((bf16[1,3,136,1088]{3,2,1,0:T(8,128)(2,1)}), bf16[1,3,4352,1088]{3,2,1,0:T(8,128)(2,1)}) %all-gather.30.cloned.1.call-update) | async-done | bytes 28409872 | tf_op jit(solution)/shard_map/all_gather | solution.py:85
  1335.4 14.4 fusion.139
  1392.1 20.7 all_to_all.10
  1413.7 61.7 %all-gather.26.cloned.1.call-done = bf16[2048,1088]{1,0:T(8,128)(2,1)} async-done(((bf16[64,1088]{1,0:T(8,128)(2,1)}), bf16[2048,1088]{1,0:T(8,128)(2,1)}) %all-gather.26.cloned.1.call-update) | async-done | bytes 4456464 | tf_op jit(solution)/shard_map/all_gather | solution.py:291
  1475.5 13.5 select_reduce_fusion.1
  1494.3 67.2 %all-gather.4 = bf16[65536]{0:T(1024)(128)(2,1)S(1)} all-gather(bf16[2048]{0:T(1024)(128)(2,1)S(1)} %get-tuple-element.239), channel_id=6, replica_groups=mesh['dp'=2,'seq'=4,'shard'=4] {'dp','seq','shard'}, dimensions={0}, use_global_device_ids=true | all-gather | bytes 135168 | tf_op jit(solution)/shard_map/all_gather | solution.py:27
  1561.6 64.3 %all-gather.3 = bf16[65536]{0:T(1024)(128)(2,1)S(1)} all-gather(bf16[2048]{0:T(1024)(128)(2,1)S(1)} %get-tuple-element.240), channel_id=5, replica_groups=mesh['dp'=2,'seq'=4,'shard'=4] {'dp','seq','shard'}, dimensions={0}, use_global_device_ids=true | all-gather | bytes 135168 | tf_op jit(solution)/shard_map/all_gather | solution.py:27
  1626.1 66.6 %all-gather.2 = bf16[65536]{0:T(1024)(128)(2,1)S(1)} all-gather(bf16[2048]{0:T(1024)(128)(2,1)S(1)} %convert_element_type.407), channel_id=4, replica_groups=mesh['dp'=2,'seq'=4,'shard'=4] {'dp','seq','shard'}, dimensions={0}, use_global_device_ids=true | all-gather | bytes 135168 | tf_op jit(solution)/shard_map/all_gather | solution.py:27
  1707.8 15.3 fusion.117
  1723.8 132.1 %reduce-scatter.6.cloned.1.call-done = f32[64,1088]{1,0:T(8,128)} async-done(((f32[2048,1088]{1,0:T(8,128)}), f32[64,1088]{1,0:T(8,128)}) %reduce-scatter.6.cloned.1.call-update) | async-done | bytes 278544 | tf_op jit(solution)/shard_map/reduce_scatter | solution.py:308
  1948.4 14.2 reduce-scatter.8.cloned.1.call-done
  1962.7 35.5 reduce-scatter.10.cloned.1.call-done
  2101.4 37.9 pad_maximum_fusion.1
  2139.4 77.0 %copy.229 = f32[3,4352,1088]{2,0,1:T(4,128)} copy(f32[3,4352,1088]{1,2,0:T(8,128)} %pad_maximum_fusion.1) | data formatting | bytes 113639424 | tf_op jit(solution)/shard_map/stack | solution.py:203
  2260.3 39.0 pad_maximum_fusion
  2299.3 78.5 %copy.227 = f32[3,4352,1088]{2,0,1:T(4,128)} copy(f32[3,4352,1088]{1,2,0:T(8,128)} %pad_maximum_fusion) | data formatting | bytes 113639424 | tf_op jit(solution)/shard_map/stack | solution.py:203
  2424.6 71.6 %all-gather.6 = s32[32,282,2]{1,2,0:T(2,128)S(1)} all-gather(s32[1,282,2]{1,2,0:T(2,128)S(1)} %add_bitcast_fusion), channel_id=1, replica_groups=mesh['dp'=2,'seq'=4,'shard'=4] {'dp','seq','shard'}, dimensions={0}, use_global_device_ids=true | all-gather | bytes 74448 | tf_op jit(solution)/shard_map/all_gather | solution.py:351
  2516.4 14.2 fusion.146
  2530.6 823.3 %all-reduce.8.cloned.1.call-done = f32[3,4352,1088]{2,0,1:T(4,128)} async-done(((f32[3,4352,1088]{2,0,1:T(4,128)}), f32[3,4352,1088]{2,0,1:T(4,128)}) %all-reduce.8.cloned.1.call-update) | async-done | bytes 56819728
  3356.1 1138.3 %all-reduce.6.cloned.1.call-done = f32[3,4352,1088]{2,0,1:T(4,128)} async-done(((f32[3,4352,1088]{2,0,1:T(4,128)}), f32[3,4352,1088]{2,0,1:T(4,128)}) %all-reduce.6.cloned.1.call-update) | async-done | bytes 56819728
  4499.5 133.4 %all-gather.34.cloned.1.call-done = bf16[32,282,1088]{2,1,0:T(8,128)(2,1)} async-done(((bf16[1,282,1088]{2,1,0:T(8,128)(2,1)}), bf16[32,282,1088]{2,1,0:T(8,128)(2,1)}) %all-gather.34.cloned.1.call-update) | async-done | bytes 19636240 | tf_op jit(solution)/shard_map/all_gather | solution.py:348
  4632.9 40.5 reshape.851
  4673.4 90.8 %scatter_fusion = f32[1604,1088]{1,0:T(8,128)} fusion(f32[1604,1088]{1,0:T(8,128)} %fusion.146, s32[9024]{0:T(1024)S(1)} %get-tuple-element.277, f32[9024,1088]{1,0:T(8,128)} %reshape.851), kind=kCustom, calls=%fused_computation.7 | custom fusion | flops 9818112 | bytes 117853440 | tf_op jit(solution)/shard_map/scatter-add | solution.py:356
  4764.2 91.0 %scatter_fusion.1 = f32[1604,1088]{1,0:T(8,128)} fusion(f32[1604,1088]{1,0:T(8,128)} %scatter_fusion, s32[9024]{0:T(1024)S(1)} %copy-done.51, f32[9024,1088]{1,0:T(8,128)} %reshape.851), kind=kCustom, calls=%fused_computation.8 | custom fusion | flops 9818112 | bytes 117853440 | tf_op jit(solution)/shard_map/scatter-add | solution.py:356
  4862.8 38.7 psum.7
  4902.2 19.6 multiply_subtract_fusion
  (619 shorter events, 528.5 us)
Async XLA Ops:
  7.2 598.0 %all-gather.32.cloned.1.call-start = ((), (), s32[]{:S(2)}) async-start(), calls=%async_computation.19 | async-start | bytes 119488512 | tf_op jit(solution)/shard_map/all_gather | solution.py:258
  12.5 1055.0 %all-gather.28.cloned.1.call-start = ((), (), s32[]{:S(2)}) async-start(), calls=%async_computation.17 | async-start | bytes 31021056 | tf_op jit(solution)/shard_map/all_gather | solution.py:85
  16.2 1081.6 %all-gather.20.cloned.1.call-start = ((), (), s32[]{:S(2)}) async-start(), calls=%async_computation.8 | async-start | bytes 2785280 | tf_op jit(solution)/shard_map/all_gather | solution.py:99
  1056.2 76.1 %copy-start.4 = (bf16[256,1088]{0,1:T(8,128)(2,1)}, bf16[256,1088]{0,1:T(8,128)(2,1)S(1)}, u32[]{:S(2)}) copy-start(bf16[256,1088]{0,1:T(8,128)(2,1)S(1)} %copy.222) | copy-start | bytes 1671172
  1060.0 72.4 %copy-start.6 = (bf16[256,1088]{0,1:T(8,128)(2,1)}, bf16[256,1088]{0,1:T(8,128)(2,1)S(1)}, u32[]{:S(2)}) copy-start(bf16[256,1088]{0,1:T(8,128)(2,1)S(1)} %copy.220) | copy-start | bytes 1671172
  1067.4 68.3 %copy-start.47 = (f32[1088]{0:T(1024)}, f32[1088]{0:T(1024)S(1)}, u32[]{:S(2)}) copy-start(f32[1088]{0:T(1024)S(1)} %get-tuple-element.270) | copy-start | bytes 13060
  1067.4 68.3 %copy-start.54 = (f32[1088]{0:T(1024)}, f32[1088]{0:T(1024)S(1)}, u32[]{:S(2)}) copy-start(f32[1088]{0:T(1024)S(1)} %get-tuple-element.269) | copy-start | bytes 13060
  1067.5 237.6 %copy-start.58 = (f32[1088]{0:T(1024)}, f32[1088]{0:T(1024)S(1)}, u32[]{:S(2)}) copy-start(f32[1088]{0:T(1024)S(1)} %get-tuple-element.267) | copy-start | bytes 13060
  1067.5 237.6 %copy-start.68 = (f32[1088]{0:T(1024)}, f32[1088]{0:T(1024)S(1)}, u32[]{:S(2)}) copy-start(f32[1088]{0:T(1024)S(1)} %get-tuple-element.266) | copy-start | bytes 13060
  1067.5 305.6 %copy-start.56 = (f32[1088]{0:T(1024)}, f32[1088]{0:T(1024)S(1)}, u32[]{:S(2)}) copy-start(f32[1088]{0:T(1024)S(1)} %get-tuple-element.261) | copy-start | bytes 13060
  1075.9 47.5 all-gather.18.cloned.1.call-start
  1078.9 226.2 %all-gather.30.cloned.1.call-start = ((), (), s32[]{:S(2)}) async-start(), calls=%async_computation.18 | async-start | bytes 31021056 | tf_op jit(solution)/shard_map/all_gather | solution.py:85
  1079.5 255.9 %all-gather.24.cloned.1.call-start = ((), (), s32[]{:S(2)}) async-start(), calls=%async_computation.10 | async-start | bytes 2785280 | tf_op jit(solution)/shard_map/all_gather | solution.py:99
  1152.8 216.9 %copy-start.16 = (f32[256,1088]{0,1:T(8,128)}, f32[256,1088]{0,1:T(8,128)S(1)}, u32[]{:S(2)}) copy-start(f32[256,1088]{0,1:T(8,128)S(1)} %get-tuple-element.330) | copy-start | bytes 3342340
  1152.8 158.0 %copy-start.78 = (f32[256]{0:T(256)}, f32[256]{0:T(256)S(1)}, u32[]{:S(2)}) copy-start(f32[256]{0:T(256)S(1)} %broadcast_multiply_fusion.2) | copy-start | bytes 3076
  1153.0 157.8 %copy-start.98 = (f32[256]{0:T(256)}, f32[256]{0:T(256)S(1)}, u32[]{:S(2)}) copy-start(f32[256]{0:T(256)S(1)} %multiply_reduce_fusion.14) | copy-start | bytes 3076
  1153.0 152.1 %copy-start.92 = (f32[256]{0:T(256)}, f32[256]{0:T(256)S(1)}, u32[]{:S(2)}) copy-start(f32[256]{0:T(256)S(1)} %fusion.98) | copy-start | bytes 3076
  1313.5 47.7 all-gather.22.cloned.1.call-start
  1316.5 159.0 %all-gather.26.cloned.1.call-start = ((), (), s32[]{:S(2)}) async-start(), calls=%async_computation.11 | async-start | bytes 4866048 | tf_op jit(solution)/shard_map/all_gather | solution.py:291
  1413.6 442.2 %reduce-scatter.6.cloned.1.call-start = ((), (), s32[]{:S(2)}) async-start(), calls=%async_computation.12 | async-start | bytes 9732096 | tf_op jit(solution)/shard_map/reduce_scatter | solution.py:308
  1413.7 75.2 %copy-start.72 = (s32[2048]{0:T(1024)S(1)}, s32[2048]{0:T(1024)}, u32[]{:S(2)}) copy-start(s32[2048]{0:T(1024)} %param.18) | copy-start | bytes 24580
  1857.8 17.8 all-to-all-start.1
  1861.4 101.2 %reduce-scatter.8.cloned.1.call-start = ((), (), s32[]{:S(2)}) async-start(), calls=%async_computation.13 | async-start | bytes 2785280 | tf_op jit(solution)/shard_map/reduce_scatter | solution.py:165
  1931.3 66.8 %reduce-scatter.10.cloned.1.call-start = ((), (), s32[]{:S(2)}) async-start(), calls=%async_computation.14 | async-start | bytes 2785280 | tf_op jit(solution)/shard_map/reduce_scatter | solution.py:171
  1940.6 57.6 %copy-start.17 = (f32[256,1088]{0,1:T(8,128)S(1)}, f32[256,1088]{0,1:T(8,128)}, u32[]{:S(2)}) copy-start(f32[256,1088]{0,1:T(8,128)} %copy-done.16) | copy-start | bytes 3342340
  1940.6 306.4 %reduce-scatter.12.cloned.1.call-start = ((), (), s32[]{:S(2)}) async-start(), calls=%async_computation.15 | async-start | bytes 2785280 | tf_op jit(solution)/shard_map/reduce_scatter | solution.py:165
  2058.9 188.1 %reduce-scatter.14.cloned.1.call-start = ((), (), s32[]{:S(2)}) async-start(), calls=%async_computation.16 | async-start | bytes 2785280 | tf_op jit(solution)/shard_map/reduce_scatter | solution.py:171
  2088.0 1265.8 %all-reduce.8.cloned.1.call-start = ((), (), s32[]{:S(2)}) async-start(), calls=%async_computation.22 | async-start | bytes 160432128
  2216.4 2278.0 %all-reduce.6.cloned.1.call-start = ((), (), s32[]{:S(2)}) async-start(), calls=%async_computation.21 | async-start | bytes 160432128
  2378.0 2254.9 %all-gather.34.cloned.1.call-start = ((), (), s32[]{:S(2)}) async-start(), calls=%async_computation.20 | async-start | bytes 21897216 | tf_op jit(solution)/shard_map/all_gather | solution.py:348
  3356.1 1140.6 %copy-start.13 = (f32[3,136,1088]{2,1,0:T(8,128)}, f32[3,136,1088]{2,1,0:T(8,128)S(1)}, u32[]{:S(2)}) copy-start(f32[3,136,1088]{2,1,0:T(8,128)S(1)} %copy.264) | copy-start | bytes 5326852
  4673.4 90.8 %copy-start.51 = (s32[9024]{0:T(1024)S(1)}, s32[9024]{0:T(1024)}, u32[]{:S(2)}) copy-start(s32[9024]{0:T(1024)} %get-tuple-element.276) | copy-start | bytes 108292
  (107 other events, 1181.5 us)
Sparse Core Ops, SparseCore 0:
  12.6 592.5 all-gather.31
  608.8 176.4 all-gather.27
  1076.0 21.6 all-gather.19
  1099.8 23.5 all-gather.17
  1126.8 178.2 all-gather.29
  1313.6 21.7 all-gather.23
  1337.5 23.5 all-gather.21
  1413.8 61.6 all-gather.25
  1723.2 132.6 reduce-scatter.5
  1931.5 31.1 reduce-scatter.7
  1965.8 32.2 reduce-scatter.9
  2059.0 32.2 reduce-scatter.11
  2094.4 32.2 reduce-scatter.13
  2216.5 1137.3 all-reduce.7
  3360.1 1134.2 all-reduce.5
  4498.0 134.8 all-gather.33
where the time goes:
time: 4980 us; the launch traced here: 4970 us
  waiting for transfers between devices  3140 us (63%)
  local copies, waits for them, and re-layouts  767 us (15%)
  other arithmetic  396 us (8%)
  blocking collectives  329 us (7%)
  matrix products  308 us (6%)
    unnamed x18, waiting for transfers between devices  1960 us
    all_gather x1, waiting for transfers between devices, on_device(): lax.all_gather(table_own, ('dp', 'seq', 'shard'), axis=0, tiled=True)  588 us
    unnamed x257, local copies, waits for them, and re-layouts  394 us
    all_gather x3, blocking collectives, joined_2(): lax.all_gather(part.astype(kind), axis)  198 us
    scatter-add x2, other arithmetic, on_device(): table_grad = table_grad.at[relative].add(gathered_vals, mode='drop')  182 us
    another operation x2, local copies, waits for them, and re-layouts, layer_backward(): jnp.stack([jnp.concatenate([grad_joined, grad_proj], 0), grad_up, grad_do...  156 us
    all_gather x2, waiting for transfers between devices, gather_layer(): return lax.all_gather(mats_one, ('dp', 'seq', 'shard'), axis=1, tiled=True)  152 us
    all_gather x1, waiting for transfers between devices, on_device(): lax.all_gather(value_all.astype(jnp.bfloat16), ('dp', 'seq', 'shard'), ax...  133 us
  transfers between devices with their start and end apart: 17, of which 14 were waited for; matrix products, arithmetic and copies ran while one was open for 19% of the time, Pallas kernels for 0%

commit v1 on v0

v1 whole, which is shorter than its diff:
```python
import itertools
from functools import partial

import jax
import jax.numpy as jnp
from jax import lax
from jax.experimental import pallas as pl
from jax.experimental.layout import Layout, with_layout_constraint
from jax.experimental.pallas import tpu as pltpu
from jax.sharding import PartitionSpec as P

HEADS = 17
HEAD = 64
VOCAB = 50278

NORM_EPS = 1e-05
CLIP_NORM = 0.02
BETA_ONE = 0.9
BETA_TWO = 0.95
ADAM_EPS = 1e-08
DECAY_RATE = 0.1
RATE_MATS = 0.05
RATE_TABLE = 0.1
RATE_SMALL = 0.5
MASK_FILL = -1e30

AXES = ("dp", "seq", "shard")
MESH = pl.DeviceIdType.MESH
SLOTS = 24


def bits_of(axis):
    return [(axis, b) for b in range(lax.axis_size(axis).bit_length() - 1)]


def bit_here(bit):
    return lax.rem(lax.axis_index(bit[0]) // 2 ** bit[1], 2)


def partner(bit):
    at = lax.axis_index(bit[0])
    return {bit[0]: at + (1 - 2 * bit_here(bit)) * 2 ** bit[1]}


def greet(bits):
    barrier = pltpu.get_barrier_semaphore()
    for bit in bits:
        pl.semaphore_signal(barrier, inc=1, device_id=partner(bit), device_id_type=MESH)
    pl.semaphore_wait(barrier, len(bits))


def block_weight(axes, bit):
    weight = 2 ** bit[1]
    for axis in axes[axes.index(bit[0]) + 1 :]:
        weight *= lax.axis_size(axis)
    return weight


def block_runs(weights):
    weights = sorted(weights)
    joined = 0
    while joined < len(weights) and weights[joined] == 2**joined:
        joined += 1
    rest = [(0, w) for w in weights[joined:]]
    return 2**joined, [sum(c) for c in itertools.product(*rest)]


def exchange_kernel(sum_axes, sum_orders, join_axes, join_orders, rows, *refs):
    it = iter(refs)
    x_ref, o_ref = next(it), next(it)
    work, parcel, recv = (next(it), next(it), next(it)) if sum_axes else (None, None, None)
    send_sems, recv_sems = next(it), next(it)
    streams = max(len(sum_orders), len(join_orders))
    share = rows // streams
    spans = [pl.ds(s * share, share) for s in range(streams)]
    greet(sorted(set(sum(sum_orders, []) + sum(join_orders, []))))
    count = itertools.count()
    if sum_axes:
        slot = [0] * streams
        for step in range(len(sum_orders[0])):
            started = []
            source = x_ref if step == 0 else work
            for s, order in enumerate(sum_orders):
                bit = order[step]
                base = sum(bit_here(b) * block_weight(sum_axes, b) for b in order[:step])
                weight = block_weight(sum_axes, bit)
                mine = bit_here(bit)
                size, offsets = block_runs([block_weight(sum_axes, b) for b in order[step + 1 :]])
                for offset in offsets:
                    k = next(count)
                    leave = base + (1 - mine) * weight + offset
                    if source.dtype == parcel.dtype:
                        packed = source.at[pl.ds(leave, size), spans[s]]
                    else:

                        def pack(i, carry, s=s, leave=leave, at=slot[s], source=source):
                            parcel[at + i, spans[s]] = source[leave + i, spans[s]].astype(parcel.dtype)
                            return carry

                        lax.fori_loop(0, size, pack, 0)
                        packed = parcel.at[pl.ds(slot[s], size), spans[s]]
                    copy = pltpu.make_async_remote_copy(
                        packed,
                        recv.at[pl.ds(slot[s], size), spans[s]],
                        send_sems.at[k],
                        recv_sems.at[k],
                        device_id=partner(bit),
                        device_id_type=MESH,
                    )
                    copy.start()
                    started.append((copy, s, base + mine * weight + offset, slot[s], size))
                    slot[s] += size
            for copy, s, keep, at, size in started:
                copy.wait()

                def add(i, carry, s=s, keep=keep, at=at, source=source):
                    total = source[keep + i, spans[s]].astype(jnp.float32)
                    total = total + recv[at + i, spans[s]].astype(jnp.float32)
                    work[keep + i, spans[s]] = total.astype(work.dtype)
                    return carry

                lax.fori_loop(0, size, add, 0)
        result = work[sum(bit_here(b) * block_weight(sum_axes, b) for b in sum_orders[0])]
    else:
        result = x_ref[0]
    result = result.astype(o_ref.dtype)
    if not join_axes:
        o_ref[...] = result
        return
    o_ref[sum(bit_here(b) * block_weight(join_axes, b) for b in join_orders[0])] = result
    for step in range(len(join_orders[0])):
        started = []
        for s, order in enumerate(join_orders):
            bit = order[step]
            base = sum(bit_here(b) * block_weight(join_axes, b) for b in order[step:])
            size, offsets = block_runs([block_weight(join_axes, b) for b in order[:step]])
            for offset in offsets:
                k = next(count)
                here = o_ref.at[pl.ds(base + offset, size), spans[s]]
                copy = pltpu.make_async_remote_copy(
                    here,
                    here,
                    send_sems.at[k],
                    recv_sems.at[k],
                    device_id=partner(bit),
                    device_id_type=MESH,
                )
                copy.start()
                started.append(copy)
        for copy in started:
            copy.wait()


def exchange(x, name, number, sum_axes=(), sum_orders=(), join_axes=(), join_orders=()):
    rows, width = x.shape[-2:]
    blocks = 1
    for axis in join_axes:
        blocks *= lax.axis_size(axis)
    out = (blocks, rows, width) if join_axes else (rows, width)
    kind = jnp.bfloat16 if sum_axes else x.dtype
    sends = 0
    for step in range(len(sum_orders[0]) if sum_orders else 0):
        for order in sum_orders:
            sends += len(block_runs([block_weight(sum_axes, b) for b in order[step + 1 :]])[1])
    for step in range(len(join_orders[0]) if join_orders else 0):
        for order in join_orders:
            sends += len(block_runs([block_weight(join_axes, b) for b in order[:step]])[1])
    scratch = []
    if sum_axes:
        if x.size * 14 > 56 * 2**20:
            x = x.astype(jnp.bfloat16)
        scratch = [
            pltpu.VMEM(x.shape, jnp.float32 if x.dtype == jnp.float32 or x.size < 2**22 else kind),
            pltpu.VMEM(x.shape, kind),
            pltpu.VMEM(x.shape, kind),
        ]
    scratch += [pltpu.SemaphoreType.DMA((sends,)), pltpu.SemaphoreType.DMA((sends,))]
    return pl.pallas_call(
        partial(exchange_kernel, sum_axes, sum_orders, join_axes, join_orders, rows),
        out_shape=jax.ShapeDtypeStruct(out, kind),
        in_specs=[pl.BlockSpec(memory_space=pltpu.VMEM)],
        out_specs=pl.BlockSpec(memory_space=pltpu.VMEM),
        scratch_shapes=scratch,
        compiler_params=pltpu.CompilerParams(
            collective_id=number, has_side_effects=True, vmem_limit_bytes=60 * 2**20
        ),
        name=name,
    )(x)


def combine_kernel(bits, combine, x_ref, o_ref, out_buf, in_buf, send_sems, recv_sems):
    greet(bits)
    current = x_ref[...]
    for i, bit in enumerate(bits):
        out_buf[i] = current
        copy = pltpu.make_async_remote_copy(
            out_buf.at[i],
            in_buf.at[i],
            send_sems.at[i],
            recv_sems.at[i],
            device_id=partner(bit),
            device_id_type=MESH,
        )
        copy.start()
        copy.wait()
        other = in_buf[i]
        low = bit_here(bit) == 0
        current = combine(jnp.where(low, current, other), jnp.where(low, other, current))
    o_ref[...] = current


def combine_all(x, combine, name, number):
    bits = [bit for axis in reversed(AXES) for bit in bits_of(axis)]
    slots = (len(bits),) + x.shape
    return pl.pallas_call(
        partial(combine_kernel, bits, combine),
        out_shape=jax.ShapeDtypeStruct(x.shape, x.dtype),
        in_specs=[pl.BlockSpec(memory_space=pltpu.VMEM)],
        out_specs=pl.BlockSpec(memory_space=pltpu.VMEM),
        scratch_shapes=[
            pltpu.VMEM(slots, x.dtype),
            pltpu.VMEM(slots, x.dtype),
            pltpu.SemaphoreType.DMA((len(bits),)),
            pltpu.SemaphoreType.DMA((len(bits),)),
        ],
        compiler_params=pltpu.CompilerParams(collective_id=number, has_side_effects=True),
        name=name,
    )(x)


def swap_kernel(x_ref, o_ref, send_sems, recv_sems, own_sem):
    seq_size, shard_size = lax.axis_size("seq"), lax.axis_size("shard")
    total = lax.axis_size("dp") * seq_size * shard_size
    me = (lax.axis_index("dp") * seq_size + lax.axis_index("seq")) * shard_size + lax.axis_index("shard")

    def place(at):
        return {
            "dp": at // (seq_size * shard_size),
            "seq": lax.rem(at // shard_size, seq_size),
            "shard": lax.rem(at, shard_size),
        }

    barrier = pltpu.get_barrier_semaphore()

    def hello(k, carry):
        pl.semaphore_signal(
            barrier, inc=1, device_id=place(lax.rem(me + k, total)), device_id_type=MESH
        )
        return carry

    lax.fori_loop(1, total, hello, 0)
    pl.semaphore_wait(barrier, total - 1)
    keep = pltpu.make_async_copy(x_ref.at[me], o_ref.at[me], own_sem)
    keep.start()

    def send(k, carry):
        to = lax.rem(me + k, total)
        pltpu.make_async_remote_copy(
            x_ref.at[to],
            o_ref.at[me],
            send_sems.at[to],
            recv_sems.at[me],
            device_id=place(to),
            device_id_type=MESH,
        ).start()
        return carry

    lax.fori_loop(1, total, send, 0)

    def finish(k, carry):
        other = lax.rem(me + k, total)
        pltpu.make_async_remote_copy(
            x_ref.at[other],
            o_ref.at[other],
            send_sems.at[other],
            recv_sems.at[other],
            device_id=place(other),
            device_id_type=MESH,
        ).wait()
        return carry

    lax.fori_loop(1, total, finish, 0)
    keep.wait()


def swap(x, name, number):
    total = x.shape[0]
    return pl.pallas_call(
        swap_kernel,
        out_shape=jax.ShapeDtypeStruct(x.shape, x.dtype),
        in_specs=[pl.BlockSpec(memory_space=pl.ANY)],
        out_specs=pl.BlockSpec(memory_space=pl.ANY),
        scratch_shapes=[
            pltpu.SemaphoreType.DMA((total,)),
            pltpu.SemaphoreType.DMA((total,)),
            pltpu.SemaphoreType.DMA,
        ],
        compiler_params=pltpu.CompilerParams(collective_id=number, has_side_effects=True),
        name=name,
    )(x)


def add_pair(first, second):
    return first + second


def merge_soft(first, second):
    highest = jnp.maximum(first[0], second[0])
    total = first[1] * jnp.exp(first[0] - highest) + second[1] * jnp.exp(second[0] - highest)
    return jnp.stack([highest, total, first[2] + second[2]])


def dot_rows(left_op, right_op):
    return lax.dot_general(
        left_op, right_op, (((1,), (1,)), ((), ())), preferred_element_type=jnp.float32
    )


def dot_cols(left_op, right_op):
    return lax.dot_general(
        left_op, right_op, (((0,), (0,)), ((), ())), preferred_element_type=jnp.float32
    )


def dot_plain(left_op, right_op):
    return jnp.dot(left_op, right_op, preferred_element_type=jnp.float32)


def column_sums(values):
    return jnp.sum(values.astype(jnp.float32), 0)


def layer_norm(values, gain, shift):
    center = values - jnp.mean(values, -1, keepdims=True)
    spread = jnp.mean(center * center, -1, keepdims=True)
    return center * lax.rsqrt(spread + NORM_EPS) * gain + shift


def norm_back(values, gain, shift, grad):
    unused, pull = jax.vjp(layer_norm, values, gain, shift)
    return pull(grad)


def one_hot(wanted, length, axis):
    shape = list(wanted.shape)
    shape.insert(axis, length)
    at = lax.broadcasted_iota(jnp.int32, shape, axis)
    return (at == jnp.expand_dims(wanted, axis)).astype(jnp.bfloat16)


def counts_before(flags):
    length = flags.shape[-1]
    earlier = (
        lax.broadcasted_iota(jnp.int32, (length, length), 0)
        < lax.broadcasted_iota(jnp.int32, (length, length), 1)
    ).astype(jnp.bfloat16)
    return dot_plain(flags.astype(jnp.bfloat16), earlier).astype(jnp.int32)


def seq_orders():
    return [bits_of("seq")]


def share_keys(key_rows, val_rows):
    rows, width = key_rows.shape
    pair = jnp.concatenate([key_rows, val_rows], 0)[None]
    both = exchange(
        pair, "share_keys", 4, join_axes=("seq",), join_orders=[bits_of("seq")[::-1]]
    )
    groups = both.shape[0]
    return (
        both[:, :rows].reshape(groups * rows, HEADS, HEAD),
        both[:, rows:].reshape(groups * rows, HEADS, HEAD),
    )


def return_grads(key_part, val_part):
    groups = lax.axis_size("seq")
    rows = key_part.shape[0] // groups
    width = HEADS * HEAD
    pair = jnp.concatenate(
        [key_part.reshape(groups, rows, width), val_part.reshape(groups, rows, width)], 1
    )
    own = exchange(pair, "return_grads", 8, sum_axes=("seq",), sum_orders=[bits_of("seq")])
    return own[:rows], own[rows:]


def layer_forward(state, weights, params, query_ids, key_ids):
    width = state.shape[1]
    scale = HEAD ** (-0.5)
    hidden = layer_norm(state, params[0], params[1]).astype(jnp.bfloat16)
    joined = dot_rows(hidden, weights[0, : 3 * width])
    queries = (joined[:, :width] + params[2]).astype(jnp.bfloat16)
    key_rows = joined[:, width : 2 * width].astype(jnp.bfloat16)
    val_rows = (joined[:, 2 * width :] + params[3]).astype(jnp.bfloat16)
    key_seq, val_seq = share_keys(key_rows, val_rows)
    query_seq = queries.reshape(-1, HEADS, HEAD)
    scores = (
        jnp.einsum("qhd,khd->hqk", query_seq, key_seq, preferred_element_type=jnp.float32) * scale
    )
    allowed = key_ids[None, None, :] <= query_ids[None, :, None]
    scores = jnp.where(allowed, scores, MASK_FILL)
    raised = jnp.exp(scores - jnp.max(scores, -1, keepdims=True))
    probs = raised / jnp.sum(raised, -1, keepdims=True)
    attended = jnp.einsum(
        "hqk,khd->qhd", probs.astype(jnp.bfloat16), val_seq, preferred_element_type=jnp.float32
    )
    attended = attended.reshape(-1, width).astype(jnp.bfloat16)
    mid_state = state + dot_plain(attended, weights[0, 3 * width :]) + params[4]
    normed = layer_norm(mid_state, params[5], params[6]).astype(jnp.bfloat16)
    upward = dot_rows(normed, weights[1]) + params[8:12].reshape(-1)
    active = jax.nn.gelu(upward, approximate=True).astype(jnp.bfloat16)
    output = mid_state + dot_plain(active, weights[2]) + params[7]
    return (
        output,
        (hidden, query_seq, key_seq, val_seq, probs, attended, mid_state, normed, upward, active),
    )


def rows_major(x):
    return with_layout_constraint(x, Layout(major_to_minor=tuple(range(x.ndim))))


def scatter_rows(grad):
    total = lax.axis_size(AXES)
    blocks = rows_major(grad.astype(jnp.bfloat16)).reshape(total, -1, grad.shape[1])
    return lax.psum_scatter(blocks, AXES, scatter_dimension=0, tiled=True)[0]


def layer_backward(state, weights, params, saved, grad_in):
    width = state.shape[1]
    scale = HEAD ** (-0.5)
    hidden, query_seq, key_seq, val_seq, probs, attended, mid_state, normed, upward, active = saved
    down_grad = grad_in.astype(jnp.bfloat16)
    grad_down = scatter_rows(dot_cols(active, down_grad))
    act_grad = dot_rows(down_grad, weights[2])
    unused_gelu, gelu_pull = jax.vjp(partial(jax.nn.gelu, approximate=True), upward)
    up_grad = gelu_pull(act_grad)[0].astype(jnp.bfloat16)
    grad_up = scatter_rows(dot_cols(up_grad, normed))
    mid_back, gain_two, shift_two = norm_back(
        mid_state, params[5], params[6], dot_plain(up_grad, weights[1])
    )
    mid_grad = grad_in + mid_back
    out_grad = mid_grad.astype(jnp.bfloat16)
    grad_proj = dot_cols(attended, out_grad)
    att_grad = dot_rows(out_grad, weights[0, 3 * width :]).astype(jnp.bfloat16)
    att_seq = att_grad.reshape(query_seq.shape)
    prob_grad = jnp.einsum("qhd,khd->hqk", att_seq, val_seq, preferred_element_type=jnp.float32)
    val_part = jnp.einsum(
        "hqk,qhd->khd", probs.astype(jnp.bfloat16), att_seq, preferred_element_type=jnp.float32
    )
    score_grad = (probs * (prob_grad - jnp.sum(probs * prob_grad, -1, keepdims=True))).astype(
        jnp.bfloat16
    )
    query_grad = (
        jnp.einsum("hqk,khd->qhd", score_grad, key_seq, preferred_element_type=jnp.float32) * scale
    )
    query_grad = query_grad.reshape(-1, width).astype(jnp.bfloat16)
    key_part = (
        jnp.einsum("hqk,qhd->khd", score_grad, query_seq, preferred_element_type=jnp.float32)
        * scale
    )
    key_grad, val_grad = return_grads(key_part, val_part)
    joined_grad = jnp.concatenate([query_grad, key_grad, val_grad], 1)
    grad_joined = dot_cols(joined_grad, hidden)
    state_back, gain_one, shift_one = norm_back(
        state, params[0], params[1], dot_plain(joined_grad, weights[0, : 3 * width])
    )
    small_grad = jnp.concatenate(
        [
            jnp.stack(
                [
                    gain_one,
                    shift_one,
                    column_sums(query_grad),
                    column_sums(val_grad),
                    column_sums(out_grad),
                    gain_two,
                    shift_two,
                    column_sums(down_grad),
                ]
            ),
            column_sums(up_grad).reshape(4, width),
        ],
        0,
    )
    grad_first = scatter_rows(jnp.concatenate([grad_joined, grad_proj], 0))
    mats_grad = jnp.stack([grad_first, grad_up, grad_down]).astype(jnp.float32)
    return (mid_grad + state_back, mats_grad, small_grad)


def adam_step(weights, moment, square, grad, rate, decay, step):
    moment = BETA_ONE * moment + (1 - BETA_ONE) * grad
    square = BETA_TWO * square + (1 - BETA_TWO) * grad * grad
    moment_hat = moment / (1 - BETA_ONE**step)
    square_hat = square / (1 - BETA_TWO**step)
    weights = weights - rate * (moment_hat / (jnp.sqrt(square_hat) + ADAM_EPS) + decay * weights)
    return (weights, moment, square)


def pad_rows(x, rows):
    return jnp.pad(x, ((0, rows - x.shape[0]), (0, 0)))


def on_device(
    tokens,
    block_ids,
    completion,
    regroup,
    targets,
    step_count,
    layer_mats,
    mats_moment,
    mats_square,
    embed_table,
    table_moment,
    table_square,
):
    seqs, tok_count = tokens.shape
    seq_length = block_ids.shape[1]
    width = embed_table.shape[1]
    table_local = embed_table.shape[0]
    layers = layer_mats.shape[0]
    replicas, groups, shards = (lax.axis_size(axis) for axis in AXES)
    total = replicas * groups * shards
    seq_at = lax.axis_index("seq")
    shard_at = lax.axis_index("shard")
    device_at = lax.axis_index(AXES)
    seq_bits, dp_bits, shard_bits = bits_of("seq"), bits_of("dp"), bits_of("shard")
    first_row = device_at * table_local
    table_own = embed_table.astype(jnp.bfloat16)
    mats_low = layer_mats.astype(jnp.bfloat16)
    token_ids = tokens.reshape(-1)
    local_rows = token_ids.shape[0]
    small_count = 12 * layers + 2
    small_rows = -(-small_count // 16) * 16

    ids_all = exchange(
        jnp.pad(token_ids, (0, -local_rows % 1024)).reshape(1, -1, 128),
        "share_ids",
        0,
        join_axes=AXES,
        join_orders=[shard_bits[::-1] + dp_bits[::-1] + seq_bits[::-1]],
    )
    ids_all = ids_all.reshape(total, -1)[:, :local_rows]
    owner_all = ids_all // table_local
    loads = jnp.sum(
        (owner_all[:, :, None] == jnp.arange(total)[None, None, :]).astype(jnp.int32), 1
    )
    rounds = (jnp.max(loads) + SLOTS - 1) // SLOTS
    asked = owner_all == device_at
    asked_rank = counts_before(asked)
    asked_row = ids_all - first_row
    own_owner = token_ids // table_local
    same = own_owner[:, None] == own_owner[None, :]
    before = jnp.arange(local_rows)[None, :] < jnp.arange(local_rows)[:, None]
    own_rank = jnp.sum((same & before).astype(jnp.int32), 1)

    def asked_rows(at):
        chosen = asked[:, None, :] & (
            asked_rank[:, None, :] == at * SLOTS + jnp.arange(SLOTS)[None, :, None]
        )
        return (jnp.sum(jnp.where(chosen, asked_row[:, None, :] + 1, 0), 2) - 1).reshape(-1)

    def own_slots(at):
        slot = own_rank - at * SLOTS
        return jnp.where((slot >= 0) & (slot < SLOTS), own_owner * SLOTS + slot, -1)

    def fetch(at, rows):
        given = swap(rows.astype(jnp.bfloat16).reshape(total, SLOTS, width), "swap_rows", 1)
        return dot_plain(
            one_hot(own_slots(at), total * SLOTS, 1), given.reshape(total * SLOTS, width)
        )

    fixed = jnp.arange(seq_length + small_rows, dtype=jnp.int32)
    fixed_row = jnp.where(fixed < seq_length + small_count, VOCAB + fixed - first_row, -1)
    wanted = jnp.concatenate([asked_rows(0), fixed_row])
    rows_out = dot_plain(one_hot(wanted, table_local, 1), table_own).astype(jnp.bfloat16)
    exchanged = total * SLOTS
    piece = seq_length // total
    place_rows = exchange(
        rows_out[exchanged : exchanged + seq_length].reshape(total, piece, width),
        "share_places",
        2,
        sum_axes=("seq", "dp", "shard"),
        sum_orders=[seq_bits + dp_bits + shard_bits],
        join_axes=("dp", "shard"),
        join_orders=[shard_bits[::-1] + dp_bits[::-1]],
    ).reshape(tok_count, width)
    small = combine_all(
        rows_out[exchanged + seq_length :], add_pair, "share_small", 3
    )[:small_count].astype(jnp.float32)
    place_state = jnp.broadcast_to(place_rows.astype(jnp.float32), (seqs, tok_count, width))
    state = fetch(0, rows_out[:exchanged]) + place_state.reshape(local_rows, width)
    state = lax.fori_loop(
        1,
        rounds,
        lambda at, held: held
        + fetch(at, dot_plain(one_hot(asked_rows(at), table_local, 1), table_own)),
        state,
    )

    query_ids = lax.dynamic_slice_in_dim(block_ids[0], seq_at * tok_count, tok_count, 0)
    inputs, kept, saved = [], [], []
    for layer_at in range(layers):
        weights = lax.all_gather(mats_low[layer_at], AXES, axis=1, tiled=True)
        inputs.append(state)
        kept.append(weights)
        state, held = layer_forward(
            state,
            weights,
            small[12 * layer_at : 12 * layer_at + 12],
            query_ids,
            block_ids[0],
        )
        saved.append(held)
    final_gain = small[12 * layers]
    final_shift = small[12 * layers + 1]
    final = layer_norm(state, final_gain, final_shift).astype(jnp.bfloat16)

    group_mask = completion[0]
    slot_of = regroup[0]
    slots = slot_of.shape[0]
    comp_rows = slots // shards
    rank_all = counts_before(group_mask[None])[0]
    mine = lax.dynamic_slice_in_dim(group_mask, shard_at * local_rows, local_rows)
    my_rank = lax.dynamic_slice_in_dim(rank_all, shard_at * local_rows, local_rows)
    my_slot = jnp.sum(
        jnp.where(my_rank[:, None] == jnp.arange(slots)[None, :], slot_of[None, :], 0), 1
    )
    to_slot = one_hot(jnp.where(mine == 1, my_slot, -1), slots, 0)
    outgoing = dot_plain(to_slot, final).astype(jnp.bfloat16).reshape(shards, comp_rows, width)
    two_ways = [seq_bits[1:] + dp_bits, dp_bits + seq_bits[1:]]
    head_in = exchange(
        outgoing,
        "share_final",
        5,
        sum_axes=("shard",),
        sum_orders=[shard_bits, shard_bits],
        join_axes=AXES,
        join_orders=[shard_bits[::-1] + way[::-1] + seq_bits[:1] for way in two_ways],
    ).reshape(-1, width)

    rows_all = targets.shape[0]
    columns = first_row + jnp.arange(table_local, dtype=jnp.int32)
    live = (columns < VOCAB)[None, :]
    logits = dot_rows(head_in, table_own)
    masked = jnp.where(live, logits, MASK_FILL)
    top_local = jnp.max(masked, 1)
    total_local = jnp.sum(jnp.where(live, jnp.exp(masked - top_local[:, None]), 0.0), 1)
    target_hit = columns[None, :] == targets[:, None]
    pick_local = jnp.sum(jnp.where(target_hit, logits, 0.0), 1)
    stats = combine_all(
        jnp.stack([top_local, total_local, pick_local]).reshape(3, -1, 128),
        merge_soft,
        "share_stats",
        6,
    ).reshape(3, rows_all)
    log_total = stats[0] + jnp.log(stats[1])
    loss_value = jnp.sum(log_total - stats[2]) / rows_all
    probs = jnp.where(live, jnp.exp(masked - log_total[:, None]), 0.0)
    logit_grad = ((probs - target_hit.astype(jnp.float32)) / rows_all).astype(jnp.bfloat16)
    head_grad = dot_cols(logit_grad, head_in)
    returned = exchange(
        dot_plain(logit_grad, table_own).reshape(total, comp_rows, width),
        "return_final",
        7,
        sum_axes=AXES,
        sum_orders=[seq_bits[:1] + way + shard_bits for way in two_ways],
        join_axes=("shard",),
        join_orders=[shard_bits[::-1], shard_bits[::-1]],
    ).reshape(slots, width)
    final_grad = dot_cols(to_slot, returned)
    state_grad, gain_final, shift_final = norm_back(state, final_gain, final_shift, final_grad)

    mats_grads = [None] * layers
    small_grads = [None] * layers
    for layer_at in reversed(range(layers)):
        state_grad, mats_grads[layer_at], small_grads[layer_at] = layer_backward(
            inputs[layer_at],
            kept[layer_at],
            small[12 * layer_at : 12 * layer_at + 12],
            saved[layer_at],
            state_grad,
        )

    low_grad = state_grad.astype(jnp.bfloat16)
    place_grad = jnp.sum(state_grad.reshape(seqs, tok_count, width), 0)
    place_grad = exchange(
        place_grad.reshape(replicas * shards, piece, width),
        "return_places",
        10,
        sum_axes=("dp", "shard"),
        sum_orders=[dp_bits + shard_bits],
        join_axes=("seq", "dp", "shard"),
        join_orders=[shard_bits[::-1] + dp_bits[::-1] + seq_bits[::-1]],
    ).reshape(seq_length, width)
    small_grad = combine_all(
        pad_rows(
            jnp.concatenate(small_grads + [jnp.stack([gain_final, shift_final])], 0), small_rows
        ),
        add_pair,
        "return_small",
        9,
    )
    small_high = small_grad.astype(jnp.bfloat16)
    small_low = (small_grad - small_high.astype(jnp.float32)).astype(jnp.bfloat16)

    def send_back(at):
        rows = dot_cols(one_hot(own_slots(at), total * SLOTS, 1), low_grad).astype(jnp.bfloat16)
        return swap(rows.reshape(total, SLOTS, width), "swap_rows", 1).reshape(-1, width)

    values = jnp.concatenate([send_back(0), place_grad, small_high, small_low], 0)
    value_row = jnp.concatenate([wanted, fixed_row[seq_length:]])
    table_grad = dot_plain(one_hot(value_row, table_local, 0), values) + head_grad
    table_grad = lax.fori_loop(
        1,
        rounds,
        lambda at, held: held + dot_plain(one_hot(asked_rows(at), table_local, 0), send_back(at)),
        table_grad,
    )
    mats_grad = jnp.stack(mats_grads)
    local_squares = jnp.sum(mats_grad * mats_grad) + jnp.sum(table_grad * table_grad)
    squares = combine_all(jnp.full((8, 128), local_squares), add_pair, "share_norm", 11)
    grad_norm = jnp.sqrt(squares[0, 0])
    factor = CLIP_NORM / grad_norm
    step = step_count[0].astype(jnp.float32)
    new_mats = adam_step(
        layer_mats, mats_moment, mats_square, factor * mats_grad, RATE_MATS, DECAY_RATE, step
    )
    plain_rows = (columns < VOCAB + seq_length)[:, None]
    rate = jnp.where(plain_rows, RATE_TABLE, RATE_SMALL)
    decay = jnp.where(plain_rows, DECAY_RATE, 0.0)
    new_table = adam_step(
        embed_table, table_moment, table_square, factor * table_grad, rate, decay, step
    )
    return (
        loss_value.reshape(1),
        grad_norm.reshape(1),
        new_mats[0],
        new_mats[1],
        new_mats[2],
        new_table[0],
        new_table[1],
        new_table[2],
    )


def solution(mesh):
    in_specs = (
        P(("dp", "shard"), "seq"),
        P(("dp", "shard"), None),
        P(("dp", "seq"), None),
        P(("dp", "seq"), None),
        P(),
        P(),
        P(None, None, ("dp", "seq", "shard"), None),
        P(None, None, ("dp", "seq", "shard"), None),
        P(None, None, ("dp", "seq", "shard"), None),
        P(("dp", "seq", "shard"), None),
        P(("dp", "seq", "shard"), None),
        P(("dp", "seq", "shard"), None),
    )
    out_specs = (
        P(),
        P(),
        P(None, None, ("dp", "seq", "shard"), None),
        P(None, None, ("dp", "seq", "shard"), None),
        P(None, None, ("dp", "seq", "shard"), None),
        P(("dp", "seq", "shard"), None),
        P(("dp", "seq", "shard"), None),
        P(("dp", "seq", "shard"), None),
    )
    return jax.shard_map(
        on_device, mesh=mesh, in_specs=in_specs, out_specs=out_specs, check_vma=False
    )
```

time: 4980 us -> 1650 us (0.33)
  waiting for transfers between devices: 3140 us -> 273 us
  Pallas kernels: 0 us -> 688 us
  local copies, waits for them, and re-layouts: 767 us -> 175 us
  blocking collectives: 329 us -> 0 us
  other arithmetic: 396 us -> 149 us
    unnamed x18 -> x14, waiting for transfers between devices: 1960 us -> 235 us
    all_gather x9 -> x2, waiting for transfers between devices: 981 us -> 37.9 us  [on_device(): weights = lax.all_gather(mats_low[layer_at], AXES, axis=1, tiled=True)]
    pallas_call x0 -> x15, Pallas kernels: none -> 688 us  [the longest x9 476 us: exchange(): pl.pallas_call(partial(exchange_kernel, sum_axes, sum_orders, join_axes,...]
    unnamed x257 -> x219, local copies, waits for them, and re-layouts: 394 us -> 16.2 us
    all_gather x4 -> x0, blocking collectives: 270 us -> none  [the longest x3 198 us: joined_2(): lax.all_gather(part.astype(kind), axis)]
    scatter-add x2 -> x0, other arithmetic: 182 us -> none  [on_device(): table_grad = table_grad.at[relative].add(gathered_vals, mode='drop')]
    reduce_scatter x5 -> x0, waiting for transfers between devices: 182 us -> none  [the longest x1 132 us: on_device(): lax.psum_scatter(dot_plain(logit_grad, table_own), ('dp', 'seq', 'shard')...]
    another operation x6 -> x3, local copies, waits for them, and re-layouts: 156 us -> 22.9 us  [the longest x2 156 us: layer_backward(): jnp.stack([jnp.concatenate([grad_joined, grad_proj], 0), grad_up, grad_do...]
  transfers between devices with their start and end apart: 17 -> 8, of which waited for: 14 -> 3; matrix products, arithmetic and copies ran while one was open for 19% -> 29% of each run, Pallas kernels for 0% -> 30%
where the time goes in v1:
time: 1650 us; the launch traced here: 1640 us
  Pallas kernels  688 us (42%)
  matrix products  331 us (20%)
  waiting for transfers between devices  273 us (17%)
  local copies, waits for them, and re-layouts  175 us (11%)
  other arithmetic  149 us (9%)
  between operations  22.8 us (1%)
    pallas_call x9, Pallas kernels, exchange(): pl.pallas_call(partial(exchange_kernel, sum_axes, sum_orders, join_axes,...  476 us
    unnamed x14, waiting for transfers between devices  235 us
    pallas_call x2, Pallas kernels, swap(): pl.pallas_call(swap_kernel, out_shape=jax.ShapeDtypeStruct(x.shape, x.dty...  121 us
    dot_general x15, matrix products, dot_plain(): return jnp.dot(left_op, right_op, preferred_element_type=jnp.float32)  98.5 us
    pallas_call x4, Pallas kernels, combine_all(): pl.pallas_call(partial(combine_kernel, bits, combine), out_shape=jax.Shap...  91.1 us
    dot_general x11, matrix products, dot_cols(): lax.dot_general(left_op, right_op, (((0,), (0,)), ((), ())), preferred_el...  64.9 us
    dot_general x9, matrix products, dot_rows(): lax.dot_general(left_op, right_op, (((1,), (1,)), ((), ())), preferred_el...  61 us
    all_gather x2, waiting for transfers between devices, on_device(): weights = lax.all_gather(mats_low[layer_at], AXES, axis=1, tiled=True)  37.9 us
  transfers between devices with their start and end apart: 8, of which 3 were waited for; matrix products, arithmetic and copies ran while one was open for 29% of the time, Pallas kernels for 30%

profile of v1, /device:TPU:0, one launch (start us, length us, event | category | flops | bytes accessed | tf_op | source)
XLA Modules:
  0.0 1639.5 jit_solution(9989315626453940848)
XLA Ops:
  19.2 19.3 %share_ids.1 = s32[32,8,128]{2,1,0:T(8,128)} custom-call(s32[1,8,128]{2,1,0:T(8,128)} %pad_bitcast_fusion.refs_0_), custom_call_target="tpu_custom_call" | custom-call | tf_op jit(solution)/shard_map/share_ids/pallas_call | solution.py:178
  57.2 30.7 %share_small.1 = bf16[32,1088]{1,0:T(8,128)(2,1)} custom-call(bf16[32,1088]{1,0:T(8,128)(2,1)} %slice.264.x_ref), custom_call_target="tpu_custom_call" | custom-call | tf_op jit(solution)/shard_map/share_small/pallas_call | solution.py:215
  87.9 94.7 %share_places.1 = bf16[8,32,1088]{2,1,0:T(8,128)(2,1)} custom-call(bf16[32,32,1088]{2,1,0:T(8,128)(2,1)} %bitcast.253), custom_call_target="tpu_custom_call" | custom-call | tf_op jit(solution)/shard_map/share_places/pallas_call | solution.py:178
  184.1 60.2 %swap_rows.10 = bf16[32,24,1088]{2,1,0:T(8,128)(2,1)} custom-call(bf16[32,24,1088]{2,1,0:T(8,128)(2,1)} %bitcast.255), custom_call_target="tpu_custom_call" | custom-call | tf_op jit(solution)/shard_map/swap_rows/pallas_call | solution.py:288
  263.3 56.9 %share_keys.2 = bf16[4,512,1088]{2,1,0:T(8,128)(2,1)} custom-call(bf16[1,512,1088]{2,1,0:T(8,128)(2,1)} %maximum_bitcast_fusion.refs_0_), custom_call_target="tpu_custom_call" | custom-call | tf_op jit(solution)/shard_map/share_keys/pallas_call | solution.py:178
  342.5 12.0 fusion.153
  383.7 37.9 %all-gather.7.cloned.1.call-done = bf16[1,3,4352,1088]{3,2,1,0:T(8,128)(2,1)} async-done(((bf16[1,3,136,1088]{3,2,1,0:T(8,128)(2,1)}), bf16[1,3,4352,1088]{3,2,1,0:T(8,128)(2,1)}) %all-gather.7.cloned.1.call-update) | async-done | bytes 28409872 | tf_op jit(solution)/shard_map/all_gather | solution.py:606
  432.2 36.0 %share_keys.3 = bf16[4,512,1088]{2,1,0:T(8,128)(2,1)} custom-call(bf16[1,512,1088]{2,1,0:T(8,128)(2,1)} %maximum_bitcast_fusion.1.refs_0_), custom_call_target="tpu_custom_call" | custom-call | tf_op jit(solution)/shard_map/share_keys/pallas_call | solution.py:178
  490.0 12.1 fusion.156
  532.8 59.1 %share_final.1 = bf16[32,64,1088]{2,1,0:T(8,128)(2,1)} custom-call(bf16[4,64,1088]{2,1,0:T(8,128)(2,1)} %bitcast.268), custom_call_target="tpu_custom_call" | custom-call | tf_op jit(solution)/shard_map/share_final/pallas_call | solution.py:178
  591.9 12.1 select_reduce_fusion.3
  609.9 16.1 share_stats.1
  635.5 12.4 fusion.159
  647.8 61.3 %return_final.1 = bf16[4,64,1088]{2,1,0:T(8,128)(2,1)} custom-call(f32[32,64,1088]{2,1,0:T(8,128)} %bitcast.252), custom_call_target="tpu_custom_call" | custom-call | tf_op jit(solution)/shard_map/return_final/pallas_call | solution.py:178
  754.5 12.9 multiply_reduce_fusion.1
  767.4 13.2 multiply_convert_fusion.1
  834.7 38.6 %return_grads.2 = bf16[512,1088]{1,0:T(8,128)(2,1)} custom-call(f32[4,512,1088]{2,1,0:T(8,128)} %pad_maximum_fusion.2.refs_0_), custom_call_target="tpu_custom_call" | custom-call | tf_op jit(solution)/shard_map/return_grads/pallas_call | solution.py:178
  886.4 11.6 copy.160
  898.9 13.8 pad_maximum_fusion.1
  961.5 11.5 multiply_reduce_fusion
  973.5 12.6 multiply_convert_fusion
  1040.5 50.9 %return_grads.3 = bf16[512,1088]{1,0:T(8,128)(2,1)} custom-call(f32[4,512,1088]{2,1,0:T(8,128)} %pad_maximum_fusion.3.refs_0_), custom_call_target="tpu_custom_call" | custom-call | tf_op jit(solution)/shard_map/return_grads/pallas_call | solution.py:178
  1136.0 28.9 %return_small.1 = f32[32,1088]{1,0:T(8,128)} custom-call(f32[32,1088]{1,0:T(8,128)} %pad.9.x_ref), custom_call_target="tpu_custom_call" | custom-call | tf_op jit(solution)/shard_map/return_small/pallas_call | solution.py:215
  1171.0 59.0 %return_places.1 = bf16[32,32,1088]{2,1,0:T(8,128)(2,1)} custom-call(f32[8,32,1088]{2,1,0:T(8,128)} %bitcast.257), custom_call_target="tpu_custom_call" | custom-call | tf_op jit(solution)/shard_map/return_places/pallas_call | solution.py:178
  1233.3 60.6 %swap_rows.11 = bf16[32,24,1088]{2,1,0:T(8,128)(2,1)} custom-call(bf16[32,24,1088]{2,1,0:T(8,128)(2,1)} %bitcast.256), custom_call_target="tpu_custom_call" | custom-call | tf_op jit(solution)/shard_map/swap_rows/pallas_call | solution.py:288
  1295.5 14.1 pad_maximum_fusion
  1309.6 13.4 fusion.160
  1324.0 13.7 fusion.20
  1344.0 95.7 %reduce-scatter.21.cloned.1.call-done = bf16[1,136,1088]{2,1,0:T(8,128)(2,1)} async-done(((bf16[32,136,1088]{2,1,0:T(8,128)(2,1)}), bf16[1,136,1088]{2,1,0:T(8,128)(2,1)}) %reduce-scatter.21.cloned.1.call-update) | async-done | bytes 295952
  1439.7 138.4 %reduce-scatter.19.cloned.1.call-done = bf16[1,136,1088]{2,1,0:T(8,128)(2,1)} async-done(((bf16[32,136,1088]{2,1,0:T(8,128)(2,1)}), bf16[1,136,1088]{2,1,0:T(8,128)(2,1)}) %reduce-scatter.19.cloned.1.call-update) | async-done | bytes 295952
  1583.0 15.4 share_norm.1
  1610.8 19.2 %multiply_subtract_fusion = (f32[1604,1088]{0,1:T(8,128)}, f32[1604,1088]{0,1:T(8,128)}, f32[1604,1088]{0,1:T(8,128)}) fusion(f32[1604,1088]{0,1:T(8,128)} %param.25, f32[1604]{0:T(1024)S(1)} %copy-done.59, f32[]{:T(128)} %bitcast.75, f32[]{:T(128)} %bitcast.74, f32[1604]{0:T(1024)S(1)} %copy-done.60, f32[1604,1088]{0,1:T(8,128)} %get-tuple-element.241, ...), kind=kLoop, calls=%fused_computation.87 | loop fusion | flops 27922432 | bytes 48877100 | tf_op jit(solution)/shard_map/sub | solution.py:497
  (429 shorter events, 472.5 us)
Async XLA Ops:
  7.2 245.5 %all-gather.5.cloned.1.call-start = ((), (), s32[]{:S(2)}) async-start(), calls=%async_computation.6 | async-start | bytes 31021056 | tf_op jit(solution)/shard_map/all_gather | solution.py:606
  10.9 410.7 %all-gather.7.cloned.1.call-start = ((), (), s32[]{:S(2)}) async-start(), calls=%async_computation.7 | async-start | bytes 31021056 | tf_op jit(solution)/shard_map/all_gather | solution.py:606
  11.6 1332.3 %reduce-scatter.29.cloned.1.call-start = ((), (), s32[]{:S(2)}) async-start(), calls=%async_computation.13 | async-start | bytes 10340352
  183.8 60.6 %copy-start.34 = (bf16[32,1088]{1,0:T(8,128)(2,1)S(1)}, bf16[32,1088]{1,0:T(8,128)(2,1)}, u32[]{:S(2)}) copy-start(bf16[32,1088]{1,0:T(8,128)(2,1)} %share_small.1) | copy-start | bytes 208900
  184.1 61.6 %copy-start.100 = (s32[1,1024]{1,0:T(1,128)S(1)}, s32[1,1024]{1,0:T(1,128)}, u32[]{:S(2)}) copy-start(s32[1,1024]{1,0:T(1,128)} %param.18) | copy-start | bytes 12292
  248.9 114.2 %copy-start = (f32[256,1088]{0,1:T(8,128)}, f32[256,1088]{0,1:T(8,128)S(1)}, u32[]{:S(2)}) copy-start(f32[256,1088]{0,1:T(8,128)S(1)} %get-tuple-element.240) | copy-start | bytes 3342340
  250.9 115.7 %copy-start.41 = (f32[1088]{0:T(1024)}, f32[1088]{0:T(1024)S(1)}, u32[]{:S(2)}) copy-start(f32[1088]{0:T(1024)S(1)} %get-tuple-element.318) | copy-start | bytes 13060
  250.9 115.7 %copy-start.57 = (f32[1088]{0:T(1024)}, f32[1088]{0:T(1024)S(1)}, u32[]{:S(2)}) copy-start(f32[1088]{0:T(1024)S(1)} %get-tuple-element.317) | copy-start | bytes 13060
  250.9 170.7 %copy-start.43 = (f32[1088]{0:T(1024)}, f32[1088]{0:T(1024)S(1)}, u32[]{:S(2)}) copy-start(f32[1088]{0:T(1024)S(1)} %get-tuple-element.315) | copy-start | bytes 13060
  250.9 170.7 %copy-start.47 = (f32[1088]{0:T(1024)}, f32[1088]{0:T(1024)S(1)}, u32[]{:S(2)}) copy-start(f32[1088]{0:T(1024)S(1)} %get-tuple-element.314) | copy-start | bytes 13060
  383.5 127.2 %copy-start.7 = (f32[256,1088]{0,1:T(8,128)}, f32[256,1088]{0,1:T(8,128)S(1)}, u32[]{:S(2)}) copy-start(f32[256,1088]{0,1:T(8,128)S(1)} %get-tuple-element.409) | copy-start | bytes 3342340
  383.5 43.9 %copy-start.66 = (f32[256]{0:T(256)}, f32[256]{0:T(256)S(1)}, u32[]{:S(2)}) copy-start(f32[256]{0:T(256)S(1)} %broadcast_multiply_fusion.2) | copy-start | bytes 3076
  383.7 43.7 %copy-start.89 = (f32[256]{0:T(256)}, f32[256]{0:T(256)S(1)}, u32[]{:S(2)}) copy-start(f32[256]{0:T(256)S(1)} %multiply_reduce_fusion.15) | copy-start | bytes 3076
  383.7 43.7 %copy-start.78 = (f32[256]{0:T(256)}, f32[256]{0:T(256)S(1)}, u32[]{:S(2)}) copy-start(f32[256]{0:T(256)S(1)} %fusion.123) | copy-start | bytes 3076
  532.8 59.1 %copy-start.77 = (pred[1604]{0:T(1024)(128)(4,1)S(1)}, pred[1604]{0:T(1024)(128)(4,1)}, u32[]{:S(2)}) copy-start(pred[1604]{0:T(1024)(128)(4,1)} %fusion.115) | copy-start | bytes 4816
  722.9 621.1 %reduce-scatter.27.cloned.1.call-start = ((), (), s32[]{:S(2)}) async-start(), calls=%async_computation.12 | async-start | bytes 10340352
  752.8 591.2 %reduce-scatter.25.cloned.1.call-start = ((), (), s32[]{:S(2)}) async-start(), calls=%async_computation.11 | async-start | bytes 10340352
  767.4 13.3 copy-start.14
  912.7 431.3 %reduce-scatter.23.cloned.1.call-start = ((), (), s32[]{:S(2)}) async-start(), calls=%async_computation.10 | async-start | bytes 10340352
  931.0 508.7 %reduce-scatter.21.cloned.1.call-start = ((), (), s32[]{:S(2)}) async-start(), calls=%async_computation.9 | async-start | bytes 10340352
  951.9 213.8 %copy-start.9 = (f32[256,1088]{0,1:T(8,128)}, f32[256,1088]{0,1:T(8,128)S(1)}, u32[]{:S(2)}) copy-start(f32[256,1088]{0,1:T(8,128)S(1)} %get-tuple-element.377) | copy-start | bytes 3342340
  973.0 605.1 %reduce-scatter.19.cloned.1.call-start = ((), (), s32[]{:S(2)}) async-start(), calls=%async_computation.8 | async-start | bytes 10340352
  1171.0 59.3 %copy-start.84 = (s32[256]{0:T(256)S(1)}, s32[256]{0:T(256)}, u32[]{:S(2)}) copy-start(s32[256]{0:T(256)} %copy-done.83) | copy-start | bytes 3076
  1233.3 61.2 %copy-start.10 = (f32[256,1088]{0,1:T(8,128)S(1)}, f32[256,1088]{0,1:T(8,128)}, u32[]{:S(2)}) copy-start(f32[256,1088]{0,1:T(8,128)} %copy-done.9) | copy-start | bytes 3342340
  1233.3 61.2 %copy-start.31 = (bf16[17,64,256]{2,1,0:T(8,128)(2,1)S(1)}, bf16[17,64,256]{2,1,0:T(8,128)(2,1)}, u32[]{:S(2)}) copy-start(bf16[17,64,256]{2,1,0:T(8,128)(2,1)} %copy-done.30) | copy-start | bytes 1671172
  1233.3 76.3 %slice-start = ((s8[4718592]{0:T(1024)(128)(4,1)}), s8[524288]{0:T(1024)(128)(4,1)S(1)}, s32[]{:S(2)}) async-start(s8[4718592]{0:T(1024)(128)(4,1)} %bitcast.259), calls=%async_computation.14 | async-start | bytes 1048576
  1295.5 14.1 slice-start.1
  1324.0 13.7 copy-start.19
  1324.0 13.7 copy-start.21
  1324.0 13.7 copy-start.28
  1324.0 13.7 copy-start.38
  1324.0 13.7 copy-start.40
  (83 other events, 598.1 us)
Sparse Core Ops, SparseCore 0:
  11.6 200.9 all-gather.4
  216.1 205.4 all-gather.6
  723.0 132.7 reduce-scatter.28
  861.8 132.3 reduce-scatter.26
  1000.2 142.3 reduce-scatter.24
  1148.5 152.4 reduce-scatter.22
  1307.1 132.5 reduce-scatter.20
  1445.8 132.2 reduce-scatter.18

commit v2 on v1

v2 whole, which is shorter than its diff:
```python
import itertools
from functools import partial

import jax
import jax.numpy as jnp
from jax import lax
from jax.experimental import pallas as pl
from jax.experimental.layout import Layout, with_layout_constraint
from jax.experimental.pallas import tpu as pltpu
from jax.sharding import PartitionSpec as P

HEADS = 17
HEAD = 64
VOCAB = 50278

NORM_EPS = 1e-05
CLIP_NORM = 0.02
BETA_ONE = 0.9
BETA_TWO = 0.95
ADAM_EPS = 1e-08
DECAY_RATE = 0.1
RATE_MATS = 0.05
RATE_TABLE = 0.1
RATE_SMALL = 0.5
MASK_FILL = -1e30

AXES = ("dp", "seq", "shard")
MESH = pl.DeviceIdType.MESH
SLOTS = 24


def bits_of(axis):
    return [(axis, b) for b in range(lax.axis_size(axis).bit_length() - 1)]


def bit_here(bit):
    return lax.rem(lax.axis_index(bit[0]) // 2 ** bit[1], 2)


def partner(bit):
    at = lax.axis_index(bit[0])
    return {bit[0]: at + (1 - 2 * bit_here(bit)) * 2 ** bit[1]}


def greet(bits):
    barrier = pltpu.get_barrier_semaphore()
    for bit in bits:
        pl.semaphore_signal(barrier, inc=1, device_id=partner(bit), device_id_type=MESH)
    pl.semaphore_wait(barrier, len(bits))


def block_weight(axes, bit):
    weight = 2 ** bit[1]
    for axis in axes[axes.index(bit[0]) + 1 :]:
        weight *= lax.axis_size(axis)
    return weight


def block_runs(weights):
    weights = sorted(weights)
    joined = 0
    while joined < len(weights) and weights[joined] == 2**joined:
        joined += 1
    rest = [(0, w) for w in weights[joined:]]
    return 2**joined, [sum(c) for c in itertools.product(*rest)]


class Job:
    def __init__(
        self, inputs, outputs, scratch, sends, keeps, bits, steps, spaces=(pltpu.VMEM, pltpu.VMEM)
    ):
        self.inputs, self.outputs, self.scratch = inputs, outputs, scratch
        self.sends, self.keeps, self.bits, self.steps, self.spaces = sends, keeps, bits, steps, spaces


def me_and_total():
    seq_size, shard_size = lax.axis_size("seq"), lax.axis_size("shard")
    at = (lax.axis_index("dp") * seq_size + lax.axis_index("seq")) * shard_size
    return at + lax.axis_index("shard"), lax.axis_size("dp") * seq_size * shard_size


def place_of(at):
    seq_size, shard_size = lax.axis_size("seq"), lax.axis_size("shard")
    return {
        "dp": at // (seq_size * shard_size),
        "seq": lax.rem(at // shard_size, seq_size),
        "shard": lax.rem(at, shard_size),
    }


def greet_all():
    me, total = me_and_total()
    barrier = pltpu.get_barrier_semaphore()

    def hello(k, carry):
        pl.semaphore_signal(
            barrier, inc=1, device_id=place_of(lax.rem(me + k, total)), device_id_type=MESH
        )
        return carry

    lax.fori_loop(1, total, hello, 0)
    pl.semaphore_wait(barrier, total - 1)


class Sems:
    def __init__(self, send, recv, keep):
        self.send, self.recv, self.keep = send, recv, keep
        self.used = self.kept = 0

    def copy(self, source, target, device):
        k = self.used
        self.used += 1
        copy = pltpu.make_async_remote_copy(
            source, target, self.send.at[k], self.recv.at[k], device_id=device, device_id_type=MESH
        )
        copy.start()
        return copy

    def local(self, source, target):
        k = self.kept
        self.kept += 1
        copy = pltpu.make_async_copy(source, target, self.keep.at[k])
        copy.start()
        return copy

    def span(self, count):
        first = self.used
        self.used += count
        return first


def jobs_kernel(jobs, *refs):
    refs = list(refs)

    def take(count):
        out = refs[:count]
        del refs[:count]
        return out

    held = [take(len(job.inputs)) for job in jobs]
    made = [take(len(job.outputs)) for job in jobs]
    used = [take(len(job.scratch)) for job in jobs]
    sems = Sems(*refs)
    if any(job.bits is None for job in jobs):
        greet_all()
    else:
        greet(sorted(set(bit for job in jobs for bit in job.bits)))
    active = []
    for job, x, o, w in zip(jobs, held, made, used):
        active += job.steps(x, o, w, sems)
    tick = 0
    while active:
        left = []
        for delay, gen in active:
            if delay > tick or next(gen, "end") != "end":
                left.append((delay, gen))
        active = left
        tick += 1


def run_jobs(jobs, name, number, vmem=60):
    inputs = [x for job in jobs for x in job.inputs]
    outputs = [o for job in jobs for o in job.outputs]
    in_specs = [pl.BlockSpec(memory_space=job.spaces[0]) for job in jobs for unused in job.inputs]
    out_specs = [pl.BlockSpec(memory_space=job.spaces[1]) for job in jobs for unused in job.outputs]
    sends = sum(job.sends for job in jobs)
    keeps = max(1, sum(job.keeps for job in jobs))
    flat = pl.pallas_call(
        partial(jobs_kernel, jobs),
        out_shape=outputs,
        in_specs=in_specs,
        out_specs=out_specs,
        scratch_shapes=[w for job in jobs for w in job.scratch]
        + [
            pltpu.SemaphoreType.DMA((sends,)),
            pltpu.SemaphoreType.DMA((sends,)),
            pltpu.SemaphoreType.DMA((keeps,)),
        ],
        compiler_params=pltpu.CompilerParams(
            collective_id=number, has_side_effects=True, vmem_limit_bytes=vmem * 2**20
        ),
        name=name,
    )(*inputs)
    out = []
    for job in jobs:
        out.append(flat[: len(job.outputs)])
        flat = flat[len(job.outputs) :]
    return out


def sum_stream(x_ref, o_ref, scratch, sems, rows, first_slot, sum_axes, sums, join_axes, joins):
    source = x_ref
    slot = first_slot
    if sums:
        work, parcel, recv = scratch
    for step, bit in enumerate(sums):
        base = sum(bit_here(b) * block_weight(sum_axes, b) for b in sums[:step])
        weight = block_weight(sum_axes, bit)
        mine = bit_here(bit)
        size, offsets = block_runs([block_weight(sum_axes, b) for b in sums[step + 1 :]])
        started = []
        for offset in offsets:
            leave = base + (1 - mine) * weight + offset
            if source.dtype == parcel.dtype:
                packed = source.at[pl.ds(leave, size), rows]
            else:

                def pack(i, carry, leave=leave, at=slot, source=source):
                    parcel[at + i, rows] = source[leave + i, rows].astype(parcel.dtype)
                    return carry

                lax.fori_loop(0, size, pack, 0)
                packed = parcel.at[pl.ds(slot, size), rows]
            copy = sems.copy(packed, recv.at[pl.ds(slot, size), rows], partner(bit))
            started.append((copy, base + mine * weight + offset, slot, size))
            slot += size
        yield
        for copy, keep, at, size in started:
            copy.wait()

            def add(i, carry, keep=keep, at=at, source=source):
                total = source[keep + i, rows].astype(jnp.float32)
                total = total + recv[at + i, rows].astype(jnp.float32)
                work[keep + i, rows] = total.astype(work.dtype)
                return carry

            lax.fori_loop(0, size, add, 0)
        source = work
    own = sum(bit_here(b) * block_weight(sum_axes, b) for b in sums) if sums else 0
    result = source[own, rows].astype(o_ref.dtype)
    if not joins:
        o_ref[rows] = result
        return
    o_ref[sum(bit_here(b) * block_weight(join_axes, b) for b in joins), rows] = result
    for step, bit in enumerate(joins):
        base = sum(bit_here(b) * block_weight(join_axes, b) for b in joins[step:])
        size, offsets = block_runs([block_weight(join_axes, b) for b in joins[:step]])
        started = []
        for offset in offsets:
            here = o_ref.at[pl.ds(base + offset, size), rows]
            started.append(sems.copy(here, here, partner(bit)))
        yield
        for copy in started:
            copy.wait()


def sum_job(x, sum_axes=(), sum_orders=(), join_axes=(), join_orders=(), chunks=1):
    rows, width = x.shape[-2:]
    blocks = 1
    for axis in join_axes:
        blocks *= lax.axis_size(axis)
    kind = jnp.bfloat16 if sum_axes else x.dtype
    streams = max(len(sum_orders), len(join_orders))
    if rows % (streams * chunks * 16):
        chunks = 1
    share = rows // (streams * chunks)
    sends = 0
    for order in sum_orders:
        for step in range(len(order)):
            sends += len(block_runs([block_weight(sum_axes, b) for b in order[step + 1 :]])[1])
    for order in join_orders:
        for step in range(len(order)):
            sends += len(block_runs([block_weight(join_axes, b) for b in order[:step]])[1])
    scratch = []
    if sum_axes:
        if x.size * 14 > 56 * 2**20:
            x = x.astype(jnp.bfloat16)
        exact = x.dtype == jnp.float32 or x.size < 2**22
        scratch = [
            pltpu.VMEM(x.shape, jnp.float32 if exact else kind),
            pltpu.VMEM(x.shape, kind),
            pltpu.VMEM(x.shape, kind),
        ]

    def steps(x_refs, o_refs, scratch_refs, sems):
        gens = []
        for c in range(chunks):
            for k in range(streams):
                rows_here = pl.ds((k * chunks + c) * share, share)
                sums = sum_orders[k] if sum_orders else []
                joins = join_orders[k] if join_orders else []
                gens.append(
                    (
                        c,
                        sum_stream(
                            x_refs[0], o_refs[0], scratch_refs, sems, rows_here, 0,
                            sum_axes, sums, join_axes, joins,
                        ),
                    )
                )
        return gens

    bits = set(bit for order in list(sum_orders) + list(join_orders) for bit in order)
    shape = (blocks, rows, width) if join_axes else (rows, width)
    return Job(
        [x], [jax.ShapeDtypeStruct(shape, kind)], scratch, sends * chunks, 0, bits, steps
    )


def exchange(x, name, number, **how):
    return run_jobs([sum_job(x, **how)], name, number)[0][0]


def combine_job(x, combine):
    bits = [bit for axis in reversed(AXES) for bit in bits_of(axis)]
    slots = (len(bits),) + x.shape

    def steps(x_refs, o_refs, scratch, sems):
        out_buf, in_buf = scratch

        def gen():
            current = x_refs[0][...]
            for i, bit in enumerate(bits):
                out_buf[i] = current
                copy = sems.copy(out_buf.at[i], in_buf.at[i], partner(bit))
                yield
                copy.wait()
                current, other = out_buf[i], in_buf[i]
                low = bit_here(bit) == 0
                current = combine(jnp.where(low, current, other), jnp.where(low, other, current))
            o_refs[0][...] = current

        return [(0, gen())]

    return Job(
        [x],
        [jax.ShapeDtypeStruct(x.shape, x.dtype)],
        [pltpu.VMEM(slots, x.dtype), pltpu.VMEM(slots, x.dtype)],
        len(bits),
        0,
        bits,
        steps,
    )


def combine_all(x, combine, name, number):
    return run_jobs([combine_job(x, combine)], name, number, 16)[0][0]


def swap_job(x, late=0):
    total = x.shape[0]

    def steps(x_refs, o_refs, scratch, sems):
        x_ref, o_ref = x_refs[0], o_refs[0]

        def gen():
            me, unused = me_and_total()
            first = sems.span(total)
            keep = sems.local(x_ref.at[me], o_ref.at[me])

            def copy_to(other, here):
                return pltpu.make_async_remote_copy(
                    x_ref.at[other],
                    o_ref.at[here],
                    sems.send.at[first + other],
                    sems.recv.at[first + here],
                    device_id=place_of(other),
                    device_id_type=MESH,
                )

            def send(k, carry):
                copy_to(lax.rem(me + k, total), me).start()
                return carry

            lax.fori_loop(1, total, send, 0)
            for unused in range(late + 1):
                yield

            def finish(k, carry):
                other = lax.rem(me + k, total)
                copy_to(other, other).wait()
                return carry

            lax.fori_loop(1, total, finish, 0)
            keep.wait()

        return [(0, gen())]

    return Job(
        [x],
        [jax.ShapeDtypeStruct(x.shape, x.dtype)],
        [],
        total,
        1,
        None,
        steps,
        spaces=(pl.ANY, pl.ANY),
    )


def swap(x, name, number):
    return run_jobs([swap_job(x)], name, number, 16)[0][0]


def sum_orders_for(rows):
    across, along, deep = bits_of("seq")[1:], bits_of("dp"), bits_of("shard")
    if rows < 64 or rows % 8:
        return [(0, rows)], [across + along + deep]
    one = rows * 6 // 17 // 16 * 16
    spans = [(0, one), (one, one), (2 * one, rows - 2 * one)]
    return spans, [across + along + deep, along + across + deep, deep + across + along]


def mats_stream(x_ref, o_ref, scratch, sems, m, span, order, weights):
    kept, work, parcel, recv = scratch
    steps = len(order)
    rows = pl.ds(*span)
    slot = 0
    rest = sorted((b for b in weights if b != order[0]), key=lambda b: weights[b])
    small = {b: 2**k for k, b in enumerate(rest)}
    for step, bit in enumerate(order):
        mine = bit_here(bit)
        base = sum(bit_here(b) * small[b] for b in order[1:step])
        runs, keeps = [], []
        if step == 0:
            size, offsets = block_runs([weights[b] for b in order[1:]])
            for offset in offsets:
                left, place = offset, 0
                for b in reversed(rest):
                    if left >= weights[b]:
                        left -= weights[b]
                        place += small[b]
                keeps.append(
                    sems.local(
                        x_ref.at[pl.ds(mine * weights[bit] + offset, size), rows],
                        kept.at[m % 2, pl.ds(place, size), rows],
                    )
                )
                runs.append(((1 - mine) * weights[bit] + offset, place))
        else:
            size, offsets = block_runs([small[b] for b in order[step + 1 :]])
            for offset in offsets:
                here = base + offset
                runs.append((here + (1 - mine) * small[bit], here + mine * small[bit]))
        started = []
        for leave, keep_at in runs:
            at = slot
            slot += size
            if step == 0:
                packed = x_ref.at[pl.ds(leave, size), rows]
            else:
                spot = at - 2 ** (steps - 1)

                def pack(i, carry, leave=leave, spot=spot):
                    parcel[m, spot + i, rows] = work[m, leave + i, rows].astype(parcel.dtype)
                    return carry

                lax.fori_loop(0, size, pack, 0)
                packed = parcel.at[m, pl.ds(spot, size), rows]
            copy = sems.copy(packed, recv.at[m, pl.ds(at, size), rows], partner(bit))
            started.append((copy, at, keep_at, size))
        yield
        for keep in keeps:
            keep.wait()
        for copy, at, keep_at, size in started:
            copy.wait()

            def add(i, carry, at=at, keep_at=keep_at, step=step):
                if step == 0:
                    total = kept[m % 2, keep_at + i, rows].astype(jnp.float32)
                else:
                    total = work[m, keep_at + i, rows]
                work[m, keep_at + i, rows] = total + recv[m, at + i, rows].astype(jnp.float32)
                return carry

            lax.fori_loop(0, size, add, 0)
    o_ref[rows] = work[m, sum(bit_here(b) * small[b] for b in order[1:]), rows]


def mats_job(mats):
    blocks, rows, width = mats[0].shape
    spans, orders = sum_orders_for(rows)
    weights = {}
    for bit in orders[0]:
        weight = block_weight(AXES, bit)
        weights[bit] = weight if bit[0] == "shard" else weight // 2
    keeps = sends = 0
    for order in orders:
        keeps += len(block_runs([weights[b] for b in order[1:]])[1])
        sends += len(block_runs([weights[b] for b in order[1:]])[1])
        rest = sorted((b for b in weights if b != order[0]), key=lambda b: weights[b])
        small = {b: 2**k for k, b in enumerate(rest)}
        for step in range(1, len(order)):
            sends += len(block_runs([small[b] for b in order[step + 1 :]])[1])
    count = len(mats)

    def steps(x_refs, o_refs, scratch, sems):
        return [
            (m, mats_stream(x_refs[m], o_refs[m], scratch, sems, m, spans[k], orders[k], weights))
            for m in range(count)
            for k in range(len(orders))
        ]

    return Job(
        mats,
        [jax.ShapeDtypeStruct((rows, width), jnp.float32)] * count,
        [
            pltpu.VMEM((min(2, count), blocks // 2, rows, width), jnp.bfloat16),
            pltpu.VMEM((count, blocks // 2, rows, width), jnp.float32),
            pltpu.VMEM((count, blocks // 2 - 1, rows, width), jnp.bfloat16),
            pltpu.VMEM((count, blocks - 1, rows, width), jnp.bfloat16),
        ],
        count * sends,
        count * keeps,
        set(orders[0]),
        steps,
        spaces=(pl.ANY, pltpu.VMEM),
    )


def trade_kernel(count, *refs):
    x_refs, o_refs = refs[:count], refs[count : 2 * count]
    send_sems, recv_sems = refs[2 * count :]
    bit = ("seq", 0)
    greet([bit])
    copies = []
    for k in range(count):
        copy = pltpu.make_async_remote_copy(
            x_refs[k],
            o_refs[k],
            send_sems.at[k],
            recv_sems.at[k],
            device_id=partner(bit),
            device_id_type=MESH,
        )
        copy.start()
        copies.append(copy)
    for copy in copies:
        copy.wait()


def trade(arrays, name, number):
    count = len(arrays)
    return pl.pallas_call(
        partial(trade_kernel, count),
        out_shape=[jax.ShapeDtypeStruct(x.shape, x.dtype) for x in arrays],
        in_specs=[pl.BlockSpec(memory_space=pl.ANY)] * count,
        out_specs=[pl.BlockSpec(memory_space=pl.ANY)] * count,
        scratch_shapes=[pltpu.SemaphoreType.DMA((count,)), pltpu.SemaphoreType.DMA((count,))],
        compiler_params=pltpu.CompilerParams(collective_id=number, has_side_effects=True),
        name=name,
    )(*arrays)


def my_rows(features, own):
    rows = features.shape[0]
    parts = features.reshape(rows, -1, 2, own)
    at = lax.rem(lax.axis_index("seq"), 2)
    mine = lax.dynamic_index_in_dim(parts, at, 2, keepdims=False)
    other = lax.dynamic_index_in_dim(parts, 1 - at, 2, keepdims=False)
    return mine.reshape(rows, -1), other.reshape(rows, -1)


def late_mats(first, up, down, number):
    joined_grad, hidden, attended, out_grad = first
    own = up[0].shape[1] // lax.axis_size(AXES) * lax.axis_size("shard")
    halves = [my_rows(x, own) for x in (joined_grad, attended, up[0], down[0])]
    tails = [hidden, out_grad, up[1], down[1]]
    got = trade([other for unused, other in halves] + tails, "trade_rows", number)
    parts = []
    for k, (mine, unused) in enumerate(halves):
        grad = dot_cols(
            jnp.concatenate([mine, got[k]], 0),
            jnp.concatenate([tails[k], got[len(halves) + k]], 0),
        )
        parts.append(rows_major(grad.astype(jnp.bfloat16)))
    mats = [jnp.concatenate(parts[:2], 0), parts[2], parts[3]]
    blocks = lax.axis_size(AXES) // 2
    return [grad.reshape(blocks, -1, grad.shape[1]) for grad in mats]


def mats_fit(mats):
    blocks, rows, width = mats[0].shape
    tile = -(-rows // 16) * 16 * -(-width // 128) * 128
    return min(len(mats), max(1, (50 * 2**20 - tile * blocks * 2) // (tile * blocks * 5)))


def head_lanes(half, shape):
    lane = lax.broadcasted_iota(jnp.int32, shape, 1)
    return (lane < HEAD) if half == 0 else (lane >= HEAD)


def attend_kernel(q_ref, kv_ref, key_ids_ref, query_ids_ref, o_ref, lse_ref, blocked):
    groups, twice, unused = kv_ref.shape
    rows = twice // 2
    keys = groups * rows
    blocked[...] = jnp.where(key_ids_ref[...] <= query_ids_ref[...], 0.0, MASK_FILL)

    def pair(p, carry):
        lanes = pl.ds(pl.multiple_of(p * 2 * HEAD, 2 * HEAD), 2 * HEAD)
        key_pair = kv_ref[:, :rows, lanes].reshape(keys, 2 * HEAD)
        val_turned = kv_ref[:, rows:, lanes].reshape(keys, 2 * HEAD).T
        query_pair = q_ref[:, lanes]
        outs = []
        for half in range(2):
            query = jnp.where(head_lanes(half, query_pair.shape), query_pair, 0)
            scores = dot_rows(key_pair, query.astype(jnp.bfloat16)) * HEAD ** (-0.5) + blocked[...]
            top = jnp.max(scores, 0, keepdims=True)
            raised = jnp.exp(scores - top)
            total = jnp.sum(raised, 0, keepdims=True)
            probs = (raised * (1.0 / total)).astype(jnp.bfloat16)
            outs.append(dot_plain(val_turned[half * HEAD : (half + 1) * HEAD], probs))
            lse_ref[p, half] = (top + jnp.log(total))[0]
        o_ref[:, lanes] = jnp.concatenate(outs, 0).T.astype(o_ref.dtype)
        return carry

    lax.fori_loop(0, q_ref.shape[1] // (2 * HEAD), pair, 0)


def attend(queries, key_vals, key_ids, query_ids):
    rows, width = queries.shape
    keys = key_ids.shape[0]
    pairs = width // (2 * HEAD)
    return pl.pallas_call(
        attend_kernel,
        out_shape=(
            jax.ShapeDtypeStruct((rows, width), jnp.bfloat16),
            jax.ShapeDtypeStruct((pairs, 2, rows), jnp.float32),
        ),
        in_specs=[pl.BlockSpec(memory_space=pltpu.VMEM)] * 4,
        out_specs=(pl.BlockSpec(memory_space=pltpu.VMEM),) * 2,
        scratch_shapes=[pltpu.VMEM((keys, rows), jnp.float32)],
        compiler_params=pltpu.CompilerParams(vmem_limit_bytes=48 * 2**20),
        cost_estimate=pl.CostEstimate(
            flops=4 * rows * keys * width,
            transcendentals=rows * keys * HEADS,
            bytes_accessed=4 * keys * width,
        ),
        name="attend",
    )(queries, key_vals, key_ids[:, None], query_ids[None, :])


def attend_back_kernel(
    q_ref, kv_ref, grad_ref, lse_ref, key_ids_ref, query_ids_ref, dq_ref, dkv_ref, blocked
):
    groups, twice, unused = kv_ref.shape
    rows = twice // 2
    keys = groups * rows
    scale = HEAD ** (-0.5)
    blocked[...] = jnp.where(key_ids_ref[...] <= query_ids_ref[...], 0.0, MASK_FILL)

    def pair(p, carry):
        lanes = pl.ds(pl.multiple_of(p * 2 * HEAD, 2 * HEAD), 2 * HEAD)
        key_pair = kv_ref[:, :rows, lanes].reshape(keys, 2 * HEAD)
        val_pair = kv_ref[:, rows:, lanes].reshape(keys, 2 * HEAD)
        key_turned = key_pair.T
        query_pair = q_ref[:, lanes]
        grad_pair = grad_ref[:, lanes]
        key_grad = jnp.zeros((keys, 2 * HEAD), jnp.float32)
        val_grad = jnp.zeros((keys, 2 * HEAD), jnp.float32)
        outs = []
        for half in range(2):
            here = head_lanes(half, query_pair.shape)
            query = jnp.where(here, query_pair, 0).astype(jnp.bfloat16)
            grad = jnp.where(here, grad_pair, 0).astype(jnp.bfloat16)
            scores = dot_rows(key_pair, query) * scale + blocked[...]
            probs = jnp.exp(scores - lse_ref[p, half][None, :])
            prob_grad = dot_rows(val_pair, grad)
            inner = jnp.sum(probs * prob_grad, 0, keepdims=True)
            score_grad = (probs * (prob_grad - inner)).astype(jnp.bfloat16)
            key_grad = key_grad + dot_plain(score_grad, query)
            val_grad = val_grad + dot_plain(probs.astype(jnp.bfloat16), grad)
            outs.append(dot_plain(key_turned[half * HEAD : (half + 1) * HEAD], score_grad))
        dq_ref[:, lanes] = (jnp.concatenate(outs, 0).T * scale).astype(dq_ref.dtype)
        dkv_ref[:, :rows, lanes] = (key_grad * scale).reshape(groups, rows, 2 * HEAD)
        dkv_ref[:, rows:, lanes] = val_grad.reshape(groups, rows, 2 * HEAD)
        return carry

    lax.fori_loop(0, q_ref.shape[1] // (2 * HEAD), pair, 0)


def attend_back(queries, key_vals, grad, lse, key_ids, query_ids):
    rows, width = queries.shape
    keys = key_ids.shape[0]
    return pl.pallas_call(
        attend_back_kernel,
        out_shape=(
            jax.ShapeDtypeStruct((rows, width), jnp.bfloat16),
            jax.ShapeDtypeStruct(key_vals.shape, jnp.float32),
        ),
        in_specs=[pl.BlockSpec(memory_space=pltpu.VMEM)] * 6,
        out_specs=(pl.BlockSpec(memory_space=pltpu.VMEM),) * 2,
        scratch_shapes=[pltpu.VMEM((keys, rows), jnp.float32)],
        compiler_params=pltpu.CompilerParams(vmem_limit_bytes=56 * 2**20),
        cost_estimate=pl.CostEstimate(
            flops=10 * rows * keys * width,
            transcendentals=rows * keys * HEADS,
            bytes_accessed=12 * keys * width,
        ),
        name="attend_back",
    )(queries, key_vals, grad, lse, key_ids[:, None], query_ids[None, :])


def add_pair(first, second):
    return first + second


def merge_soft(first, second):
    highest = jnp.maximum(first[0], second[0])
    total = first[1] * jnp.exp(first[0] - highest) + second[1] * jnp.exp(second[0] - highest)
    return jnp.stack([highest, total, first[2] + second[2]])


def dot_rows(left_op, right_op):
    return lax.dot_general(
        left_op, right_op, (((1,), (1,)), ((), ())), preferred_element_type=jnp.float32
    )


def dot_cols(left_op, right_op):
    return lax.dot_general(
        left_op, right_op, (((0,), (0,)), ((), ())), preferred_element_type=jnp.float32
    )


def dot_plain(left_op, right_op):
    return jnp.dot(left_op, right_op, preferred_element_type=jnp.float32)


def column_sums(values):
    return jnp.sum(values.astype(jnp.float32), 0)


def layer_norm(values, gain, shift):
    center = values - jnp.mean(values, -1, keepdims=True)
    spread = jnp.mean(center * center, -1, keepdims=True)
    return center * lax.rsqrt(spread + NORM_EPS) * gain + shift


def norm_back(values, gain, shift, grad):
    unused, pull = jax.vjp(layer_norm, values, gain, shift)
    return pull(grad)


def one_hot(wanted, length, axis):
    shape = list(wanted.shape)
    shape.insert(axis, length)
    at = lax.broadcasted_iota(jnp.int32, shape, axis)
    return (at == jnp.expand_dims(wanted, axis)).astype(jnp.bfloat16)


def counts_before(flags):
    length = flags.shape[-1]
    earlier = (
        lax.broadcasted_iota(jnp.int32, (length, length), 0)
        < lax.broadcasted_iota(jnp.int32, (length, length), 1)
    ).astype(jnp.bfloat16)
    return dot_plain(flags.astype(jnp.bfloat16), earlier).astype(jnp.int32)


def wide(rows_in):
    return jnp.pad(rows_in, ((0, 0), (0, -rows_in.shape[1] % (2 * HEAD))))


def share_keys(key_rows, val_rows):
    pair = jnp.concatenate([wide(key_rows), wide(val_rows)], 0)[None]
    return exchange(
        pair, "share_keys", 4, join_axes=("seq",), join_orders=[bits_of("seq")[::-1]]
    )


def rows_major(x):
    return with_layout_constraint(x, Layout(major_to_minor=tuple(range(x.ndim))))


def scatter_rows(features, cotangents):
    total = lax.axis_size(AXES)
    grad = dot_cols(features, cotangents)
    blocks = rows_major(grad.astype(jnp.bfloat16)).reshape(total, -1, grad.shape[1])
    return lax.psum_scatter(blocks, AXES, scatter_dimension=0, tiled=True)[0]


def layer_forward(state, weights, params, query_ids, key_ids):
    width = state.shape[1]
    hidden = layer_norm(state, params[0], params[1]).astype(jnp.bfloat16)
    joined = dot_rows(hidden, weights[0][: 3 * width])
    queries = wide((joined[:, :width] + params[2]).astype(jnp.bfloat16))
    key_rows = joined[:, width : 2 * width].astype(jnp.bfloat16)
    val_rows = (joined[:, 2 * width :] + params[3]).astype(jnp.bfloat16)
    key_vals = share_keys(key_rows, val_rows)
    attended, lse = attend(queries, key_vals, key_ids, query_ids)
    attended = attended[:, :width]
    mid_state = state + dot_plain(attended, weights[0][3 * width :]) + params[4]
    normed = layer_norm(mid_state, params[5], params[6]).astype(jnp.bfloat16)
    upward = dot_rows(normed, weights[1]) + params[8:12].reshape(-1)
    active = jax.nn.gelu(upward, approximate=True).astype(jnp.bfloat16)
    output = mid_state + dot_plain(active, weights[2]) + params[7]
    return (
        output,
        (hidden, queries, key_vals, lse, attended, mid_state, normed, upward, active),
    )


def layer_backward(state, weights, params, saved, query_ids, key_ids, grad_in):
    width = state.shape[1]
    hidden, queries, key_vals, lse, attended, mid_state, normed, upward, active = saved
    down_grad = grad_in.astype(jnp.bfloat16)
    act_grad = dot_rows(down_grad, weights[2])
    unused_gelu, gelu_pull = jax.vjp(partial(jax.nn.gelu, approximate=True), upward)
    up_grad = gelu_pull(act_grad)[0].astype(jnp.bfloat16)
    mid_back, gain_two, shift_two = norm_back(
        mid_state, params[5], params[6], dot_plain(up_grad, weights[1])
    )
    mid_grad = grad_in + mid_back
    out_grad = mid_grad.astype(jnp.bfloat16)
    att_grad = wide(dot_rows(out_grad, weights[0][3 * width :]).astype(jnp.bfloat16))
    query_grad, pair_grad = attend_back(queries, key_vals, att_grad, lse, key_ids, query_ids)
    own = exchange(
        pair_grad, "return_grads", 8, sum_axes=("seq",), sum_orders=[bits_of("seq")]
    )
    query_grad = query_grad[:, :width]
    key_grad, val_grad = own[: own.shape[0] // 2, :width], own[own.shape[0] // 2 :, :width]
    joined_grad = jnp.concatenate([query_grad, key_grad, val_grad], 1)
    state_back, gain_one, shift_one = norm_back(
        state, params[0], params[1], dot_plain(joined_grad, weights[0][: 3 * width])
    )
    small_grad = jnp.concatenate(
        [
            jnp.stack(
                [
                    gain_one,
                    shift_one,
                    column_sums(query_grad),
                    column_sums(val_grad),
                    column_sums(out_grad),
                    gain_two,
                    shift_two,
                    column_sums(down_grad),
                ]
            ),
            column_sums(up_grad).reshape(4, width),
        ],
        0,
    )
    factors = [(joined_grad, hidden, attended, out_grad), (up_grad, normed), (active, down_grad)]
    return (mid_grad + state_back, factors, small_grad)


def adam_step(weights, moment, square, grad, rate, decay, step):
    moment = BETA_ONE * moment + (1 - BETA_ONE) * grad
    square = BETA_TWO * square + (1 - BETA_TWO) * grad * grad
    moment_hat = moment / (1 - BETA_ONE**step)
    square_hat = square / (1 - BETA_TWO**step)
    weights = weights - rate * (moment_hat / (jnp.sqrt(square_hat) + ADAM_EPS) + decay * weights)
    return (weights, moment, square)


def pad_rows(x, rows):
    return jnp.pad(x, ((0, rows - x.shape[0]), (0, 0)))


def on_device(
    tokens,
    block_ids,
    completion,
    regroup,
    targets,
    step_count,
    layer_mats,
    mats_moment,
    mats_square,
    embed_table,
    table_moment,
    table_square,
):
    seqs, tok_count = tokens.shape
    seq_length = block_ids.shape[1]
    width = embed_table.shape[1]
    table_local = embed_table.shape[0]
    layers = layer_mats.shape[0]
    replicas, groups, shards = (lax.axis_size(axis) for axis in AXES)
    total = replicas * groups * shards
    seq_at = lax.axis_index("seq")
    shard_at = lax.axis_index("shard")
    device_at = lax.axis_index(AXES)
    seq_bits, dp_bits, shard_bits = bits_of("seq"), bits_of("dp"), bits_of("shard")
    first_row = device_at * table_local
    table_own = embed_table.astype(jnp.bfloat16)
    mats_low = layer_mats.astype(jnp.bfloat16)
    token_ids = tokens.reshape(-1)
    local_rows = token_ids.shape[0]
    small_count = 12 * layers + 2
    small_rows = -(-small_count // 16) * 16

    ids_all = exchange(
        jnp.pad(token_ids, (0, -local_rows % 1024)).reshape(1, -1, 128),
        "share_ids",
        0,
        join_axes=AXES,
        join_orders=[shard_bits[::-1] + dp_bits[::-1] + seq_bits[::-1]],
    )
    ids_all = ids_all.reshape(total, -1)[:, :local_rows]
    owner_all = ids_all // table_local
    loads = jnp.sum(
        (owner_all[:, :, None] == jnp.arange(total)[None, None, :]).astype(jnp.int32), 1
    )
    rounds = (jnp.max(loads) + SLOTS - 1) // SLOTS
    asked = owner_all == device_at
    asked_rank = counts_before(asked)
    asked_row = ids_all - first_row
    own_owner = token_ids // table_local
    same = own_owner[:, None] == own_owner[None, :]
    before = jnp.arange(local_rows)[None, :] < jnp.arange(local_rows)[:, None]
    own_rank = jnp.sum((same & before).astype(jnp.int32), 1)

    def asked_rows(at):
        chosen = asked[:, None, :] & (
            asked_rank[:, None, :] == at * SLOTS + jnp.arange(SLOTS)[None, :, None]
        )
        return (jnp.sum(jnp.where(chosen, asked_row[:, None, :] + 1, 0), 2) - 1).reshape(-1)

    def own_slots(at):
        slot = own_rank - at * SLOTS
        return jnp.where((slot >= 0) & (slot < SLOTS), own_owner * SLOTS + slot, -1)

    def fetch(at, given):
        return dot_plain(
            one_hot(own_slots(at), total * SLOTS, 1), given.reshape(total * SLOTS, width)
        )

    fixed = jnp.arange(seq_length + small_rows, dtype=jnp.int32)
    fixed_row = jnp.where(fixed < seq_length + small_count, VOCAB + fixed - first_row, -1)
    wanted = jnp.concatenate([asked_rows(0), fixed_row])
    rows_out = dot_plain(one_hot(wanted, table_local, 1), table_own).astype(jnp.bfloat16)
    exchanged = total * SLOTS
    piece = seq_length // total
    (place_rows,), (small,), (given,) = run_jobs(
        [
            sum_job(
                rows_out[exchanged : exchanged + seq_length].reshape(total, piece, width),
                sum_axes=("seq", "dp", "shard"),
                sum_orders=[seq_bits + dp_bits + shard_bits],
                join_axes=("dp", "shard"),
                join_orders=[shard_bits[::-1] + dp_bits[::-1]],
            ),
            combine_job(rows_out[exchanged + seq_length :], add_pair),
            swap_job(rows_out[:exchanged].reshape(total, SLOTS, width), late=7),
        ],
        "open_rows",
        2,
        32,
    )
    place_rows = place_rows.reshape(tok_count, width)
    small = small[:small_count].astype(jnp.float32)
    place_state = jnp.broadcast_to(place_rows.astype(jnp.float32), (seqs, tok_count, width))
    state = fetch(0, given) + place_state.reshape(local_rows, width)

    def fetch_more(at, held):
        rows = dot_plain(one_hot(asked_rows(at), table_local, 1), table_own).astype(jnp.bfloat16)
        return held + fetch(at, swap(rows.reshape(total, SLOTS, width), "swap_rows", 1))

    state = lax.fori_loop(1, rounds, fetch_more, state)

    query_ids = lax.dynamic_slice_in_dim(block_ids[0], seq_at * tok_count, tok_count, 0)
    inputs, kept, saved = [], [], []
    for layer_at in range(layers):
        weights = [
            lax.all_gather(mats_low[layer_at, k], AXES, axis=0, tiled=True)
            for k in range(layer_mats.shape[1])
        ]
        inputs.append(state)
        kept.append(weights)
        state, held = layer_forward(
            state,
            weights,
            small[12 * layer_at : 12 * layer_at + 12],
            query_ids,
            block_ids[0],
        )
        saved.append(held)
    final_gain = small[12 * layers]
    final_shift = small[12 * layers + 1]
    final = layer_norm(state, final_gain, final_shift).astype(jnp.bfloat16)

    group_mask = completion[0]
    slot_of = regroup[0]
    slots = slot_of.shape[0]
    comp_rows = slots // shards
    rank_all = counts_before(group_mask[None])[0]
    mine = lax.dynamic_slice_in_dim(group_mask, shard_at * local_rows, local_rows)
    my_rank = lax.dynamic_slice_in_dim(rank_all, shard_at * local_rows, local_rows)
    my_slot = jnp.sum(
        jnp.where(my_rank[:, None] == jnp.arange(slots)[None, :], slot_of[None, :], 0), 1
    )
    to_slot = one_hot(jnp.where(mine == 1, my_slot, -1), slots, 0)
    outgoing = dot_plain(to_slot, final).astype(jnp.bfloat16).reshape(shards, comp_rows, width)
    two_ways = [seq_bits[1:] + dp_bits, dp_bits + seq_bits[1:]]
    head_in = exchange(
        outgoing,
        "share_final",
        5,
        sum_axes=("shard",),
        sum_orders=[shard_bits, shard_bits],
        join_axes=AXES,
        join_orders=[shard_bits[::-1] + way[::-1] + seq_bits[:1] for way in two_ways],
        chunks=2,
    ).reshape(-1, width)

    rows_all = targets.shape[0]
    columns = first_row + jnp.arange(table_local, dtype=jnp.int32)
    live = (columns < VOCAB)[None, :]
    logits = dot_rows(head_in, table_own)
    masked = jnp.where(live, logits, MASK_FILL)
    top_local = jnp.max(masked, 1)
    total_local = jnp.sum(jnp.where(live, jnp.exp(masked - top_local[:, None]), 0.0), 1)
    target_hit = columns[None, :] == targets[:, None]
    pick_local = jnp.sum(jnp.where(target_hit, logits, 0.0), 1)
    stats = combine_all(
        jnp.stack([top_local, total_local, pick_local]).reshape(3, -1, 128),
        merge_soft,
        "share_stats",
        6,
    ).reshape(3, rows_all)
    log_total = stats[0] + jnp.log(stats[1])
    loss_value = jnp.sum(log_total - stats[2]) / rows_all
    probs = jnp.where(live, jnp.exp(masked - log_total[:, None]), 0.0)
    logit_grad = ((probs - target_hit.astype(jnp.float32)) / rows_all).astype(jnp.bfloat16)
    head_grad = dot_cols(logit_grad, head_in)
    returned = exchange(
        dot_plain(logit_grad, table_own).reshape(total, comp_rows, width),
        "return_final",
        7,
        sum_axes=AXES,
        sum_orders=[seq_bits[:1] + way + shard_bits for way in two_ways],
        join_axes=("shard",),
        join_orders=[shard_bits[::-1], shard_bits[::-1]],
        chunks=2,
    ).reshape(slots, width)
    final_grad = dot_cols(to_slot, returned)
    state_grad, gain_final, shift_final = norm_back(state, final_gain, final_shift, final_grad)

    mats_grads = [None] * layers
    small_grads = [None] * layers
    for layer_at in reversed(range(layers)):
        state_grad, factors, small_grads[layer_at] = layer_backward(
            inputs[layer_at],
            kept[layer_at],
            small[12 * layer_at : 12 * layer_at + 12],
            saved[layer_at],
            query_ids,
            block_ids[0],
            state_grad,
        )
        first, up, down = factors
        if layer_at > 0:
            joined_grad, hidden, attended, out_grad = first
            total_rows = lax.axis_size(AXES)
            parts = [dot_cols(joined_grad, hidden), dot_cols(attended, out_grad)]
            grad = jnp.concatenate([rows_major(part.astype(jnp.bfloat16)) for part in parts], 0)
            blocks = grad.reshape(total_rows, -1, width)
            state_grad, blocks = lax.optimization_barrier((state_grad, blocks))
            mats_grads[layer_at] = jnp.stack(
                [
                    lax.psum_scatter(blocks, AXES, scatter_dimension=0, tiled=True)[0],
                    scatter_rows(*up),
                    scatter_rows(*down),
                ]
            ).astype(jnp.float32)
        else:
            late = late_mats(first, up, down, 12)

    low_grad = state_grad.astype(jnp.bfloat16)
    place_grad = jnp.sum(state_grad.reshape(seqs, tok_count, width), 0)
    small_grad = pad_rows(
        jnp.concatenate(small_grads + [jnp.stack([gain_final, shift_final])], 0), small_rows
    )

    def leaving(at):
        rows = dot_cols(one_hot(own_slots(at), total * SLOTS, 1), low_grad).astype(jnp.bfloat16)
        return rows.reshape(total, SLOTS, width)

    fits = mats_fit(late)
    own_mats, (place_grad,), (small_grad,), (came,) = run_jobs(
        [
            mats_job(late[:fits]),
            sum_job(
                place_grad.reshape(replicas * shards, piece, width),
                sum_axes=("dp", "shard"),
                sum_orders=[dp_bits + shard_bits],
                join_axes=("seq", "dp", "shard"),
                join_orders=[shard_bits[::-1] + dp_bits[::-1] + seq_bits[::-1]],
            ),
            combine_job(small_grad, add_pair),
            swap_job(leaving(0), late=5),
        ],
        "close_rows",
        10,
        61,
    )
    for k in range(fits, len(late), fits):
        own_mats = own_mats + run_jobs([mats_job(late[k : k + fits])], "sum_mats", 14 + k, 61)[0]
    mats_grads[0] = jnp.stack(own_mats)
    place_grad = place_grad.reshape(seq_length, width)
    small_high = small_grad.astype(jnp.bfloat16)
    small_low = (small_grad - small_high.astype(jnp.float32)).astype(jnp.bfloat16)
    values = jnp.concatenate([came.reshape(-1, width), place_grad, small_high, small_low], 0)
    value_row = jnp.concatenate([wanted, fixed_row[seq_length:]])
    table_grad = dot_plain(one_hot(value_row, table_local, 0), values) + head_grad

    def return_more(at, held):
        rows = swap(leaving(at), "swap_rows", 1).reshape(-1, width)
        return held + dot_plain(one_hot(asked_rows(at), table_local, 0), rows)

    table_grad = lax.fori_loop(1, rounds, return_more, table_grad)
    mats_grad = jnp.stack(mats_grads)
    local_squares = jnp.sum(mats_grad * mats_grad) + jnp.sum(table_grad * table_grad)
    squares = combine_all(jnp.full((8, 128), local_squares), add_pair, "share_norm", 11)
    grad_norm = jnp.sqrt(squares[0, 0])
    factor = CLIP_NORM / grad_norm
    step = step_count[0].astype(jnp.float32)
    new_mats = adam_step(
        layer_mats, mats_moment, mats_square, factor * mats_grad, RATE_MATS, DECAY_RATE, step
    )
    plain_rows = (columns < VOCAB + seq_length)[:, None]
    rate = jnp.where(plain_rows, RATE_TABLE, RATE_SMALL)
    decay = jnp.where(plain_rows, DECAY_RATE, 0.0)
    new_table = adam_step(
        embed_table, table_moment, table_square, factor * table_grad, rate, decay, step
    )
    return (
        loss_value.reshape(1),
        grad_norm.reshape(1),
        new_mats[0],
        new_mats[1],
        new_mats[2],
        new_table[0],
        new_table[1],
        new_table[2],
    )


def solution(mesh):
    in_specs = (
        P(("dp", "shard"), "seq"),
        P(("dp", "shard"), None),
        P(("dp", "seq"), None),
        P(("dp", "seq"), None),
        P(),
        P(),
        P(None, None, ("dp", "seq", "shard"), None),
        P(None, None, ("dp", "seq", "shard"), None),
        P(None, None, ("dp", "seq", "shard"), None),
        P(("dp", "seq", "shard"), None),
        P(("dp", "seq", "shard"), None),
        P(("dp", "seq", "shard"), None),
    )
    out_specs = (
        P(),
        P(),
        P(None, None, ("dp", "seq", "shard"), None),
        P(None, None, ("dp", "seq", "shard"), None),
        P(None, None, ("dp", "seq", "shard"), None),
        P(("dp", "seq", "shard"), None),
        P(("dp", "seq", "shard"), None),
        P(("dp", "seq", "shard"), None),
    )
    return jax.shard_map(
        on_device, mesh=mesh, in_specs=in_specs, out_specs=out_specs, check_vma=False
    )
```

time: 1650 us -> 1480 us (0.90)
  matrix products: 331 us -> 227 us
  Pallas kernels: 688 us -> 770 us
  waiting for transfers between devices: 273 us -> 213 us
  other arithmetic: 149 us -> 106 us
  local copies, waits for them, and re-layouts: 175 us -> 133 us
    unnamed x14 -> x12, waiting for transfers between devices: 235 us -> 3.03 us
    all_gather x2 -> x6, waiting for transfers between devices: 37.9 us -> 210 us  [on_device(): lax.all_gather(mats_low[layer_at, k], AXES, axis=0, tiled=True)]
    pallas_call x15 -> x16, Pallas kernels: 688 us -> 770 us  [the longest x11 669 us: run_jobs(): pl.pallas_call(partial(jobs_kernel, jobs), out_shape=outputs, in_specs=in...]
    dot_general x10 -> x0, matrix products: 82.1 us -> none  [the longest x2 24.4 us: layer_backward(): jnp.einsum('qhd,khd->hqk', att_seq, val_seq, preferred_element_type=jnp.f...]
    reshape x12 -> x6, local copies, waits for them, and re-layouts: 68.8 us -> 10.8 us  [my_rows(): return (mine.reshape(rows, -1), other.reshape(rows, -1))]
    concatenate x4 -> x2, other arithmetic: 44.5 us -> 17.1 us  [the longest x1 14.1 us: on_device(): jnp.concatenate([rows_major(part.astype(jnp.bfloat16)) for part in parts]...]
    convert_element_type x5, other arithmetic: 28 us -> 2.08 us  [the longest x1 1.45 us: on_device(): mats_grads[layer_at] = jnp.stack([lax.psum_scatter(blocks, AXES, scatter_...]
    sub x2 -> x0, matrix products: 24.1 us -> none  [layer_forward(): raised = jnp.exp(scores - jnp.max(scores, -1, keepdims=True))]
  transfers between devices with their start and end apart: 8 -> 9, of which waited for: 3 -> 4; matrix products, arithmetic and copies ran while one was open for 29% -> 24% of each run, Pallas kernels for 30% -> 44%
where the time goes in v2:
time: 1480 us; the launch traced here: 1470 us
  Pallas kernels  770 us (52%)
  matrix products  227 us (15%)
  waiting for transfers between devices  213 us (14%)
  local copies, waits for them, and re-layouts  133 us (9%)
  other arithmetic  106 us (7%)
  between operations  22.4 us (2%)
    pallas_call x11, Pallas kernels, run_jobs(): pl.pallas_call(partial(jobs_kernel, jobs), out_shape=outputs, in_specs=in...  669 us
    all_gather x6, waiting for transfers between devices, on_device(): lax.all_gather(mats_low[layer_at, k], AXES, axis=0, tiled=True)  210 us
    dot_general x15, matrix products, dot_plain(): return jnp.dot(left_op, right_op, preferred_element_type=jnp.float32)  98.6 us
    dot_general x9, matrix products, dot_rows(): lax.dot_general(left_op, right_op, (((1,), (1,)), ((), ())), preferred_el...  70.7 us
    dot_general x11, matrix products, dot_cols(): lax.dot_general(left_op, right_op, (((0,), (0,)), ((), ())), preferred_el...  57.3 us
    pallas_call x2, Pallas kernels, attend_back(): pl.pallas_call(attend_back_kernel, out_shape=(jax.ShapeDtypeStruct((rows,...  51.7 us
    pallas_call x2, Pallas kernels, attend(): pl.pallas_call(attend_kernel, out_shape=(jax.ShapeDtypeStruct((rows, widt...  38.6 us
    unnamed x255, local copies, waits for them, and re-layouts  35.5 us
  transfers between devices with their start and end apart: 9, of which 4 were waited for; matrix products, arithmetic and copies ran while one was open for 24% of the time, Pallas kernels for 44%

profile of v2, /device:TPU:0, one launch (start us, length us, event | category | flops | bytes accessed | tf_op | source)
XLA Modules:
  0.0 1471.9 jit_solution(7714722822149431473)
XLA Ops:
  14.7 18.4 %share_ids.1 = s32[32,8,128]{2,1,0:T(8,128)} custom-call(s32[1,8,128]{2,1,0:T(8,128)} %pad_bitcast_fusion.refs_0_), custom_call_target="tpu_custom_call" | custom-call | tf_op jit(solution)/shard_map/share_ids/pallas_call | solution.py:168
  41.9 11.3 fusion.29
  58.2 99.6 %open_rows.1 = (bf16[8,32,1088]{2,1,0:T(8,128)(2,1)S(1)}, bf16[32,1088]{1,0:T(8,128)(2,1)S(1)}, bf16[32,24,1088]{2,1,0:T(8,128)(2,1)S(1)}) custom-call(bf16[32,32,1088]{2,1,0:T(8,128)(2,1)S(1)} %bitcast.199, bf16[32,1088]{1,0:T(8,128)(2,1)S(1)} %slice.257.refs_1_, bf16[32,24,1088]{2,1,0:T(8,128)(2,1)S(1)} %bitcast.200), custom_call_target="tpu_custom_call" | custom-call | tf_op jit(solution)/shard_map/open_rows/pallas_call | solution.py:168
  188.3 46.3 %share_keys.2.kv_ref = bf16[4,512,1152]{2,1,0:T(8,128)(2,1)} custom-call(bf16[1,512,1152]{2,1,0:T(8,128)(2,1)} %fusion.98.refs_0_), custom_call_target="tpu_custom_call" | custom-call | tf_op jit(solution)/shard_map/share_keys/pallas_call | solution.py:168
  234.8 19.4 %attend.2 = (bf16[256,1152]{1,0:T(8,128)(2,1)S(1)}, f32[9,2,256]{2,1,0:T(2,128)S(1)}) custom-call(bf16[256,1152]{1,0:T(8,128)(2,1)S(1)} %pad.34.q_ref, bf16[4,512,1152]{2,1,0:T(8,128)(2,1)} %share_keys.2.kv_ref, s32[1024,1]{1,0:T(8,128)S(1)} %copy.213.key_ids_ref, s32[1,256]{1,0:T(1,128)S(1)} %constant_dynamic-slice_fusion.7.query_ids_ref), custom_call_target="tpu_custom_call" | custom-call | flops 1207959552 | bytes 4718592 | tf_op jit(solution)/shard_map/attend/pallas_call | solution.py:614
  258.6 10.1 multiply_convert_fusion.1
  268.7 46.2 %all-gather.17.cloned.1.call-done = bf16[1,1,4352,1088]{3,2,1,0:T(8,128)(2,1)} async-done(((bf16[1,1,136,1088]{3,2,1,0:T(8,128)(2,1)}), bf16[1,1,4352,1088]{3,2,1,0:T(8,128)(2,1)}) %all-gather.17.cloned.1.call-update) | async-done | bytes 9469968 | tf_op jit(solution)/shard_map/all_gather | solution.py:958
  323.2 78.3 %all-gather.19.cloned.1.call-done = bf16[1,1,4352,1088]{3,2,1,0:T(8,128)(2,1)} async-done(((bf16[1,1,136,1088]{3,2,1,0:T(8,128)(2,1)}), bf16[1,1,4352,1088]{3,2,1,0:T(8,128)(2,1)}) %all-gather.19.cloned.1.call-update) | async-done | bytes 9469968 | tf_op jit(solution)/shard_map/all_gather | solution.py:958
  419.4 45.1 %share_keys.3.kv_ref = bf16[4,512,1152]{2,1,0:T(8,128)(2,1)} custom-call(bf16[1,512,1152]{2,1,0:T(8,128)(2,1)} %fusion.100.refs_0_), custom_call_target="tpu_custom_call" | custom-call | tf_op jit(solution)/shard_map/share_keys/pallas_call | solution.py:168
  464.6 19.2 %attend.3 = (bf16[256,1152]{1,0:T(8,128)(2,1)S(1)}, f32[9,2,256]{2,1,0:T(2,128)S(1)}) custom-call(bf16[256,1152]{1,0:T(8,128)(2,1)S(1)} %pad.37.q_ref, bf16[4,512,1152]{2,1,0:T(8,128)(2,1)} %share_keys.3.kv_ref, s32[1024,1]{1,0:T(8,128)S(1)} %copy.213.key_ids_ref, s32[1,256]{1,0:T(1,128)S(1)} %constant_dynamic-slice_fusion.7.query_ids_ref), custom_call_target="tpu_custom_call" | custom-call | flops 1207959552 | bytes 4718592 | tf_op jit(solution)/shard_map/attend/pallas_call | solution.py:614
  496.7 9.4 fusion.34
  506.2 76.5 %all-gather.23.cloned.1.call-done = bf16[1,1,4352,1088]{3,2,1,0:T(8,128)(2,1)} async-done(((bf16[1,1,136,1088]{3,2,1,0:T(8,128)(2,1)}), bf16[1,1,4352,1088]{3,2,1,0:T(8,128)(2,1)}) %all-gather.23.cloned.1.call-update) | async-done | bytes 9469968 | tf_op jit(solution)/shard_map/all_gather | solution.py:958
  594.1 47.7 %share_final.1 = bf16[32,64,1088]{2,1,0:T(8,128)(2,1)} custom-call(bf16[4,64,1088]{2,1,0:T(8,128)(2,1)} %bitcast.226), custom_call_target="tpu_custom_call" | custom-call | tf_op jit(solution)/shard_map/share_final/pallas_call | solution.py:168
  641.9 12.5 select_reduce_fusion.3
  659.7 14.1 share_stats.1
  679.5 12.4 fusion.175
  691.9 53.4 %return_final.1 = bf16[4,64,1088]{2,1,0:T(8,128)(2,1)} custom-call(f32[32,64,1088]{2,1,0:T(8,128)} %bitcast.207), custom_call_target="tpu_custom_call" | custom-call | tf_op jit(solution)/shard_map/return_final/pallas_call | solution.py:168
  753.9 10.1 convolution_convert_fusion.1
  779.9 9.9 fusion.173
  801.2 25.7 %attend_back.2 = (bf16[256,1152]{1,0:T(8,128)(2,1)}, f32[4,512,1152]{2,1,0:T(8,128)}) custom-call(bf16[256,1152]{1,0:T(8,128)(2,1)} %copy-done.6, bf16[4,512,1152]{2,1,0:T(8,128)(2,1)} %share_keys.3.kv_ref, bf16[256,1152]{1,0:T(8,128)(2,1)} %pad.40.grad_ref, f32[9,2,256]{2,1,0:T(2,128)} %copy-done.10, s32[1024,1]{1,0:T(8,128)} %copy-done.7, s32[1,256]{1,0:T(1,128)} %copy-done.8), custom_call_target="tpu_custom_call" | custom-call | flops 3019898880 | bytes 14155776 | tf_op jit(solution)/shard_map/attend_back/pallas_call | solution.py:675
  826.9 49.4 %return_grads.2 = bf16[512,1152]{1,0:T(8,128)(2,1)} custom-call(f32[4,512,1152]{2,1,0:T(8,128)} %get-tuple-element.275.refs_0_), custom_call_target="tpu_custom_call" | custom-call | tf_op jit(solution)/shard_map/return_grads/pallas_call | solution.py:168
  911.1 14.1 pad_maximum_fusion
  925.9 13.0 convert_reduce_fusion.1
  943.1 10.4 fusion.171
  963.1 26.0 %attend_back.3 = (bf16[256,1152]{1,0:T(8,128)(2,1)}, f32[4,512,1152]{2,1,0:T(8,128)}) custom-call(bf16[256,1152]{1,0:T(8,128)(2,1)} %copy-done.5, bf16[4,512,1152]{2,1,0:T(8,128)(2,1)} %share_keys.2.kv_ref, bf16[256,1152]{1,0:T(8,128)(2,1)} %pad.41.grad_ref, f32[9,2,256]{2,1,0:T(2,128)} %copy-done.9, s32[1024,1]{1,0:T(8,128)} %copy-done.7, s32[1,256]{1,0:T(1,128)} %copy-done.8), custom_call_target="tpu_custom_call" | custom-call | flops 3019898880 | bytes 14155776 | tf_op jit(solution)/shard_map/attend_back/pallas_call | solution.py:675
  989.1 43.8 %return_grads.3 = bf16[512,1152]{1,0:T(8,128)(2,1)} custom-call(f32[4,512,1152]{2,1,0:T(8,128)} %get-tuple-element.279.refs_0_), custom_call_target="tpu_custom_call" | custom-call | tf_op jit(solution)/shard_map/return_grads/pallas_call | solution.py:168
  1110.1 14.2 fusion.176
  1124.3 11.1 trade_rows.1
  1154.7 238.1 %close_rows.1 = (f32[136,1088]{1,0:T(8,128)}, f32[136,1088]{1,0:T(8,128)}, f32[136,1088]{1,0:T(8,128)}, bf16[32,32,1088]{2,1,0:T(8,128)(2,1)}, f32[32,1088]{1,0:T(8,128)}, /*index=5*/bf16[32,24,1088]{2,1,0:T(8,128)(2,1)}) custom-call(bf16[16,136,1088]{2,1,0:T(8,128)(2,1)} %bitcast.205, bf16[16,136,1088]{2,1,0:T(8,128)(2,1)} %bitcast.212, ...), custom_call_target="tpu_custom_call" | custom-call | tf_op jit(solution)/shard_map/close_rows/pallas_call | solution.py:168
  1396.0 13.3 fusion.28
  1420.6 12.7 share_norm.1
  1443.5 19.2 %multiply_subtract_fusion = (f32[1604,1088]{0,1:T(8,128)}, f32[1604,1088]{0,1:T(8,128)}, f32[1604,1088]{0,1:T(8,128)}) fusion(f32[1604,1088]{0,1:T(8,128)} %param.25, f32[1604]{0:T(1024)S(1)} %copy-done.84, f32[]{:T(128)} %bitcast.67, f32[]{:T(128)} %bitcast.66, f32[1604]{0:T(1024)S(1)} %copy-done.85, f32[1604,1088]{0,1:T(8,128)} %get-tuple-element.295, ...), kind=kLoop, calls=%fused_computation.65 | loop fusion | flops 27922432 | bytes 48877100 | tf_op jit(solution)/shard_map/sub | solution.py:844
  (469 shorter events, 318.5 us)
Async XLA Ops:
  7.2 164.8 %all-gather.13.cloned.1.call-start = ((), (), s32[]{:S(2)}) async-start(), calls=%async_computation.3 | async-start | bytes 10340352 | tf_op jit(solution)/shard_map/all_gather | solution.py:958
  10.8 247.8 %all-gather.15.cloned.1.call-start = ((), (), s32[]{:S(2)}) async-start(), calls=%async_computation.4 | async-start | bytes 10340352 | tf_op jit(solution)/shard_map/all_gather | solution.py:958
  11.5 303.4 %all-gather.17.cloned.1.call-start = ((), (), s32[]{:S(2)}) async-start(), calls=%async_computation.5 | async-start | bytes 10340352 | tf_op jit(solution)/shard_map/all_gather | solution.py:958
  12.3 389.2 %all-gather.19.cloned.1.call-start = ((), (), s32[]{:S(2)}) async-start(), calls=%async_computation.6 | async-start | bytes 10340352 | tf_op jit(solution)/shard_map/all_gather | solution.py:958
  12.8 483.9 %all-gather.21.cloned.1.call-start = ((), (), s32[]{:S(2)}) async-start(), calls=%async_computation.7 | async-start | bytes 10340352 | tf_op jit(solution)/shard_map/all_gather | solution.py:958
  13.4 569.3 %all-gather.23.cloned.1.call-start = ((), (), s32[]{:S(2)}) async-start(), calls=%async_computation.8 | async-start | bytes 10340352 | tf_op jit(solution)/shard_map/all_gather | solution.py:958
  14.0 1401.0 %reduce-scatter.14.cloned.1.call-start = ((), (), s32[]{:S(2)}) async-start(), calls=%async_computation.11 | async-start | bytes 10340352
  14.1 27.8 %copy-start.74 = (s32[1056]{0:T(1024)}, s32[1056]{0:T(1024)S(1)}, u32[]{:S(2)}) copy-start(s32[1056]{0:T(1024)S(1)} %subtract_select_fusion) | copy-start | bytes 12676
  166.1 88.1 %copy-start.11 = (f32[256,1088]{1,0:T(8,128)}, f32[256,1088]{1,0:T(8,128)S(1)}, u32[]{:S(2)}) copy-start(f32[256,1088]{1,0:T(8,128)S(1)} %copy.214) | copy-start | bytes 3342340
  166.6 297.9 %copy-start.7 = (s32[1024,1]{1,0:T(8,128)}, s32[1024,1]{1,0:T(8,128)S(1)}, u32[]{:S(2)}) copy-start(s32[1024,1]{1,0:T(8,128)S(1)} %copy.213.key_ids_ref) | copy-start | bytes 12292
  168.5 296.0 %copy-start.8 = (s32[1,256]{1,0:T(1,128)}, s32[1,256]{1,0:T(1,128)S(1)}, u32[]{:S(2)}) copy-start(s32[1,256]{1,0:T(1,128)S(1)} %constant_dynamic-slice_fusion.7.query_ids_ref) | copy-start | bytes 3076
  170.7 86.8 %copy-start.68 = (f32[1088]{0:T(1024)}, f32[1088]{0:T(1024)S(1)}, u32[]{:S(2)}) copy-start(f32[1088]{0:T(1024)S(1)} %get-tuple-element.320) | copy-start | bytes 13060
  170.7 230.8 %copy-start.70 = (f32[1088]{0:T(1024)}, f32[1088]{0:T(1024)S(1)}, u32[]{:S(2)}) copy-start(f32[1088]{0:T(1024)S(1)} %get-tuple-element.317) | copy-start | bytes 13060
  170.7 230.8 %copy-start.80 = (f32[1088]{0:T(1024)}, f32[1088]{0:T(1024)S(1)}, u32[]{:S(2)}) copy-start(f32[1088]{0:T(1024)S(1)} %get-tuple-element.316) | copy-start | bytes 13060
  234.8 19.4 %copy-start.5 = (bf16[256,1152]{1,0:T(8,128)(2,1)}, bf16[256,1152]{1,0:T(8,128)(2,1)S(1)}, u32[]{:S(2)}) copy-start(bf16[256,1152]{1,0:T(8,128)(2,1)S(1)} %pad.34.q_ref) | copy-start | bytes 1769476
  234.8 19.4 %copy-start.111 = (f32[1088]{0:T(1024)S(1)}, f32[1088]{0:T(1024)}, u32[]{:S(2)}) copy-start(f32[1088]{0:T(1024)} %get-tuple-element.321) | copy-start | bytes 13060
  258.6 56.4 %copy-start.110 = (f32[1088]{0:T(1024)S(1)}, f32[1088]{0:T(1024)}, u32[]{:S(2)}) copy-start(f32[1088]{0:T(1024)} %get-tuple-element.318) | copy-start | bytes 13060
  416.7 47.9 %copy-start.6 = (bf16[256,1152]{1,0:T(8,128)(2,1)}, bf16[256,1152]{1,0:T(8,128)(2,1)S(1)}, u32[]{:S(2)}) copy-start(bf16[256,1152]{1,0:T(8,128)(2,1)S(1)} %pad.37.q_ref) | copy-start | bytes 1769476
  464.6 19.2 %copy-start.109 = (f32[1088]{0:T(1024)S(1)}, f32[1088]{0:T(1024)}, u32[]{:S(2)}) copy-start(f32[1088]{0:T(1024)} %get-tuple-element.313) | copy-start | bytes 13060
  483.8 12.9 copy-start.79
  483.8 12.9 copy-start.93
  496.7 85.9 %copy-start.108 = (f32[1088]{0:T(1024)S(1)}, f32[1088]{0:T(1024)}, u32[]{:S(2)}) copy-start(f32[1088]{0:T(1024)} %get-tuple-element.310) | copy-start | bytes 13060
  594.1 47.7 %copy-start.95 = (pred[1604]{0:T(1024)(128)(4,1)S(1)}, pred[1604]{0:T(1024)(128)(4,1)}, u32[]{:S(2)}) copy-start(pred[1604]{0:T(1024)(128)(4,1)} %fusion.132) | copy-start | bytes 4816
  641.8 12.5 copy-start.73
  641.8 12.5 copy-start.78
  764.0 651.1 %reduce-scatter.12.cloned.1.call-start = ((), (), s32[]{:S(2)}) async-start(), calls=%async_computation.10 | async-start | bytes 10340352
  908.7 506.4 %reduce-scatter.10.cloned.1.call-start = ((), (), s32[]{:S(2)}) async-start(), calls=%async_computation.9 | async-start | bytes 10340352
  925.9 13.0 copy-start.44
  1071.9 22.1 %copy-start.86 = (f32[1088]{0:T(1024)S(1)}, f32[1088]{0:T(1024)}, u32[]{:S(2)}) copy-start(f32[1088]{0:T(1024)} %get-tuple-element.444) | copy-start | bytes 13060
  1395.9 13.3 copy-start.56
  1395.9 13.3 copy-start.62
  1396.0 13.3 copy-start.64
  (101 other events, 404.7 us)
Sparse Core Ops, SparseCore 0:
  10.9 118.8 all-gather.12
  132.6 94.7 all-gather.14
  230.8 84.1 all-gather.16
  318.2 83.2 all-gather.18
  404.2 92.4 all-gather.20
  499.4 83.2 all-gather.22
  764.1 139.6 reduce-scatter.13
  909.9 132.2 reduce-scatter.11
  1124.4 190.4 reduce-scatter.9

commit v3 on v2

--- a/solution.py
+++ b/solution.py
@@ -403,6 +403,7 @@
 
 def mats_stream(x_ref, o_ref, scratch, sems, m, span, order, weights):
     kept, work, parcel, recv = scratch
+    turn, m = m % 2, m % work.shape[0]
     steps = len(order)
     rows = pl.ds(*span)
     slot = 0
@@ -423,7 +424,7 @@
                 keeps.append(
                     sems.local(
                         x_ref.at[pl.ds(mine * weights[bit] + offset, size), rows],
-                        kept.at[m % 2, pl.ds(place, size), rows],
+                        kept.at[turn, pl.ds(place, size), rows],
                     )
                 )
                 runs.append(((1 - mine) * weights[bit] + offset, place))
@@ -457,7 +458,7 @@
 
             def add(i, carry, at=at, keep_at=keep_at, step=step):
                 if step == 0:
-                    total = kept[m % 2, keep_at + i, rows].astype(jnp.float32)
+                    total = kept[turn, keep_at + i, rows].astype(jnp.float32)
                 else:
                     total = work[m, keep_at + i, rows]
                 work[m, keep_at + i, rows] = total + recv[m, at + i, rows].astype(jnp.float32)
@@ -496,15 +497,63 @@
         [jax.ShapeDtypeStruct((rows, width), jnp.float32)] * count,
         [
             pltpu.VMEM((min(2, count), blocks // 2, rows, width), jnp.bfloat16),
-            pltpu.VMEM((count, blocks // 2, rows, width), jnp.float32),
-            pltpu.VMEM((count, blocks // 2 - 1, rows, width), jnp.bfloat16),
-            pltpu.VMEM((count, blocks - 1, rows, width), jnp.bfloat16),
+            pltpu.VMEM((min(3, count), blocks // 2, rows, width), jnp.float32),
+            pltpu.VMEM((min(3, count), blocks // 2 - 1, rows, width), jnp.bfloat16),
+            pltpu.VMEM((min(3, count), blocks - 1, rows, width), jnp.bfloat16),
         ],
         count * sends,
         count * keeps,
         set(orders[0]),
         steps,
         spaces=(pl.ANY, pltpu.VMEM),
+    )
+
+
+def gather_job(parts):
+    rows, width = parts[0].shape
+    spans, orders = sum_orders_for(rows)
+    orders = [order[::-1] + bits_of("seq")[:1] for order in orders]
+    total = lax.axis_size(AXES)
+    sends = 0
+    for order in orders:
+        for step in range(len(order)):
+            sends += len(block_runs([block_weight(AXES, b) for b in order[:step]])[1])
+
+    def gen(x_ref, o_ref, sems, span, order):
+        here = pl.ds(*span)
+        own = me_and_total()[0]
+        keep = sems.local(x_ref.at[here], o_ref.at[own, here])
+        for step, bit in enumerate(order):
+            base = sum(bit_here(b) * block_weight(AXES, b) for b in order[step:])
+            size, offsets = block_runs([block_weight(AXES, b) for b in order[:step]])
+            started = []
+            for offset in offsets:
+                target = o_ref.at[pl.ds(base + offset, size), here]
+                source = x_ref.at[here] if step == 0 else target
+                target = o_ref.at[own, here] if step == 0 else target
+                started.append(sems.copy(source, target, partner(bit)))
+            yield
+            if step == 0:
+                keep.wait()
+            for copy in started:
+                copy.wait()
+
+    def steps(x_refs, o_refs, scratch, sems):
+        return [
+            (m, gen(x_refs[m], o_refs[m], sems, spans[k], orders[k]))
+            for m in range(len(parts))
+            for k in range(len(orders))
+        ]
+
+    return Job(
+        parts,
+        [jax.ShapeDtypeStruct((total, rows, width), parts[0].dtype)] * len(parts),
+        [],
+        sends * len(parts),
+        len(orders) * len(parts),
+        set(orders[0]),
+        steps,
+        spaces=(pl.ANY, pl.ANY),
     )
 
 
@@ -551,11 +600,13 @@
     return mine.reshape(rows, -1), other.reshape(rows, -1)
 
 
-def late_mats(first, up, down, number):
-    joined_grad, hidden, attended, out_grad = first
-    own = up[0].shape[1] // lax.axis_size(AXES) * lax.axis_size("shard")
-    halves = [my_rows(x, own) for x in (joined_grad, attended, up[0], down[0])]
-    tails = [hidden, out_grad, up[1], down[1]]
+def late_mats(groups, number):
+    pairs = [pair for group in groups for pair in group]
+    total = lax.axis_size(AXES)
+    height = sum(features.shape[1] for features, unused in groups[0])
+    own = height // total * lax.axis_size("shard")
+    halves = [my_rows(features, own) for features, unused in pairs]
+    tails = [tail for unused, tail in pairs]
     got = trade([other for unused, other in halves] + tails, "trade_rows", number)
     parts = []
     for k, (mine, unused) in enumerate(halves):
@@ -564,15 +615,19 @@
             jnp.concatenate([tails[k], got[len(halves) + k]], 0),
         )
         parts.append(rows_major(grad.astype(jnp.bfloat16)))
-    mats = [jnp.concatenate(parts[:2], 0), parts[2], parts[3]]
-    blocks = lax.axis_size(AXES) // 2
-    return [grad.reshape(blocks, -1, grad.shape[1]) for grad in mats]
+    mats = []
+    for group in groups:
+        grad = jnp.concatenate(parts[: len(group)], 0) if len(group) > 1 else parts[0]
+        parts = parts[len(group) :]
+        mats.append(grad.reshape(total // 2, -1, grad.shape[1]))
+    return mats
 
 
 def mats_fit(mats):
     blocks, rows, width = mats[0].shape
     tile = -(-rows // 16) * 16 * -(-width // 128) * 128
-    return min(len(mats), max(1, (50 * 2**20 - tile * blocks * 2) // (tile * blocks * 5)))
+    fits = (50 * 2**20 - tile * blocks * 2) // (tile * blocks * 5)
+    return len(mats) if fits >= 3 else max(1, fits)
 
 
 def head_lanes(half, shape):
@@ -791,7 +846,7 @@
     )
 
 
-def layer_backward(state, weights, params, saved, query_ids, key_ids, grad_in):
+def layer_backward(state, weights, params, saved, query_ids, key_ids, grad_in, arrived):
     width = state.shape[1]
     hidden, queries, key_vals, lse, attended, mid_state, normed, upward, active = saved
     down_grad = grad_in.astype(jnp.bfloat16)
@@ -804,6 +859,8 @@
     mid_grad = grad_in + mid_back
     out_grad = mid_grad.astype(jnp.bfloat16)
     att_grad = wide(dot_rows(out_grad, weights[0][3 * width :]).astype(jnp.bfloat16))
+    if arrived:
+        att_grad, arrived[0] = lax.optimization_barrier((att_grad, arrived[0]))
     query_grad, pair_grad = attend_back(queries, key_vals, att_grad, lse, key_ids, query_ids)
     own = exchange(
         pair_grad, "return_grads", 8, sum_axes=("seq",), sum_orders=[bits_of("seq")]
@@ -832,7 +889,11 @@
         ],
         0,
     )
-    factors = [(joined_grad, hidden, attended, out_grad), (up_grad, normed), (active, down_grad)]
+    factors = [
+        [(joined_grad, hidden), (attended, out_grad)],
+        [(up_grad, normed)],
+        [(active, down_grad)],
+    ]
     return (mid_grad + state_back, factors, small_grad)
 
 
@@ -924,8 +985,16 @@
     rows_out = dot_plain(one_hot(wanted, table_local, 1), table_own).astype(jnp.bfloat16)
     exchanged = total * SLOTS
     piece = seq_length // total
-    (place_rows,), (small,), (given,) = run_jobs(
+    gathered = []
+    for layer_at in range(layers):
+        first = lax.all_gather(mats_low[layer_at, 0], AXES, axis=0, tiled=True)
+        rest = [None, None]
+        if layer_at > 0:
+            rest = lax.all_gather(mats_low[layer_at, 1:], AXES, axis=1, tiled=True)
+        gathered.append([first, rest[0], rest[1]])
+    rest, (place_rows,), (small,), (given,) = run_jobs(
         [
+            gather_job([mats_low[0, 1], mats_low[0, 2]]),
             sum_job(
                 rows_out[exchanged : exchanged + seq_length].reshape(total, piece, width),
                 sum_axes=("seq", "dp", "shard"),
@@ -940,6 +1009,7 @@
         2,
         32,
     )
+    gathered[0][1:] = [x.reshape(-1, width) for x in rest]
     place_rows = place_rows.reshape(tok_count, width)
     small = small[:small_count].astype(jnp.float32)
     place_state = jnp.broadcast_to(place_rows.astype(jnp.float32), (seqs, tok_count, width))
@@ -954,10 +1024,7 @@
     query_ids = lax.dynamic_slice_in_dim(block_ids[0], seq_at * tok_count, tok_count, 0)
     inputs, kept, saved = [], [], []
     for layer_at in range(layers):
-        weights = [
-            lax.all_gather(mats_low[layer_at, k], AXES, axis=0, tiled=True)
-            for k in range(layer_mats.shape[1])
-        ]
+        weights = gathered[layer_at]
         inputs.append(state)
         kept.append(weights)
         state, held = layer_forward(
@@ -1029,7 +1096,9 @@
     final_grad = dot_cols(to_slot, returned)
     state_grad, gain_final, shift_final = norm_back(state, final_gain, final_shift, final_grad)
 
-    mats_grads = [None] * layers
+    mats_grads = {}
+    late = []
+    arrived = []
     small_grads = [None] * layers
     for layer_at in reversed(range(layers)):
         state_grad, factors, small_grads[layer_at] = layer_backward(
@@ -1040,24 +1109,13 @@
             query_ids,
             block_ids[0],
             state_grad,
+            arrived,
         )
-        first, up, down = factors
+        late.append(factors[0])
         if layer_at > 0:
-            joined_grad, hidden, attended, out_grad = first
-            total_rows = lax.axis_size(AXES)
-            parts = [dot_cols(joined_grad, hidden), dot_cols(attended, out_grad)]
-            grad = jnp.concatenate([rows_major(part.astype(jnp.bfloat16)) for part in parts], 0)
-            blocks = grad.reshape(total_rows, -1, width)
-            state_grad, blocks = lax.optimization_barrier((state_grad, blocks))
-            mats_grads[layer_at] = jnp.stack(
-                [
-                    lax.psum_scatter(blocks, AXES, scatter_dimension=0, tiled=True)[0],
-                    scatter_rows(*up),
-                    scatter_rows(*down),
-                ]
-            ).astype(jnp.float32)
+            arrived = [scatter_rows(*factors[k][0]) for k in (2, 1)]
         else:
-            late = late_mats(first, up, down, 12)
+            late += factors[1:]
 
     low_grad = state_grad.astype(jnp.bfloat16)
     place_grad = jnp.sum(state_grad.reshape(seqs, tok_count, width), 0)
@@ -1069,6 +1127,9 @@
         rows = dot_cols(one_hot(own_slots(at), total * SLOTS, 1), low_grad).astype(jnp.bfloat16)
         return rows.reshape(total, SLOTS, width)
 
+    (low_grad, arrived[1]) = lax.optimization_barrier((low_grad, arrived[1]))
+    mats_grads[1, 2], mats_grads[1, 1] = (x.astype(jnp.float32) for x in arrived)
+    late = late_mats(late, 12)
     fits = mats_fit(late)
     own_mats, (place_grad,), (small_grad,), (came,) = run_jobs(
         [
@@ -1089,7 +1150,10 @@
     )
     for k in range(fits, len(late), fits):
         own_mats = own_mats + run_jobs([mats_job(late[k : k + fits])], "sum_mats", 14 + k, 61)[0]
-    mats_grads[0] = jnp.stack(own_mats)
+    own_mats = list(own_mats)
+    for layer_at in reversed(range(layers)):
+        mats_grads[layer_at, 0] = own_mats.pop(0)
+    mats_grads[0, 1], mats_grads[0, 2] = own_mats
     place_grad = place_grad.reshape(seq_length, width)
     small_high = small_grad.astype(jnp.bfloat16)
     small_low = (small_grad - small_high.astype(jnp.float32)).astype(jnp.bfloat16)
@@ -1102,7 +1166,9 @@
         return held + dot_plain(one_hot(asked_rows(at), table_local, 0), rows)
 
     table_grad = lax.fori_loop(1, rounds, return_more, table_grad)
-    mats_grad = jnp.stack(mats_grads)
+    mats_grad = jnp.stack(
+        [jnp.stack([mats_grads[layer_at, k] for k in range(3)]) for layer_at in range(layers)]
+    )
     local_squares = jnp.sum(mats_grad * mats_grad) + jnp.sum(table_grad * table_grad)
     squares = combine_all(jnp.full((8, 128), local_squares), add_pair, "share_norm", 11)
     grad_norm = jnp.sqrt(squares[0, 0])

time: 1480 us -> 1340 us (0.905)
  waiting for transfers between devices: 213 us -> 0.83 us
  Pallas kernels: 770 us -> 873 us
  other arithmetic: 106 us -> 88.8 us
    all_gather x6 -> x3, waiting for transfers between devices: 210 us -> 0.06 us  [the longest x2 0.04 us: on_device(): first = lax.all_gather(mats_low[layer_at, 0], AXES, axis=0, tiled=True)]
    pallas_call x11, Pallas kernels: 669 us -> 770 us  [run_jobs(): pl.pallas_call(partial(jobs_kernel, jobs), out_shape=outputs, in_specs=in...]
    unnamed x255 -> x329, local copies, waits for them, and re-layouts: 35.5 us -> 41.6 us
  transfers between devices with their start and end apart: 9 -> 5, of which waited for: 4 -> 0; matrix products, arithmetic and copies ran while one was open for 24% -> 19% of each run, Pallas kernels for 44% -> 38%
where the time goes in v3:
time: 1340 us; the launch traced here: 1330 us
  Pallas kernels  873 us (65%)
  matrix products  218 us (16%)
  local copies, waits for them, and re-layouts  128 us (10%)
  other arithmetic  88.8 us (7%)
  between operations  22.8 us (2%)
    pallas_call x11, Pallas kernels, run_jobs(): pl.pallas_call(partial(jobs_kernel, jobs), out_shape=outputs, in_specs=in...  770 us
    dot_general x15, matrix products, dot_plain(): return jnp.dot(left_op, right_op, preferred_element_type=jnp.float32)  99.1 us
    dot_general x9, matrix products, dot_rows(): lax.dot_general(left_op, right_op, (((1,), (1,)), ((), ())), preferred_el...  63.8 us
    dot_general x11, matrix products, dot_cols(): lax.dot_general(left_op, right_op, (((0,), (0,)), ((), ())), preferred_el...  55.5 us
    pallas_call x2, Pallas kernels, attend_back(): pl.pallas_call(attend_back_kernel, out_shape=(jax.ShapeDtypeStruct((rows,...  51.5 us
    unnamed x329, local copies, waits for them, and re-layouts  41.6 us
    pallas_call x2, Pallas kernels, attend(): pl.pallas_call(attend_kernel, out_shape=(jax.ShapeDtypeStruct((rows, widt...  38.3 us
    sub x2, other arithmetic, adam_step(): weights - rate * (moment_hat / (jnp.sqrt(square_hat) + ADAM_EPS) + decay...  28.1 us
  transfers between devices with their start and end apart: 5, of which 0 were waited for; matrix products, arithmetic and copies ran while one was open for 19% of the time, Pallas kernels for 38%

profile of v3, /device:TPU:0, one launch (start us, length us, event | category | flops | bytes accessed | tf_op | source)
XLA Modules:
  0.0 1332.5 jit_solution(13613482420562258727)
XLA Ops:
  19.8 18.5 %share_ids.1 = s32[32,8,128]{2,1,0:T(8,128)} custom-call(s32[1,8,128]{2,1,0:T(8,128)} %pad_bitcast_fusion.refs_0_), custom_call_target="tpu_custom_call" | custom-call | tf_op jit(solution)/shard_map/share_ids/pallas_call | solution.py:168
  40.3 11.5 fusion.17
  56.8 230.3 %open_rows.1 = (bf16[32,136,1088]{2,1,0:T(8,128)(2,1)S(1)}, bf16[32,136,1088]{2,1,0:T(8,128)(2,1)}, bf16[8,32,1088]{2,1,0:T(8,128)(2,1)S(1)}, bf16[32,1088]{1,0:T(8,128)(2,1)S(1)}, bf16[32,24,1088]{2,1,0:T(8,128)(2,1)S(1)}) custom-call(bf16[136,1088]{1,0:T(8,128)(2,1)S(1)} %get-tuple-element.427.refs_0_, bf16[136,1088]{1,0:T(8,128)(2,1)S(1)} %get-tuple-element.426.refs_1_, ...), custom_call_target="tpu_custom_call" | custom-call | tf_op jit(solution)/shard_map/open_rows/pallas_call | solution.py:168
  322.6 48.6 %share_keys.2.kv_ref = bf16[4,512,1152]{2,1,0:T(8,128)(2,1)} custom-call(bf16[1,512,1152]{2,1,0:T(8,128)(2,1)} %fusion.71.refs_0_), custom_call_target="tpu_custom_call" | custom-call | tf_op jit(solution)/shard_map/share_keys/pallas_call | solution.py:168
  371.4 19.3 %attend.2 = (bf16[256,1152]{1,0:T(8,128)(2,1)S(1)}, f32[9,2,256]{2,1,0:T(2,128)S(1)}) custom-call(bf16[256,1152]{1,0:T(8,128)(2,1)S(1)} %pad.34.q_ref, bf16[4,512,1152]{2,1,0:T(8,128)(2,1)} %share_keys.2.kv_ref, s32[1024,1]{1,0:T(8,128)S(1)} %copy.235.key_ids_ref, s32[1,256]{1,0:T(1,128)S(1)} %constant_dynamic-slice_fusion.11.query_ids_ref), custom_call_target="tpu_custom_call" | custom-call | flops 1207959552 | bytes 4718592 | tf_op jit(solution)/shard_map/attend/pallas_call | solution.py:669
  402.5 8.2 fusion.149
  431.2 36.2 %share_keys.3.kv_ref = bf16[4,512,1152]{2,1,0:T(8,128)(2,1)} custom-call(bf16[1,512,1152]{2,1,0:T(8,128)(2,1)} %fusion.73.refs_0_), custom_call_target="tpu_custom_call" | custom-call | tf_op jit(solution)/shard_map/share_keys/pallas_call | solution.py:168
  467.4 19.0 %attend.3 = (bf16[256,1152]{1,0:T(8,128)(2,1)S(1)}, f32[9,2,256]{2,1,0:T(2,128)S(1)}) custom-call(bf16[256,1152]{1,0:T(8,128)(2,1)S(1)} %pad.37.q_ref, bf16[4,512,1152]{2,1,0:T(8,128)(2,1)} %share_keys.3.kv_ref, s32[1024,1]{1,0:T(8,128)S(1)} %copy.235.key_ids_ref, s32[1,256]{1,0:T(1,128)S(1)} %constant_dynamic-slice_fusion.11.query_ids_ref), custom_call_target="tpu_custom_call" | custom-call | flops 1207959552 | bytes 4718592 | tf_op jit(solution)/shard_map/attend/pallas_call | solution.py:669
  498.6 8.9 fusion.151
  510.1 49.9 %share_final.1 = bf16[32,64,1088]{2,1,0:T(8,128)(2,1)} custom-call(bf16[4,64,1088]{2,1,0:T(8,128)(2,1)} %bitcast.232), custom_call_target="tpu_custom_call" | custom-call | tf_op jit(solution)/shard_map/share_final/pallas_call | solution.py:168
  560.1 12.1 select_reduce_fusion.3
  577.5 14.5 %share_stats.1 = f32[3,16,128]{2,1,0:T(8,128)S(1)} custom-call(f32[3,16,128]{2,1,0:T(8,128)S(1)} %pad_maximum_fusion.3.refs_0_), custom_call_target="tpu_custom_call" | custom-call | tf_op jit(solution)/shard_map/share_stats/pallas_call | solution.py:168
  597.6 12.6 fusion.157
  610.2 52.9 %return_final.1 = bf16[4,64,1088]{2,1,0:T(8,128)(2,1)} custom-call(f32[32,64,1088]{2,1,0:T(8,128)} %bitcast.210), custom_call_target="tpu_custom_call" | custom-call | tf_op jit(solution)/shard_map/return_final/pallas_call | solution.py:168
  670.1 10.2 convolution_convert_fusion.2
  699.6 8.8 convert_reduce_fusion
  708.5 9.9 fusion.155
  731.2 25.9 %attend_back.2 = (bf16[256,1152]{1,0:T(8,128)(2,1)}, f32[4,512,1152]{2,1,0:T(8,128)}) custom-call(bf16[256,1152]{1,0:T(8,128)(2,1)} %copy-done.4, bf16[4,512,1152]{2,1,0:T(8,128)(2,1)} %share_keys.3.kv_ref, bf16[256,1152]{1,0:T(8,128)(2,1)} %pad.40.grad_ref, f32[9,2,256]{2,1,0:T(2,128)} %copy-done.9, s32[1024,1]{1,0:T(8,128)} %copy-done.5, s32[1,256]{1,0:T(1,128)} %copy-done.6), custom_call_target="tpu_custom_call" | custom-call | flops 3019898880 | bytes 14155776 | tf_op jit(solution)/shard_map/attend_back/pallas_call | solution.py:730
  757.1 43.3 %return_grads.2 = bf16[512,1152]{1,0:T(8,128)(2,1)} custom-call(f32[4,512,1152]{2,1,0:T(8,128)} %get-tuple-element.286.refs_0_), custom_call_target="tpu_custom_call" | custom-call | tf_op jit(solution)/shard_map/return_grads/pallas_call | solution.py:168
  810.5 8.7 convolution_convert_fusion.1
  820.6 7.9 fusion.154
  832.2 9.2 convert_reduce_fusion.1
  843.9 9.0 fusion.153
  883.2 14.3 %fusion.158 = f32[1604,1088]{0,1:T(8,128)} fusion(bf16[2048,1604]{0,1:T(8,128)(2,1)} %copy-done.36, bf16[2048,1088]{1,0:T(8,128)(2,1)} %bitcast.220), kind=kOutput, calls=%fused_computation.359 | convolution fusion | flops 7148142592 | bytes 18007040 | tf_op jit(solution)/shard_map/dot_general | solution.py:766
  897.5 25.7 %attend_back.3 = (bf16[256,1152]{1,0:T(8,128)(2,1)}, f32[4,512,1152]{2,1,0:T(8,128)}) custom-call(bf16[256,1152]{1,0:T(8,128)(2,1)} %copy-done.3, bf16[4,512,1152]{2,1,0:T(8,128)(2,1)} %share_keys.2.kv_ref, bf16[256,1152]{1,0:T(8,128)(2,1)} %pad.41.grad_ref, f32[9,2,256]{2,1,0:T(2,128)} %copy-done.8, s32[1024,1]{1,0:T(8,128)} %copy-done.5, s32[1,256]{1,0:T(1,128)} %copy-done.6), custom_call_target="tpu_custom_call" | custom-call | flops 3019898880 | bytes 14155776 | tf_op jit(solution)/shard_map/attend_back/pallas_call | solution.py:730
  923.1 41.0 %return_grads.3 = bf16[512,1152]{1,0:T(8,128)(2,1)} custom-call(f32[4,512,1152]{2,1,0:T(8,128)} %get-tuple-element.290.refs_0_), custom_call_target="tpu_custom_call" | custom-call | tf_op jit(solution)/shard_map/return_grads/pallas_call | solution.py:168
  994.1 13.4 %trade_rows.1 = (bf16[256,1632]{1,0:T(8,128)(2,1)}, bf16[256,544]{1,0:T(8,128)(2,1)}, bf16[256,1632]{1,0:T(8,128)(2,1)}, bf16[256,544]{1,0:T(8,128)(2,1)}, bf16[...) custom-call(bf16[256,1632]{1,0:T(8,128)(2,1)} %copy.263.refs_0_, ...), custom_call_target="tpu_custom_call" | custom-call | tf_op jit(solution)/shard_map/trade_rows/pallas_call | solution.py:583
  1033.2 221.2 %close_rows.1 = (f32[136,1088]{1,0:T(8,128)}, f32[136,1088]{1,0:T(8,128)}, f32[136,1088]{1,0:T(8,128)}, f32[136,1088]{1,0:T(8,128)}, bf16[32,32,1088]{2,1,0:T(8,...) custom-call(bf16[16,136,1088]{2,1,0:T(8,128)(2,1)} %bitcast.207, bf16[16,136,1088]{2,1,0:T(8,128)(2,1)} %bitcast.208, ...), custom_call_target="tpu_custom_call" | custom-call | tf_op jit(solution)/shard_map/close_rows/pallas_call | solution.py:168
  1255.4 13.4 %fusion.12 = f32[1604,1088]{0,1:T(8,128)} fusion(f32[1604,1088]{0,1:T(8,128)} %fusion.158, s32[1856]{0:T(1024)S(1)} %copy-done.146, bf16[32,1088]{1,0:T(8,128)(2,1)S(1)} %get-tuple-element.386, bf16[32,1088]{1,0:T(8,128)(2,1)S(1)} %get-tuple-element.387, bf16[1024,1088]{1,0:T(8,128)(2,1)} %bitcast.263, bf16[768,1088]{1,0:T(8,128)(2,1)} %bitcast.264), kind=kOutput, calls=%fused_computation.42 | convolution fusion | flops 6498880512 | bytes 18007296 | tf_op jit(solution)/shard_map/dot_general | solution.py:772
  1280.5 13.6 %share_norm.1 = f32[8,128]{1,0:T(8,128)S(1)} custom-call(f32[8,128]{1,0:T(8,128)S(1)} %broadcast_in_dim.231.refs_0_), custom_call_target="tpu_custom_call" | custom-call | tf_op jit(solution)/shard_map/share_norm/pallas_call | solution.py:168
  1295.4 8.9 multiply_subtract_fusion.1
  1304.3 19.2 %multiply_subtract_fusion = (f32[1604,1088]{0,1:T(8,128)}, f32[1604,1088]{0,1:T(8,128)}, f32[1604,1088]{0,1:T(8,128)}) fusion(f32[1604,1088]{0,1:T(8,128)} %param.25, f32[1604]{0:T(1024)S(1)} %copy-done.99, f32[]{:T(128)} %bitcast.78, f32[]{:T(128)} %bitcast.77, f32[1604]{0:T(1024)S(1)} %copy-done.100, f32[1604,1088]{0,1:T(8,128)} %get-tuple-element.313, ...), kind=kLoop, calls=%fused_computation.53 | loop fusion | flops 27922432 | bytes 48877100 | tf_op jit(solution)/shard_map/sub | solution.py:905
  (543 shorter events, 263.6 us)
Async XLA Ops:
  7.2 299.2 %all-gather.7.cloned.1.call-start = ((), (), s32[]{:S(2)}) async-start(), calls=%async_computation.2 | async-start | bytes 10340352 | tf_op jit(solution)/shard_map/all_gather | solution.py:990
  10.4 400.9 %all-gather.9.cloned.1.call-start = ((), (), s32[]{:S(2)}) async-start(), calls=%async_computation.3 | async-start | bytes 10340352 | tf_op jit(solution)/shard_map/all_gather | solution.py:990
  11.2 479.4 %all-gather.11.cloned.1.call-start = ((), (), s32[]{:S(2)}) async-start(), calls=%async_computation.4 | async-start | bytes 20680704 | tf_op jit(solution)/shard_map/all_gather | solution.py:993
  12.2 885.2 %reduce-scatter.7.cloned.1.call-start = ((), (), s32[]{:S(2)}) async-start(), calls=%async_computation.5 | async-start | bytes 10340352
  40.2 11.6 copy-start.94
  40.2 11.6 copy-start.92
  301.3 90.0 %copy-start.13 = (f32[256,1088]{1,0:T(8,128)}, f32[256,1088]{1,0:T(8,128)S(1)}, u32[]{:S(2)}) copy-start(f32[256,1088]{1,0:T(8,128)S(1)} %copy.236) | copy-start | bytes 3342340
  301.7 165.7 %copy-start.5 = (s32[1024,1]{1,0:T(8,128)}, s32[1024,1]{1,0:T(8,128)S(1)}, u32[]{:S(2)}) copy-start(s32[1024,1]{1,0:T(8,128)S(1)} %copy.235.key_ids_ref) | copy-start | bytes 12292
  303.0 164.4 %copy-start.6 = (s32[1,256]{1,0:T(1,128)}, s32[1,256]{1,0:T(1,128)S(1)}, u32[]{:S(2)}) copy-start(s32[1,256]{1,0:T(1,128)S(1)} %constant_dynamic-slice_fusion.11.query_ids_ref) | copy-start | bytes 3076
  305.1 89.4 %copy-start.83 = (f32[1088]{0:T(1024)}, f32[1088]{0:T(1024)S(1)}, u32[]{:S(2)}) copy-start(f32[1088]{0:T(1024)S(1)} %get-tuple-element.338) | copy-start | bytes 13060
  305.1 105.9 %copy-start.85 = (f32[1088]{0:T(1024)}, f32[1088]{0:T(1024)S(1)}, u32[]{:S(2)}) copy-start(f32[1088]{0:T(1024)S(1)} %get-tuple-element.335) | copy-start | bytes 13060
  371.2 23.7 %slice-start = ((s8[10027008]{0:T(1024)(128)(4,1)}), s8[1638400]{0:T(1024)(128)(4,1)S(1)}, s32[]{:S(2)}) async-start(s8[10027008]{0:T(1024)(128)(4,1)} %bitcast.203), calls=%async_computation.7 | async-start | bytes 3276800
  371.4 19.3 %copy-start.3 = (bf16[256,1152]{1,0:T(8,128)(2,1)}, bf16[256,1152]{1,0:T(8,128)(2,1)S(1)}, u32[]{:S(2)}) copy-start(bf16[256,1152]{1,0:T(8,128)(2,1)S(1)} %pad.34.q_ref) | copy-start | bytes 1769476
  371.4 20.0 %copy-start.141 = (f32[1088]{0:T(1024)S(1)}, f32[1088]{0:T(1024)}, u32[]{:S(2)}) copy-start(f32[1088]{0:T(1024)} %get-tuple-element.339) | copy-start | bytes 13060
  371.4 23.5 %slice-start.1 = ((s8[10027008]{0:T(1024)(128)(4,1)}), s8[4194304]{0:T(1024)(128)(4,1)S(1)}, s32[]{:S(2)}) async-start(s8[10027008]{0:T(1024)(128)(4,1)} %bitcast.203), calls=%async_computation.8 | async-start | bytes 8388608
  427.5 40.0 %copy-start.4 = (bf16[256,1152]{1,0:T(8,128)(2,1)}, bf16[256,1152]{1,0:T(8,128)(2,1)S(1)}, u32[]{:S(2)}) copy-start(bf16[256,1152]{1,0:T(8,128)(2,1)S(1)} %pad.37.q_ref) | copy-start | bytes 1769476
  467.4 19.0 %copy-start.139 = (f32[1088]{0:T(1024)S(1)}, f32[1088]{0:T(1024)}, u32[]{:S(2)}) copy-start(f32[1088]{0:T(1024)} %get-tuple-element.331) | copy-start | bytes 13060
  498.6 10.0 copy-start.88
  498.6 10.0 copy-start.98
  498.6 10.0 copy-start.131
  510.1 49.9 %copy-start.109 = (pred[1604]{0:T(1024)(128)(4,1)S(1)}, pred[1604]{0:T(1024)(128)(4,1)}, u32[]{:S(2)}) copy-start(pred[1604]{0:T(1024)(128)(4,1)} %fusion.112) | copy-start | bytes 4816
  560.1 12.1 copy-start.89
  560.1 12.1 copy-start.96
  597.6 12.6 copy-start.36
  670.1 10.2 copy-start.72
  680.3 304.1 %reduce-scatter.9.cloned.1.call-start = ((), (), s32[]{:S(2)}) async-start(), calls=%async_computation.6 | async-start | bytes 10340352
  994.1 13.4 %copy-start.51 = (bf16[256,1088]{1,0:T(8,128)(2,1)S(1)}, bf16[256,1088]{1,0:T(8,128)(2,1)}, u32[]{:S(2)}) copy-start(bf16[256,1088]{1,0:T(8,128)(2,1)} %copy-done.50) | copy-start | bytes 1671172
  994.1 13.4 %copy-start.75 = (bf16[256,1,1,544]{3,0,2,1:T(8,128)(2,1)S(1)}, bf16[256,1,1,544]{3,0,2,1:T(8,128)(2,1)}, u32[]{:S(2)}) copy-start(bf16[256,1,1,544]{3,0,2,1:T(8,128)(2,1)} %copy.268) | copy-start | bytes 835588
  1033.2 222.2 %copy-start.146 = (s32[1856]{0:T(1024)S(1)}, s32[1856]{0:T(1024)}, u32[]{:S(2)}) copy-start(s32[1856]{0:T(1024)} %concatenate.88) | copy-start | bytes 22276
  1255.4 13.5 %copy-start.64 = (pred[32,256]{1,0:T(32,128)(4,1)S(1)}, pred[32,256]{1,0:T(32,128)(4,1)}, u32[]{:S(2)}) copy-start(pred[32,256]{1,0:T(32,128)(4,1)} %copy-done.63) | copy-start | bytes 24580
  1255.4 13.5 %copy-start.78 = (s32[256]{0:T(256)S(1)}, s32[256]{0:T(256)}, u32[]{:S(2)}) copy-start(s32[256]{0:T(256)} %copy-done.77) | copy-start | bytes 3076
  1255.4 13.5 %copy-start.80 = (s32[256]{0:T(256)S(1)}, s32[256]{0:T(256)}, u32[]{:S(2)}) copy-start(s32[256]{0:T(256)} %copy-done.79) | copy-start | bytes 3076
  (134 other events, 479.3 us)
Sparse Core Ops, SparseCore 0:
  11.4 117.7 all-gather.6
  132.7 131.9 all-gather.8
  267.7 143.4 all-gather.10
  680.4 132.4 reduce-scatter.6
  819.3 134.0 reduce-scatter.8

commit v4 on v3

--- a/solution.py
+++ b/solution.py
@@ -396,9 +396,9 @@
     across, along, deep = bits_of("seq")[1:], bits_of("dp"), bits_of("shard")
     if rows < 64 or rows % 8:
         return [(0, rows)], [across + along + deep]
-    one = rows * 6 // 17 // 16 * 16
-    spans = [(0, one), (one, one), (2 * one, rows - 2 * one)]
-    return spans, [across + along + deep, along + across + deep, deep + across + along]
+    one, two = rows * 8 // 17 // 16 * 16, rows * 6 // 17 // 16 * 16
+    spans = [(0, one), (one, two), (one + two, rows - one - two)]
+    return spans, [across + along + deep, along + across + deep, deep + along + across]
 
 
 def mats_stream(x_ref, o_ref, scratch, sems, m, span, order, weights):
@@ -509,54 +509,6 @@
     )
 
 
-def gather_job(parts):
-    rows, width = parts[0].shape
-    spans, orders = sum_orders_for(rows)
-    orders = [order[::-1] + bits_of("seq")[:1] for order in orders]
-    total = lax.axis_size(AXES)
-    sends = 0
-    for order in orders:
-        for step in range(len(order)):
-            sends += len(block_runs([block_weight(AXES, b) for b in order[:step]])[1])
-
-    def gen(x_ref, o_ref, sems, span, order):
-        here = pl.ds(*span)
-        own = me_and_total()[0]
-        keep = sems.local(x_ref.at[here], o_ref.at[own, here])
-        for step, bit in enumerate(order):
-            base = sum(bit_here(b) * block_weight(AXES, b) for b in order[step:])
-            size, offsets = block_runs([block_weight(AXES, b) for b in order[:step]])
-            started = []
-            for offset in offsets:
-                target = o_ref.at[pl.ds(base + offset, size), here]
-                source = x_ref.at[here] if step == 0 else target
-                target = o_ref.at[own, here] if step == 0 else target
-                started.append(sems.copy(source, target, partner(bit)))
-            yield
-            if step == 0:
-                keep.wait()
-            for copy in started:
-                copy.wait()
-
-    def steps(x_refs, o_refs, scratch, sems):
-        return [
-            (m, gen(x_refs[m], o_refs[m], sems, spans[k], orders[k]))
-            for m in range(len(parts))
-            for k in range(len(orders))
-        ]
-
-    return Job(
-        parts,
-        [jax.ShapeDtypeStruct((total, rows, width), parts[0].dtype)] * len(parts),
-        [],
-        sends * len(parts),
-        len(orders) * len(parts),
-        set(orders[0]),
-        steps,
-        spaces=(pl.ANY, pl.ANY),
-    )
-
-
 def trade_kernel(count, *refs):
     x_refs, o_refs = refs[:count], refs[count : 2 * count]
     send_sems, recv_sems = refs[2 * count :]
@@ -635,14 +587,71 @@
     return (lane < HEAD) if half == 0 else (lane >= HEAD)
 
 
-def attend_kernel(q_ref, kv_ref, key_ids_ref, query_ids_ref, o_ref, lse_ref, blocked):
-    groups, twice, unused = kv_ref.shape
-    rows = twice // 2
-    keys = groups * rows
+def pair_lanes(p):
+    return pl.ds(pl.multiple_of(p * 2 * HEAD, 2 * HEAD), 2 * HEAD)
+
+
+def seq_places():
+    me = lax.axis_index("seq")
+    return me, partner(("seq", 0))["seq"], partner(("seq", 1))["seq"]
+
+
+def to_seq(source, target, sems, k, place):
+    return pltpu.make_async_remote_copy(
+        source,
+        target,
+        sems.at[0, k],
+        sems.at[1, k],
+        device_id={"seq": place},
+        device_id_type=MESH,
+    )
+
+
+def attend_kernel(
+    q_ref, own_ref, key_ids_ref, query_ids_ref, o_ref, lse_ref, kv_ref, blocked, far, near, pass_on, own_sem
+):
+    rows = own_ref.shape[0] // 2
+    keys = kv_ref.shape[0] * rows
+    pairs = q_ref.shape[1] // (2 * HEAD)
+    me, near_at, far_at = seq_places()
+    beyond = near_at + far_at - me
+    greet([("seq", 0), ("seq", 1)])
+
+    def far_copy(p, at):
+        return to_seq(own_ref.at[:, pair_lanes(p)], kv_ref.at[at, :, pair_lanes(p)], far, p, far_at)
+
+    def near_copy(p, at):
+        return to_seq(own_ref.at[:, pair_lanes(p)], kv_ref.at[at, :, pair_lanes(p)], near, p, near_at)
+
+    def pass_copy(p, at):
+        here = kv_ref.at[far_at, :, pair_lanes(p)]
+        return to_seq(here, kv_ref.at[at, :, pair_lanes(p)], pass_on, p, near_at)
+
+    def send(p, carry):
+        far_copy(p, me).start()
+        near_copy(p, me).start()
+        return carry
+
+    lax.fori_loop(0, pairs, send, 0)
+    own = pltpu.make_async_copy(own_ref, kv_ref.at[me], own_sem)
+    own.start()
     blocked[...] = jnp.where(key_ids_ref[...] <= query_ids_ref[...], 0.0, MASK_FILL)
+    own.wait()
+
+    def forward_one(p):
+        far_copy(p, far_at).wait_recv()
+        pass_copy(p, far_at).start()
+
+    forward_one(0)
 
     def pair(p, carry):
-        lanes = pl.ds(pl.multiple_of(p * 2 * HEAD, 2 * HEAD), 2 * HEAD)
+        @pl.when(p + 1 < pairs)
+        def _():
+            forward_one(p + 1)
+
+        near_copy(p, near_at).wait_recv()
+        pass_copy(p, beyond).wait_recv()
+        lanes = pair_lanes(p)
         key_pair = kv_ref[:, :rows, lanes].reshape(keys, 2 * HEAD)
         val_turned = kv_ref[:, rows:, lanes].reshape(keys, 2 * HEAD).T
         query_pair = q_ref[:, lanes]
@@ -659,43 +668,100 @@
         o_ref[:, lanes] = jnp.concatenate(outs, 0).T.astype(o_ref.dtype)
         return carry
 
-    lax.fori_loop(0, q_ref.shape[1] // (2 * HEAD), pair, 0)
-
-
-def attend(queries, key_vals, key_ids, query_ids):
+    lax.fori_loop(0, pairs, pair, 0)
+
+    def sent(p, carry):
+        far_copy(p, me).wait_send()
+        near_copy(p, me).wait_send()
+        pass_copy(p, far_at).wait_send()
+        return carry
+
+    lax.fori_loop(0, pairs, sent, 0)
+
+
+def attend(queries, own_pair, key_ids, query_ids, number):
     rows, width = queries.shape
     keys = key_ids.shape[0]
     pairs = width // (2 * HEAD)
+    groups = lax.axis_size("seq")
+    copies = pltpu.SemaphoreType.DMA((2, pairs))
     return pl.pallas_call(
         attend_kernel,
         out_shape=(
             jax.ShapeDtypeStruct((rows, width), jnp.bfloat16),
             jax.ShapeDtypeStruct((pairs, 2, rows), jnp.float32),
+            jax.ShapeDtypeStruct((groups,) + own_pair.shape, jnp.bfloat16),
         ),
         in_specs=[pl.BlockSpec(memory_space=pltpu.VMEM)] * 4,
-        out_specs=(pl.BlockSpec(memory_space=pltpu.VMEM),) * 2,
-        scratch_shapes=[pltpu.VMEM((keys, rows), jnp.float32)],
-        compiler_params=pltpu.CompilerParams(vmem_limit_bytes=48 * 2**20),
+        out_specs=(pl.BlockSpec(memory_space=pltpu.VMEM),) * 3,
+        scratch_shapes=[
+            pltpu.VMEM((keys, rows), jnp.float32),
+            copies,
+            copies,
+            copies,
+            pltpu.SemaphoreType.DMA,
+        ],
+        compiler_params=pltpu.CompilerParams(
+            collective_id=number, has_side_effects=True, vmem_limit_bytes=48 * 2**20
+        ),
         cost_estimate=pl.CostEstimate(
             flops=4 * rows * keys * width,
             transcendentals=rows * keys * HEADS,
             bytes_accessed=4 * keys * width,
         ),
         name="attend",
-    )(queries, key_vals, key_ids[:, None], query_ids[None, :])
+    )(queries, own_pair, key_ids[:, None], query_ids[None, :])
 
 
 def attend_back_kernel(
-    q_ref, kv_ref, grad_ref, lse_ref, key_ids_ref, query_ids_ref, dq_ref, dkv_ref, blocked
+    q_ref,
+    kv_ref,
+    grad_ref,
+    lse_ref,
+    key_ids_ref,
+    query_ids_ref,
+    dq_ref,
+    own_ref,
+    blocked,
+    fresh,
+    kept,
+    near_out,
+    near_in,
+    far_out,
+    far_in,
+    near,
+    far,
 ):
     groups, twice, unused = kv_ref.shape
     rows = twice // 2
     keys = groups * rows
+    pairs = q_ref.shape[1] // (2 * HEAD)
     scale = HEAD ** (-0.5)
+    me, near_at, far_at = seq_places()
+    low, high = lax.rem(me, 2), me // 2
+    greet([("seq", 0), ("seq", 1)])
     blocked[...] = jnp.where(key_ids_ref[...] <= query_ids_ref[...], 0.0, MASK_FILL)
 
+    def near_copy(p):
+        return to_seq(near_out.at[p], near_in.at[p], near, p, near_at)
+
+    def far_copy(p):
+        return to_seq(far_out.at[p], far_in.at[p], far, p, far_at)
+
+    def middle(p):
+        near_copy(p).wait()
+        for k in range(2):
+            kept[p, k] = kept[p, k] + near_in[p, k].astype(jnp.float32)
+        far_out[p] = kept[p, 1 - high].astype(far_out.dtype)
+        far_copy(p).start()
+
+    def last(p):
+        far_copy(p).wait()
+        total = kept[p, high] + far_in[p].astype(jnp.float32)
+        own_ref[:, pair_lanes(p)] = total.astype(own_ref.dtype)
+
     def pair(p, carry):
-        lanes = pl.ds(pl.multiple_of(p * 2 * HEAD, 2 * HEAD), 2 * HEAD)
+        lanes = pair_lanes(p)
         key_pair = kv_ref[:, :rows, lanes].reshape(keys, 2 * HEAD)
         val_pair = kv_ref[:, rows:, lanes].reshape(keys, 2 * HEAD)
         key_turned = key_pair.T
@@ -717,26 +783,57 @@
             val_grad = val_grad + dot_plain(probs.astype(jnp.bfloat16), grad)
             outs.append(dot_plain(key_turned[half * HEAD : (half + 1) * HEAD], score_grad))
         dq_ref[:, lanes] = (jnp.concatenate(outs, 0).T * scale).astype(dq_ref.dtype)
-        dkv_ref[:, :rows, lanes] = (key_grad * scale).reshape(groups, rows, 2 * HEAD)
-        dkv_ref[:, rows:, lanes] = val_grad.reshape(groups, rows, 2 * HEAD)
+        fresh[:, :rows] = (key_grad * scale).reshape(groups, rows, 2 * HEAD)
+        fresh[:, rows:] = val_grad.reshape(groups, rows, 2 * HEAD)
+        for k in range(2):
+            near_out[p, k] = fresh[2 * k + 1 - low].astype(near_out.dtype)
+            kept[p, k] = fresh[2 * k + low]
+        near_copy(p).start()
+
+        @pl.when(p >= 1)
+        def _():
+            middle(p - 1)
+
+        @pl.when(p >= 2)
+        def _():
+            last(p - 2)
+
         return carry
 
-    lax.fori_loop(0, q_ref.shape[1] // (2 * HEAD), pair, 0)
-
-
-def attend_back(queries, key_vals, grad, lse, key_ids, query_ids):
+    lax.fori_loop(0, pairs, pair, 0)
+    middle(pairs - 1)
+    last(pairs - 2)
+    last(pairs - 1)
+
+
+def attend_back(queries, key_vals, grad, lse, key_ids, query_ids, number):
     rows, width = queries.shape
     keys = key_ids.shape[0]
+    pairs = width // (2 * HEAD)
+    piece = (2 * rows, 2 * HEAD)
+    copies = pltpu.SemaphoreType.DMA((2, pairs))
     return pl.pallas_call(
         attend_back_kernel,
         out_shape=(
             jax.ShapeDtypeStruct((rows, width), jnp.bfloat16),
-            jax.ShapeDtypeStruct(key_vals.shape, jnp.float32),
+            jax.ShapeDtypeStruct((2 * rows, width), jnp.bfloat16),
         ),
         in_specs=[pl.BlockSpec(memory_space=pltpu.VMEM)] * 6,
         out_specs=(pl.BlockSpec(memory_space=pltpu.VMEM),) * 2,
-        scratch_shapes=[pltpu.VMEM((keys, rows), jnp.float32)],
-        compiler_params=pltpu.CompilerParams(vmem_limit_bytes=56 * 2**20),
+        scratch_shapes=[
+            pltpu.VMEM((keys, rows), jnp.float32),
+            pltpu.VMEM((lax.axis_size("seq"),) + piece, jnp.float32),
+            pltpu.VMEM((pairs, 2) + piece, jnp.float32),
+            pltpu.VMEM((pairs, 2) + piece, jnp.bfloat16),
+            pltpu.VMEM((pairs, 2) + piece, jnp.bfloat16),
+            pltpu.VMEM((pairs,) + piece, jnp.bfloat16),
+            pltpu.VMEM((pairs,) + piece, jnp.bfloat16),
+            copies,
+            copies,
+        ],
+        compiler_params=pltpu.CompilerParams(
+            collective_id=number, has_side_effects=True, vmem_limit_bytes=58 * 2**20
+        ),
         cost_estimate=pl.CostEstimate(
             flops=10 * rows * keys * width,
             transcendentals=rows * keys * HEADS,
@@ -807,22 +904,20 @@
     return jnp.pad(rows_in, ((0, 0), (0, -rows_in.shape[1] % (2 * HEAD))))
 
 
-def share_keys(key_rows, val_rows):
-    pair = jnp.concatenate([wide(key_rows), wide(val_rows)], 0)[None]
-    return exchange(
-        pair, "share_keys", 4, join_axes=("seq",), join_orders=[bits_of("seq")[::-1]]
-    )
-
-
 def rows_major(x):
     return with_layout_constraint(x, Layout(major_to_minor=tuple(range(x.ndim))))
 
 
-def scatter_rows(features, cotangents):
+def scatter_rows(groups):
     total = lax.axis_size(AXES)
-    grad = dot_cols(features, cotangents)
-    blocks = rows_major(grad.astype(jnp.bfloat16)).reshape(total, -1, grad.shape[1])
-    return lax.psum_scatter(blocks, AXES, scatter_dimension=0, tiled=True)[0]
+    mats = []
+    for group in groups:
+        parts = [rows_major(dot_cols(*pair).astype(jnp.bfloat16)) for pair in group]
+        grad = jnp.concatenate(parts, 0) if len(parts) > 1 else parts[0]
+        mats.append(grad.reshape(total, -1, grad.shape[1]))
+    blocks = jnp.concatenate(mats, 1) if len(mats) > 1 else mats[0]
+    own = lax.psum_scatter(blocks, AXES, scatter_dimension=0, tiled=True)[0]
+    return own.reshape(len(mats), -1, own.shape[1])
 
 
 def layer_forward(state, weights, params, query_ids, key_ids):
@@ -832,8 +927,8 @@
     queries = wide((joined[:, :width] + params[2]).astype(jnp.bfloat16))
     key_rows = joined[:, width : 2 * width].astype(jnp.bfloat16)
     val_rows = (joined[:, 2 * width :] + params[3]).astype(jnp.bfloat16)
-    key_vals = share_keys(key_rows, val_rows)
-    attended, lse = attend(queries, key_vals, key_ids, query_ids)
+    own_pair = jnp.concatenate([wide(key_rows), wide(val_rows)], 0)
+    attended, lse, key_vals = attend(queries, own_pair, key_ids, query_ids, 4)
     attended = attended[:, :width]
     mid_state = state + dot_plain(attended, weights[0][3 * width :]) + params[4]
     normed = layer_norm(mid_state, params[5], params[6]).astype(jnp.bfloat16)
@@ -861,10 +956,7 @@
     att_grad = wide(dot_rows(out_grad, weights[0][3 * width :]).astype(jnp.bfloat16))
     if arrived:
         att_grad, arrived[0] = lax.optimization_barrier((att_grad, arrived[0]))
-    query_grad, pair_grad = attend_back(queries, key_vals, att_grad, lse, key_ids, query_ids)
-    own = exchange(
-        pair_grad, "return_grads", 8, sum_axes=("seq",), sum_orders=[bits_of("seq")]
-    )
+    query_grad, own = attend_back(queries, key_vals, att_grad, lse, key_ids, query_ids, 8)
     query_grad = query_grad[:, :width]
     key_grad, val_grad = own[: own.shape[0] // 2, :width], own[own.shape[0] // 2 :, :width]
     joined_grad = jnp.concatenate([query_grad, key_grad, val_grad], 1)
@@ -987,14 +1079,15 @@
     piece = seq_length // total
     gathered = []
     for layer_at in range(layers):
-        first = lax.all_gather(mats_low[layer_at, 0], AXES, axis=0, tiled=True)
-        rest = [None, None]
-        if layer_at > 0:
+        if layer_at == 0:
+            whole = lax.all_gather(mats_low[0], AXES, axis=1, tiled=True)
+            gathered.append([whole[k] for k in range(3)])
+        else:
+            first = lax.all_gather(mats_low[layer_at, 0], AXES, axis=0, tiled=True)
             rest = lax.all_gather(mats_low[layer_at, 1:], AXES, axis=1, tiled=True)
-        gathered.append([first, rest[0], rest[1]])
-    rest, (place_rows,), (small,), (given,) = run_jobs(
+            gathered.append([first, rest[0], rest[1]])
+    (place_rows,), (small,), (given,) = run_jobs(
         [
-            gather_job([mats_low[0, 1], mats_low[0, 2]]),
             sum_job(
                 rows_out[exchanged : exchanged + seq_length].reshape(total, piece, width),
                 sum_axes=("seq", "dp", "shard"),
@@ -1009,7 +1102,6 @@
         2,
         32,
     )
-    gathered[0][1:] = [x.reshape(-1, width) for x in rest]
     place_rows = place_rows.reshape(tok_count, width)
     small = small[:small_count].astype(jnp.float32)
     place_state = jnp.broadcast_to(place_rows.astype(jnp.float32), (seqs, tok_count, width))
@@ -1096,7 +1188,6 @@
     final_grad = dot_cols(to_slot, returned)
     state_grad, gain_final, shift_final = norm_back(state, final_gain, final_shift, final_grad)
 
-    mats_grads = {}
     late = []
     arrived = []
     small_grads = [None] * layers
@@ -1111,11 +1202,10 @@
             state_grad,
             arrived,
         )
-        late.append(factors[0])
         if layer_at > 0:
-            arrived = [scatter_rows(*factors[k][0]) for k in (2, 1)]
+            arrived = [scatter_rows(factors[2:]), scatter_rows(factors[:2])]
         else:
-            late += factors[1:]
+            late = factors
 
     low_grad = state_grad.astype(jnp.bfloat16)
     place_grad = jnp.sum(state_grad.reshape(seqs, tok_count, width), 0)
@@ -1128,7 +1218,7 @@
         return rows.reshape(total, SLOTS, width)
 
     (low_grad, arrived[1]) = lax.optimization_barrier((low_grad, arrived[1]))
-    mats_grads[1, 2], mats_grads[1, 1] = (x.astype(jnp.float32) for x in arrived)
+    upper = jnp.concatenate([arrived[1], arrived[0]], 0).astype(jnp.float32)
     late = late_mats(late, 12)
     fits = mats_fit(late)
     own_mats, (place_grad,), (small_grad,), (came,) = run_jobs(
@@ -1149,11 +1239,8 @@
         61,
     )
     for k in range(fits, len(late), fits):
-        own_mats = own_mats + run_jobs([mats_job(late[k : k + fits])], "sum_mats", 14 + k, 61)[0]
-    own_mats = list(own_mats)
-    for layer_at in reversed(range(layers)):
-        mats_grads[layer_at, 0] = own_mats.pop(0)
-    mats_grads[0, 1], mats_grads[0, 2] = own_mats
+        more = run_jobs([mats_job(late[k : k + fits])], "sum_mats", 14 + k, 61)[0]
+        own_mats = list(own_mats) + list(more)
     place_grad = place_grad.reshape(seq_length, width)
     small_high = small_grad.astype(jnp.bfloat16)
     small_low = (small_grad - small_high.astype(jnp.float32)).astype(jnp.bfloat16)
@@ -1166,9 +1253,7 @@
         return held + dot_plain(one_hot(asked_rows(at), table_local, 0), rows)
 
     table_grad = lax.fori_loop(1, rounds, return_more, table_grad)
-    mats_grad = jnp.stack(
-        [jnp.stack([mats_grads[layer_at, k] for k in range(3)]) for layer_at in range(layers)]
-    )
+    mats_grad = jnp.stack([jnp.stack(own_mats), upper])
     local_squares = jnp.sum(mats_grad * mats_grad) + jnp.sum(table_grad * table_grad)
     squares = combine_all(jnp.full((8, 128), local_squares), add_pair, "share_norm", 11)
     grad_norm = jnp.sqrt(squares[0, 0])

time: 1340 us -> 1300 us (0.970)
  Pallas kernels: 873 us -> 671 us
  waiting for transfers between devices: 0.83 us -> 177 us
  local copies, waits for them, and re-layouts: 128 us -> 111 us
    pallas_call x11 -> x7, Pallas kernels: 770 us -> 474 us  [run_jobs(): pl.pallas_call(partial(jobs_kernel, jobs), out_shape=outputs, in_specs=in...]
    all_gather x1, waiting for transfers between devices: 0.02 us -> 75.4 us  [on_device(): rest = lax.all_gather(mats_low[layer_at, 1:], AXES, axis=1, tiled=True)]
    pallas_call x2, Pallas kernels: 38.3 us -> 89.5 us  [attend(): pl.pallas_call(attend_kernel, out_shape=(jax.ShapeDtypeStruct((rows, widt...]
    reduce_scatter x0 -> x1, waiting for transfers between devices: none -> 50.9 us  [scatter_rows(): own = lax.psum_scatter(blocks, AXES, scatter_dimension=0, tiled=True)[0]]
    pallas_call x2, Pallas kernels: 51.5 us -> 98.5 us  [attend_back(): pl.pallas_call(attend_back_kernel, out_shape=(jax.ShapeDtypeStruct((rows,...]
    all_gather x0 -> x1, waiting for transfers between devices: none -> 34.1 us  [on_device(): whole = lax.all_gather(mats_low[0], AXES, axis=1, tiled=True)]
    concatenate x0 -> x4, other arithmetic: none -> 21.1 us  [the longest x1 11.2 us: scatter_rows(): grad = jnp.concatenate(parts, 0) if len(parts) > 1 else parts[0]]
    all_gather x2 -> x1, waiting for transfers between devices: 0.04 us -> 16.2 us  [on_device(): first = lax.all_gather(mats_low[layer_at, 0], AXES, axis=0, tiled=True)]
  transfers between devices with their start and end apart: 5 -> 5, of which waited for: 0 -> 4; matrix products, arithmetic and copies ran while one was open for 19% -> 21% of each run, Pallas kernels for 38% -> 27%
where the time goes in v4:
time: 1300 us; the launch traced here: 1290 us
  Pallas kernels  671 us (52%)
  matrix products  216 us (17%)
  waiting for transfers between devices  177 us (14%)
  local copies, waits for them, and re-layouts  111 us (9%)
  other arithmetic  96.1 us (7%)
  between operations  22.6 us (2%)
    pallas_call x7, Pallas kernels, run_jobs(): pl.pallas_call(partial(jobs_kernel, jobs), out_shape=outputs, in_specs=in...  474 us
    pallas_call x2, Pallas kernels, attend_back(): pl.pallas_call(attend_back_kernel, out_shape=(jax.ShapeDtypeStruct((rows,...  98.5 us
    dot_general x15, matrix products, dot_plain(): return jnp.dot(left_op, right_op, preferred_element_type=jnp.float32)  96.6 us
    pallas_call x2, Pallas kernels, attend(): pl.pallas_call(attend_kernel, out_shape=(jax.ShapeDtypeStruct((rows, widt...  89.5 us
    all_gather x1, waiting for transfers between devices, on_device(): rest = lax.all_gather(mats_low[layer_at, 1:], AXES, axis=1, tiled=True)  75.4 us
    dot_general x9, matrix products, dot_rows(): lax.dot_general(left_op, right_op, (((1,), (1,)), ((), ())), preferred_el...  64.3 us
    dot_general x11, matrix products, dot_cols(): lax.dot_general(left_op, right_op, (((0,), (0,)), ((), ())), preferred_el...  54.9 us
    reduce_scatter x1, waiting for transfers between devices, scatter_rows(): own = lax.psum_scatter(blocks, AXES, scatter_dimension=0, tiled=True)[0]  50.9 us
  transfers between devices with their start and end apart: 5, of which 4 were waited for; matrix products, arithmetic and copies ran while one was open for 21% of the time, Pallas kernels for 27%

profile of v4, /device:TPU:0, one launch (start us, length us, event | category | flops | bytes accessed | tf_op | source)
XLA Modules:
  0.0 1293.7 jit_solution(8109045109953083355)
XLA Ops:
  19.9 18.8 %share_ids.1 = s32[32,8,128]{2,1,0:T(8,128)} custom-call(s32[1,8,128]{2,1,0:T(8,128)} %pad_bitcast_fusion.refs_0_), custom_call_target="tpu_custom_call" | custom-call | tf_op jit(solution)/shard_map/share_ids/pallas_call | solution.py:168
  40.6 11.3 fusion.21
  56.8 132.7 %open_rows.1 = (bf16[8,32,1088]{2,1,0:T(8,128)(2,1)S(1)}, bf16[32,1088]{1,0:T(8,128)(2,1)S(1)}, bf16[32,24,1088]{2,1,0:T(8,128)(2,1)S(1)}) custom-call(bf16[32,32,1088]{2,1,0:T(8,128)(2,1)S(1)} %bitcast.192, bf16[32,1088]{1,0:T(8,128)(2,1)S(1)} %slice.274.refs_1_, bf16[32,24,1088]{2,1,0:T(8,128)(2,1)S(1)} %bitcast.193), custom_call_target="tpu_custom_call" | custom-call | tf_op jit(solution)/shard_map/open_rows/pallas_call | solution.py:168
  203.3 34.1 %all-gather.7.cloned.1.call-done = bf16[1,3,4352,1088]{3,2,1,0:T(8,128)(2,1)} async-done(((bf16[1,3,136,1088]{3,2,1,0:T(8,128)(2,1)}), bf16[1,3,4352,1088]{3,2,1,0:T(8,128)(2,1)}) %all-gather.7.cloned.1.call-update) | async-done | bytes 28409872 | tf_op jit(solution)/shard_map/all_gather | solution.py:1083
  251.1 43.9 %attend.2 = (bf16[256,1152]{1,0:T(8,128)(2,1)S(1)}, f32[9,2,256]{2,1,0:T(2,128)S(1)}, bf16[4,512,1152]{2,1,0:T(8,128)(2,1)}) custom-call(bf16[256,1152]{1,0:T(8,128)(2,1)S(1)} %pad.34.q_ref, bf16[512,1152]{1,0:T(8,128)(2,1)S(1)} %fusion.73.own_ref, s32[1024,1]{1,0:T(8,128)S(1)} %copy.213.key_ids_ref, s32[1,256]{1,0:T(1,128)S(1)} %constant_dynamic-slice_fusion.7.query_ids_ref), custom_call_target="tpu_custom_call" | custom-call | flops 1207959552 | bytes 4718592 | tf_op jit(solution)/shard_map/attend/pallas_call | solution.py:688
  298.8 10.4 multiply_convert_fusion.1
  317.6 16.2 %all-gather.9.cloned.1.call-done = bf16[1,1,4352,1088]{3,2,1,0:T(8,128)(2,1)} async-done(((bf16[1,1,136,1088]{3,2,1,0:T(8,128)(2,1)}), bf16[1,1,4352,1088]{3,2,1,0:T(8,128)(2,1)}) %all-gather.9.cloned.1.call-update) | async-done | bytes 9469968 | tf_op jit(solution)/shard_map/all_gather | solution.py:1086
  350.9 45.6 %attend.3 = (bf16[256,1152]{1,0:T(8,128)(2,1)S(1)}, f32[9,2,256]{2,1,0:T(2,128)S(1)}, bf16[4,512,1152]{2,1,0:T(8,128)(2,1)}) custom-call(bf16[256,1152]{1,0:T(8,128)(2,1)S(1)} %pad.37.q_ref, bf16[512,1152]{1,0:T(8,128)(2,1)S(1)} %fusion.74.own_ref, s32[1024,1]{1,0:T(8,128)S(1)} %copy.213.key_ids_ref, s32[1,256]{1,0:T(1,128)S(1)} %constant_dynamic-slice_fusion.7.query_ids_ref), custom_call_target="tpu_custom_call" | custom-call | flops 1207959552 | bytes 4718592 | tf_op jit(solution)/shard_map/attend/pallas_call | solution.py:688
  400.7 75.4 %all-gather.11.cloned.1.call-done = bf16[1,2,4352,1088]{3,2,1,0:T(8,128)(2,1)} async-done(((bf16[1,2,136,1088]{3,2,1,0:T(8,128)(2,1)}), bf16[1,2,4352,1088]{3,2,1,0:T(8,128)(2,1)}) %all-gather.11.cloned.1.call-update) | async-done | bytes 18939920 | tf_op jit(solution)/shard_map/all_gather | solution.py:1087
  483.9 8.9 fusion.142
  495.4 47.5 %share_final.1 = bf16[32,64,1088]{2,1,0:T(8,128)(2,1)} custom-call(bf16[4,64,1088]{2,1,0:T(8,128)(2,1)} %bitcast.219), custom_call_target="tpu_custom_call" | custom-call | tf_op jit(solution)/shard_map/share_final/pallas_call | solution.py:168
  543.0 12.3 select_reduce_fusion.3
  560.7 13.8 %share_stats.1 = f32[3,16,128]{2,1,0:T(8,128)S(1)} custom-call(f32[3,16,128]{2,1,0:T(8,128)S(1)} %pad_maximum_fusion.4.refs_0_), custom_call_target="tpu_custom_call" | custom-call | tf_op jit(solution)/shard_map/share_stats/pallas_call | solution.py:168
  580.1 12.4 fusion.148
  592.5 52.6 %return_final.1 = bf16[4,64,1088]{2,1,0:T(8,128)(2,1)} custom-call(f32[32,64,1088]{2,1,0:T(8,128)} %bitcast.200), custom_call_target="tpu_custom_call" | custom-call | tf_op jit(solution)/shard_map/return_final/pallas_call | solution.py:168
  652.1 9.9 convolution_convert_fusion.2
  662.1 8.6 convert_reduce_fusion
  670.8 9.9 fusion.146
  691.1 47.4 %attend_back.2 = (bf16[256,1152]{1,0:T(8,128)(2,1)}, bf16[512,1152]{1,0:T(8,128)(2,1)}) custom-call(bf16[256,1152]{1,0:T(8,128)(2,1)} %copy-done.6, bf16[4,512,1152]{2,1,0:T(8,128)(2,1)} %get-tuple-element.278.kv_ref, bf16[256,1152]{1,0:T(8,128)(2,1)} %pad.40.grad_ref, f32[9,2,256]{2,1,0:T(2,128)} %copy-done.10, s32[1024,1]{1,0:T(8,128)} %copy-done.7, ...), custom_call_target="tpu_custom_call" | custom-call | flops 3019898880 | bytes 14155776 | tf_op jit(solution)/shard_map/attend_back/pallas_call | solution.py:815
  756.0 11.2 pad_maximum_fusion.1
  767.2 9.7 pad_maximum_fusion
  795.6 8.4 convert_reduce_fusion.1
  806.5 8.9 fusion.144
  847.6 14.9 %fusion.149 = f32[1604,1088]{0,1:T(8,128)} fusion(bf16[2048,1604]{0,1:T(8,128)(2,1)} %copy-done.35, bf16[2048,1088]{1,0:T(8,128)(2,1)} %bitcast.209), kind=kOutput, calls=%fused_computation.344 | convolution fusion | flops 7148142592 | bytes 18007040 | tf_op jit(solution)/shard_map/dot_general | solution.py:863
  862.5 51.2 %attend_back.3 = (bf16[256,1152]{1,0:T(8,128)(2,1)}, bf16[512,1152]{1,0:T(8,128)(2,1)}) custom-call(bf16[256,1152]{1,0:T(8,128)(2,1)} %copy-done.3, bf16[4,512,1152]{2,1,0:T(8,128)(2,1)} %get-tuple-element.277.kv_ref, bf16[256,1152]{1,0:T(8,128)(2,1)} %pad.41.grad_ref, f32[9,2,256]{2,1,0:T(2,128)} %copy-done.9, s32[1024,1]{1,0:T(8,128)} %copy-done.7, ...), custom_call_target="tpu_custom_call" | custom-call | flops 3019898880 | bytes 14155776 | tf_op jit(solution)/shard_map/attend_back/pallas_call | solution.py:815
  934.9 9.9 trade_rows.1
  966.0 50.9 %reduce-scatter.5.cloned.1.call-done = bf16[1,272,1088]{2,1,0:T(8,128)(2,1)} async-done(((bf16[32,272,1088]{2,1,0:T(8,128)(2,1)}), bf16[1,272,1088]{2,1,0:T(8,128)(2,1)}) %reduce-scatter.5.cloned.1.call-update) | async-done | bytes 591888 | tf_op jit(solution)/shard_map/reduce_scatter | solution.py:919
  1021.1 188.9 %close_rows.1 = (f32[136,1088]{1,0:T(8,128)}, f32[136,1088]{1,0:T(8,128)}, f32[136,1088]{1,0:T(8,128)}, bf16[32,32,1088]{2,1,0:T(8,128)(2,1)}, f32[32,1088]{1,0:T(8,128)}, /*index=5*/bf16[32,24,1088]{2,1,0:T(8,128)(2,1)}) custom-call(bf16[16,136,1088]{2,1,0:T(8,128)(2,1)} %bitcast.198, bf16[16,136,1088]{2,1,0:T(8,128)(2,1)} %bitcast.205, ...), custom_call_target="tpu_custom_call" | custom-call | tf_op jit(solution)/shard_map/close_rows/pallas_call | solution.py:168
  1211.1 13.4 %fusion.12 = f32[1604,1088]{0,1:T(8,128)} fusion(f32[1604,1088]{0,1:T(8,128)} %fusion.149, s32[1856]{0:T(1024)S(1)} %copy-done.141, bf16[32,1088]{1,0:T(8,128)(2,1)S(1)} %get-tuple-element.376, bf16[32,1088]{1,0:T(8,128)(2,1)S(1)} %get-tuple-element.377, bf16[1024,1088]{1,0:T(8,128)(2,1)} %bitcast.248, bf16[768,1088]{1,0:T(8,128)(2,1)} %bitcast.249), kind=kOutput, calls=%fused_computation.47 | convolution fusion | flops 6498880512 | bytes 18007296 | tf_op jit(solution)/shard_map/dot_general | solution.py:869
  1236.2 19.2 %share_norm.1 = f32[8,128]{1,0:T(8,128)S(1)} custom-call(f32[8,128]{1,0:T(8,128)S(1)} %broadcast_in_dim.223.refs_0_), custom_call_target="tpu_custom_call" | custom-call | tf_op jit(solution)/shard_map/share_norm/pallas_call | solution.py:168
  1256.6 8.9 multiply_subtract_fusion.1
  1265.5 19.2 %multiply_subtract_fusion = (f32[1604,1088]{0,1:T(8,128)}, f32[1604,1088]{0,1:T(8,128)}, f32[1604,1088]{0,1:T(8,128)}) fusion(f32[1604,1088]{0,1:T(8,128)} %param.25, f32[1604]{0:T(1024)S(1)} %copy-done.91, f32[]{:T(128)} %bitcast.66, f32[]{:T(128)} %bitcast.65, f32[1604]{0:T(1024)S(1)} %copy-done.92, f32[1604,1088]{0,1:T(8,128)} %get-tuple-element.303, ...), kind=kLoop, calls=%fused_computation.62 | loop fusion | flops 27922432 | bytes 48877100 | tf_op jit(solution)/shard_map/sub | solution.py:997
  (509 shorter events, 244.7 us)
Async XLA Ops:
  7.2 230.2 %all-gather.7.cloned.1.call-start = ((), (), s32[]{:S(2)}) async-start(), calls=%async_computation.3 | async-start | bytes 31021056 | tf_op jit(solution)/shard_map/all_gather | solution.py:1083
  10.5 323.3 %all-gather.9.cloned.1.call-start = ((), (), s32[]{:S(2)}) async-start(), calls=%async_computation.4 | async-start | bytes 10340352 | tf_op jit(solution)/shard_map/all_gather | solution.py:1086
  11.3 464.8 %all-gather.11.cloned.1.call-start = ((), (), s32[]{:S(2)}) async-start(), calls=%async_computation.5 | async-start | bytes 20680704 | tf_op jit(solution)/shard_map/all_gather | solution.py:1087
  12.3 850.2 %reduce-scatter.7.cloned.1.call-start = ((), (), s32[]{:S(2)}) async-start(), calls=%async_computation.6 | async-start | bytes 10340352
  197.6 97.4 %copy-start.11 = (f32[256,1088]{1,0:T(8,128)}, f32[256,1088]{1,0:T(8,128)S(1)}, u32[]{:S(2)}) copy-start(f32[256,1088]{1,0:T(8,128)S(1)} %copy.214) | copy-start | bytes 3342340
  198.1 152.8 %copy-start.7 = (s32[1024,1]{1,0:T(8,128)}, s32[1024,1]{1,0:T(8,128)S(1)}, u32[]{:S(2)}) copy-start(s32[1024,1]{1,0:T(8,128)S(1)} %copy.213.key_ids_ref) | copy-start | bytes 12292
  200.0 150.9 %copy-start.8 = (s32[1,256]{1,0:T(1,128)}, s32[1,256]{1,0:T(1,128)S(1)}, u32[]{:S(2)}) copy-start(s32[1,256]{1,0:T(1,128)S(1)} %constant_dynamic-slice_fusion.7.query_ids_ref) | copy-start | bytes 3076
  202.2 40.8 %copy-start.75 = (f32[1088]{0:T(1024)}, f32[1088]{0:T(1024)S(1)}, u32[]{:S(2)}) copy-start(f32[1088]{0:T(1024)S(1)} %get-tuple-element.333) | copy-start | bytes 13060
  202.2 96.2 %copy-start.77 = (f32[1088]{0:T(1024)}, f32[1088]{0:T(1024)S(1)}, u32[]{:S(2)}) copy-start(f32[1088]{0:T(1024)S(1)} %get-tuple-element.328) | copy-start | bytes 13060
  202.2 131.6 %copy-start.88 = (f32[1088]{0:T(1024)}, f32[1088]{0:T(1024)S(1)}, u32[]{:S(2)}) copy-start(f32[1088]{0:T(1024)S(1)} %get-tuple-element.324) | copy-start | bytes 13060
  202.2 40.8 %copy-start.93 = (f32[256]{0:T(256)}, f32[256]{0:T(256)S(1)}, u32[]{:S(2)}) copy-start(f32[256]{0:T(256)S(1)} %broadcast_multiply_fusion.4) | copy-start | bytes 3076
  202.4 40.6 %copy-start.127 = (f32[256]{0:T(256)}, f32[256]{0:T(256)S(1)}, u32[]{:S(2)}) copy-start(f32[256]{0:T(256)S(1)} %multiply_reduce_fusion.16) | copy-start | bytes 3076
  202.5 40.6 %copy-start.116 = (f32[256]{0:T(256)}, f32[256]{0:T(256)S(1)}, u32[]{:S(2)}) copy-start(f32[256]{0:T(256)S(1)} %fusion.112) | copy-start | bytes 3076
  203.3 39.7 %copy-start.52 = (bf16[256,1088]{1,0:T(8,128)(2,1)}, bf16[256,1088]{1,0:T(8,128)(2,1)S(1)}, u32[]{:S(2)}) copy-start(bf16[256,1088]{1,0:T(8,128)(2,1)S(1)} %add_convert_fusion.8.refs_4_) | copy-start | bytes 1671172
  250.9 44.1 %copy-start.3 = (bf16[256,1152]{1,0:T(8,128)(2,1)}, bf16[256,1152]{1,0:T(8,128)(2,1)S(1)}, u32[]{:S(2)}) copy-start(bf16[256,1152]{1,0:T(8,128)(2,1)S(1)} %pad.34.q_ref) | copy-start | bytes 1769476
  251.1 43.9 %copy-start.136 = (f32[1088]{0:T(1024)S(1)}, f32[1088]{0:T(1024)}, u32[]{:S(2)}) copy-start(f32[1088]{0:T(1024)} %get-tuple-element.329) | copy-start | bytes 13060
  317.5 22.0 %copy-start.131 = (f32[256]{0:T(256)}, f32[256]{0:T(256)S(1)}, u32[]{:S(2)}) copy-start(f32[256]{0:T(256)S(1)} %multiply_reduce_fusion.14) | copy-start | bytes 3076
  317.5 21.9 %copy-start.120 = (f32[256]{0:T(256)}, f32[256]{0:T(256)S(1)}, u32[]{:S(2)}) copy-start(f32[256]{0:T(256)S(1)} %fusion.114) | copy-start | bytes 3076
  349.2 47.3 %copy-start.6 = (bf16[256,1152]{1,0:T(8,128)(2,1)}, bf16[256,1152]{1,0:T(8,128)(2,1)S(1)}, u32[]{:S(2)}) copy-start(bf16[256,1152]{1,0:T(8,128)(2,1)S(1)} %pad.37.q_ref) | copy-start | bytes 1769476
  350.9 45.7 %copy-start.134 = (f32[1088]{0:T(1024)S(1)}, f32[1088]{0:T(1024)}, u32[]{:S(2)}) copy-start(f32[1088]{0:T(1024)} %get-tuple-element.321) | copy-start | bytes 13060
  396.6 79.6 %copy-start.79 = (f32[1088]{0:T(1024)S(1)}, f32[1088]{0:T(1024)}, u32[]{:S(2)}) copy-start(f32[1088]{0:T(1024)} %get-tuple-element.320) | copy-start | bytes 13060
  396.6 79.5 %copy-start.87 = (f32[1088]{0:T(1024)S(1)}, f32[1088]{0:T(1024)}, u32[]{:S(2)}) copy-start(f32[1088]{0:T(1024)} %get-tuple-element.319) | copy-start | bytes 13060
  396.6 79.5 %copy-start.98 = (f32[4352]{0:T(1024)S(1)}, f32[4352]{0:T(1024)}, u32[]{:S(2)}) copy-start(f32[4352]{0:T(1024)} %add.574) | copy-start | bytes 52228
  400.7 283.6 %copy-start.122 = (f32[256]{0:T(256)}, f32[256]{0:T(256)S(1)}, u32[]{:S(2)}) copy-start(f32[256]{0:T(256)S(1)} %fusion.115) | copy-start | bytes 3076
  495.4 47.5 %copy-start.101 = (pred[1604]{0:T(1024)(128)(4,1)S(1)}, pred[1604]{0:T(1024)(128)(4,1)}, u32[]{:S(2)}) copy-start(pred[1604]{0:T(1024)(128)(4,1)} %fusion.106) | copy-start | bytes 4816
  580.1 12.4 copy-start.35
  662.1 354.8 %reduce-scatter.5.cloned.1.call-start = ((), (), s32[]{:S(2)}) async-start(), calls=%async_computation.2 | async-start | bytes 20680704 | tf_op jit(solution)/shard_map/reduce_scatter | solution.py:919
  963.3 53.6 %copy-start.125 = (s32[256]{0:T(256)S(1)}, s32[256]{0:T(256)}, u32[]{:S(2)}) copy-start(s32[256]{0:T(256)} %copy-done.124) | copy-start | bytes 3076
  1021.1 189.9 %copy-start.141 = (s32[1856]{0:T(1024)S(1)}, s32[1856]{0:T(1024)}, u32[]{:S(2)}) copy-start(s32[1856]{0:T(1024)} %concatenate.93) | copy-start | bytes 22276
  1211.1 13.5 %copy-start.60 = (pred[32,256]{1,0:T(32,128)(4,1)S(1)}, pred[32,256]{1,0:T(32,128)(4,1)}, u32[]{:S(2)}) copy-start(pred[32,256]{1,0:T(32,128)(4,1)} %copy-done.59) | copy-start | bytes 24580
  1211.1 13.5 %copy-start.72 = (s32[256]{0:T(256)S(1)}, s32[256]{0:T(256)}, u32[]{:S(2)}) copy-start(s32[256]{0:T(256)} %copy-done.71) | copy-start | bytes 3076
  1211.1 13.5 %copy-start.74 = (s32[256]{0:T(256)S(1)}, s32[256]{0:T(256)}, u32[]{:S(2)}) copy-start(s32[256]{0:T(256)} %copy-done.73) | copy-start | bytes 3076
  (124 other events, 496.2 us)
Sparse Core Ops, SparseCore 0:
  11.6 225.7 all-gather.6
  240.8 92.9 all-gather.8
  336.8 139.2 all-gather.10
  662.2 135.9 reduce-scatter.6
  804.5 212.3 reduce-scatter.4

commit v5 on v4

--- a/solution.py
+++ b/solution.py
@@ -385,6 +385,58 @@
         None,
         steps,
         spaces=(pl.ANY, pl.ANY),
+    )
+
+
+def spread_job(x, add):
+    total = lax.axis_size(AXES)
+    all_shape = (total,) + x.shape
+
+    def steps(x_refs, o_refs, scratch, sems):
+        x_ref = x_refs[0]
+        target = scratch[0] if add else o_refs[0]
+
+        def gen():
+            me, unused = me_and_total()
+            first = sems.span(total)
+            target[me] = x_ref[...]
+
+            def copy_to(other, here):
+                return pltpu.make_async_remote_copy(
+                    x_ref,
+                    target.at[here],
+                    sems.send.at[first + other],
+                    sems.recv.at[first + here],
+                    device_id=place_of(other),
+                    device_id_type=MESH,
+                )
+
+            def send(k, carry):
+                copy_to(lax.rem(me + k, total), me).start()
+                return carry
+
+            lax.fori_loop(1, total, send, 0)
+            yield
+
+            def finish(k, carry):
+                other = lax.rem(me + k, total)
+                copy_to(other, other).wait()
+                return carry
+
+            lax.fori_loop(1, total, finish, 0)
+            if add:
+                o_refs[0][...] = jnp.sum(target[...], 0)
+
+        return [(0, gen())]
+
+    return Job(
+        [x],
+        [jax.ShapeDtypeStruct(x.shape if add else all_shape, x.dtype)],
+        [pltpu.VMEM(all_shape, x.dtype)] if add else [],
+        total,
+        0,
+        None,
+        steps,
     )
 
 
@@ -509,6 +561,54 @@
     )
 
 
+def gather_job(parts):
+    rows, width = parts[0].shape
+    spans, orders = sum_orders_for(rows)
+    orders = [order[::-1] + bits_of("seq")[:1] for order in orders]
+    total = lax.axis_size(AXES)
+    sends = 0
+    for order in orders:
+        for step in range(len(order)):
+            sends += len(block_runs([block_weight(AXES, b) for b in order[:step]])[1])
+
+    def gen(x_ref, o_ref, sems, span, order):
+        here = pl.ds(*span)
+        own = me_and_total()[0]
+        keep = sems.local(x_ref.at[here], o_ref.at[own, here])
+        for step, bit in enumerate(order):
+            base = sum(bit_here(b) * block_weight(AXES, b) for b in order[step:])
+            size, offsets = block_runs([block_weight(AXES, b) for b in order[:step]])
+            started = []
+            for offset in offsets:
+                target = o_ref.at[pl.ds(base + offset, size), here]
+                source = x_ref.at[here] if step == 0 else target
+                target = o_ref.at[own, here] if step == 0 else target
+                started.append(sems.copy(source, target, partner(bit)))
+            yield
+            if step == 0:
+                keep.wait()
+            for copy in started:
+                copy.wait()
+
+    def steps(x_refs, o_refs, scratch, sems):
+        return [
+            (m, gen(x_refs[m], o_refs[m], sems, spans[k], orders[k]))
+            for m in range(len(parts))
+            for k in range(len(orders))
+        ]
+
+    return Job(
+        parts,
+        [jax.ShapeDtypeStruct((total, rows, width), parts[0].dtype)] * len(parts),
+        [],
+        sends * len(parts),
+        len(orders) * len(parts),
+        set(orders[0]),
+        steps,
+        spaces=(pl.ANY, pl.ANY),
+    )
+
+
 def trade_kernel(count, *refs):
     x_refs, o_refs = refs[:count], refs[count : 2 * count]
     send_sems, recv_sems = refs[2 * count :]
@@ -870,7 +970,7 @@
 
 
 def column_sums(values):
-    return jnp.sum(values.astype(jnp.float32), 0)
+    return jnp.sum(values.astype(jnp.float32), 0, keepdims=True)
 
 
 def layer_norm(values, gain, shift):
@@ -922,19 +1022,19 @@
 
 def layer_forward(state, weights, params, query_ids, key_ids):
     width = state.shape[1]
-    hidden = layer_norm(state, params[0], params[1]).astype(jnp.bfloat16)
-    joined = dot_rows(hidden, weights[0][: 3 * width])
-    queries = wide((joined[:, :width] + params[2]).astype(jnp.bfloat16))
+    hidden = layer_norm(state, params[0 : 1], params[1 : 2]).astype(jnp.bfloat16)
+    joined = rows_major(dot_rows(hidden, weights[0][: 3 * width]))
+    queries = wide((joined[:, :width] + params[2 : 3]).astype(jnp.bfloat16))
     key_rows = joined[:, width : 2 * width].astype(jnp.bfloat16)
-    val_rows = (joined[:, 2 * width :] + params[3]).astype(jnp.bfloat16)
+    val_rows = (joined[:, 2 * width :] + params[3 : 4]).astype(jnp.bfloat16)
     own_pair = jnp.concatenate([wide(key_rows), wide(val_rows)], 0)
     attended, lse, key_vals = attend(queries, own_pair, key_ids, query_ids, 4)
     attended = attended[:, :width]
-    mid_state = state + dot_plain(attended, weights[0][3 * width :]) + params[4]
-    normed = layer_norm(mid_state, params[5], params[6]).astype(jnp.bfloat16)
-    upward = dot_rows(normed, weights[1]) + params[8:12].reshape(-1)
+    mid_state = state + dot_plain(attended, weights[0][3 * width :]) + params[4 : 5]
+    normed = layer_norm(mid_state, params[5 : 6], params[6 : 7]).astype(jnp.bfloat16)
+    upward = dot_rows(normed, weights[1]) + params[8:12].reshape(1, -1)
     active = jax.nn.gelu(upward, approximate=True).astype(jnp.bfloat16)
-    output = mid_state + dot_plain(active, weights[2]) + params[7]
+    output = mid_state + dot_plain(active, weights[2]) + params[7 : 8]
     return (
         output,
         (hidden, queries, key_vals, lse, attended, mid_state, normed, upward, active),
@@ -949,7 +1049,7 @@
     unused_gelu, gelu_pull = jax.vjp(partial(jax.nn.gelu, approximate=True), upward)
     up_grad = gelu_pull(act_grad)[0].astype(jnp.bfloat16)
     mid_back, gain_two, shift_two = norm_back(
-        mid_state, params[5], params[6], dot_plain(up_grad, weights[1])
+        mid_state, params[5 : 6], params[6 : 7], dot_plain(up_grad, weights[1])
     )
     mid_grad = grad_in + mid_back
     out_grad = mid_grad.astype(jnp.bfloat16)
@@ -961,26 +1061,19 @@
     key_grad, val_grad = own[: own.shape[0] // 2, :width], own[own.shape[0] // 2 :, :width]
     joined_grad = jnp.concatenate([query_grad, key_grad, val_grad], 1)
     state_back, gain_one, shift_one = norm_back(
-        state, params[0], params[1], dot_plain(joined_grad, weights[0][: 3 * width])
-    )
-    small_grad = jnp.concatenate(
-        [
-            jnp.stack(
-                [
-                    gain_one,
-                    shift_one,
-                    column_sums(query_grad),
-                    column_sums(val_grad),
-                    column_sums(out_grad),
-                    gain_two,
-                    shift_two,
-                    column_sums(down_grad),
-                ]
-            ),
-            column_sums(up_grad).reshape(4, width),
-        ],
-        0,
-    )
+        state, params[0 : 1], params[1 : 2], dot_plain(joined_grad, weights[0][: 3 * width])
+    )
+    up_sums = column_sums(up_grad)
+    small_grad = [
+        gain_one,
+        shift_one,
+        column_sums(query_grad),
+        column_sums(val_grad),
+        column_sums(out_grad),
+        gain_two,
+        shift_two,
+        column_sums(down_grad),
+    ] + [up_sums[:, k * width : (k + 1) * width] for k in range(4)]
     factors = [
         [(joined_grad, hidden), (attended, out_grad)],
         [(up_grad, normed)],
@@ -1035,13 +1128,8 @@
     small_count = 12 * layers + 2
     small_rows = -(-small_count // 16) * 16
 
-    ids_all = exchange(
-        jnp.pad(token_ids, (0, -local_rows % 1024)).reshape(1, -1, 128),
-        "share_ids",
-        0,
-        join_axes=AXES,
-        join_orders=[shard_bits[::-1] + dp_bits[::-1] + seq_bits[::-1]],
-    )
+    packed_ids = jnp.pad(token_ids, (0, -local_rows % 1024)).reshape(-1, 128)
+    ids_all = run_jobs([spread_job(packed_ids, False)], "share_ids", 0, 16)[0][0]
     ids_all = ids_all.reshape(total, -1)[:, :local_rows]
     owner_all = ids_all // table_local
     loads = jnp.sum(
@@ -1083,11 +1171,12 @@
             whole = lax.all_gather(mats_low[0], AXES, axis=1, tiled=True)
             gathered.append([whole[k] for k in range(3)])
         else:
-            first = lax.all_gather(mats_low[layer_at, 0], AXES, axis=0, tiled=True)
-            rest = lax.all_gather(mats_low[layer_at, 1:], AXES, axis=1, tiled=True)
-            gathered.append([first, rest[0], rest[1]])
-    (place_rows,), (small,), (given,) = run_jobs(
+            gathered.append(
+                [lax.all_gather(mats_low[layer_at, k], AXES, axis=0, tiled=True) for k in range(2)]
+            )
+    (last_down,), (place_rows,), (small,), (given,) = run_jobs(
         [
+            gather_job([mats_low[1, 2]]),
             sum_job(
                 rows_out[exchanged : exchanged + seq_length].reshape(total, piece, width),
                 sum_axes=("seq", "dp", "shard"),
@@ -1102,6 +1191,7 @@
         2,
         32,
     )
+    gathered[1].append(last_down.reshape(-1, width))
     place_rows = place_rows.reshape(tok_count, width)
     small = small[:small_count].astype(jnp.float32)
     place_state = jnp.broadcast_to(place_rows.astype(jnp.float32), (seqs, tok_count, width))
@@ -1127,8 +1217,8 @@
             block_ids[0],
         )
         saved.append(held)
-    final_gain = small[12 * layers]
-    final_shift = small[12 * layers + 1]
+    final_gain = small[12 * layers : 12 * layers + 1]
+    final_shift = small[12 * layers + 1 : 12 * layers + 2]
     final = layer_norm(state, final_gain, final_shift).astype(jnp.bfloat16)
 
     group_mask = completion[0]
@@ -1203,14 +1293,15 @@
             arrived,
         )
         if layer_at > 0:
-            arrived = [scatter_rows(factors[2:]), scatter_rows(factors[:2])]
+            arrived = [scatter_rows(factors[2:]), scatter_rows(factors[1:2])]
+            late = factors[:1]
         else:
-            late = factors
+            late = factors + late
 
     low_grad = state_grad.astype(jnp.bfloat16)
     place_grad = jnp.sum(state_grad.reshape(seqs, tok_count, width), 0)
     small_grad = pad_rows(
-        jnp.concatenate(small_grads + [jnp.stack([gain_final, shift_final])], 0), small_rows
+        jnp.concatenate(sum(small_grads, []) + [gain_final, shift_final], 0), small_rows
     )
 
     def leaving(at):
@@ -1240,7 +1331,7 @@
     )
     for k in range(fits, len(late), fits):
         more = run_jobs([mats_job(late[k : k + fits])], "sum_mats", 14 + k, 61)[0]
-        own_mats = list(own_mats) + list(more)
+        own_mats = list(own_mats) + list(lax.optimization_barrier(tuple(more)))
     place_grad = place_grad.reshape(seq_length, width)
     small_high = small_grad.astype(jnp.bfloat16)
     small_low = (small_grad - small_high.astype(jnp.float32)).astype(jnp.bfloat16)
@@ -1253,9 +1344,10 @@
         return held + dot_plain(one_hot(asked_rows(at), table_local, 0), rows)
 
     table_grad = lax.fori_loop(1, rounds, return_more, table_grad)
-    mats_grad = jnp.stack([jnp.stack(own_mats), upper])
+    mats_grad = jnp.concatenate([jnp.stack(own_mats), upper], 0).reshape(layer_mats.shape)
     local_squares = jnp.sum(mats_grad * mats_grad) + jnp.sum(table_grad * table_grad)
-    squares = combine_all(jnp.full((8, 128), local_squares), add_pair, "share_norm", 11)
+    squares = jnp.full((8, 128), local_squares)
+    squares = run_jobs([spread_job(squares, True)], "share_norm", 11, 16)[0][0]
     grad_norm = jnp.sqrt(squares[0, 0])
     factor = CLIP_NORM / grad_norm
     step = step_count[0].astype(jnp.float32)

time: 1300 us -> 1270 us (0.977)
  waiting for transfers between devices: 177 us -> 78.3 us
  Pallas kernels: 671 us -> 742 us
  other arithmetic: 96.1 us -> 74.1 us
  local copies, waits for them, and re-layouts: 111 us -> 127 us
    pallas_call x7, Pallas kernels: 474 us -> 546 us  [run_jobs(): pl.pallas_call(partial(jobs_kernel, jobs), out_shape=outputs, in_specs=in...]
    reduce_scatter x1 -> x0, waiting for transfers between devices: 50.9 us -> none  [scatter_rows(): own = lax.psum_scatter(blocks, AXES, scatter_dimension=0, tiled=True)[0]]
    all_gather x2, waiting for transfers between devices: 91.6 us -> 62.1 us  [on_device(): lax.all_gather(mats_low[layer_at, k], AXES, axis=0, tiled=True)]
    all_gather x1, waiting for transfers between devices: 34.1 us -> 7.13 us  [on_device(): whole = lax.all_gather(mats_low[0], AXES, axis=1, tiled=True)]
    concatenate x2 -> x1, other arithmetic: 20.9 us -> 0.08 us  [on_device(): jnp.concatenate([jnp.stack(own_mats), upper], 0).reshape(layer_mats.shape)]
    unnamed x309 -> x283, local copies, waits for them, and re-layouts: 37 us -> 32.2 us
  transfers between devices with their start and end apart: 5 -> 5, of which waited for: 4 -> 4; matrix products, arithmetic and copies ran while one was open for 21% -> 19% of each run, Pallas kernels for 27% -> 31%
where the time goes in v5:
time: 1270 us; the launch traced here: 1260 us
  Pallas kernels  742 us (58%)
  matrix products  211 us (17%)
  local copies, waits for them, and re-layouts  127 us (10%)
  waiting for transfers between devices  78.3 us (6%)
  other arithmetic  74.1 us (6%)
  between operations  22.4 us (2%)
    pallas_call x7, Pallas kernels, run_jobs(): pl.pallas_call(partial(jobs_kernel, jobs), out_shape=outputs, in_specs=in...  546 us
    pallas_call x2, Pallas kernels, attend_back(): pl.pallas_call(attend_back_kernel, out_shape=(jax.ShapeDtypeStruct((rows,...  100 us
    dot_general x15, matrix products, dot_plain(): return jnp.dot(left_op, right_op, preferred_element_type=jnp.float32)  92.2 us
    pallas_call x2, Pallas kernels, attend(): pl.pallas_call(attend_kernel, out_shape=(jax.ShapeDtypeStruct((rows, widt...  83 us
    dot_general x9, matrix products, dot_rows(): lax.dot_general(left_op, right_op, (((1,), (1,)), ((), ())), preferred_el...  62.8 us
    all_gather x2, waiting for transfers between devices, on_device(): lax.all_gather(mats_low[layer_at, k], AXES, axis=0, tiled=True)  62.1 us
    dot_general x11, matrix products, dot_cols(): lax.dot_general(left_op, right_op, (((0,), (0,)), ((), ())), preferred_el...  56.5 us
    unnamed x283, local copies, waits for them, and re-layouts  32.2 us
  transfers between devices with their start and end apart: 5, of which 4 were waited for; matrix products, arithmetic and copies ran while one was open for 19% of the time, Pallas kernels for 31%

profile of v5, /device:TPU:0, one launch (start us, length us, event | category | flops | bytes accessed | tf_op | source)
XLA Modules:
  0.0 1255.8 jit_solution(8786168853513588823)
XLA Ops:
  12.3 12.5 share_ids.1
  32.7 11.3 fusion.21
  49.0 196.8 %open_rows.1 = (bf16[32,136,1088]{2,1,0:T(8,128)(2,1)S(1)}, bf16[8,32,1088]{2,1,0:T(8,128)(2,1)S(1)}, bf16[32,1088]{1,0:T(8,128)(2,1)S(1)}, bf16[32,24,1088]{2,1,0:T(8,128)(2,1)S(1)}) custom-call(bf16[136,1088]{1,0:T(8,128)(2,1)S(1)} %get-tuple-element.428.refs_0_, bf16[32,32,1088]{2,1,0:T(8,128)(2,1)S(1)} %bitcast.193, ...), custom_call_target="tpu_custom_call" | custom-call | tf_op jit(solution)/shard_map/open_rows/pallas_call | solution.py:168
  259.8 7.1 all-gather.7.cloned.1.call-done
  273.1 42.0 %attend.2 = (bf16[256,1152]{1,0:T(8,128)(2,1)S(1)}, f32[9,2,256]{2,1,0:T(2,128)S(1)}, bf16[4,512,1152]{2,1,0:T(8,128)(2,1)}) custom-call(bf16[256,1152]{1,0:T(8,128)(2,1)S(1)} %pad.34.q_ref, bf16[512,1152]{1,0:T(8,128)(2,1)S(1)} %fusion.77.own_ref, s32[1024,1]{1,0:T(8,128)S(1)} %copy.208.key_ids_ref, s32[1,256]{1,0:T(1,128)S(1)} %constant_dynamic-slice_fusion.11.query_ids_ref), custom_call_target="tpu_custom_call" | custom-call | flops 1207959552 | bytes 4718592 | tf_op jit(solution)/shard_map/attend/pallas_call | solution.py:788
  318.7 9.4 multiply_convert_fusion.1
  328.2 8.0 fusion.158
  336.7 21.6 %all-gather.9.cloned.1.call-done = bf16[1,1,4352,1088]{3,2,1,0:T(8,128)(2,1)} async-done(((bf16[1,1,136,1088]{3,2,1,0:T(8,128)(2,1)}), bf16[1,1,4352,1088]{3,2,1,0:T(8,128)(2,1)}) %all-gather.9.cloned.1.call-update) | async-done | bytes 9469968 | tf_op jit(solution)/shard_map/all_gather | solution.py:1175
  364.5 41.1 %attend.3 = (bf16[256,1152]{1,0:T(8,128)(2,1)S(1)}, f32[9,2,256]{2,1,0:T(2,128)S(1)}, bf16[4,512,1152]{2,1,0:T(8,128)(2,1)}) custom-call(bf16[256,1152]{1,0:T(8,128)(2,1)S(1)} %pad.37.q_ref, bf16[512,1152]{1,0:T(8,128)(2,1)S(1)} %fusion.78.own_ref, s32[1024,1]{1,0:T(8,128)S(1)} %copy.208.key_ids_ref, s32[1,256]{1,0:T(1,128)S(1)} %constant_dynamic-slice_fusion.11.query_ids_ref), custom_call_target="tpu_custom_call" | custom-call | flops 1207959552 | bytes 4718592 | tf_op jit(solution)/shard_map/attend/pallas_call | solution.py:788
  410.0 40.5 %all-gather.11.cloned.1.call-done = bf16[1,1,4352,1088]{3,2,1,0:T(8,128)(2,1)} async-done(((bf16[1,1,136,1088]{3,2,1,0:T(8,128)(2,1)}), bf16[1,1,4352,1088]{3,2,1,0:T(8,128)(2,1)}) %all-gather.11.cloned.1.call-update) | async-done | bytes 9469968 | tf_op jit(solution)/shard_map/all_gather | solution.py:1175
  463.6 47.5 %share_final.1 = bf16[32,64,1088]{2,1,0:T(8,128)(2,1)} custom-call(bf16[4,64,1088]{2,1,0:T(8,128)(2,1)} %bitcast.230), custom_call_target="tpu_custom_call" | custom-call | tf_op jit(solution)/shard_map/share_final/pallas_call | solution.py:168
  511.1 12.3 select_reduce_fusion.3
  528.8 14.3 %share_stats.1 = f32[3,16,128]{2,1,0:T(8,128)S(1)} custom-call(f32[3,16,128]{2,1,0:T(8,128)S(1)} %pad_maximum_fusion.2.refs_0_), custom_call_target="tpu_custom_call" | custom-call | tf_op jit(solution)/shard_map/share_stats/pallas_call | solution.py:168
  548.7 12.4 fusion.166
  561.1 53.4 %return_final.1 = bf16[4,64,1088]{2,1,0:T(8,128)(2,1)} custom-call(f32[32,64,1088]{2,1,0:T(8,128)} %bitcast.208), custom_call_target="tpu_custom_call" | custom-call | tf_op jit(solution)/shard_map/return_final/pallas_call | solution.py:168
  623.2 9.9 convolution_convert_fusion.2
  640.2 8.8 convert_reduce_fusion
  649.0 10.8 fusion.164
  673.6 52.1 %attend_back.2 = (bf16[256,1152]{1,0:T(8,128)(2,1)}, bf16[512,1152]{1,0:T(8,128)(2,1)}) custom-call(bf16[256,1152]{1,0:T(8,128)(2,1)} %copy-done.8, bf16[4,512,1152]{2,1,0:T(8,128)(2,1)} %get-tuple-element.285.kv_ref, bf16[256,1152]{1,0:T(8,128)(2,1)} %pad.40.grad_ref, f32[9,2,256]{2,1,0:T(2,128)} %copy-done.13, s32[1024,1]{1,0:T(8,128)} %copy-done.9, ...), custom_call_target="tpu_custom_call" | custom-call | flops 3019898880 | bytes 14155776 | tf_op jit(solution)/shard_map/attend_back/pallas_call | solution.py:915
  736.0 8.7 convolution_convert_fusion.1
  746.1 7.8 fusion.163
  757.4 8.4 convert_reduce_fusion.1
  768.7 8.5 fusion.162
  814.5 14.6 %fusion.167 = f32[1604,1088]{0,1:T(8,128)} fusion(bf16[2048,1604]{0,1:T(8,128)(2,1)} %copy-done.36, bf16[2048,1088]{1,0:T(8,128)(2,1)} %bitcast.218), kind=kOutput, calls=%fused_computation.365 | convolution fusion | flops 7148142592 | bytes 18007040 | tf_op jit(solution)/shard_map/dot_general | solution.py:963
  829.1 47.9 %attend_back.3 = (bf16[256,1152]{1,0:T(8,128)(2,1)}, bf16[512,1152]{1,0:T(8,128)(2,1)}) custom-call(bf16[256,1152]{1,0:T(8,128)(2,1)} %copy-done.3, bf16[4,512,1152]{2,1,0:T(8,128)(2,1)} %get-tuple-element.284.kv_ref, bf16[256,1152]{1,0:T(8,128)(2,1)} %pad.41.grad_ref, f32[9,2,256]{2,1,0:T(2,128)} %copy-done.12, s32[1024,1]{1,0:T(8,128)} %copy-done.9, ...), custom_call_target="tpu_custom_call" | custom-call | flops 3019898880 | bytes 14155776 | tf_op jit(solution)/shard_map/attend_back/pallas_call | solution.py:915
  892.0 7.8 fusion.161
  915.1 8.3 reduce-scatter.9.cloned.1.call-done
  927.9 13.4 %trade_rows.1 = (bf16[256,1632]{1,0:T(8,128)(2,1)}, bf16[256,544]{1,0:T(8,128)(2,1)}, bf16[256,2176]{1,0:T(8,128)(2,1)}, bf16[256,2176]{1,0:T(8,128)(2,1)}, bf16...) custom-call(bf16[256,1632]{1,0:T(8,128)(2,1)} %copy.233.refs_0_, ...), custom_call_target="tpu_custom_call" | custom-call | tf_op jit(solution)/shard_map/trade_rows/pallas_call | solution.py:635
  967.2 210.1 %close_rows.1 = (f32[136,1088]{1,0:T(8,128)}, f32[136,1088]{1,0:T(8,128)}, f32[136,1088]{1,0:T(8,128)}, f32[136,1088]{1,0:T(8,128)}, bf16[32,32,1088]{2,1,0:T(8,...) custom-call(bf16[16,136,1088]{2,1,0:T(8,128)(2,1)} %bitcast.204, bf16[16,136,1088]{2,1,0:T(8,128)(2,1)} %bitcast.214, ...), custom_call_target="tpu_custom_call" | custom-call | tf_op jit(solution)/shard_map/close_rows/pallas_call | solution.py:168
  1183.8 13.0 %fusion.16 = f32[1604,1088]{0,1:T(8,128)} fusion(f32[1604,1088]{0,1:T(8,128)} %fusion.167, s32[1856]{0:T(1024)S(1)} %copy-done.120, bf16[32,1088]{1,0:T(8,128)(2,1)S(1)} %get-tuple-element.388, bf16[32,1088]{1,0:T(8,128)(2,1)S(1)} %get-tuple-element.389, bf16[1024,1088]{1,0:T(8,128)(2,1)S(1)} %bitcast.256, bf16[768,1088]{1,0:T(8,128)(2,1)S(1)} %bitcast.257), kind=kOutput, calls=%fused_computation.46 | convolution fusion | flops 6498880512 | bytes 18007296 | tf_op jit(solution)/shard_map/dot_general | solution.py:969
  1203.9 11.3 share_norm.1
  1227.6 19.2 %multiply_subtract_fusion = (f32[1604,1088]{0,1:T(8,128)}, f32[1604,1088]{0,1:T(8,128)}, f32[1604,1088]{0,1:T(8,128)}) fusion(f32[1604,1088]{0,1:T(8,128)} %param.25, f32[1604]{0:T(1024)S(1)} %copy-done.98, f32[]{:T(128)} %bitcast.71, f32[]{:T(128)} %bitcast.70, f32[1604]{0:T(1024)S(1)} %copy-done.99, f32[1604,1088]{0,1:T(8,128)} %get-tuple-element.315, ...), kind=kLoop, calls=%fused_computation.57 | loop fusion | flops 27922432 | bytes 48877100 | tf_op jit(solution)/shard_map/sub | solution.py:1090
  (484 shorter events, 242.6 us)
Async XLA Ops:
  7.2 259.7 %all-gather.7.cloned.1.call-start = ((), (), s32[]{:S(2)}) async-start(), calls=%async_computation.2 | async-start | bytes 31021056 | tf_op jit(solution)/shard_map/all_gather | solution.py:1171
  10.5 347.8 %all-gather.9.cloned.1.call-start = ((), (), s32[]{:S(2)}) async-start(), calls=%async_computation.3 | async-start | bytes 10340352 | tf_op jit(solution)/shard_map/all_gather | solution.py:1175
  11.5 439.0 %all-gather.11.cloned.1.call-start = ((), (), s32[]{:S(2)}) async-start(), calls=%async_computation.4 | async-start | bytes 10340352 | tf_op jit(solution)/shard_map/all_gather | solution.py:1175
  12.2 816.9 %reduce-scatter.7.cloned.1.call-start = ((), (), s32[]{:S(2)}) async-start(), calls=%async_computation.5 | async-start | bytes 10340352
  12.3 20.4 %copy-start.93 = (s32[1056]{0:T(1024)}, s32[1056]{0:T(1024)S(1)}, u32[]{:S(2)}) copy-start(s32[1056]{0:T(1024)S(1)} %subtract_select_fusion) | copy-start | bytes 12676
  32.7 11.3 copy-start.95
  257.6 57.5 %copy-start.14 = (f32[256,1088]{1,0:T(8,128)}, f32[256,1088]{1,0:T(8,128)S(1)}, u32[]{:S(2)}) copy-start(f32[256,1088]{1,0:T(8,128)S(1)} %copy.209) | copy-start | bytes 3342340
  258.1 106.4 %copy-start.9 = (s32[1024,1]{1,0:T(8,128)}, s32[1024,1]{1,0:T(8,128)S(1)}, u32[]{:S(2)}) copy-start(s32[1024,1]{1,0:T(8,128)S(1)} %copy.208.key_ids_ref) | copy-start | bytes 12292
  258.7 105.8 %copy-start.10 = (s32[1,256]{1,0:T(1,128)}, s32[1,256]{1,0:T(1,128)S(1)}, u32[]{:S(2)}) copy-start(s32[1,256]{1,0:T(1,128)S(1)} %constant_dynamic-slice_fusion.11.query_ids_ref) | copy-start | bytes 3076
  259.1 13.3 %copy-start.89 = (f32[1088]{0:T(1024)}, f32[1088]{0:T(1024)S(1)}, u32[]{:S(2)}) copy-start(f32[1088]{0:T(1024)S(1)} %get-tuple-element.345) | copy-start | bytes 13060
  259.1 59.3 %copy-start.91 = (f32[1088]{0:T(1024)}, f32[1088]{0:T(1024)S(1)}, u32[]{:S(2)}) copy-start(f32[1088]{0:T(1024)S(1)} %get-tuple-element.340) | copy-start | bytes 13060
  259.2 13.3 %copy-start.100 = (f32[256]{0:T(256)}, f32[256]{0:T(256)S(1)}, u32[]{:S(2)}) copy-start(f32[256]{0:T(256)S(1)} %broadcast_multiply_fusion.5) | copy-start | bytes 3076
  259.4 13.1 %copy-start.113 = (f32[256]{0:T(256)}, f32[256]{0:T(256)S(1)}, u32[]{:S(2)}) copy-start(f32[256]{0:T(256)S(1)} %multiply_reduce_fusion.16) | copy-start | bytes 3076
  259.5 13.0 %copy-start.107 = (f32[256]{0:T(256)}, f32[256]{0:T(256)S(1)}, u32[]{:S(2)}) copy-start(f32[256]{0:T(256)S(1)} %fusion.127) | copy-start | bytes 3076
  259.8 12.7 %copy-start.60 = (bf16[256,1088]{1,0:T(8,128)(2,1)}, bf16[256,1088]{1,0:T(8,128)(2,1)S(1)}, u32[]{:S(2)}) copy-start(bf16[256,1088]{1,0:T(8,128)(2,1)S(1)} %add_convert_fusion.4.refs_6_) | copy-start | bytes 1671172
  273.0 42.1 %copy-start.3 = (bf16[256,1152]{1,0:T(8,128)(2,1)}, bf16[256,1152]{1,0:T(8,128)(2,1)S(1)}, u32[]{:S(2)}) copy-start(bf16[256,1152]{1,0:T(8,128)(2,1)S(1)} %pad.34.q_ref) | copy-start | bytes 1769476
  318.1 10.1 copy-start.16
  318.1 10.0 copy-start.102
  318.4 9.7 copy-start.114
  336.7 27.2 %copy-start.64 = (bf16[256,1088]{1,0:T(8,128)(2,1)}, bf16[256,1088]{1,0:T(8,128)(2,1)S(1)}, u32[]{:S(2)}) copy-start(bf16[256,1088]{1,0:T(8,128)(2,1)S(1)} %add_convert_fusion.2.refs_10_) | copy-start | bytes 1671172
  364.4 41.2 %copy-start.8 = (bf16[256,1152]{1,0:T(8,128)(2,1)}, bf16[256,1152]{1,0:T(8,128)(2,1)S(1)}, u32[]{:S(2)}) copy-start(bf16[256,1152]{1,0:T(8,128)(2,1)S(1)} %pad.37.q_ref) | copy-start | bytes 1769476
  405.6 51.5 %slice-start = ((s8[10027008]{0:T(1024)(128)(4,1)}), s8[1638400]{0:T(1024)(128)(4,1)S(1)}, s32[]{:S(2)}) async-start(s8[10027008]{0:T(1024)(128)(4,1)} %bitcast.200), calls=%async_computation.7 | async-start | bytes 3276800
  511.1 12.3 copy-start.97
  548.7 12.4 copy-start.36
  633.1 290.3 %reduce-scatter.9.cloned.1.call-start = ((), (), s32[]{:S(2)}) async-start(), calls=%async_computation.6 | async-start | bytes 10340352
  649.0 10.8 copy-start.41
  913.6 9.8 copy-start.112
  927.8 13.4 %copy-start.59 = (bf16[256,1088]{1,0:T(8,128)(2,1)S(1)}, bf16[256,1088]{1,0:T(8,128)(2,1)}, u32[]{:S(2)}) copy-start(bf16[256,1088]{1,0:T(8,128)(2,1)} %copy-done.58) | copy-start | bytes 1671172
  927.8 13.4 %copy-start.81 = (bf16[256,1,1,544]{3,0,2,1:T(8,128)(2,1)S(1)}, bf16[256,1,1,544]{3,0,2,1:T(8,128)(2,1)}, u32[]{:S(2)}) copy-start(bf16[256,1,1,544]{3,0,2,1:T(8,128)(2,1)} %copy.238) | copy-start | bytes 835588
  1183.8 13.1 %copy-start.70 = (pred[32,256]{1,0:T(32,128)(4,1)S(1)}, pred[32,256]{1,0:T(32,128)(4,1)}, u32[]{:S(2)}) copy-start(pred[32,256]{1,0:T(32,128)(4,1)} %copy-done.69) | copy-start | bytes 24580
  1183.8 13.1 %copy-start.85 = (s32[256]{0:T(256)S(1)}, s32[256]{0:T(256)}, u32[]{:S(2)}) copy-start(s32[256]{0:T(256)} %copy-done.84) | copy-start | bytes 3076
  1183.8 13.1 %copy-start.87 = (s32[256]{0:T(256)S(1)}, s32[256]{0:T(256)}, u32[]{:S(2)}) copy-start(s32[256]{0:T(256)} %copy-done.86) | copy-start | bytes 3076
  (112 other events, 347.8 us)
Sparse Core Ops, SparseCore 0:
  11.6 255.2 all-gather.6
  269.7 88.5 all-gather.8
  361.8 88.6 all-gather.10
  633.3 143.0 reduce-scatter.6
  782.3 141.0 reduce-scatter.8

commit v6 on v5

--- a/solution.py
+++ b/solution.py
@@ -609,47 +609,57 @@
     )
 
 
-def trade_kernel(count, *refs):
+def trade_kernel(halved, count, *refs):
     x_refs, o_refs = refs[:count], refs[count : 2 * count]
-    send_sems, recv_sems = refs[2 * count :]
+    send_sems, recv_sems, keep_sems = refs[2 * count :]
     bit = ("seq", 0)
+    mine = bit_here(bit)
     greet([bit])
     copies = []
     for k in range(count):
+        if k < halved:
+            tokens = x_refs[k].shape[-1]
+            keep, leave = x_refs[k].at[:, mine], x_refs[k].at[:, 1 - mine]
+            near = o_refs[k].at[:, :, pl.ds(0, tokens)]
+            far = o_refs[k].at[:, :, pl.ds(tokens, tokens)]
+        else:
+            tokens = x_refs[k].shape[0]
+            keep = leave = x_refs[k]
+            near, far = o_refs[k].at[pl.ds(0, tokens)], o_refs[k].at[pl.ds(tokens, tokens)]
+        local = pltpu.make_async_copy(keep, near, keep_sems.at[k])
+        local.start()
         copy = pltpu.make_async_remote_copy(
-            x_refs[k],
-            o_refs[k],
+            leave,
+            far,
             send_sems.at[k],
             recv_sems.at[k],
             device_id=partner(bit),
             device_id_type=MESH,
         )
         copy.start()
-        copies.append(copy)
+        copies += [local, copy]
     for copy in copies:
         copy.wait()
 
 
-def trade(arrays, name, number):
+def trade(features, cotangents, name, number):
+    arrays = features + cotangents
     count = len(arrays)
+    outs = []
+    for x in features:
+        runs, unused, rows, tokens = x.shape
+        outs.append(jax.ShapeDtypeStruct((runs, rows, 2 * tokens), x.dtype))
+    for x in cotangents:
+        outs.append(jax.ShapeDtypeStruct((2 * x.shape[0], x.shape[1]), x.dtype))
     return pl.pallas_call(
-        partial(trade_kernel, count),
-        out_shape=[jax.ShapeDtypeStruct(x.shape, x.dtype) for x in arrays],
+        partial(trade_kernel, len(features), count),
+        out_shape=outs,
         in_specs=[pl.BlockSpec(memory_space=pl.ANY)] * count,
         out_specs=[pl.BlockSpec(memory_space=pl.ANY)] * count,
-        scratch_shapes=[pltpu.SemaphoreType.DMA((count,)), pltpu.SemaphoreType.DMA((count,))],
+        scratch_shapes=[pltpu.SemaphoreType.DMA((count,))] * 3,
         compiler_params=pltpu.CompilerParams(collective_id=number, has_side_effects=True),
         name=name,
     )(*arrays)
-
-
-def my_rows(features, own):
-    rows = features.shape[0]
-    parts = features.reshape(rows, -1, 2, own)
-    at = lax.rem(lax.axis_index("seq"), 2)
-    mine = lax.dynamic_index_in_dim(parts, at, 2, keepdims=False)
-    other = lax.dynamic_index_in_dim(parts, 1 - at, 2, keepdims=False)
-    return mine.reshape(rows, -1), other.reshape(rows, -1)
 
 
 def late_mats(groups, number):
@@ -657,16 +667,12 @@
     total = lax.axis_size(AXES)
     height = sum(features.shape[1] for features, unused in groups[0])
     own = height // total * lax.axis_size("shard")
-    halves = [my_rows(features, own) for features, unused in pairs]
-    tails = [tail for unused, tail in pairs]
-    got = trade([other for unused, other in halves] + tails, "trade_rows", number)
+    features = [x.T.reshape(-1, 2, own, x.shape[0]) for x, unused in pairs]
+    got = trade(features, [tail for unused, tail in pairs], "trade_rows", number)
     parts = []
-    for k, (mine, unused) in enumerate(halves):
-        grad = dot_cols(
-            jnp.concatenate([mine, got[k]], 0),
-            jnp.concatenate([tails[k], got[len(halves) + k]], 0),
-        )
-        parts.append(rows_major(grad.astype(jnp.bfloat16)))
+    for k in range(len(pairs)):
+        both = got[k].reshape(-1, got[k].shape[2])
+        parts.append(rows_major(dot_plain(both, got[len(pairs) + k]).astype(jnp.bfloat16)))
     mats = []
     for group in groups:
         grad = jnp.concatenate(parts[: len(group)], 0) if len(group) > 1 else parts[0]
@@ -970,7 +976,7 @@
 
 
 def column_sums(values):
-    return jnp.sum(values.astype(jnp.float32), 0, keepdims=True)
+    return jnp.sum(values.astype(jnp.float32), 0)
 
 
 def layer_norm(values, gain, shift):
@@ -1049,11 +1055,11 @@
     unused_gelu, gelu_pull = jax.vjp(partial(jax.nn.gelu, approximate=True), upward)
     up_grad = gelu_pull(act_grad)[0].astype(jnp.bfloat16)
     mid_back, gain_two, shift_two = norm_back(
-        mid_state, params[5 : 6], params[6 : 7], dot_plain(up_grad, weights[1])
+        mid_state, params[5 : 6], params[6 : 7], rows_major(dot_plain(up_grad, weights[1]))
     )
     mid_grad = grad_in + mid_back
     out_grad = mid_grad.astype(jnp.bfloat16)
-    att_grad = wide(dot_rows(out_grad, weights[0][3 * width :]).astype(jnp.bfloat16))
+    att_grad = wide(rows_major(dot_rows(out_grad, weights[0][3 * width :]).astype(jnp.bfloat16)))
     if arrived:
         att_grad, arrived[0] = lax.optimization_barrier((att_grad, arrived[0]))
     query_grad, own = attend_back(queries, key_vals, att_grad, lse, key_ids, query_ids, 8)
@@ -1061,7 +1067,10 @@
     key_grad, val_grad = own[: own.shape[0] // 2, :width], own[own.shape[0] // 2 :, :width]
     joined_grad = jnp.concatenate([query_grad, key_grad, val_grad], 1)
     state_back, gain_one, shift_one = norm_back(
-        state, params[0 : 1], params[1 : 2], dot_plain(joined_grad, weights[0][: 3 * width])
+        state,
+        params[0 : 1],
+        params[1 : 2],
+        rows_major(dot_plain(joined_grad, weights[0][: 3 * width])),
     )
     up_sums = column_sums(up_grad)
     small_grad = [
@@ -1073,7 +1082,8 @@
         gain_two,
         shift_two,
         column_sums(down_grad),
-    ] + [up_sums[:, k * width : (k + 1) * width] for k in range(4)]
+        up_sums,
+    ]
     factors = [
         [(joined_grad, hidden), (attended, out_grad)],
         [(up_grad, normed)],
@@ -1171,12 +1181,11 @@
             whole = lax.all_gather(mats_low[0], AXES, axis=1, tiled=True)
             gathered.append([whole[k] for k in range(3)])
         else:
-            gathered.append(
-                [lax.all_gather(mats_low[layer_at, k], AXES, axis=0, tiled=True) for k in range(2)]
-            )
-    (last_down,), (place_rows,), (small,), (given,) = run_jobs(
+            rest = lax.all_gather(mats_low[layer_at, 1:], AXES, axis=1, tiled=True)
+            gathered.append([rest[0], rest[1]])
+    (upper_first,), (place_rows,), (small,), (given,) = run_jobs(
         [
-            gather_job([mats_low[1, 2]]),
+            gather_job([mats_low[1, 0]]),
             sum_job(
                 rows_out[exchanged : exchanged + seq_length].reshape(total, piece, width),
                 sum_axes=("seq", "dp", "shard"),
@@ -1191,7 +1200,7 @@
         2,
         32,
     )
-    gathered[1].append(last_down.reshape(-1, width))
+    gathered[1].insert(0, upper_first.reshape(-1, width))
     place_rows = place_rows.reshape(tok_count, width)
     small = small[:small_count].astype(jnp.float32)
     place_state = jnp.broadcast_to(place_rows.astype(jnp.float32), (seqs, tok_count, width))
@@ -1275,7 +1284,7 @@
         join_orders=[shard_bits[::-1], shard_bits[::-1]],
         chunks=2,
     ).reshape(slots, width)
-    final_grad = dot_cols(to_slot, returned)
+    final_grad = rows_major(dot_cols(to_slot, returned))
     state_grad, gain_final, shift_final = norm_back(state, final_gain, final_shift, final_grad)
 
     late = []
@@ -1300,9 +1309,11 @@
 
     low_grad = state_grad.astype(jnp.bfloat16)
     place_grad = jnp.sum(state_grad.reshape(seqs, tok_count, width), 0)
-    small_grad = pad_rows(
-        jnp.concatenate(sum(small_grads, []) + [gain_final, shift_final], 0), small_rows
-    )
+    small_grad = jnp.concatenate(
+        [x.reshape(-1) for x in sum(small_grads, []) + [gain_final, shift_final]]
+    )
+    small_size = small_grad.shape[0]
+    small_grad = jnp.pad(small_grad, (0, -small_size % 1024)).reshape(-1, 128)
 
     def leaving(at):
         rows = dot_cols(one_hot(own_slots(at), total * SLOTS, 1), low_grad).astype(jnp.bfloat16)
@@ -1333,6 +1344,7 @@
         more = run_jobs([mats_job(late[k : k + fits])], "sum_mats", 14 + k, 61)[0]
         own_mats = list(own_mats) + list(lax.optimization_barrier(tuple(more)))
     place_grad = place_grad.reshape(seq_length, width)
+    small_grad = pad_rows(small_grad.reshape(-1)[:small_size].reshape(-1, width), small_rows)
     small_high = small_grad.astype(jnp.bfloat16)
     small_low = (small_grad - small_high.astype(jnp.float32)).astype(jnp.bfloat16)
     values = jnp.concatenate([came.reshape(-1, width), place_grad, small_high, small_low], 0)

time: 1270 us -> 1450 us (1.14)
  Pallas kernels: 742 us -> 980 us
  local copies, waits for them, and re-layouts: 127 us -> 67 us
    pallas_call x1, Pallas kernels: 13.4 us -> 244 us  [trade(): pl.pallas_call(partial(trade_kernel, len(features), count), out_shape=out...]
    optimization_barrier x1, waiting for transfers between devices: 8.33 us -> 62.8 us  [on_device(): low_grad, arrived[1] = lax.optimization_barrier((low_grad, arrived[1]))]
    all_gather x2 -> x1, waiting for transfers between devices: 62.1 us -> 24.7 us  [on_device(): rest = lax.all_gather(mats_low[layer_at, 1:], AXES, axis=1, tiled=True)]
    dot_general x11 -> x5, matrix products: 56.5 us -> 32.8 us  [dot_cols(): lax.dot_general(left_op, right_op, (((0,), (0,)), ((), ())), preferred_el...]
    dot_general x15 -> x21, matrix products: 92.2 us -> 112 us  [dot_plain(): return jnp.dot(left_op, right_op, preferred_element_type=jnp.float32)]
    reshape x18 -> x2, local copies, waits for them, and re-layouts: 20.2 us -> 1.64 us  [the longest x1 0.99 us: on_device(): small_grad.reshape(-1)[:small_size].reshape(-1, width)]
    pallas_call x2, Pallas kernels: 83 us -> 102 us  [attend(): pl.pallas_call(attend_kernel, out_shape=(jax.ShapeDtypeStruct((rows, widt...]
    unnamed x283 -> x237, local copies, waits for them, and re-layouts: 32.2 us -> 20.4 us
  transfers between devices with their start and end apart: 5 -> 4, of which waited for: 4 -> 3; matrix products, arithmetic and copies ran while one was open for 19% -> 13% of each run, Pallas kernels for 31% -> 28%
where the time goes in v6:
time: 1450 us; the launch traced here: 1440 us
  Pallas kernels  980 us (68%)
  matrix products  203 us (14%)
  waiting for transfers between devices  92.1 us (6%)
  other arithmetic  77.2 us (5%)
  local copies, waits for them, and re-layouts  67 us (5%)
  between operations  22.2 us (2%)
    pallas_call x7, Pallas kernels, run_jobs(): pl.pallas_call(partial(jobs_kernel, jobs), out_shape=outputs, in_specs=in...  544 us
    pallas_call x1, Pallas kernels, trade(): pl.pallas_call(partial(trade_kernel, len(features), count), out_shape=out...  244 us
    dot_general x21, matrix products, dot_plain(): return jnp.dot(left_op, right_op, preferred_element_type=jnp.float32)  112 us
    pallas_call x2, Pallas kernels, attend(): pl.pallas_call(attend_kernel, out_shape=(jax.ShapeDtypeStruct((rows, widt...  102 us
    pallas_call x2, Pallas kernels, attend_back(): pl.pallas_call(attend_back_kernel, out_shape=(jax.ShapeDtypeStruct((rows,...  90.3 us
    optimization_barrier x1, waiting for transfers between devices, on_device(): low_grad, arrived[1] = lax.optimization_barrier((low_grad, arrived[1]))  62.8 us
    dot_general x9, matrix products, dot_rows(): lax.dot_general(left_op, right_op, (((1,), (1,)), ((), ())), preferred_el...  58.1 us
    dot_general x5, matrix products, dot_cols(): lax.dot_general(left_op, right_op, (((0,), (0,)), ((), ())), preferred_el...  32.8 us
  transfers between devices with their start and end apart: 4, of which 3 were waited for; matrix products, arithmetic and copies ran while one was open for 13% of the time, Pallas kernels for 28%

profile of v6, /device:TPU:0, one launch (start us, length us, event | category | flops | bytes accessed | tf_op | source)
XLA Modules:
  0.0 1442.6 jit_solution(7521322163512723373)
XLA Ops:
  11.6 12.5 share_ids.1
  27.0 6.9 copy.90
  33.9 11.3 fusion.21
  45.6 196.1 %open_rows.1 = (bf16[32,136,1088]{2,1,0:T(8,128)(2,1)S(1)}, bf16[8,32,1088]{2,1,0:T(8,128)(2,1)S(1)}, bf16[32,1088]{1,0:T(8,128)(2,1)S(1)}, bf16[32,24,1088]{2,1,0:T(8,128)(2,1)S(1)}) custom-call(bf16[136,1088]{1,0:T(8,128)(2,1)S(1)} %slice_bitcast_fusion.34.refs_0_, bf16[32,32,1088]{2,1,0:T(8,128)(2,1)S(1)} %bitcast.233, ...), custom_call_target="tpu_custom_call" | custom-call | tf_op jit(solution)/shard_map/open_rows/pallas_call | solution.py:168
  270.0 41.2 %attend.2 = (bf16[256,1152]{1,0:T(8,128)(2,1)S(1)}, f32[9,2,256]{2,1,0:T(2,128)S(1)}, bf16[4,512,1152]{2,1,0:T(8,128)(2,1)}) custom-call(bf16[256,1152]{1,0:T(8,128)(2,1)S(1)} %pad.38.q_ref, bf16[512,1152]{1,0:T(8,128)(2,1)S(1)} %fusion.77.own_ref, s32[1024,1]{1,0:T(8,128)S(1)} %copy.94.key_ids_ref, s32[1,256]{1,0:T(1,128)S(1)} %constant_dynamic-slice_fusion.query_ids_ref), custom_call_target="tpu_custom_call" | custom-call | flops 1207959552 | bytes 4718592 | tf_op jit(solution)/shard_map/attend/pallas_call | solution.py:794
  314.8 9.3 fusion.24
  324.1 8.8 fusion.131
  336.6 60.4 %attend.3 = (bf16[256,1152]{1,0:T(8,128)(2,1)S(1)}, f32[9,2,256]{2,1,0:T(2,128)S(1)}, bf16[4,512,1152]{2,1,0:T(8,128)(2,1)}) custom-call(bf16[256,1152]{1,0:T(8,128)(2,1)S(1)} %pad.41.q_ref, bf16[512,1152]{1,0:T(8,128)(2,1)S(1)} %fusion.78.own_ref, s32[1024,1]{1,0:T(8,128)S(1)} %copy.94.key_ids_ref, s32[1,256]{1,0:T(1,128)S(1)} %constant_dynamic-slice_fusion.query_ids_ref), custom_call_target="tpu_custom_call" | custom-call | flops 1207959552 | bytes 4718592 | tf_op jit(solution)/shard_map/attend/pallas_call | solution.py:794
  398.5 24.7 %all-gather.7.cloned.1.call-done = bf16[1,2,4352,1088]{3,2,1,0:T(8,128)(2,1)} async-done(((bf16[1,2,136,1088]{3,2,1,0:T(8,128)(2,1)}), bf16[1,2,4352,1088]{3,2,1,0:T(8,128)(2,1)}) %all-gather.7.cloned.1.call-update) | async-done | bytes 18939920 | tf_op jit(solution)/shard_map/all_gather | solution.py:1184
  429.3 9.2 fusion.133
  440.3 47.6 %share_final.1 = bf16[32,64,1088]{2,1,0:T(8,128)(2,1)} custom-call(bf16[4,64,1088]{2,1,0:T(8,128)(2,1)} %bitcast.266), custom_call_target="tpu_custom_call" | custom-call | tf_op jit(solution)/shard_map/share_final/pallas_call | solution.py:168
  488.0 12.6 select_reduce_fusion.3
  505.9 16.3 %share_stats.1 = f32[3,16,128]{2,1,0:T(8,128)S(1)} custom-call(f32[3,16,128]{2,1,0:T(8,128)S(1)} %pad_maximum_fusion.2.refs_0_), custom_call_target="tpu_custom_call" | custom-call | tf_op jit(solution)/shard_map/share_stats/pallas_call | solution.py:168
  527.8 12.4 fusion.135
  540.2 51.1 %return_final.1 = bf16[4,64,1088]{2,1,0:T(8,128)(2,1)} custom-call(f32[32,64,1088]{2,1,0:T(8,128)} %bitcast.242), custom_call_target="tpu_custom_call" | custom-call | tf_op jit(solution)/shard_map/return_final/pallas_call | solution.py:168
  594.7 10.0 convolution_convert_fusion.2
  608.0 8.6 convert_reduce_fusion
  616.6 9.0 multiply_reduce_fusion.3
  630.0 47.4 %attend_back.2 = (bf16[256,1152]{1,0:T(8,128)(2,1)}, bf16[512,1152]{1,0:T(8,128)(2,1)}) custom-call(bf16[256,1152]{1,0:T(8,128)(2,1)} %copy-done.3, bf16[4,512,1152]{2,1,0:T(8,128)(2,1)} %get-tuple-element.285.kv_ref, bf16[256,1152]{1,0:T(8,128)(2,1)} %pad.44.grad_ref, f32[9,2,256]{2,1,0:T(2,128)} %copy-done.7, s32[1024,1]{1,0:T(8,128)} %copy-done.4, ...), custom_call_target="tpu_custom_call" | custom-call | flops 3019898880 | bytes 14155776 | tf_op jit(solution)/shard_map/attend_back/pallas_call | solution.py:921
  683.9 8.1 multiply_reduce_fusion.4
  708.1 9.4 convert_reduce_fusion.1
  726.3 8.6 multiply_reduce_fusion.5
  745.9 14.2 fusion.136
  760.1 42.9 %attend_back.3 = (bf16[256,1152]{1,0:T(8,128)(2,1)}, bf16[512,1152]{1,0:T(8,128)(2,1)}) custom-call(bf16[256,1152]{1,0:T(8,128)(2,1)} %copy-done.2, bf16[4,512,1152]{2,1,0:T(8,128)(2,1)} %get-tuple-element.284.kv_ref, bf16[256,1152]{1,0:T(8,128)(2,1)} %pad.45.grad_ref, f32[9,2,256]{2,1,0:T(2,128)} %copy-done.6, s32[1024,1]{1,0:T(8,128)} %copy-done.4, ...), custom_call_target="tpu_custom_call" | custom-call | flops 3019898880 | bytes 14155776 | tf_op jit(solution)/shard_map/attend_back/pallas_call | solution.py:921
  809.5 6.7 multiply_reduce_fusion.6
  820.1 62.8 %reduce-scatter.9.cloned.1.call-done = bf16[1,136,1088]{2,1,0:T(8,128)(2,1)} async-done(((bf16[32,136,1088]{2,1,0:T(8,128)(2,1)}), bf16[1,136,1088]{2,1,0:T(8,128)(2,1)}) %reduce-scatter.9.cloned.1.call-update) | async-done | bytes 295952 | tf_op jit(solution)/shard_map/optimization_barrier | solution.py:1322
  886.0 243.7 %trade_rows.1 = (bf16[3,544,512]{2,1,0:T(8,128)(2,1)}, bf16[1,544,512]{2,1,0:T(8,128)(2,1)}, bf16[4,544,512]{2,1,0:T(8,128)(2,1)}, bf16[4,544,512]{2,1,0:T(8,128...) custom-call(bf16[3,2,544,256]{3,2,1,0:T(8,128)(2,1)} %bitcast.253, ...), custom_call_target="tpu_custom_call" | custom-call | tf_op jit(solution)/shard_map/trade_rows/pallas_call | solution.py:654
  1154.6 210.3 %close_rows.1 = (f32[136,1088]{1,0:T(8,128)}, f32[136,1088]{1,0:T(8,128)}, f32[136,1088]{1,0:T(8,128)}, f32[136,1088]{1,0:T(8,128)}, bf16[32,32,1088]{2,1,0:T(8,...) custom-call(bf16[16,136,1088]{2,1,0:T(8,128)(2,1)} %bitcast.238, bf16[16,136,1088]{2,1,0:T(8,128)(2,1)} %bitcast.254, ...), custom_call_target="tpu_custom_call" | custom-call | tf_op jit(solution)/shard_map/close_rows/pallas_call | solution.py:168
  1366.0 13.4 fusion.12
  1391.6 10.5 share_norm.1
  1407.7 6.8 multiply_subtract_fusion.1
  1414.5 19.2 %multiply_subtract_fusion = (f32[1604,1088]{0,1:T(8,128)}, f32[1604,1088]{0,1:T(8,128)}, f32[1604,1088]{0,1:T(8,128)}) fusion(f32[1604,1088]{0,1:T(8,128)} %param.25, f32[1604]{0:T(1024)S(1)} %copy-done.71, f32[]{:T(128)} %bitcast.72, f32[]{:T(128)} %bitcast.71, f32[1604]{0:T(1024)S(1)} %copy-done.72, f32[1604,1088]{0,1:T(8,128)} %get-tuple-element.315, ...), kind=kLoop, calls=%fused_computation.58 | loop fusion | flops 27922432 | bytes 48877100 | tf_op jit(solution)/shard_map/sub | solution.py:1100
  (396 shorter events, 168.5 us)
Async XLA Ops:
  7.2 256.6 %all-gather.5.cloned.1.call-start = ((), (), s32[]{:S(2)}) async-start(), calls=%async_computation.2 | async-start | bytes 31021056 | tf_op jit(solution)/shard_map/all_gather | solution.py:1181
  10.5 412.6 %all-gather.7.cloned.1.call-start = ((), (), s32[]{:S(2)}) async-start(), calls=%async_computation.3 | async-start | bytes 20680704 | tf_op jit(solution)/shard_map/all_gather | solution.py:1184
  11.5 748.6 %reduce-scatter.7.cloned.1.call-start = ((), (), s32[]{:S(2)}) async-start(), calls=%async_computation.4 | async-start | bytes 10340352
  33.9 11.3 copy-start.65
  248.7 87.9 %copy-start.4 = (s32[1024,1]{1,0:T(8,128)}, s32[1024,1]{1,0:T(8,128)S(1)}, u32[]{:S(2)}) copy-start(s32[1024,1]{1,0:T(8,128)S(1)} %copy.94.key_ids_ref) | copy-start | bytes 12292
  257.3 12.1 copy-start.10
  257.5 79.0 %copy-start.5 = (s32[1,256]{1,0:T(1,128)}, s32[1,256]{1,0:T(1,128)S(1)}, u32[]{:S(2)}) copy-start(s32[1,256]{1,0:T(1,128)S(1)} %constant_dynamic-slice_fusion.query_ids_ref) | copy-start | bytes 3076
  258.0 11.4 copy-start.61
  258.0 56.3 %copy-start.63 = (f32[1088]{0:T(1024)}, f32[1088]{0:T(1024)S(1)}, u32[]{:S(2)}) copy-start(f32[1088]{0:T(1024)S(1)} %get-tuple-element.345) | copy-start | bytes 13060
  258.0 11.3 copy-start.78
  258.4 11.0 copy-start.88
  259.2 10.2 copy-start.42
  269.9 41.3 %copy-start.2 = (bf16[256,1152]{1,0:T(8,128)(2,1)}, bf16[256,1152]{1,0:T(8,128)(2,1)S(1)}, u32[]{:S(2)}) copy-start(bf16[256,1152]{1,0:T(8,128)(2,1)S(1)} %pad.38.q_ref) | copy-start | bytes 1769476
  270.0 41.2 %copy-start.11 = (f32[256,1088]{1,0:T(8,128)S(1)}, f32[256,1088]{1,0:T(8,128)}, u32[]{:S(2)}) copy-start(f32[256,1088]{1,0:T(8,128)} %copy-done.10) | copy-start | bytes 3342340
  314.0 10.1 copy-start.17
  314.0 10.0 copy-start.80
  332.9 64.2 %copy-start.19 = (f32[256,1088]{1,0:T(8,128)}, f32[256,1088]{1,0:T(8,128)S(1)}, u32[]{:S(2)}) copy-start(f32[256,1088]{1,0:T(8,128)S(1)} %get-tuple-element.438) | copy-start | bytes 3342340
  336.4 60.6 %copy-start.3 = (bf16[256,1152]{1,0:T(8,128)(2,1)}, bf16[256,1152]{1,0:T(8,128)(2,1)S(1)}, u32[]{:S(2)}) copy-start(bf16[256,1152]{1,0:T(8,128)(2,1)S(1)} %pad.41.q_ref) | copy-start | bytes 1769476
  336.6 60.5 %copy-start.38 = (bf16[8,136,1088]{2,1,0:T(8,128)(2,1)S(1)}, bf16[8,136,1088]{2,1,0:T(8,128)(2,1)}, u32[]{:S(2)}) copy-start(bf16[8,136,1088]{2,1,0:T(8,128)(2,1)} %slice.255) | copy-start | bytes 7102468
  397.1 26.1 %copy-start.75 = (f32[4352]{0:T(1024)S(1)}, f32[4352]{0:T(1024)}, u32[]{:S(2)}) copy-start(f32[4352]{0:T(1024)} %add.573) | copy-start | bytes 52228
  398.2 31.1 %copy-start.23 = (f32[256,1088]{1,0:T(8,128)}, f32[256,1088]{1,0:T(8,128)S(1)}, u32[]{:S(2)}) copy-start(f32[256,1088]{1,0:T(8,128)S(1)} %get-tuple-element.440) | copy-start | bytes 3342340
  488.0 12.6 copy-start.69
  527.8 12.4 copy-start.27
  604.8 278.1 %reduce-scatter.9.cloned.1.call-start = ((), (), s32[]{:S(2)}) async-start(), calls=%async_computation.5 | async-start | bytes 10340352
  704.9 12.6 slice-start.2
  818.7 64.1 %copy-start.83 = (s32[256]{0:T(256)S(1)}, s32[256]{0:T(256)}, u32[]{:S(2)}) copy-start(s32[256]{0:T(256)} %copy-done.82) | copy-start | bytes 3076
  1154.6 211.4 %copy-start.98 = (s32[1856]{0:T(1024)S(1)}, s32[1856]{0:T(1024)}, u32[]{:S(2)}) copy-start(s32[1856]{0:T(1024)} %concatenate.48) | copy-start | bytes 22276
  1366.0 13.5 copy-start.32
  1366.0 13.5 copy-start.34
  1366.0 13.5 copy-start.48
  1366.0 13.5 copy-start.58
  1366.0 13.5 copy-start.60
  (88 other events, 388.5 us)
Sparse Core Ops, SparseCore 0:
  11.6 252.1 all-gather.4
  266.8 156.3 all-gather.6
  604.9 138.7 reduce-scatter.6
  749.6 133.1 reduce-scatter.8

commit v7 on v6

--- a/solution.py
+++ b/solution.py
@@ -655,9 +655,11 @@
         partial(trade_kernel, len(features), count),
         out_shape=outs,
         in_specs=[pl.BlockSpec(memory_space=pl.ANY)] * count,
-        out_specs=[pl.BlockSpec(memory_space=pl.ANY)] * count,
+        out_specs=[pl.BlockSpec(memory_space=pltpu.VMEM)] * count,
         scratch_shapes=[pltpu.SemaphoreType.DMA((count,))] * 3,
-        compiler_params=pltpu.CompilerParams(collective_id=number, has_side_effects=True),
+        compiler_params=pltpu.CompilerParams(
+            collective_id=number, has_side_effects=True, vmem_limit_bytes=40 * 2**20
+        ),
         name=name,
     )(*arrays)
 
@@ -1319,9 +1321,9 @@
         rows = dot_cols(one_hot(own_slots(at), total * SLOTS, 1), low_grad).astype(jnp.bfloat16)
         return rows.reshape(total, SLOTS, width)
 
-    (low_grad, arrived[1]) = lax.optimization_barrier((low_grad, arrived[1]))
+    late = late_mats(late, 12)
+    late, arrived[1] = lax.optimization_barrier((late, arrived[1]))
     upper = jnp.concatenate([arrived[1], arrived[0]], 0).astype(jnp.float32)
-    late = late_mats(late, 12)
     fits = mats_fit(late)
     own_mats, (place_grad,), (small_grad,), (came,) = run_jobs(
         [

time: 1450 us -> 1180 us (0.81)
  Pallas kernels: 980 us -> 754 us
  waiting for transfers between devices: 92.1 us -> 28.9 us
    pallas_call x1, Pallas kernels: 244 us -> 15.6 us  [trade(): pl.pallas_call(partial(trade_kernel, len(features), count), out_shape=out...]
    optimization_barrier x1, waiting for transfers between devices: 62.8 us -> 2.27 us  [on_device(): late, arrived[1] = lax.optimization_barrier((late, arrived[1]))]
    unnamed x237 -> x277, local copies, waits for them, and re-layouts: 20.4 us -> 32.2 us
  transfers between devices with their start and end apart: 4 -> 4, of which waited for: 3 -> 3; matrix products, arithmetic and copies ran while one was open for 13% -> 19% of each run, Pallas kernels for 28% -> 36%
where the time goes in v7:
time: 1180 us; the launch traced here: 1170 us
  Pallas kernels  754 us (64%)
  matrix products  207 us (18%)
  local copies, waits for them, and re-layouts  81.2 us (7%)
  other arithmetic  77.9 us (7%)
  waiting for transfers between devices  28.9 us (2%)
  between operations  22.4 us (2%)
    pallas_call x7, Pallas kernels, run_jobs(): pl.pallas_call(partial(jobs_kernel, jobs), out_shape=outputs, in_specs=in...  544 us
    dot_general x21, matrix products, dot_plain(): return jnp.dot(left_op, right_op, preferred_element_type=jnp.float32)  112 us
    pallas_call x2, Pallas kernels, attend(): pl.pallas_call(attend_kernel, out_shape=(jax.ShapeDtypeStruct((rows, widt...  102 us
    pallas_call x2, Pallas kernels, attend_back(): pl.pallas_call(attend_back_kernel, out_shape=(jax.ShapeDtypeStruct((rows,...  91.8 us
    dot_general x9, matrix products, dot_rows(): lax.dot_general(left_op, right_op, (((1,), (1,)), ((), ())), preferred_el...  57.9 us
    dot_general x5, matrix products, dot_cols(): lax.dot_general(left_op, right_op, (((0,), (0,)), ((), ())), preferred_el...  37.3 us
    unnamed x277, local copies, waits for them, and re-layouts  32.2 us
    sub x2, other arithmetic, adam_step(): weights - rate * (moment_hat / (jnp.sqrt(square_hat) + ADAM_EPS) + decay...  25.9 us
  transfers between devices with their start and end apart: 4, of which 3 were waited for; matrix products, arithmetic and copies ran while one was open for 19% of the time, Pallas kernels for 36%

profile of v7, /device:TPU:0, one launch (start us, length us, event | category | flops | bytes accessed | tf_op | source)
XLA Modules:
  0.0 1171.6 jit_solution(3601114816434699440)
XLA Ops:
  11.6 12.5 %share_ids.1 = s32[32,8,128]{2,1,0:T(8,128)S(1)} custom-call(s32[8,128]{1,0:T(8,128)S(1)} %pad_bitcast_fusion.1.refs_0_), custom_call_target="tpu_custom_call" | custom-call | tf_op jit(solution)/shard_map/share_ids/pallas_call | solution.py:168
  27.0 6.9 copy.90
  33.9 11.3 fusion.21
  45.6 196.1 %open_rows.1 = (bf16[32,136,1088]{2,1,0:T(8,128)(2,1)S(1)}, bf16[8,32,1088]{2,1,0:T(8,128)(2,1)S(1)}, bf16[32,1088]{1,0:T(8,128)(2,1)S(1)}, bf16[32,24,1088]{2,1,0:T(8,128)(2,1)S(1)}) custom-call(bf16[136,1088]{1,0:T(8,128)(2,1)S(1)} %slice_bitcast_fusion.34.refs_0_, bf16[32,32,1088]{2,1,0:T(8,128)(2,1)S(1)} %bitcast.233, ...), custom_call_target="tpu_custom_call" | custom-call | tf_op jit(solution)/shard_map/open_rows/pallas_call | solution.py:168
  270.0 41.4 %attend.2 = (bf16[256,1152]{1,0:T(8,128)(2,1)S(1)}, f32[9,2,256]{2,1,0:T(2,128)S(1)}, bf16[4,512,1152]{2,1,0:T(8,128)(2,1)}) custom-call(bf16[256,1152]{1,0:T(8,128)(2,1)S(1)} %pad.38.q_ref, bf16[512,1152]{1,0:T(8,128)(2,1)S(1)} %fusion.77.own_ref, s32[1024,1]{1,0:T(8,128)S(1)} %copy.94.key_ids_ref, s32[1,256]{1,0:T(1,128)S(1)} %constant_dynamic-slice_fusion.query_ids_ref), custom_call_target="tpu_custom_call" | custom-call | flops 1207959552 | bytes 4718592 | tf_op jit(solution)/shard_map/attend/pallas_call | solution.py:796
  315.0 9.3 fusion.24
  324.4 8.8 fusion.131
  336.9 60.5 %attend.3 = (bf16[256,1152]{1,0:T(8,128)(2,1)S(1)}, f32[9,2,256]{2,1,0:T(2,128)S(1)}, bf16[4,512,1152]{2,1,0:T(8,128)(2,1)}) custom-call(bf16[256,1152]{1,0:T(8,128)(2,1)S(1)} %pad.41.q_ref, bf16[512,1152]{1,0:T(8,128)(2,1)S(1)} %fusion.78.own_ref, s32[1024,1]{1,0:T(8,128)S(1)} %copy.94.key_ids_ref, s32[1,256]{1,0:T(1,128)S(1)} %constant_dynamic-slice_fusion.query_ids_ref), custom_call_target="tpu_custom_call" | custom-call | flops 1207959552 | bytes 4718592 | tf_op jit(solution)/shard_map/attend/pallas_call | solution.py:796
  398.9 24.4 %all-gather.7.cloned.1.call-done = bf16[1,2,4352,1088]{3,2,1,0:T(8,128)(2,1)} async-done(((bf16[1,2,136,1088]{3,2,1,0:T(8,128)(2,1)}), bf16[1,2,4352,1088]{3,2,1,0:T(8,128)(2,1)}) %all-gather.7.cloned.1.call-update) | async-done | bytes 18939920 | tf_op jit(solution)/shard_map/all_gather | solution.py:1186
  429.5 9.2 fusion.133
  440.6 47.5 %share_final.1 = bf16[32,64,1088]{2,1,0:T(8,128)(2,1)} custom-call(bf16[4,64,1088]{2,1,0:T(8,128)(2,1)} %bitcast.269), custom_call_target="tpu_custom_call" | custom-call | tf_op jit(solution)/shard_map/share_final/pallas_call | solution.py:168
  488.1 12.3 %select_reduce_fusion.3 = (f32[2048]{0:T(1024)S(1)}, f32[2048,1604]{0,1:T(8,128)S(1)}) fusion(pred[1604]{0:T(1024)(128)(4,1)S(1)} %copy-done.97, bf16[2048,1088]{1,0:T(8,128)(2,1)} %bitcast.260, bf16[1604,1088]{1,0:T(8,128)(2,1)} %get-tuple-element.667), kind=kOutput, calls=%fused_computation.36 | convolution fusion | flops 7154710528 | bytes 21096516 | tf_op jit(solution)/shard_map/dot_general | solution.py:965
  505.7 14.7 %share_stats.1 = f32[3,16,128]{2,1,0:T(8,128)S(1)} custom-call(f32[3,16,128]{2,1,0:T(8,128)S(1)} %pad_maximum_fusion.2.refs_0_), custom_call_target="tpu_custom_call" | custom-call | tf_op jit(solution)/shard_map/share_stats/pallas_call | solution.py:168
  526.0 12.4 %fusion.135 = f32[2048,1088]{1,0:T(8,128)} fusion(bf16[2048,1604]{0,1:T(8,128)(2,1)S(1)} %fusion.9, bf16[1604,1088]{1,0:T(8,128)(2,1)S(1)} %copy-done.58), kind=kOutput, calls=%fused_computation.330 | convolution fusion | flops 7148142592 | bytes 18973184 | tf_op jit(solution)/shard_map/dot_general | solution.py:977
  538.4 53.1 %return_final.1 = bf16[4,64,1088]{2,1,0:T(8,128)(2,1)} custom-call(f32[32,64,1088]{2,1,0:T(8,128)} %bitcast.245), custom_call_target="tpu_custom_call" | custom-call | tf_op jit(solution)/shard_map/return_final/pallas_call | solution.py:168
  596.2 10.0 convolution_convert_fusion.2
  610.5 9.0 convert_reduce_fusion
  619.5 9.0 multiply_reduce_fusion.3
  632.9 47.6 %attend_back.2 = (bf16[256,1152]{1,0:T(8,128)(2,1)}, bf16[512,1152]{1,0:T(8,128)(2,1)}) custom-call(bf16[256,1152]{1,0:T(8,128)(2,1)} %copy-done.11, bf16[4,512,1152]{2,1,0:T(8,128)(2,1)} %get-tuple-element.288.kv_ref, bf16[256,1152]{1,0:T(8,128)(2,1)} %pad.44.grad_ref, f32[9,2,256]{2,1,0:T(2,128)} %copy-done.31, s32[1024,1]{1,0:T(8,128)} %copy-done.12, ...), custom_call_target="tpu_custom_call" | custom-call | flops 3019898880 | bytes 14155776 | tf_op jit(solution)/shard_map/attend_back/pallas_call | solution.py:923
  687.9 7.0 multiply_reduce_fusion.4
  697.3 9.3 convert_reduce_fusion.1
  715.3 9.0 convolution_convert_fusion.1
  725.1 9.0 multiply_reduce_fusion.5
  747.0 14.0 %fusion.136 = f32[1604,1088]{0,1:T(8,128)} fusion(bf16[2048,1604]{0,1:T(8,128)(2,1)} %copy-done.50, bf16[2048,1088]{1,0:T(8,128)(2,1)} %bitcast.261), kind=kOutput, calls=%fused_computation.331 | convolution fusion | flops 7148142592 | bytes 18007040 | tf_op jit(solution)/shard_map/dot_general | solution.py:971
  761.0 44.2 %attend_back.3 = (bf16[256,1152]{1,0:T(8,128)(2,1)}, bf16[512,1152]{1,0:T(8,128)(2,1)}) custom-call(bf16[256,1152]{1,0:T(8,128)(2,1)} %copy-done.10, bf16[4,512,1152]{2,1,0:T(8,128)(2,1)} %get-tuple-element.287.kv_ref, bf16[256,1152]{1,0:T(8,128)(2,1)} %pad.45.grad_ref, f32[9,2,256]{2,1,0:T(2,128)} %copy-done.30, s32[1024,1]{1,0:T(8,128)} %copy-done.12, ...), custom_call_target="tpu_custom_call" | custom-call | flops 3019898880 | bytes 14155776 | tf_op jit(solution)/shard_map/attend_back/pallas_call | solution.py:923
  812.7 7.0 multiply_reduce_fusion.6
  830.9 15.6 %trade_rows.1 = (bf16[3,544,512]{2,1,0:T(8,128)(2,1)S(1)}, bf16[1,544,512]{2,1,0:T(8,128)(2,1)S(1)}, bf16[4,544,512]{2,1,0:T(8,128)(2,1)}, bf16[4,544,512]{2,1,0...) custom-call(bf16[3,2,544,256]{3,2,1,0:T(8,128)(2,1)} %bitcast.256, ...), custom_call_target="tpu_custom_call" | custom-call | tf_op jit(solution)/shard_map/trade_rows/pallas_call | solution.py:654
  883.6 210.2 %close_rows.1 = (f32[136,1088]{1,0:T(8,128)}, f32[136,1088]{1,0:T(8,128)}, f32[136,1088]{1,0:T(8,128)}, f32[136,1088]{1,0:T(8,128)}, bf16[32,32,1088]{2,1,0:T(8,...) custom-call(bf16[16,136,1088]{2,1,0:T(8,128)(2,1)} %bitcast.241, bf16[16,136,1088]{2,1,0:T(8,128)(2,1)} %bitcast.257, ...), custom_call_target="tpu_custom_call" | custom-call | tf_op jit(solution)/shard_map/close_rows/pallas_call | solution.py:168
  1094.9 13.5 %fusion.12 = f32[1604,1088]{0,1:T(8,128)} fusion(f32[1604,1088]{0,1:T(8,128)} %fusion.136, s32[1856]{0:T(1024)S(1)} %copy-done.124, bf16[32,1088]{1,0:T(8,128)(2,1)S(1)} %subtract_convert_fusion, bf16[32,1088]{1,0:T(8,128)(2,1)S(1)} %pad_convert_fusion, bf16[1024,1088]{1,0:T(8,128)(2,1)} %bitcast.290, bf16[768,1088]{1,0:T(8,128)(2,1)} %bitcast.293), kind=kOutput, calls=%fused_computation.44 | convolution fusion | flops 6498880512 | bytes 18007296 | tf_op jit(solution)/shard_map/dot_general | solution.py:977
  1120.6 10.2 share_norm.1
  1136.4 6.8 multiply_subtract_fusion.1
  1143.2 19.2 %multiply_subtract_fusion = (f32[1604,1088]{0,1:T(8,128)}, f32[1604,1088]{0,1:T(8,128)}, f32[1604,1088]{0,1:T(8,128)}) fusion(f32[1604,1088]{0,1:T(8,128)} %param.25, f32[1604]{0:T(1024)S(1)} %copy-done.93, f32[]{:T(128)} %bitcast.72, f32[]{:T(128)} %bitcast.71, f32[1604]{0:T(1024)S(1)} %copy-done.94, f32[1604,1088]{0,1:T(8,128)} %get-tuple-element.650, ...), kind=kLoop, calls=%fused_computation.58 | loop fusion | flops 27922432 | bytes 48877100 | tf_op jit(solution)/shard_map/sub | solution.py:1102
  (436 shorter events, 178.1 us)
Async XLA Ops:
  7.2 256.6 %all-gather.5.cloned.1.call-start = ((), (), s32[]{:S(2)}) async-start(), calls=%async_computation.2 | async-start | bytes 31021056 | tf_op jit(solution)/shard_map/all_gather | solution.py:1183
  10.5 412.8 %all-gather.7.cloned.1.call-start = ((), (), s32[]{:S(2)}) async-start(), calls=%async_computation.3 | async-start | bytes 20680704 | tf_op jit(solution)/shard_map/all_gather | solution.py:1186
  11.5 749.5 %reduce-scatter.7.cloned.1.call-start = ((), (), s32[]{:S(2)}) async-start(), calls=%async_computation.4 | async-start | bytes 10340352
  248.7 88.2 %copy-start.12 = (s32[1024,1]{1,0:T(8,128)}, s32[1024,1]{1,0:T(8,128)S(1)}, u32[]{:S(2)}) copy-start(s32[1024,1]{1,0:T(8,128)S(1)} %copy.94.key_ids_ref) | copy-start | bytes 12292
  257.3 79.6 %copy-start.13 = (s32[1,256]{1,0:T(1,128)}, s32[1,256]{1,0:T(1,128)S(1)}, u32[]{:S(2)}) copy-start(s32[1,256]{1,0:T(1,128)S(1)} %constant_dynamic-slice_fusion.query_ids_ref) | copy-start | bytes 3076
  258.5 56.1 %copy-start.82 = (f32[1088]{0:T(1024)}, f32[1088]{0:T(1024)S(1)}, u32[]{:S(2)}) copy-start(f32[1088]{0:T(1024)S(1)} %get-tuple-element.351) | copy-start | bytes 13060
  258.5 164.8 %copy-start.91 = (f32[1088]{0:T(1024)}, f32[1088]{0:T(1024)S(1)}, u32[]{:S(2)}) copy-start(f32[1088]{0:T(1024)S(1)} %get-tuple-element.342) | copy-start | bytes 13060
  269.9 41.5 %copy-start.10 = (bf16[256,1152]{1,0:T(8,128)(2,1)}, bf16[256,1152]{1,0:T(8,128)(2,1)S(1)}, u32[]{:S(2)}) copy-start(bf16[256,1152]{1,0:T(8,128)(2,1)S(1)} %pad.38.q_ref) | copy-start | bytes 1769476
  270.0 41.5 %copy-start.36 = (f32[256,1088]{1,0:T(8,128)S(1)}, f32[256,1088]{1,0:T(8,128)}, u32[]{:S(2)}) copy-start(f32[256,1088]{1,0:T(8,128)} %copy-done.35) | copy-start | bytes 3342340
  333.1 64.3 %copy-start.44 = (f32[256,1088]{1,0:T(8,128)}, f32[256,1088]{1,0:T(8,128)S(1)}, u32[]{:S(2)}) copy-start(f32[256,1088]{1,0:T(8,128)S(1)} %get-tuple-element.444) | copy-start | bytes 3342340
  336.8 60.7 %copy-start.11 = (bf16[256,1152]{1,0:T(8,128)(2,1)}, bf16[256,1152]{1,0:T(8,128)(2,1)S(1)}, u32[]{:S(2)}) copy-start(bf16[256,1152]{1,0:T(8,128)(2,1)S(1)} %pad.41.q_ref) | copy-start | bytes 1769476
  336.9 60.6 %copy-start.61 = (bf16[8,136,1088]{2,1,0:T(8,128)(2,1)S(1)}, bf16[8,136,1088]{2,1,0:T(8,128)(2,1)}, u32[]{:S(2)}) copy-start(bf16[8,136,1088]{2,1,0:T(8,128)(2,1)} %slice.255) | copy-start | bytes 7102468
  397.5 25.9 %copy-start.95 = (f32[4352]{0:T(1024)S(1)}, f32[4352]{0:T(1024)}, u32[]{:S(2)}) copy-start(f32[4352]{0:T(1024)} %add.573) | copy-start | bytes 52228
  398.6 30.9 %copy-start.48 = (f32[256,1088]{1,0:T(8,128)}, f32[256,1088]{1,0:T(8,128)S(1)}, u32[]{:S(2)}) copy-start(f32[256,1088]{1,0:T(8,128)S(1)} %get-tuple-element.446) | copy-start | bytes 3342340
  398.6 230.0 %copy-start.105 = (f32[256]{0:T(256)}, f32[256]{0:T(256)S(1)}, u32[]{:S(2)}) copy-start(f32[256]{0:T(256)S(1)} %broadcast_multiply_fusion.2) | copy-start | bytes 3076
  398.9 229.7 %copy-start.122 = (f32[256]{0:T(256)}, f32[256]{0:T(256)S(1)}, u32[]{:S(2)}) copy-start(f32[256]{0:T(256)S(1)} %fusion.110) | copy-start | bytes 3076
  440.5 47.5 %copy-start.97 = (pred[1604]{0:T(1024)(128)(4,1)S(1)}, pred[1604]{0:T(1024)(128)(4,1)}, u32[]{:S(2)}) copy-start(pred[1604]{0:T(1024)(128)(4,1)} %fusion.101) | copy-start | bytes 4816
  488.0 12.4 %copy-start.88 = (s32[2048]{0:T(1024)S(1)}, s32[2048]{0:T(1024)}, u32[]{:S(2)}) copy-start(s32[2048]{0:T(1024)} %param.20) | copy-start | bytes 24580
  526.0 12.4 %copy-start.50 = (bf16[2048,1604]{0,1:T(8,128)(2,1)}, bf16[2048,1604]{0,1:T(8,128)(2,1)S(1)}, u32[]{:S(2)}) copy-start(bf16[2048,1604]{0,1:T(8,128)(2,1)S(1)} %fusion.9) | copy-start | bytes 19709956
  606.2 277.4 %reduce-scatter.9.cloned.1.call-start = ((), (), s32[]{:S(2)}) async-start(), calls=%async_computation.5 | async-start | bytes 10340352
  694.9 11.7 slice-start.2
  830.9 24.7 %copy-start.60 = (bf16[512,1152]{1,0:T(8,128)(2,1)S(1)}, bf16[512,1152]{1,0:T(8,128)(2,1)}, u32[]{:S(2)}) copy-start(bf16[512,1152]{1,0:T(8,128)(2,1)} %get-tuple-element.295) | copy-start | bytes 3538948
  830.9 24.7 %copy-start.65 = (bf16[256,1152]{1,0:T(8,128)(2,1)S(1)}, bf16[256,1152]{1,0:T(8,128)(2,1)}, u32[]{:S(2)}) copy-start(bf16[256,1152]{1,0:T(8,128)(2,1)} %get-tuple-element.294) | copy-start | bytes 1769476
  830.9 24.9 %copy-start.89 = (f32[1088]{0:T(1024)S(1)}, f32[1088]{0:T(1024)}, u32[]{:S(2)}) copy-start(f32[1088]{0:T(1024)} %get-tuple-element.324) | copy-start | bytes 13060
  830.9 24.9 %copy-start.90 = (f32[1088]{0:T(1024)S(1)}, f32[1088]{0:T(1024)}, u32[]{:S(2)}) copy-start(f32[1088]{0:T(1024)} %get-tuple-element.334) | copy-start | bytes 13060
  883.6 211.3 %copy-start.124 = (s32[1856]{0:T(1024)S(1)}, s32[1856]{0:T(1024)}, u32[]{:S(2)}) copy-start(s32[1856]{0:T(1024)} %concatenate.48) | copy-start | bytes 22276
  1094.9 13.5 %copy-start.33 = (bf16[256,1088]{1,0:T(8,128)(2,1)S(1)}, bf16[256,1088]{1,0:T(8,128)(2,1)}, u32[]{:S(2)}) copy-start(bf16[256,1088]{1,0:T(8,128)(2,1)} %copy-done.32) | copy-start | bytes 1671172
  1094.9 13.5 %copy-start.54 = (s32[32,256]{1,0:T(8,128)S(1)}, s32[32,256]{1,0:T(8,128)}, u32[]{:S(2)}) copy-start(s32[32,256]{1,0:T(8,128)} %copy-done.53) | copy-start | bytes 98308
  1094.9 13.5 %copy-start.56 = (s32[32,256]{1,0:T(8,128)S(1)}, s32[32,256]{1,0:T(8,128)}, u32[]{:S(2)}) copy-start(s32[32,256]{1,0:T(8,128)} %copy-done.55) | copy-start | bytes 98308
  1094.9 13.5 %copy-start.67 = (pred[32,256]{1,0:T(32,128)(4,1)S(1)}, pred[32,256]{1,0:T(32,128)(4,1)}, u32[]{:S(2)}) copy-start(pred[32,256]{1,0:T(32,128)(4,1)} %copy-done.66) | copy-start | bytes 24580
  1094.9 13.5 %copy-start.77 = (s32[256]{0:T(256)S(1)}, s32[256]{0:T(256)}, u32[]{:S(2)}) copy-start(s32[256]{0:T(256)} %copy-done.76) | copy-start | bytes 3076
  1094.9 13.5 %copy-start.79 = (s32[256]{0:T(256)S(1)}, s32[256]{0:T(256)}, u32[]{:S(2)}) copy-start(s32[256]{0:T(256)} %copy-done.78) | copy-start | bytes 3076
  (108 other events, 454.9 us)
Sparse Core Ops, SparseCore 0:
  11.6 252.1 all-gather.4
  266.8 156.4 all-gather.6
  606.3 137.1 reduce-scatter.6
  749.4 134.1 reduce-scatter.8

commit v8 on v7

--- a/solution.py
+++ b/solution.py
@@ -455,7 +455,7 @@
 
 def mats_stream(x_ref, o_ref, scratch, sems, m, span, order, weights):
     kept, work, parcel, recv = scratch
-    turn, m = m % 2, m % work.shape[0]
+    which, turn, m = m, m % 2, m % work.shape[0]
     steps = len(order)
     rows = pl.ds(*span)
     slot = 0
@@ -517,7 +517,7 @@
                 return carry
 
             lax.fori_loop(0, size, add, 0)
-    o_ref[rows] = work[m, sum(bit_here(b) * small[b] for b in order[1:]), rows]
+    o_ref[which, rows] = work[m, sum(bit_here(b) * small[b] for b in order[1:]), rows]
 
 
 def mats_job(mats):
@@ -538,15 +538,16 @@
     count = len(mats)
 
     def steps(x_refs, o_refs, scratch, sems):
+        o_ref = o_refs[0]
         return [
-            (m, mats_stream(x_refs[m], o_refs[m], scratch, sems, m, spans[k], orders[k], weights))
+            (m, mats_stream(x_refs[m], o_ref, scratch, sems, m, spans[k], orders[k], weights))
             for m in range(count)
             for k in range(len(orders))
         ]
 
     return Job(
         mats,
-        [jax.ShapeDtypeStruct((rows, width), jnp.float32)] * count,
+        [jax.ShapeDtypeStruct((count, rows, width), jnp.float32)],
         [
             pltpu.VMEM((min(2, count), blocks // 2, rows, width), jnp.bfloat16),
             pltpu.VMEM((min(3, count), blocks // 2, rows, width), jnp.float32),
@@ -1016,6 +1017,10 @@
     return with_layout_constraint(x, Layout(major_to_minor=tuple(range(x.ndim))))
 
 
+def turned(x):
+    return with_layout_constraint(x, Layout(major_to_minor=(1, 0)))
+
+
 def scatter_rows(groups):
     total = lax.axis_size(AXES)
     mats = []
@@ -1040,8 +1045,8 @@
     attended = attended[:, :width]
     mid_state = state + dot_plain(attended, weights[0][3 * width :]) + params[4 : 5]
     normed = layer_norm(mid_state, params[5 : 6], params[6 : 7]).astype(jnp.bfloat16)
-    upward = dot_rows(normed, weights[1]) + params[8:12].reshape(1, -1)
-    active = jax.nn.gelu(upward, approximate=True).astype(jnp.bfloat16)
+    upward = turned(dot_rows(normed, weights[1]) + params[8:12].reshape(1, -1))
+    active = turned(jax.nn.gelu(upward, approximate=True).astype(jnp.bfloat16))
     output = mid_state + dot_plain(active, weights[2]) + params[7 : 8]
     return (
         output,
@@ -1055,7 +1060,7 @@
     down_grad = grad_in.astype(jnp.bfloat16)
     act_grad = dot_rows(down_grad, weights[2])
     unused_gelu, gelu_pull = jax.vjp(partial(jax.nn.gelu, approximate=True), upward)
-    up_grad = gelu_pull(act_grad)[0].astype(jnp.bfloat16)
+    up_grad = turned(gelu_pull(act_grad)[0].astype(jnp.bfloat16))
     mid_back, gain_two, shift_two = norm_back(
         mid_state, params[5 : 6], params[6 : 7], rows_major(dot_plain(up_grad, weights[1]))
     )
@@ -1325,7 +1330,7 @@
     late, arrived[1] = lax.optimization_barrier((late, arrived[1]))
     upper = jnp.concatenate([arrived[1], arrived[0]], 0).astype(jnp.float32)
     fits = mats_fit(late)
-    own_mats, (place_grad,), (small_grad,), (came,) = run_jobs(
+    (own_mats,), (place_grad,), (small_grad,), (came,) = run_jobs(
         [
             mats_job(late[:fits]),
             sum_job(
@@ -1343,8 +1348,8 @@
         61,
     )
     for k in range(fits, len(late), fits):
-        more = run_jobs([mats_job(late[k : k + fits])], "sum_mats", 14 + k, 61)[0]
-        own_mats = list(own_mats) + list(lax.optimization_barrier(tuple(more)))
+        more = run_jobs([mats_job(late[k : k + fits])], "sum_mats", 14 + k, 61)[0][0]
+        own_mats = jnp.concatenate([own_mats, lax.optimization_barrier(more)], 0)
     place_grad = place_grad.reshape(seq_length, width)
     small_grad = pad_rows(small_grad.reshape(-1)[:small_size].reshape(-1, width), small_rows)
     small_high = small_grad.astype(jnp.bfloat16)
@@ -1358,7 +1363,7 @@
         return held + dot_plain(one_hot(asked_rows(at), table_local, 0), rows)
 
     table_grad = lax.fori_loop(1, rounds, return_more, table_grad)
-    mats_grad = jnp.concatenate([jnp.stack(own_mats), upper], 0).reshape(layer_mats.shape)
+    mats_grad = jnp.concatenate([own_mats, upper], 0).reshape(layer_mats.shape)
     local_squares = jnp.sum(mats_grad * mats_grad) + jnp.sum(table_grad * table_grad)
     squares = jnp.full((8, 128), local_squares)
     squares = run_jobs([spread_job(squares, True)], "share_norm", 11, 16)[0][0]

time: 1180 us -> 1180 us (level)
  waiting for transfers between devices: 28.9 us -> 45 us
  local copies, waits for them, and re-layouts: 81.2 us -> 69 us
    optimization_barrier x1, waiting for transfers between devices: 2.27 us -> 17.2 us  [on_device(): late, arrived[1] = lax.optimization_barrier((late, arrived[1]))]
    unnamed x277 -> x265, local copies, waits for them, and re-layouts: 32.2 us -> 28.3 us
  transfers between devices with their start and end apart: 4 -> 4, of which waited for: 3 -> 3; matrix products, arithmetic and copies ran while one was open for 19% -> 18% of each run, Pallas kernels for 36% -> 36%
where the time goes in v8:
time: 1180 us; the launch traced here: 1170 us
  Pallas kernels  753 us (64%)
  matrix products  203 us (17%)
  other arithmetic  74.6 us (6%)
  local copies, waits for them, and re-layouts  69 us (6%)
  waiting for transfers between devices  45 us (4%)
  between operations  22.4 us (2%)
    pallas_call x7, Pallas kernels, run_jobs(): pl.pallas_call(partial(jobs_kernel, jobs), out_shape=outputs, in_specs=in...  544 us
    dot_general x21, matrix products, dot_plain(): return jnp.dot(left_op, right_op, preferred_element_type=jnp.float32)  110 us
    pallas_call x2, Pallas kernels, attend(): pl.pallas_call(attend_kernel, out_shape=(jax.ShapeDtypeStruct((rows, widt...  102 us
    pallas_call x2, Pallas kernels, attend_back(): pl.pallas_call(attend_back_kernel, out_shape=(jax.ShapeDtypeStruct((rows,...  90.6 us
    dot_general x9, matrix products, dot_rows(): lax.dot_general(left_op, right_op, (((1,), (1,)), ((), ())), preferred_el...  58.3 us
    dot_general x5, matrix products, dot_cols(): lax.dot_general(left_op, right_op, (((0,), (0,)), ((), ())), preferred_el...  34.4 us
    unnamed x265, local copies, waits for them, and re-layouts  28.3 us
    sub x2, other arithmetic, adam_step(): weights - rate * (moment_hat / (jnp.sqrt(square_hat) + ADAM_EPS) + decay...  25.9 us
  transfers between devices with their start and end apart: 4, of which 3 were waited for; matrix products, arithmetic and copies ran while one was open for 18% of the time, Pallas kernels for 36%

profile of v8, /device:TPU:0, one launch (start us, length us, event | category | flops | bytes accessed | tf_op | source)
XLA Modules:
  0.0 1167.4 jit_solution(12036319794427172191)
XLA Ops:
  11.6 12.5 %share_ids.1 = s32[32,8,128]{2,1,0:T(8,128)S(1)} custom-call(s32[8,128]{1,0:T(8,128)S(1)} %pad_bitcast_fusion.1.refs_0_), custom_call_target="tpu_custom_call" | custom-call | tf_op jit(solution)/shard_map/share_ids/pallas_call | solution.py:168
  27.0 6.9 copy.96
  33.9 11.3 fusion.21
  45.6 196.1 %open_rows.1 = (bf16[32,136,1088]{2,1,0:T(8,128)(2,1)S(1)}, bf16[8,32,1088]{2,1,0:T(8,128)(2,1)S(1)}, bf16[32,1088]{1,0:T(8,128)(2,1)S(1)}, bf16[32,24,1088]{2,1,0:T(8,128)(2,1)S(1)}) custom-call(bf16[136,1088]{1,0:T(8,128)(2,1)S(1)} %slice_bitcast_fusion.36.refs_0_, bf16[32,32,1088]{2,1,0:T(8,128)(2,1)S(1)} %bitcast.208, ...), custom_call_target="tpu_custom_call" | custom-call | tf_op jit(solution)/shard_map/open_rows/pallas_call | solution.py:168
  270.0 41.8 %attend.2 = (bf16[256,1152]{1,0:T(8,128)(2,1)S(1)}, f32[9,2,256]{2,1,0:T(2,128)S(1)}, bf16[4,512,1152]{2,1,0:T(8,128)(2,1)}) custom-call(bf16[256,1152]{1,0:T(8,128)(2,1)S(1)} %pad.38.q_ref, bf16[512,1152]{1,0:T(8,128)(2,1)S(1)} %fusion.63.own_ref, s32[1024,1]{1,0:T(8,128)S(1)} %copy.100.key_ids_ref, s32[1,256]{1,0:T(1,128)S(1)} %constant_dynamic-slice_fusion.query_ids_ref), custom_call_target="tpu_custom_call" | custom-call | flops 1207959552 | bytes 4718592 | tf_op jit(solution)/shard_map/attend/pallas_call | solution.py:797
  315.4 8.0 multiply_convert_fusion.1
  323.4 7.9 fusion.112
  335.1 60.4 %attend.3 = (bf16[256,1152]{1,0:T(8,128)(2,1)S(1)}, f32[9,2,256]{2,1,0:T(2,128)S(1)}, bf16[4,512,1152]{2,1,0:T(8,128)(2,1)}) custom-call(bf16[256,1152]{1,0:T(8,128)(2,1)S(1)} %pad.41.q_ref, bf16[512,1152]{1,0:T(8,128)(2,1)S(1)} %fusion.64.own_ref, s32[1024,1]{1,0:T(8,128)S(1)} %copy.100.key_ids_ref, s32[1,256]{1,0:T(1,128)S(1)} %constant_dynamic-slice_fusion.query_ids_ref), custom_call_target="tpu_custom_call" | custom-call | flops 1207959552 | bytes 4718592 | tf_op jit(solution)/shard_map/attend/pallas_call | solution.py:797
  397.0 24.9 %all-gather.7.cloned.1.call-done = bf16[1,2,4352,1088]{3,2,1,0:T(8,128)(2,1)} async-done(((bf16[1,2,136,1088]{3,2,1,0:T(8,128)(2,1)}), bf16[1,2,4352,1088]{3,2,1,0:T(8,128)(2,1)}) %all-gather.7.cloned.1.call-update) | async-done | bytes 18939920 | tf_op jit(solution)/shard_map/all_gather | solution.py:1191
  428.5 9.0 fusion.114
  439.4 47.4 %share_final.1 = bf16[32,64,1088]{2,1,0:T(8,128)(2,1)} custom-call(bf16[4,64,1088]{2,1,0:T(8,128)(2,1)} %bitcast.240), custom_call_target="tpu_custom_call" | custom-call | tf_op jit(solution)/shard_map/share_final/pallas_call | solution.py:168
  486.8 12.3 %select_reduce_fusion.3 = (f32[2048]{0:T(1024)S(1)}, f32[2048,1604]{0,1:T(8,128)S(1)}) fusion(pred[1604]{0:T(1024)(128)(4,1)S(1)} %copy-done.96, bf16[2048,1088]{1,0:T(8,128)(2,1)} %bitcast.233, bf16[1604,1088]{1,0:T(8,128)(2,1)} %get-tuple-element.660), kind=kOutput, calls=%fused_computation.36 | convolution fusion | flops 7154710528 | bytes 21096516 | tf_op jit(solution)/shard_map/dot_general | solution.py:966
  504.4 16.7 %share_stats.1 = f32[3,16,128]{2,1,0:T(8,128)S(1)} custom-call(f32[3,16,128]{2,1,0:T(8,128)S(1)} %pad_maximum_fusion.3.refs_0_), custom_call_target="tpu_custom_call" | custom-call | tf_op jit(solution)/shard_map/share_stats/pallas_call | solution.py:168
  526.7 12.4 %fusion.116 = f32[2048,1088]{1,0:T(8,128)} fusion(bf16[2048,1604]{0,1:T(8,128)(2,1)S(1)} %fusion.9, bf16[1604,1088]{1,0:T(8,128)(2,1)S(1)} %copy-done.59), kind=kOutput, calls=%fused_computation.303 | convolution fusion | flops 7148142592 | bytes 18973184 | tf_op jit(solution)/shard_map/dot_general | solution.py:978
  539.1 50.9 %return_final.1 = bf16[4,64,1088]{2,1,0:T(8,128)(2,1)} custom-call(f32[32,64,1088]{2,1,0:T(8,128)} %bitcast.220), custom_call_target="tpu_custom_call" | custom-call | tf_op jit(solution)/shard_map/return_final/pallas_call | solution.py:168
  594.6 10.0 convolution_convert_fusion.2
  608.9 10.0 convert_reduce_fusion
  618.9 9.2 multiply_reduce_fusion.3
  632.5 50.3 %attend_back.2 = (bf16[256,1152]{1,0:T(8,128)(2,1)}, bf16[512,1152]{1,0:T(8,128)(2,1)}) custom-call(bf16[256,1152]{1,0:T(8,128)(2,1)} %copy-done.11, bf16[4,512,1152]{2,1,0:T(8,128)(2,1)} %get-tuple-element.285.kv_ref, bf16[256,1152]{1,0:T(8,128)(2,1)} %pad.44.grad_ref, f32[9,2,256]{2,1,0:T(2,128)} %copy-done.31, s32[1024,1]{1,0:T(8,128)} %copy-done.12, ...), custom_call_target="tpu_custom_call" | custom-call | flops 3019898880 | bytes 14155776 | tf_op jit(solution)/shard_map/attend_back/pallas_call | solution.py:924
  690.7 6.8 multiply_reduce_fusion.4
  707.7 9.4 convert_reduce_fusion.1
  717.2 8.6 multiply_reduce_fusion.5
  734.3 14.4 %fusion.117 = f32[1604,1088]{0,1:T(8,128)} fusion(bf16[2048,1604]{0,1:T(8,128)(2,1)} %copy-done.50, bf16[2048,1088]{1,0:T(8,128)(2,1)} %bitcast.234), kind=kOutput, calls=%fused_computation.304 | convolution fusion | flops 7148142592 | bytes 18007040 | tf_op jit(solution)/shard_map/dot_general | solution.py:972
  748.7 40.3 %attend_back.3 = (bf16[256,1152]{1,0:T(8,128)(2,1)}, bf16[512,1152]{1,0:T(8,128)(2,1)}) custom-call(bf16[256,1152]{1,0:T(8,128)(2,1)} %copy-done.10, bf16[4,512,1152]{2,1,0:T(8,128)(2,1)} %get-tuple-element.284.kv_ref, bf16[256,1152]{1,0:T(8,128)(2,1)} %pad.45.grad_ref, f32[9,2,256]{2,1,0:T(2,128)} %copy-done.30, s32[1024,1]{1,0:T(8,128)} %copy-done.12, ...), custom_call_target="tpu_custom_call" | custom-call | flops 3019898880 | bytes 14155776 | tf_op jit(solution)/shard_map/attend_back/pallas_call | solution.py:924
  796.5 6.8 multiply_reduce_fusion.6
  814.6 15.7 %trade_rows.1 = (bf16[3,544,512]{2,1,0:T(8,128)(2,1)S(1)}, bf16[1,544,512]{2,1,0:T(8,128)(2,1)S(1)}, bf16[4,544,512]{2,1,0:T(8,128)(2,1)}, bf16[4,544,512]{2,1,0...) custom-call(bf16[3,2,544,256]{3,2,1,0:T(8,128)(2,1)} %bitcast.229, ...), custom_call_target="tpu_custom_call" | custom-call | tf_op jit(solution)/shard_map/trade_rows/pallas_call | solution.py:655
  865.5 17.2 %reduce-scatter.9.cloned.1.call-done = bf16[1,136,1088]{2,1,0:T(8,128)(2,1)} async-done(((bf16[32,136,1088]{2,1,0:T(8,128)(2,1)}), bf16[1,136,1088]{2,1,0:T(8,128)(2,1)}) %reduce-scatter.9.cloned.1.call-update) | async-done | bytes 295952 | tf_op jit(solution)/shard_map/optimization_barrier | solution.py:1330
  882.6 208.9 %close_rows.1 = (f32[4,136,1088]{2,1,0:T(8,128)}, bf16[32,32,1088]{2,1,0:T(8,128)(2,1)}, f32[224,128]{1,0:T(8,128)}, bf16[32,24,1088]{2,1,0:T(8,128)(2,1)}) custom-call(bf16[16,136,1088]{2,1,0:T(8,128)(2,1)} %bitcast.216, bf16[16,136,1088]{2,1,0:T(8,128)(2,1)} %bitcast.230, bf16[16,136,1088]{2,1,0:T(8,128)(2,1)} %bitcast.231, ...), custom_call_target="tpu_custom_call" | custom-call | tf_op jit(solution)/shard_map/close_rows/pallas_call | solution.py:168
  1092.6 13.5 %fusion.12 = f32[1604,1088]{0,1:T(8,128)} fusion(f32[1604,1088]{0,1:T(8,128)} %fusion.117, s32[1856]{0:T(1024)S(1)} %copy-done.122, bf16[32,1088]{1,0:T(8,128)(2,1)S(1)} %subtract_convert_fusion, bf16[32,1088]{1,0:T(8,128)(2,1)S(1)} %pad_convert_fusion, bf16[1024,1088]{1,0:T(8,128)(2,1)} %bitcast.263, bf16[768,1088]{1,0:T(8,128)(2,1)} %bitcast.266), kind=kOutput, calls=%fused_computation.44 | convolution fusion | flops 6498880512 | bytes 18007296 | tf_op jit(solution)/shard_map/dot_general | solution.py:978
  1115.1 11.9 %share_norm.1 = f32[8,128]{1,0:T(8,128)S(1)} custom-call(f32[8,128]{1,0:T(8,128)S(1)} %broadcast_in_dim.223.refs_0_), custom_call_target="tpu_custom_call" | custom-call | tf_op jit(solution)/shard_map/share_norm/pallas_call | solution.py:168
  1132.2 6.8 multiply_subtract_fusion.1
  1139.0 19.2 %multiply_subtract_fusion = (f32[1604,1088]{0,1:T(8,128)}, f32[1604,1088]{0,1:T(8,128)}, f32[1604,1088]{0,1:T(8,128)}) fusion(f32[1604,1088]{0,1:T(8,128)} %param.25, f32[1604]{0:T(1024)S(1)} %copy-done.92, f32[]{:T(128)} %bitcast.68, f32[]{:T(128)} %bitcast.67, f32[1604]{0:T(1024)S(1)} %copy-done.93, f32[1604,1088]{0,1:T(8,128)} %get-tuple-element.643, ...), kind=kLoop, calls=%fused_computation.58 | loop fusion | flops 27922432 | bytes 48877100 | tf_op jit(solution)/shard_map/sub | solution.py:1107
  (420 shorter events, 167.6 us)
Async XLA Ops:
  7.2 256.6 %all-gather.5.cloned.1.call-start = ((), (), s32[]{:S(2)}) async-start(), calls=%async_computation.2 | async-start | bytes 31021056 | tf_op jit(solution)/shard_map/all_gather | solution.py:1188
  10.5 411.4 %all-gather.7.cloned.1.call-start = ((), (), s32[]{:S(2)}) async-start(), calls=%async_computation.3 | async-start | bytes 20680704 | tf_op jit(solution)/shard_map/all_gather | solution.py:1191
  11.5 737.2 %reduce-scatter.7.cloned.1.call-start = ((), (), s32[]{:S(2)}) async-start(), calls=%async_computation.4 | async-start | bytes 10340352
  33.9 11.3 copy-start.83
  248.7 86.4 %copy-start.12 = (s32[1024,1]{1,0:T(8,128)}, s32[1024,1]{1,0:T(8,128)S(1)}, u32[]{:S(2)}) copy-start(s32[1024,1]{1,0:T(8,128)S(1)} %copy.100.key_ids_ref) | copy-start | bytes 12292
  257.2 77.9 %copy-start.13 = (s32[1,256]{1,0:T(1,128)}, s32[1,256]{1,0:T(1,128)S(1)}, u32[]{:S(2)}) copy-start(s32[1,256]{1,0:T(1,128)S(1)} %constant_dynamic-slice_fusion.query_ids_ref) | copy-start | bytes 3076
  258.4 56.5 %copy-start.81 = (f32[1088]{0:T(1024)}, f32[1088]{0:T(1024)S(1)}, u32[]{:S(2)}) copy-start(f32[1088]{0:T(1024)S(1)} %get-tuple-element.345) | copy-start | bytes 13060
  258.4 163.6 %copy-start.90 = (f32[1088]{0:T(1024)}, f32[1088]{0:T(1024)S(1)}, u32[]{:S(2)}) copy-start(f32[1088]{0:T(1024)S(1)} %get-tuple-element.336) | copy-start | bytes 13060
  269.9 41.9 %copy-start.10 = (bf16[256,1152]{1,0:T(8,128)(2,1)}, bf16[256,1152]{1,0:T(8,128)(2,1)S(1)}, u32[]{:S(2)}) copy-start(bf16[256,1152]{1,0:T(8,128)(2,1)S(1)} %pad.38.q_ref) | copy-start | bytes 1769476
  270.0 41.8 %copy-start.36 = (f32[256,1088]{1,0:T(8,128)S(1)}, f32[256,1088]{1,0:T(8,128)}, u32[]{:S(2)}) copy-start(f32[256,1088]{1,0:T(8,128)} %copy-done.35) | copy-start | bytes 3342340
  331.3 64.2 %copy-start.43 = (f32[256,1088]{1,0:T(8,128)}, f32[256,1088]{1,0:T(8,128)S(1)}, u32[]{:S(2)}) copy-start(f32[256,1088]{1,0:T(8,128)S(1)} %get-tuple-element.436) | copy-start | bytes 3342340
  335.0 60.6 %copy-start.11 = (bf16[256,1152]{1,0:T(8,128)(2,1)}, bf16[256,1152]{1,0:T(8,128)(2,1)S(1)}, u32[]{:S(2)}) copy-start(bf16[256,1152]{1,0:T(8,128)(2,1)S(1)} %pad.41.q_ref) | copy-start | bytes 1769476
  335.1 60.5 %copy-start.62 = (bf16[8,136,1088]{2,1,0:T(8,128)(2,1)S(1)}, bf16[8,136,1088]{2,1,0:T(8,128)(2,1)}, u32[]{:S(2)}) copy-start(bf16[8,136,1088]{2,1,0:T(8,128)(2,1)} %slice.255) | copy-start | bytes 7102468
  395.6 26.4 %copy-start.94 = (f32[4352]{0:T(1024)S(1)}, f32[4352]{0:T(1024)}, u32[]{:S(2)}) copy-start(f32[4352]{0:T(1024)} %add.560) | copy-start | bytes 52228
  396.7 31.8 %copy-start.46 = (f32[256,1088]{1,0:T(8,128)}, f32[256,1088]{1,0:T(8,128)S(1)}, u32[]{:S(2)}) copy-start(f32[256,1088]{1,0:T(8,128)S(1)} %get-tuple-element.438) | copy-start | bytes 3342340
  396.7 231.5 %copy-start.104 = (f32[256]{0:T(256)}, f32[256]{0:T(256)S(1)}, u32[]{:S(2)}) copy-start(f32[256]{0:T(256)S(1)} %broadcast_multiply_fusion.1) | copy-start | bytes 3076
  397.0 231.2 %copy-start.120 = (f32[256]{0:T(256)}, f32[256]{0:T(256)S(1)}, u32[]{:S(2)}) copy-start(f32[256]{0:T(256)S(1)} %fusion.96) | copy-start | bytes 3076
  439.4 47.4 %copy-start.96 = (pred[1604]{0:T(1024)(128)(4,1)S(1)}, pred[1604]{0:T(1024)(128)(4,1)}, u32[]{:S(2)}) copy-start(pred[1604]{0:T(1024)(128)(4,1)} %fusion.87) | copy-start | bytes 4816
  486.8 12.4 %copy-start.87 = (s32[2048]{0:T(1024)S(1)}, s32[2048]{0:T(1024)}, u32[]{:S(2)}) copy-start(s32[2048]{0:T(1024)} %param.20) | copy-start | bytes 24580
  526.7 12.4 %copy-start.50 = (bf16[2048,1604]{0,1:T(8,128)(2,1)}, bf16[2048,1604]{0,1:T(8,128)(2,1)S(1)}, u32[]{:S(2)}) copy-start(bf16[2048,1604]{0,1:T(8,128)(2,1)S(1)} %fusion.9) | copy-start | bytes 19709956
  604.6 278.0 %reduce-scatter.9.cloned.1.call-start = ((), (), s32[]{:S(2)}) async-start(), calls=%async_computation.5 | async-start | bytes 10340352
  814.6 24.8 %copy-start.61 = (bf16[512,1152]{1,0:T(8,128)(2,1)S(1)}, bf16[512,1152]{1,0:T(8,128)(2,1)}, u32[]{:S(2)}) copy-start(bf16[512,1152]{1,0:T(8,128)(2,1)} %get-tuple-element.292) | copy-start | bytes 3538948
  814.6 24.8 %copy-start.66 = (bf16[256,1152]{1,0:T(8,128)(2,1)S(1)}, bf16[256,1152]{1,0:T(8,128)(2,1)}, u32[]{:S(2)}) copy-start(bf16[256,1152]{1,0:T(8,128)(2,1)} %get-tuple-element.291) | copy-start | bytes 1769476
  814.6 25.0 %copy-start.88 = (f32[1088]{0:T(1024)S(1)}, f32[1088]{0:T(1024)}, u32[]{:S(2)}) copy-start(f32[1088]{0:T(1024)} %get-tuple-element.318) | copy-start | bytes 13060
  814.6 25.0 %copy-start.89 = (f32[1088]{0:T(1024)S(1)}, f32[1088]{0:T(1024)}, u32[]{:S(2)}) copy-start(f32[1088]{0:T(1024)} %get-tuple-element.328) | copy-start | bytes 13060
  882.6 209.9 %copy-start.122 = (s32[1856]{0:T(1024)S(1)}, s32[1856]{0:T(1024)}, u32[]{:S(2)}) copy-start(s32[1856]{0:T(1024)} %concatenate.48) | copy-start | bytes 22276
  1092.6 13.5 %copy-start.33 = (bf16[256,1088]{1,0:T(8,128)(2,1)S(1)}, bf16[256,1088]{1,0:T(8,128)(2,1)}, u32[]{:S(2)}) copy-start(bf16[256,1088]{1,0:T(8,128)(2,1)} %copy-done.32) | copy-start | bytes 1671172
  1092.6 13.5 %copy-start.55 = (s32[32,256]{1,0:T(8,128)S(1)}, s32[32,256]{1,0:T(8,128)}, u32[]{:S(2)}) copy-start(s32[32,256]{1,0:T(8,128)} %copy-done.54) | copy-start | bytes 98308
  1092.6 13.5 %copy-start.57 = (s32[32,256]{1,0:T(8,128)S(1)}, s32[32,256]{1,0:T(8,128)}, u32[]{:S(2)}) copy-start(s32[32,256]{1,0:T(8,128)} %copy-done.56) | copy-start | bytes 98308
  1092.6 13.5 %copy-start.70 = (pred[32,256]{1,0:T(32,128)(4,1)S(1)}, pred[32,256]{1,0:T(32,128)(4,1)}, u32[]{:S(2)}) copy-start(pred[32,256]{1,0:T(32,128)(4,1)} %copy-done.69) | copy-start | bytes 24580
  1092.6 13.5 %copy-start.76 = (s32[256]{0:T(256)S(1)}, s32[256]{0:T(256)}, u32[]{:S(2)}) copy-start(s32[256]{0:T(256)} %copy-done.75) | copy-start | bytes 3076
  1092.6 13.5 %copy-start.78 = (s32[256]{0:T(256)S(1)}, s32[256]{0:T(256)}, u32[]{:S(2)}) copy-start(s32[256]{0:T(256)} %copy-done.77) | copy-start | bytes 3076
  (104 other events, 442.6 us)
Sparse Core Ops, SparseCore 0:
  11.6 252.1 all-gather.4
  266.8 155.0 all-gather.6
  604.8 139.0 reduce-scatter.6
  749.8 132.7 reduce-scatter.8

commit v9 on v8

--- a/solution.py
+++ b/solution.py
@@ -1327,8 +1327,6 @@
         return rows.reshape(total, SLOTS, width)
 
     late = late_mats(late, 12)
-    late, arrived[1] = lax.optimization_barrier((late, arrived[1]))
-    upper = jnp.concatenate([arrived[1], arrived[0]], 0).astype(jnp.float32)
     fits = mats_fit(late)
     (own_mats,), (place_grad,), (small_grad,), (came,) = run_jobs(
         [
@@ -1351,6 +1349,8 @@
         more = run_jobs([mats_job(late[k : k + fits])], "sum_mats", 14 + k, 61)[0][0]
         own_mats = jnp.concatenate([own_mats, lax.optimization_barrier(more)], 0)
     place_grad = place_grad.reshape(seq_length, width)
+    came, arrived[1] = lax.optimization_barrier((came, arrived[1]))
+    upper = jnp.concatenate([arrived[1], arrived[0]], 0).astype(jnp.float32)
     small_grad = pad_rows(small_grad.reshape(-1)[:small_size].reshape(-1, width), small_rows)
     small_high = small_grad.astype(jnp.bfloat16)
     small_low = (small_grad - small_high.astype(jnp.float32)).astype(jnp.bfloat16)

time: 1180 us -> 1170 us (level)
  waiting for transfers between devices: 45 us -> 24 us
    optimization_barrier x1, waiting for transfers between devices: 17.2 us -> 0.02 us  [on_device(): came, arrived[1] = lax.optimization_barrier((came, arrived[1]))]
    unnamed x265 -> x267, local copies, waits for them, and re-layouts: 28.3 us -> 27.6 us
  transfers between devices with their start and end apart: 4 -> 4, of which waited for: 3 -> 1; matrix products, arithmetic and copies ran while one was open for 18% -> 19% of each run, Pallas kernels for 36% -> 54%
where the time goes in v9:
time: 1170 us; the launch traced here: 1160 us
  Pallas kernels  751 us (64%)
  matrix products  205 us (18%)
  other arithmetic  77.2 us (7%)
  local copies, waits for them, and re-layouts  75.8 us (6%)
  waiting for transfers between devices  24 us (2%)
  between operations  22.2 us (2%)
    pallas_call x7, Pallas kernels, run_jobs(): pl.pallas_call(partial(jobs_kernel, jobs), out_shape=outputs, in_specs=in...  543 us
    dot_general x21, matrix products, dot_plain(): return jnp.dot(left_op, right_op, preferred_element_type=jnp.float32)  112 us
    pallas_call x2, Pallas kernels, attend(): pl.pallas_call(attend_kernel, out_shape=(jax.ShapeDtypeStruct((rows, widt...  104 us
    pallas_call x2, Pallas kernels, attend_back(): pl.pallas_call(attend_back_kernel, out_shape=(jax.ShapeDtypeStruct((rows,...  88.2 us
    dot_general x9, matrix products, dot_rows(): lax.dot_general(left_op, right_op, (((1,), (1,)), ((), ())), preferred_el...  58.8 us
    dot_general x5, matrix products, dot_cols(): lax.dot_general(left_op, right_op, (((0,), (0,)), ((), ())), preferred_el...  34 us
    unnamed x267, local copies, waits for them, and re-layouts  27.6 us
    sub x2, other arithmetic, adam_step(): weights - rate * (moment_hat / (jnp.sqrt(square_hat) + ADAM_EPS) + decay...  25.9 us
  transfers between devices with their start and end apart: 4, of which 1 were waited for; matrix products, arithmetic and copies ran while one was open for 19% of the time, Pallas kernels for 54%

profile of v9, /device:TPU:0, one launch (start us, length us, event | category | flops | bytes accessed | tf_op | source)
XLA Modules:
  0.0 1156.2 jit_solution(2970398572219529647)
XLA Ops:
  11.6 12.5 %share_ids.1 = s32[32,8,128]{2,1,0:T(8,128)S(1)} custom-call(s32[8,128]{1,0:T(8,128)S(1)} %pad_bitcast_fusion.1.refs_0_), custom_call_target="tpu_custom_call" | custom-call | tf_op jit(solution)/shard_map/share_ids/pallas_call | solution.py:168
  27.0 6.9 copy.96
  33.9 11.3 fusion.21
  45.6 196.1 %open_rows.1 = (bf16[32,136,1088]{2,1,0:T(8,128)(2,1)S(1)}, bf16[8,32,1088]{2,1,0:T(8,128)(2,1)S(1)}, bf16[32,1088]{1,0:T(8,128)(2,1)S(1)}, bf16[32,24,1088]{2,1,0:T(8,128)(2,1)S(1)}) custom-call(bf16[136,1088]{1,0:T(8,128)(2,1)S(1)} %slice_bitcast_fusion.36.refs_0_, bf16[32,32,1088]{2,1,0:T(8,128)(2,1)S(1)} %bitcast.208, ...), custom_call_target="tpu_custom_call" | custom-call | tf_op jit(solution)/shard_map/open_rows/pallas_call | solution.py:168
  270.5 43.6 %attend.2 = (bf16[256,1152]{1,0:T(8,128)(2,1)S(1)}, f32[9,2,256]{2,1,0:T(2,128)S(1)}, bf16[4,512,1152]{2,1,0:T(8,128)(2,1)}) custom-call(bf16[256,1152]{1,0:T(8,128)(2,1)S(1)} %pad.38.q_ref, bf16[512,1152]{1,0:T(8,128)(2,1)S(1)} %fusion.63.own_ref, s32[1024,1]{1,0:T(8,128)S(1)} %copy.100.key_ids_ref, s32[1,256]{1,0:T(1,128)S(1)} %constant_dynamic-slice_fusion.query_ids_ref), custom_call_target="tpu_custom_call" | custom-call | flops 1207959552 | bytes 4718592 | tf_op jit(solution)/shard_map/attend/pallas_call | solution.py:797
  317.8 8.1 multiply_convert_fusion.1
  325.9 7.9 fusion.112
  337.6 60.3 %attend.3 = (bf16[256,1152]{1,0:T(8,128)(2,1)S(1)}, f32[9,2,256]{2,1,0:T(2,128)S(1)}, bf16[4,512,1152]{2,1,0:T(8,128)(2,1)}) custom-call(bf16[256,1152]{1,0:T(8,128)(2,1)S(1)} %pad.41.q_ref, bf16[512,1152]{1,0:T(8,128)(2,1)S(1)} %fusion.64.own_ref, s32[1024,1]{1,0:T(8,128)S(1)} %copy.100.key_ids_ref, s32[1,256]{1,0:T(1,128)S(1)} %constant_dynamic-slice_fusion.query_ids_ref), custom_call_target="tpu_custom_call" | custom-call | flops 1207959552 | bytes 4718592 | tf_op jit(solution)/shard_map/attend/pallas_call | solution.py:797
  400.3 23.9 %all-gather.7.cloned.1.call-done = bf16[1,2,4352,1088]{3,2,1,0:T(8,128)(2,1)} async-done(((bf16[1,2,136,1088]{3,2,1,0:T(8,128)(2,1)}), bf16[1,2,4352,1088]{3,2,1,0:T(8,128)(2,1)}) %all-gather.7.cloned.1.call-update) | async-done | bytes 18939920 | tf_op jit(solution)/shard_map/all_gather | solution.py:1191
  424.2 7.0 fusion.23
  431.2 8.7 fusion.114
  441.8 48.4 %share_final.1 = bf16[32,64,1088]{2,1,0:T(8,128)(2,1)} custom-call(bf16[4,64,1088]{2,1,0:T(8,128)(2,1)} %bitcast.240), custom_call_target="tpu_custom_call" | custom-call | tf_op jit(solution)/shard_map/share_final/pallas_call | solution.py:168
  490.3 12.6 %select_reduce_fusion.3 = (f32[2048]{0:T(1024)S(1)}, f32[2048,1604]{0,1:T(8,128)S(1)}) fusion(pred[1604]{0:T(1024)(128)(4,1)S(1)} %copy-done.97, bf16[2048,1088]{1,0:T(8,128)(2,1)} %bitcast.233, bf16[1604,1088]{1,0:T(8,128)(2,1)} %get-tuple-element.654), kind=kOutput, calls=%fused_computation.36 | convolution fusion | flops 7154710528 | bytes 21096516 | tf_op jit(solution)/shard_map/dot_general | solution.py:966
  508.1 15.4 %share_stats.1 = f32[3,16,128]{2,1,0:T(8,128)S(1)} custom-call(f32[3,16,128]{2,1,0:T(8,128)S(1)} %pad_maximum_fusion.3.refs_0_), custom_call_target="tpu_custom_call" | custom-call | tf_op jit(solution)/shard_map/share_stats/pallas_call | solution.py:168
  529.2 12.4 %fusion.116 = f32[2048,1088]{1,0:T(8,128)} fusion(bf16[2048,1604]{0,1:T(8,128)(2,1)S(1)} %fusion.9, bf16[1604,1088]{1,0:T(8,128)(2,1)S(1)} %copy-done.60), kind=kOutput, calls=%fused_computation.303 | convolution fusion | flops 7148142592 | bytes 18973184 | tf_op jit(solution)/shard_map/dot_general | solution.py:978
  541.6 52.8 %return_final.1 = bf16[4,64,1088]{2,1,0:T(8,128)(2,1)} custom-call(f32[32,64,1088]{2,1,0:T(8,128)} %bitcast.220), custom_call_target="tpu_custom_call" | custom-call | tf_op jit(solution)/shard_map/return_final/pallas_call | solution.py:168
  599.0 10.0 convolution_convert_fusion.2
  611.0 9.7 convert_reduce_fusion
  620.7 9.2 multiply_reduce_fusion.3
  634.3 47.6 %attend_back.2 = (bf16[256,1152]{1,0:T(8,128)(2,1)}, bf16[512,1152]{1,0:T(8,128)(2,1)}) custom-call(bf16[256,1152]{1,0:T(8,128)(2,1)} %copy-done.11, bf16[4,512,1152]{2,1,0:T(8,128)(2,1)} %get-tuple-element.282.kv_ref, bf16[256,1152]{1,0:T(8,128)(2,1)} %pad.44.grad_ref, f32[9,2,256]{2,1,0:T(2,128)} %copy-done.31, s32[1024,1]{1,0:T(8,128)} %copy-done.12, ...), custom_call_target="tpu_custom_call" | custom-call | flops 3019898880 | bytes 14155776 | tf_op jit(solution)/shard_map/attend_back/pallas_call | solution.py:924
  688.5 7.5 multiply_reduce_fusion.4
  706.7 9.4 convert_reduce_fusion.1
  716.2 9.7 multiply_reduce_fusion.5
  743.7 14.1 %fusion.117 = f32[1604,1088]{0,1:T(8,128)} fusion(bf16[2048,1604]{0,1:T(8,128)(2,1)} %copy-done.51, bf16[2048,1088]{1,0:T(8,128)(2,1)} %bitcast.234), kind=kOutput, calls=%fused_computation.304 | convolution fusion | flops 7148142592 | bytes 18007040 | tf_op jit(solution)/shard_map/dot_general | solution.py:972
  757.7 40.6 %attend_back.3 = (bf16[256,1152]{1,0:T(8,128)(2,1)}, bf16[512,1152]{1,0:T(8,128)(2,1)}) custom-call(bf16[256,1152]{1,0:T(8,128)(2,1)} %copy-done.10, bf16[4,512,1152]{2,1,0:T(8,128)(2,1)} %get-tuple-element.281.kv_ref, bf16[256,1152]{1,0:T(8,128)(2,1)} %pad.45.grad_ref, f32[9,2,256]{2,1,0:T(2,128)} %copy-done.30, s32[1024,1]{1,0:T(8,128)} %copy-done.12, ...), custom_call_target="tpu_custom_call" | custom-call | flops 3019898880 | bytes 14155776 | tf_op jit(solution)/shard_map/attend_back/pallas_call | solution.py:924
  805.9 6.8 multiply_reduce_fusion.6
  824.0 15.7 %trade_rows.1 = (bf16[3,544,512]{2,1,0:T(8,128)(2,1)S(1)}, bf16[1,544,512]{2,1,0:T(8,128)(2,1)S(1)}, bf16[4,544,512]{2,1,0:T(8,128)(2,1)}, bf16[4,544,512]{2,1,0...) custom-call(bf16[3,2,544,256]{3,2,1,0:T(8,128)(2,1)} %bitcast.229, ...), custom_call_target="tpu_custom_call" | custom-call | tf_op jit(solution)/shard_map/trade_rows/pallas_call | solution.py:655
  874.4 208.3 %close_rows.1 = (f32[4,136,1088]{2,1,0:T(8,128)}, bf16[32,32,1088]{2,1,0:T(8,128)(2,1)}, f32[224,128]{1,0:T(8,128)}, bf16[32,24,1088]{2,1,0:T(8,128)(2,1)}) custom-call(bf16[16,136,1088]{2,1,0:T(8,128)(2,1)} %bitcast.216, bf16[16,136,1088]{2,1,0:T(8,128)(2,1)} %bitcast.230, bf16[16,136,1088]{2,1,0:T(8,128)(2,1)} %bitcast.231, ...), custom_call_target="tpu_custom_call" | custom-call | tf_op jit(solution)/shard_map/close_rows/pallas_call | solution.py:168
  1083.8 13.5 %fusion.12 = f32[1604,1088]{0,1:T(8,128)} fusion(f32[1604,1088]{0,1:T(8,128)} %fusion.117, s32[1856]{0:T(1024)S(1)} %copy-done.123, bf16[32,1088]{1,0:T(8,128)(2,1)S(1)} %subtract_convert_fusion, bf16[32,1088]{1,0:T(8,128)(2,1)S(1)} %pad_convert_fusion, bf16[1024,1088]{1,0:T(8,128)(2,1)} %bitcast.263, bf16[768,1088]{1,0:T(8,128)(2,1)} %bitcast.266), kind=kOutput, calls=%fused_computation.44 | convolution fusion | flops 6498880512 | bytes 18007296 | tf_op jit(solution)/shard_map/dot_general | solution.py:978
  1106.2 9.8 share_norm.1
  1121.2 6.8 multiply_subtract_fusion.1
  1128.0 19.2 %multiply_subtract_fusion = (f32[1604,1088]{0,1:T(8,128)}, f32[1604,1088]{0,1:T(8,128)}, f32[1604,1088]{0,1:T(8,128)}) fusion(f32[1604,1088]{0,1:T(8,128)} %param.25, f32[1604]{0:T(1024)S(1)} %copy-done.93, f32[]{:T(128)} %bitcast.68, f32[]{:T(128)} %bitcast.67, f32[1604]{0:T(1024)S(1)} %copy-done.94, f32[1604,1088]{0,1:T(8,128)} %get-tuple-element.637, ...), kind=kLoop, calls=%fused_computation.58 | loop fusion | flops 27922432 | bytes 48877100 | tf_op jit(solution)/shard_map/sub | solution.py:1107
  (422 shorter events, 168.6 us)
Async XLA Ops:
  7.2 257.0 %all-gather.5.cloned.1.call-start = ((), (), s32[]{:S(2)}) async-start(), calls=%async_computation.2 | async-start | bytes 31021056 | tf_op jit(solution)/shard_map/all_gather | solution.py:1188
  10.5 413.7 %all-gather.7.cloned.1.call-start = ((), (), s32[]{:S(2)}) async-start(), calls=%async_computation.3 | async-start | bytes 20680704 | tf_op jit(solution)/shard_map/all_gather | solution.py:1191
  11.5 746.2 %reduce-scatter.7.cloned.1.call-start = ((), (), s32[]{:S(2)}) async-start(), calls=%async_computation.4 | async-start | bytes 10340352
  33.9 11.3 copy-start.84
  248.7 88.9 %copy-start.12 = (s32[1024,1]{1,0:T(8,128)}, s32[1024,1]{1,0:T(8,128)S(1)}, u32[]{:S(2)}) copy-start(s32[1024,1]{1,0:T(8,128)S(1)} %copy.100.key_ids_ref) | copy-start | bytes 12292
  259.4 54.8 %copy-start.35 = (f32[256,1088]{1,0:T(8,128)}, f32[256,1088]{1,0:T(8,128)S(1)}, u32[]{:S(2)}) copy-start(f32[256,1088]{1,0:T(8,128)S(1)} %copy.101) | copy-start | bytes 3342340
  261.3 76.2 %copy-start.13 = (s32[1,256]{1,0:T(1,128)}, s32[1,256]{1,0:T(1,128)S(1)}, u32[]{:S(2)}) copy-start(s32[1,256]{1,0:T(1,128)S(1)} %constant_dynamic-slice_fusion.query_ids_ref) | copy-start | bytes 3076
  262.8 54.5 %copy-start.82 = (f32[1088]{0:T(1024)}, f32[1088]{0:T(1024)S(1)}, u32[]{:S(2)}) copy-start(f32[1088]{0:T(1024)S(1)} %get-tuple-element.339) | copy-start | bytes 13060
  262.8 161.4 %copy-start.91 = (f32[1088]{0:T(1024)}, f32[1088]{0:T(1024)S(1)}, u32[]{:S(2)}) copy-start(f32[1088]{0:T(1024)S(1)} %get-tuple-element.330) | copy-start | bytes 13060
  270.4 43.7 %copy-start.10 = (bf16[256,1152]{1,0:T(8,128)(2,1)}, bf16[256,1152]{1,0:T(8,128)(2,1)S(1)}, u32[]{:S(2)}) copy-start(bf16[256,1152]{1,0:T(8,128)(2,1)S(1)} %pad.38.q_ref) | copy-start | bytes 1769476
  333.8 64.1 %copy-start.43 = (f32[256,1088]{1,0:T(8,128)}, f32[256,1088]{1,0:T(8,128)S(1)}, u32[]{:S(2)}) copy-start(f32[256,1088]{1,0:T(8,128)S(1)} %get-tuple-element.430) | copy-start | bytes 3342340
  337.4 60.5 %copy-start.11 = (bf16[256,1152]{1,0:T(8,128)(2,1)}, bf16[256,1152]{1,0:T(8,128)(2,1)S(1)}, u32[]{:S(2)}) copy-start(bf16[256,1152]{1,0:T(8,128)(2,1)S(1)} %pad.41.q_ref) | copy-start | bytes 1769476
  337.6 60.4 %copy-start.63 = (bf16[8,136,1088]{2,1,0:T(8,128)(2,1)S(1)}, bf16[8,136,1088]{2,1,0:T(8,128)(2,1)}, u32[]{:S(2)}) copy-start(bf16[8,136,1088]{2,1,0:T(8,128)(2,1)} %slice.255) | copy-start | bytes 7102468
  397.9 26.3 %copy-start.95 = (f32[4352]{0:T(1024)S(1)}, f32[4352]{0:T(1024)}, u32[]{:S(2)}) copy-start(f32[4352]{0:T(1024)} %add.560) | copy-start | bytes 52228
  399.0 230.9 %copy-start.105 = (f32[256]{0:T(256)}, f32[256]{0:T(256)S(1)}, u32[]{:S(2)}) copy-start(f32[256]{0:T(256)S(1)} %broadcast_multiply_fusion.1) | copy-start | bytes 3076
  400.3 229.6 %copy-start.120 = (f32[256]{0:T(256)}, f32[256]{0:T(256)S(1)}, u32[]{:S(2)}) copy-start(f32[256]{0:T(256)S(1)} %fusion.96) | copy-start | bytes 3076
  441.8 48.4 %copy-start.97 = (pred[1604]{0:T(1024)(128)(4,1)S(1)}, pred[1604]{0:T(1024)(128)(4,1)}, u32[]{:S(2)}) copy-start(pred[1604]{0:T(1024)(128)(4,1)} %fusion.87) | copy-start | bytes 4816
  490.2 12.6 %copy-start.88 = (s32[2048]{0:T(1024)S(1)}, s32[2048]{0:T(1024)}, u32[]{:S(2)}) copy-start(s32[2048]{0:T(1024)} %param.20) | copy-start | bytes 24580
  529.2 12.4 %copy-start.51 = (bf16[2048,1604]{0,1:T(8,128)(2,1)}, bf16[2048,1604]{0,1:T(8,128)(2,1)S(1)}, u32[]{:S(2)}) copy-start(bf16[2048,1604]{0,1:T(8,128)(2,1)S(1)} %fusion.9) | copy-start | bytes 19709956
  609.0 474.8 %reduce-scatter.9.cloned.1.call-start = ((), (), s32[]{:S(2)}) async-start(), calls=%async_computation.5 | async-start | bytes 10340352
  716.2 10.6 copy-start.65
  823.9 24.8 %copy-start.62 = (bf16[512,1152]{1,0:T(8,128)(2,1)S(1)}, bf16[512,1152]{1,0:T(8,128)(2,1)}, u32[]{:S(2)}) copy-start(bf16[512,1152]{1,0:T(8,128)(2,1)} %get-tuple-element.289) | copy-start | bytes 3538948
  823.9 24.8 %copy-start.69 = (bf16[256,1152]{1,0:T(8,128)(2,1)S(1)}, bf16[256,1152]{1,0:T(8,128)(2,1)}, u32[]{:S(2)}) copy-start(bf16[256,1152]{1,0:T(8,128)(2,1)} %get-tuple-element.288) | copy-start | bytes 1769476
  823.9 25.0 %copy-start.89 = (f32[1088]{0:T(1024)S(1)}, f32[1088]{0:T(1024)}, u32[]{:S(2)}) copy-start(f32[1088]{0:T(1024)} %get-tuple-element.312) | copy-start | bytes 13060
  823.9 25.0 %copy-start.90 = (f32[1088]{0:T(1024)S(1)}, f32[1088]{0:T(1024)}, u32[]{:S(2)}) copy-start(f32[1088]{0:T(1024)} %get-tuple-element.322) | copy-start | bytes 13060
  874.4 209.3 %copy-start.123 = (s32[1856]{0:T(1024)S(1)}, s32[1856]{0:T(1024)}, u32[]{:S(2)}) copy-start(s32[1856]{0:T(1024)} %concatenate.48) | copy-start | bytes 22276
  1083.8 13.5 %copy-start.33 = (bf16[256,1088]{1,0:T(8,128)(2,1)S(1)}, bf16[256,1088]{1,0:T(8,128)(2,1)}, u32[]{:S(2)}) copy-start(bf16[256,1088]{1,0:T(8,128)(2,1)} %copy-done.32) | copy-start | bytes 1671172
  1083.8 13.5 %copy-start.56 = (s32[32,256]{1,0:T(8,128)S(1)}, s32[32,256]{1,0:T(8,128)}, u32[]{:S(2)}) copy-start(s32[32,256]{1,0:T(8,128)} %copy-done.55) | copy-start | bytes 98308
  1083.8 13.5 %copy-start.58 = (s32[32,256]{1,0:T(8,128)S(1)}, s32[32,256]{1,0:T(8,128)}, u32[]{:S(2)}) copy-start(s32[32,256]{1,0:T(8,128)} %copy-done.57) | copy-start | bytes 98308
  1083.8 13.5 %copy-start.73 = (pred[32,256]{1,0:T(32,128)(4,1)S(1)}, pred[32,256]{1,0:T(32,128)(4,1)}, u32[]{:S(2)}) copy-start(pred[32,256]{1,0:T(32,128)(4,1)} %copy-done.72) | copy-start | bytes 24580
  1083.8 13.5 %copy-start.77 = (s32[256]{0:T(256)S(1)}, s32[256]{0:T(256)}, u32[]{:S(2)}) copy-start(s32[256]{0:T(256)} %copy-done.76) | copy-start | bytes 3076
  1083.8 13.5 %copy-start.79 = (s32[256]{0:T(256)S(1)}, s32[256]{0:T(256)}, u32[]{:S(2)}) copy-start(s32[256]{0:T(256)} %copy-done.78) | copy-start | bytes 3076
  (105 other events, 461.4 us)
Sparse Core Ops, SparseCore 0:
  11.6 252.1 all-gather.4
  266.8 157.3 all-gather.6
  609.1 136.5 reduce-scatter.6
  751.6 134.8 reduce-scatter.8

commit v10 on v9

--- a/solution.py
+++ b/solution.py
@@ -564,8 +564,12 @@
 
 def gather_job(parts):
     rows, width = parts[0].shape
-    spans, orders = sum_orders_for(rows)
-    orders = [order[::-1] + bits_of("seq")[:1] for order in orders]
+    across, along, deep = bits_of("seq")[1:], bits_of("dp"), bits_of("shard")
+    spans, ways = [(0, rows)], [across + along]
+    if rows >= 64 and rows % 8 == 0:
+        half = rows // 32 * 16
+        spans, ways = [(0, half), (half, rows - half)], [across + along, along + across]
+    orders = [deep[::-1] + way[::-1] + bits_of("seq")[:1] for way in ways]
     total = lax.axis_size(AXES)
     sends = 0
     for order in orders:
@@ -1324,7 +1328,7 @@
 
     def leaving(at):
         rows = dot_cols(one_hot(own_slots(at), total * SLOTS, 1), low_grad).astype(jnp.bfloat16)
-        return rows.reshape(total, SLOTS, width)
+        return rows_major(rows).reshape(total, SLOTS, width)
 
     late = late_mats(late, 12)
     fits = mats_fit(late)

time: 1170 us -> 1180 us (level)
  Pallas kernels: 751 us -> 774 us
    pallas_call x7, Pallas kernels: 543 us -> 567 us  [run_jobs(): pl.pallas_call(partial(jobs_kernel, jobs), out_shape=outputs, in_specs=in...]
  transfers between devices with their start and end apart: 4 -> 4, of which waited for: 1 -> 1; matrix products, arithmetic and copies ran while one was open for 19% -> 19% of each run, Pallas kernels for 54% -> 55%
where the time goes in v10:
time: 1180 us; the launch traced here: 1170 us
  Pallas kernels  774 us (66%)
  matrix products  206 us (17%)
  other arithmetic  79.2 us (7%)
  local copies, waits for them, and re-layouts  64.2 us (5%)
  between operations  22.5 us (2%)
  waiting for transfers between devices  20.5 us (2%)
    pallas_call x7, Pallas kernels, run_jobs(): pl.pallas_call(partial(jobs_kernel, jobs), out_shape=outputs, in_specs=in...  567 us
    dot_general x21, matrix products, dot_plain(): return jnp.dot(left_op, right_op, preferred_element_type=jnp.float32)  113 us
    pallas_call x2, Pallas kernels, attend(): pl.pallas_call(attend_kernel, out_shape=(jax.ShapeDtypeStruct((rows, widt...  103 us
    pallas_call x2, Pallas kernels, attend_back(): pl.pallas_call(attend_back_kernel, out_shape=(jax.ShapeDtypeStruct((rows,...  88.8 us
    dot_general x9, matrix products, dot_rows(): lax.dot_general(left_op, right_op, (((1,), (1,)), ((), ())), preferred_el...  59.4 us
    dot_general x5, matrix products, dot_cols(): lax.dot_general(left_op, right_op, (((0,), (0,)), ((), ())), preferred_el...  34.1 us
    sub x2, other arithmetic, adam_step(): weights - rate * (moment_hat / (jnp.sqrt(square_hat) + ADAM_EPS) + decay...  25.9 us
  transfers between devices with their start and end apart: 4, of which 1 were waited for; matrix products, arithmetic and copies ran while one was open for 19% of the time, Pallas kernels for 55%

profile of v10, /device:TPU:0, one launch (start us, length us, event | category | flops | bytes accessed | tf_op | source)
XLA Modules:
  0.0 1167.4 jit_solution(13318005720306859867)
XLA Ops:
  11.6 12.5 %share_ids.1 = s32[32,8,128]{2,1,0:T(8,128)S(1)} custom-call(s32[8,128]{1,0:T(8,128)S(1)} %pad_bitcast_fusion.1.refs_0_), custom_call_target="tpu_custom_call" | custom-call | tf_op jit(solution)/shard_map/share_ids/pallas_call | solution.py:168
  27.0 6.9 copy.89
  33.9 11.3 fusion.21
  45.6 216.1 %open_rows.1 = (bf16[32,136,1088]{2,1,0:T(8,128)(2,1)S(1)}, bf16[8,32,1088]{2,1,0:T(8,128)(2,1)S(1)}, bf16[32,1088]{1,0:T(8,128)(2,1)S(1)}, bf16[32,24,1088]{2,1,0:T(8,128)(2,1)S(1)}) custom-call(bf16[136,1088]{1,0:T(8,128)(2,1)S(1)} %slice_bitcast_fusion.36.refs_0_, bf16[32,32,1088]{2,1,0:T(8,128)(2,1)S(1)} %bitcast.208, ...), custom_call_target="tpu_custom_call" | custom-call | tf_op jit(solution)/shard_map/open_rows/pallas_call | solution.py:168
  291.0 42.6 %attend.2 = (bf16[256,1152]{1,0:T(8,128)(2,1)S(1)}, f32[9,2,256]{2,1,0:T(2,128)S(1)}, bf16[4,512,1152]{2,1,0:T(8,128)(2,1)}) custom-call(bf16[256,1152]{1,0:T(8,128)(2,1)S(1)} %pad.38.q_ref, bf16[512,1152]{1,0:T(8,128)(2,1)S(1)} %fusion.63.own_ref, s32[1024,1]{1,0:T(8,128)S(1)} %copy.93.key_ids_ref, s32[1,256]{1,0:T(1,128)S(1)} %constant_dynamic-slice_fusion.query_ids_ref), custom_call_target="tpu_custom_call" | custom-call | flops 1207959552 | bytes 4718592 | tf_op jit(solution)/shard_map/attend/pallas_call | solution.py:801
  337.3 8.2 multiply_convert_fusion.1
  345.5 7.9 fusion.112
  357.2 60.4 %attend.3 = (bf16[256,1152]{1,0:T(8,128)(2,1)S(1)}, f32[9,2,256]{2,1,0:T(2,128)S(1)}, bf16[4,512,1152]{2,1,0:T(8,128)(2,1)}) custom-call(bf16[256,1152]{1,0:T(8,128)(2,1)S(1)} %pad.41.q_ref, bf16[512,1152]{1,0:T(8,128)(2,1)S(1)} %fusion.64.own_ref, s32[1024,1]{1,0:T(8,128)S(1)} %copy.93.key_ids_ref, s32[1,256]{1,0:T(1,128)S(1)} %constant_dynamic-slice_fusion.query_ids_ref), custom_call_target="tpu_custom_call" | custom-call | flops 1207959552 | bytes 4718592 | tf_op jit(solution)/shard_map/attend/pallas_call | solution.py:801
  420.1 20.4 %all-gather.7.cloned.1.call-done = bf16[1,2,4352,1088]{3,2,1,0:T(8,128)(2,1)} async-done(((bf16[1,2,136,1088]{3,2,1,0:T(8,128)(2,1)}), bf16[1,2,4352,1088]{3,2,1,0:T(8,128)(2,1)}) %all-gather.7.cloned.1.call-update) | async-done | bytes 18939920 | tf_op jit(solution)/shard_map/all_gather | solution.py:1195
  440.6 7.0 fusion.23
  447.6 8.7 fusion.114
  458.2 46.4 %share_final.1 = bf16[32,64,1088]{2,1,0:T(8,128)(2,1)} custom-call(bf16[4,64,1088]{2,1,0:T(8,128)(2,1)} %bitcast.240), custom_call_target="tpu_custom_call" | custom-call | tf_op jit(solution)/shard_map/share_final/pallas_call | solution.py:168
  504.6 12.5 %select_reduce_fusion.3 = (f32[2048]{0:T(1024)S(1)}, f32[2048,1604]{0,1:T(8,128)S(1)}) fusion(pred[1604]{0:T(1024)(128)(4,1)S(1)} %copy-done.97, bf16[2048,1088]{1,0:T(8,128)(2,1)} %bitcast.233, bf16[1604,1088]{1,0:T(8,128)(2,1)} %get-tuple-element.642), kind=kOutput, calls=%fused_computation.36 | convolution fusion | flops 7154710528 | bytes 21096516 | tf_op jit(solution)/shard_map/dot_general | solution.py:970
  522.5 14.9 %share_stats.1 = f32[3,16,128]{2,1,0:T(8,128)S(1)} custom-call(f32[3,16,128]{2,1,0:T(8,128)S(1)} %pad_maximum_fusion.3.refs_0_), custom_call_target="tpu_custom_call" | custom-call | tf_op jit(solution)/shard_map/share_stats/pallas_call | solution.py:168
  543.0 12.4 %fusion.116 = f32[2048,1088]{1,0:T(8,128)} fusion(bf16[2048,1604]{0,1:T(8,128)(2,1)S(1)} %fusion.9, bf16[1604,1088]{1,0:T(8,128)(2,1)S(1)} %copy-done.61), kind=kOutput, calls=%fused_computation.303 | convolution fusion | flops 7148142592 | bytes 18973184 | tf_op jit(solution)/shard_map/dot_general | solution.py:982
  555.4 53.3 %return_final.1 = bf16[4,64,1088]{2,1,0:T(8,128)(2,1)} custom-call(f32[32,64,1088]{2,1,0:T(8,128)} %bitcast.220), custom_call_target="tpu_custom_call" | custom-call | tf_op jit(solution)/shard_map/return_final/pallas_call | solution.py:168
  613.3 10.0 convolution_convert_fusion.2
  625.4 9.7 convert_reduce_fusion
  635.1 9.2 multiply_reduce_fusion.3
  648.6 48.3 %attend_back.2 = (bf16[256,1152]{1,0:T(8,128)(2,1)}, bf16[512,1152]{1,0:T(8,128)(2,1)}) custom-call(bf16[256,1152]{1,0:T(8,128)(2,1)} %copy-done.11, bf16[4,512,1152]{2,1,0:T(8,128)(2,1)} %get-tuple-element.282.kv_ref, bf16[256,1152]{1,0:T(8,128)(2,1)} %pad.44.grad_ref, f32[9,2,256]{2,1,0:T(2,128)} %copy-done.33, s32[1024,1]{1,0:T(8,128)} %copy-done.12, ...), custom_call_target="tpu_custom_call" | custom-call | flops 3019898880 | bytes 14155776 | tf_op jit(solution)/shard_map/attend_back/pallas_call | solution.py:928
  703.4 7.4 multiply_reduce_fusion.4
  721.5 9.4 convert_reduce_fusion.1
  731.0 9.7 multiply_reduce_fusion.5
  758.6 14.0 %fusion.117 = f32[1604,1088]{0,1:T(8,128)} fusion(bf16[2048,1604]{0,1:T(8,128)(2,1)} %copy-done.52, bf16[2048,1088]{1,0:T(8,128)(2,1)} %bitcast.234), kind=kOutput, calls=%fused_computation.304 | convolution fusion | flops 7148142592 | bytes 18007040 | tf_op jit(solution)/shard_map/dot_general | solution.py:976
  772.6 40.5 %attend_back.3 = (bf16[256,1152]{1,0:T(8,128)(2,1)}, bf16[512,1152]{1,0:T(8,128)(2,1)}) custom-call(bf16[256,1152]{1,0:T(8,128)(2,1)} %copy-done.10, bf16[4,512,1152]{2,1,0:T(8,128)(2,1)} %get-tuple-element.281.kv_ref, bf16[256,1152]{1,0:T(8,128)(2,1)} %pad.45.grad_ref, f32[9,2,256]{2,1,0:T(2,128)} %copy-done.32, s32[1024,1]{1,0:T(8,128)} %copy-done.12, ...), custom_call_target="tpu_custom_call" | custom-call | flops 3019898880 | bytes 14155776 | tf_op jit(solution)/shard_map/attend_back/pallas_call | solution.py:928
  822.8 15.5 %trade_rows.1 = (bf16[3,544,512]{2,1,0:T(8,128)(2,1)S(1)}, bf16[1,544,512]{2,1,0:T(8,128)(2,1)S(1)}, bf16[4,544,512]{2,1,0:T(8,128)(2,1)}, bf16[4,544,512]{2,1,0...) custom-call(bf16[3,2,544,256]{3,2,1,0:T(8,128)(2,1)} %bitcast.229, ...), custom_call_target="tpu_custom_call" | custom-call | tf_op jit(solution)/shard_map/trade_rows/pallas_call | solution.py:659
  839.5 8.8 multiply_reduce_fusion.6
  880.0 209.0 %close_rows.1 = (f32[4,136,1088]{2,1,0:T(8,128)}, bf16[32,32,1088]{2,1,0:T(8,128)(2,1)}, f32[224,128]{1,0:T(8,128)}, bf16[32,24,1088]{2,1,0:T(8,128)(2,1)}) custom-call(bf16[16,136,1088]{2,1,0:T(8,128)(2,1)} %bitcast.216, bf16[16,136,1088]{2,1,0:T(8,128)(2,1)} %bitcast.230, bf16[16,136,1088]{2,1,0:T(8,128)(2,1)} %bitcast.231, ...), custom_call_target="tpu_custom_call" | custom-call | tf_op jit(solution)/shard_map/close_rows/pallas_call | solution.py:168
  1090.2 13.4 %fusion.12 = f32[1604,1088]{0,1:T(8,128)} fusion(f32[1604,1088]{0,1:T(8,128)} %fusion.117, s32[1856]{0:T(1024)S(1)} %copy-done.122, bf16[32,1088]{1,0:T(8,128)(2,1)S(1)} %subtract_convert_fusion, bf16[32,1088]{1,0:T(8,128)(2,1)S(1)} %pad_convert_fusion, bf16[1024,1088]{1,0:T(8,128)(2,1)} %bitcast.263, bf16[768,1088]{1,0:T(8,128)(2,1)} %bitcast.266), kind=kOutput, calls=%fused_computation.44 | convolution fusion | flops 6498880512 | bytes 18007296 | tf_op jit(solution)/shard_map/dot_general | solution.py:982
  1112.6 14.4 %share_norm.1 = f32[8,128]{1,0:T(8,128)S(1)} custom-call(f32[8,128]{1,0:T(8,128)S(1)} %broadcast_in_dim.223.refs_0_), custom_call_target="tpu_custom_call" | custom-call | tf_op jit(solution)/shard_map/share_norm/pallas_call | solution.py:168
  1132.2 6.8 multiply_subtract_fusion.1
  1139.0 19.2 %multiply_subtract_fusion = (f32[1604,1088]{0,1:T(8,128)}, f32[1604,1088]{0,1:T(8,128)}, f32[1604,1088]{0,1:T(8,128)}) fusion(f32[1604,1088]{0,1:T(8,128)} %param.25, f32[1604]{0:T(1024)S(1)} %copy-done.93, f32[]{:T(128)} %bitcast.68, f32[]{:T(128)} %bitcast.67, f32[1604]{0:T(1024)S(1)} %copy-done.94, f32[1604,1088]{0,1:T(8,128)} %get-tuple-element.309, ...), kind=kLoop, calls=%fused_computation.58 | loop fusion | flops 27922432 | bytes 48877100 | tf_op jit(solution)/shard_map/sub | solution.py:1111
  (421 shorter events, 158.1 us)
Async XLA Ops:
  7.2 277.0 %all-gather.5.cloned.1.call-start = ((), (), s32[]{:S(2)}) async-start(), calls=%async_computation.2 | async-start | bytes 31021056 | tf_op jit(solution)/shard_map/all_gather | solution.py:1192
  10.5 430.0 %all-gather.7.cloned.1.call-start = ((), (), s32[]{:S(2)}) async-start(), calls=%async_computation.3 | async-start | bytes 20680704 | tf_op jit(solution)/shard_map/all_gather | solution.py:1195
  11.5 761.2 %reduce-scatter.7.cloned.1.call-start = ((), (), s32[]{:S(2)}) async-start(), calls=%async_computation.4 | async-start | bytes 10340352
  268.7 88.5 %copy-start.12 = (s32[1024,1]{1,0:T(8,128)}, s32[1024,1]{1,0:T(8,128)S(1)}, u32[]{:S(2)}) copy-start(s32[1024,1]{1,0:T(8,128)S(1)} %copy.93.key_ids_ref) | copy-start | bytes 12292
  279.4 54.3 %copy-start.34 = (f32[256,1088]{1,0:T(8,128)}, f32[256,1088]{1,0:T(8,128)S(1)}, u32[]{:S(2)}) copy-start(f32[256,1088]{1,0:T(8,128)S(1)} %copy.94) | copy-start | bytes 3342340
  281.4 75.8 %copy-start.13 = (s32[1,256]{1,0:T(1,128)}, s32[1,256]{1,0:T(1,128)S(1)}, u32[]{:S(2)}) copy-start(s32[1,256]{1,0:T(1,128)S(1)} %constant_dynamic-slice_fusion.query_ids_ref) | copy-start | bytes 3076
  282.8 54.0 %copy-start.83 = (f32[1088]{0:T(1024)}, f32[1088]{0:T(1024)S(1)}, u32[]{:S(2)}) copy-start(f32[1088]{0:T(1024)S(1)} %get-tuple-element.339) | copy-start | bytes 13060
  282.8 157.7 %copy-start.91 = (f32[1088]{0:T(1024)}, f32[1088]{0:T(1024)S(1)}, u32[]{:S(2)}) copy-start(f32[1088]{0:T(1024)S(1)} %get-tuple-element.330) | copy-start | bytes 13060
  290.9 42.7 %copy-start.10 = (bf16[256,1152]{1,0:T(8,128)(2,1)}, bf16[256,1152]{1,0:T(8,128)(2,1)S(1)}, u32[]{:S(2)}) copy-start(bf16[256,1152]{1,0:T(8,128)(2,1)S(1)} %pad.38.q_ref) | copy-start | bytes 1769476
  353.4 64.2 %copy-start.43 = (f32[256,1088]{1,0:T(8,128)}, f32[256,1088]{1,0:T(8,128)S(1)}, u32[]{:S(2)}) copy-start(f32[256,1088]{1,0:T(8,128)S(1)} %get-tuple-element.430) | copy-start | bytes 3342340
  357.1 60.6 %copy-start.11 = (bf16[256,1152]{1,0:T(8,128)(2,1)}, bf16[256,1152]{1,0:T(8,128)(2,1)S(1)}, u32[]{:S(2)}) copy-start(bf16[256,1152]{1,0:T(8,128)(2,1)S(1)} %pad.41.q_ref) | copy-start | bytes 1769476
  357.2 60.5 %copy-start.64 = (bf16[8,136,1088]{2,1,0:T(8,128)(2,1)S(1)}, bf16[8,136,1088]{2,1,0:T(8,128)(2,1)}, u32[]{:S(2)}) copy-start(bf16[8,136,1088]{2,1,0:T(8,128)(2,1)} %slice.255) | copy-start | bytes 7102468
  417.7 22.8 %copy-start.95 = (f32[4352]{0:T(1024)S(1)}, f32[4352]{0:T(1024)}, u32[]{:S(2)}) copy-start(f32[4352]{0:T(1024)} %add.560) | copy-start | bytes 52228
  418.8 225.4 %copy-start.105 = (f32[256]{0:T(256)}, f32[256]{0:T(256)S(1)}, u32[]{:S(2)}) copy-start(f32[256]{0:T(256)S(1)} %broadcast_multiply_fusion.1) | copy-start | bytes 3076
  420.1 224.2 %copy-start.119 = (f32[256]{0:T(256)}, f32[256]{0:T(256)S(1)}, u32[]{:S(2)}) copy-start(f32[256]{0:T(256)S(1)} %fusion.96) | copy-start | bytes 3076
  458.2 46.4 %copy-start.97 = (pred[1604]{0:T(1024)(128)(4,1)S(1)}, pred[1604]{0:T(1024)(128)(4,1)}, u32[]{:S(2)}) copy-start(pred[1604]{0:T(1024)(128)(4,1)} %fusion.87) | copy-start | bytes 4816
  504.6 12.5 %copy-start.89 = (s32[2048]{0:T(1024)S(1)}, s32[2048]{0:T(1024)}, u32[]{:S(2)}) copy-start(s32[2048]{0:T(1024)} %param.20) | copy-start | bytes 24580
  623.3 466.8 %reduce-scatter.9.cloned.1.call-start = ((), (), s32[]{:S(2)}) async-start(), calls=%async_computation.5 | async-start | bytes 10340352
  822.8 15.6 %copy-start.63 = (bf16[512,1152]{1,0:T(8,128)(2,1)S(1)}, bf16[512,1152]{1,0:T(8,128)(2,1)}, u32[]{:S(2)}) copy-start(bf16[512,1152]{1,0:T(8,128)(2,1)} %get-tuple-element.289) | copy-start | bytes 3538948
  822.8 15.6 %copy-start.70 = (bf16[256,1152]{1,0:T(8,128)(2,1)S(1)}, bf16[256,1152]{1,0:T(8,128)(2,1)}, u32[]{:S(2)}) copy-start(bf16[256,1152]{1,0:T(8,128)(2,1)} %get-tuple-element.288) | copy-start | bytes 1769476
  822.8 16.7 %copy-start.35 = (f32[256,1088]{1,0:T(8,128)S(1)}, f32[256,1088]{1,0:T(8,128)}, u32[]{:S(2)}) copy-start(f32[256,1088]{1,0:T(8,128)} %copy-done.34) | copy-start | bytes 3342340
  822.8 16.7 %copy-start.51 = (bf16[256,3264]{1,0:T(8,128)(2,1)S(1)}, bf16[256,3264]{1,0:T(8,128)(2,1)}, u32[]{:S(2)}) copy-start(bf16[256,3264]{1,0:T(8,128)(2,1)} %concatenate.42) | copy-start | bytes 5013508
  822.8 16.7 %copy-start.82 = (f32[1088]{0:T(1024)S(1)}, f32[1088]{0:T(1024)}, u32[]{:S(2)}) copy-start(f32[1088]{0:T(1024)} %copy-done.81) | copy-start | bytes 13060
  822.8 16.7 %copy-start.100 = (f32[256]{0:T(256)S(1)}, f32[256]{0:T(256)}, u32[]{:S(2)}) copy-start(f32[256]{0:T(256)} %copy-done.99) | copy-start | bytes 3076
  822.8 16.7 %copy-start.114 = (f32[256]{0:T(256)S(1)}, f32[256]{0:T(256)}, u32[]{:S(2)}) copy-start(f32[256]{0:T(256)} %copy-done.113) | copy-start | bytes 3076
  839.5 12.8 %copy-start.36 = (f32[256,1088]{1,0:T(8,128)S(1)}, f32[256,1088]{1,0:T(8,128)}, u32[]{:S(2)}) copy-start(f32[256,1088]{1,0:T(8,128)} %copy-done.34) | copy-start | bytes 3342340
  880.0 210.1 %copy-start.122 = (s32[1856]{0:T(1024)S(1)}, s32[1856]{0:T(1024)}, u32[]{:S(2)}) copy-start(s32[1856]{0:T(1024)} %concatenate.48) | copy-start | bytes 22276
  1090.1 13.5 %copy-start.57 = (s32[32,256]{1,0:T(8,128)S(1)}, s32[32,256]{1,0:T(8,128)}, u32[]{:S(2)}) copy-start(s32[32,256]{1,0:T(8,128)} %copy-done.56) | copy-start | bytes 98308
  1090.1 13.5 %copy-start.59 = (s32[32,256]{1,0:T(8,128)S(1)}, s32[32,256]{1,0:T(8,128)}, u32[]{:S(2)}) copy-start(s32[32,256]{1,0:T(8,128)} %copy-done.58) | copy-start | bytes 98308
  1090.1 13.5 %copy-start.74 = (pred[32,256]{1,0:T(32,128)(4,1)S(1)}, pred[32,256]{1,0:T(32,128)(4,1)}, u32[]{:S(2)}) copy-start(pred[32,256]{1,0:T(32,128)(4,1)} %copy-done.73) | copy-start | bytes 24580
  1090.1 13.5 %copy-start.78 = (s32[256]{0:T(256)S(1)}, s32[256]{0:T(256)}, u32[]{:S(2)}) copy-start(s32[256]{0:T(256)} %copy-done.77) | copy-start | bytes 3076
  1090.2 13.5 %copy-start.80 = (s32[256]{0:T(256)S(1)}, s32[256]{0:T(256)}, u32[]{:S(2)}) copy-start(s32[256]{0:T(256)} %copy-done.79) | copy-start | bytes 3076
  (105 other events, 566.7 us)
Sparse Core Ops, SparseCore 0:
  11.6 262.7 all-gather.4
  277.4 163.1 all-gather.6
  623.4 135.9 reduce-scatter.6
  765.4 137.3 reduce-scatter.8

commit v11 on v9

--- a/solution.py
+++ b/solution.py
@@ -1324,7 +1324,7 @@
 
     def leaving(at):
         rows = dot_cols(one_hot(own_slots(at), total * SLOTS, 1), low_grad).astype(jnp.bfloat16)
-        return rows.reshape(total, SLOTS, width)
+        return rows_major(rows).reshape(total, SLOTS, width)
 
     late = late_mats(late, 12)
     fits = mats_fit(late)

time: 1170 us -> 1160 us (level)
  local copies, waits for them, and re-layouts: 75.8 us -> 64 us
where the time goes in v11:
time: 1160 us; the launch traced here: 1150 us
  Pallas kernels  755 us (65%)
  matrix products  206 us (18%)
  other arithmetic  79.1 us (7%)
  local copies, waits for them, and re-layouts  64 us (6%)
  waiting for transfers between devices  24 us (2%)
  between operations  22.5 us (2%)
    pallas_call x7, Pallas kernels, run_jobs(): pl.pallas_call(partial(jobs_kernel, jobs), out_shape=outputs, in_specs=in...  547 us
    dot_general x21, matrix products, dot_plain(): return jnp.dot(left_op, right_op, preferred_element_type=jnp.float32)  113 us
    pallas_call x2, Pallas kernels, attend(): pl.pallas_call(attend_kernel, out_shape=(jax.ShapeDtypeStruct((rows, widt...  104 us
    pallas_call x2, Pallas kernels, attend_back(): pl.pallas_call(attend_back_kernel, out_shape=(jax.ShapeDtypeStruct((rows,...  88.3 us
    dot_general x9, matrix products, dot_rows(): lax.dot_general(left_op, right_op, (((1,), (1,)), ((), ())), preferred_el...  58.8 us
    dot_general x5, matrix products, dot_cols(): lax.dot_general(left_op, right_op, (((0,), (0,)), ((), ())), preferred_el...  34.2 us
    sub x2, other arithmetic, adam_step(): weights - rate * (moment_hat / (jnp.sqrt(square_hat) + ADAM_EPS) + decay...  25.9 us
    all_gather x1, waiting for transfers between devices, on_device(): rest = lax.all_gather(mats_low[layer_at, 1:], AXES, axis=1, tiled=True)  23.9 us
  transfers between devices with their start and end apart: 4, of which 1 were waited for; matrix products, arithmetic and copies ran while one was open for 19% of the time, Pallas kernels for 54%

profile of v11, /device:TPU:0, one launch (start us, length us, event | category | flops | bytes accessed | tf_op | source)
XLA Modules:
  0.0 1150.9 jit_solution(5823606938523264578)
XLA Ops:
  11.6 12.5 %share_ids.1 = s32[32,8,128]{2,1,0:T(8,128)S(1)} custom-call(s32[8,128]{1,0:T(8,128)S(1)} %pad_bitcast_fusion.1.refs_0_), custom_call_target="tpu_custom_call" | custom-call | tf_op jit(solution)/shard_map/share_ids/pallas_call | solution.py:168
  27.0 6.9 copy.89
  33.9 11.3 fusion.21
  45.6 196.1 %open_rows.1 = (bf16[32,136,1088]{2,1,0:T(8,128)(2,1)S(1)}, bf16[8,32,1088]{2,1,0:T(8,128)(2,1)S(1)}, bf16[32,1088]{1,0:T(8,128)(2,1)S(1)}, bf16[32,24,1088]{2,1,0:T(8,128)(2,1)S(1)}) custom-call(bf16[136,1088]{1,0:T(8,128)(2,1)S(1)} %slice_bitcast_fusion.36.refs_0_, bf16[32,32,1088]{2,1,0:T(8,128)(2,1)S(1)} %bitcast.208, ...), custom_call_target="tpu_custom_call" | custom-call | tf_op jit(solution)/shard_map/open_rows/pallas_call | solution.py:168
  270.3 43.8 %attend.2 = (bf16[256,1152]{1,0:T(8,128)(2,1)S(1)}, f32[9,2,256]{2,1,0:T(2,128)S(1)}, bf16[4,512,1152]{2,1,0:T(8,128)(2,1)}) custom-call(bf16[256,1152]{1,0:T(8,128)(2,1)S(1)} %pad.38.q_ref, bf16[512,1152]{1,0:T(8,128)(2,1)S(1)} %fusion.63.own_ref, s32[1024,1]{1,0:T(8,128)S(1)} %copy.93.key_ids_ref, s32[1,256]{1,0:T(1,128)S(1)} %constant_dynamic-slice_fusion.query_ids_ref), custom_call_target="tpu_custom_call" | custom-call | flops 1207959552 | bytes 4718592 | tf_op jit(solution)/shard_map/attend/pallas_call | solution.py:797
  317.7 8.1 multiply_convert_fusion.1
  325.9 7.9 fusion.112
  337.5 60.4 %attend.3 = (bf16[256,1152]{1,0:T(8,128)(2,1)S(1)}, f32[9,2,256]{2,1,0:T(2,128)S(1)}, bf16[4,512,1152]{2,1,0:T(8,128)(2,1)}) custom-call(bf16[256,1152]{1,0:T(8,128)(2,1)S(1)} %pad.41.q_ref, bf16[512,1152]{1,0:T(8,128)(2,1)S(1)} %fusion.64.own_ref, s32[1024,1]{1,0:T(8,128)S(1)} %copy.93.key_ids_ref, s32[1,256]{1,0:T(1,128)S(1)} %constant_dynamic-slice_fusion.query_ids_ref), custom_call_target="tpu_custom_call" | custom-call | flops 1207959552 | bytes 4718592 | tf_op jit(solution)/shard_map/attend/pallas_call | solution.py:797
  400.4 23.9 %all-gather.7.cloned.1.call-done = bf16[1,2,4352,1088]{3,2,1,0:T(8,128)(2,1)} async-done(((bf16[1,2,136,1088]{3,2,1,0:T(8,128)(2,1)}), bf16[1,2,4352,1088]{3,2,1,0:T(8,128)(2,1)}) %all-gather.7.cloned.1.call-update) | async-done | bytes 18939920 | tf_op jit(solution)/shard_map/all_gather | solution.py:1191
  424.4 7.0 fusion.23
  431.4 8.7 fusion.114
  442.0 48.5 %share_final.1 = bf16[32,64,1088]{2,1,0:T(8,128)(2,1)} custom-call(bf16[4,64,1088]{2,1,0:T(8,128)(2,1)} %bitcast.240), custom_call_target="tpu_custom_call" | custom-call | tf_op jit(solution)/shard_map/share_final/pallas_call | solution.py:168
  490.5 12.5 %select_reduce_fusion.3 = (f32[2048]{0:T(1024)S(1)}, f32[2048,1604]{0,1:T(8,128)S(1)}) fusion(pred[1604]{0:T(1024)(128)(4,1)S(1)} %copy-done.97, bf16[2048,1088]{1,0:T(8,128)(2,1)} %bitcast.233, bf16[1604,1088]{1,0:T(8,128)(2,1)} %get-tuple-element.642), kind=kOutput, calls=%fused_computation.36 | convolution fusion | flops 7154710528 | bytes 21096516 | tf_op jit(solution)/shard_map/dot_general | solution.py:966
  508.4 15.3 %share_stats.1 = f32[3,16,128]{2,1,0:T(8,128)S(1)} custom-call(f32[3,16,128]{2,1,0:T(8,128)S(1)} %pad_maximum_fusion.3.refs_0_), custom_call_target="tpu_custom_call" | custom-call | tf_op jit(solution)/shard_map/share_stats/pallas_call | solution.py:168
  529.4 12.4 %fusion.116 = f32[2048,1088]{1,0:T(8,128)} fusion(bf16[2048,1604]{0,1:T(8,128)(2,1)S(1)} %fusion.9, bf16[1604,1088]{1,0:T(8,128)(2,1)S(1)} %copy-done.61), kind=kOutput, calls=%fused_computation.303 | convolution fusion | flops 7148142592 | bytes 18973184 | tf_op jit(solution)/shard_map/dot_general | solution.py:978
  541.8 52.7 %return_final.1 = bf16[4,64,1088]{2,1,0:T(8,128)(2,1)} custom-call(f32[32,64,1088]{2,1,0:T(8,128)} %bitcast.220), custom_call_target="tpu_custom_call" | custom-call | tf_op jit(solution)/shard_map/return_final/pallas_call | solution.py:168
  599.1 10.0 convolution_convert_fusion.2
  611.2 9.7 convert_reduce_fusion
  620.9 9.2 multiply_reduce_fusion.3
  634.4 47.6 %attend_back.2 = (bf16[256,1152]{1,0:T(8,128)(2,1)}, bf16[512,1152]{1,0:T(8,128)(2,1)}) custom-call(bf16[256,1152]{1,0:T(8,128)(2,1)} %copy-done.11, bf16[4,512,1152]{2,1,0:T(8,128)(2,1)} %get-tuple-element.282.kv_ref, bf16[256,1152]{1,0:T(8,128)(2,1)} %pad.44.grad_ref, f32[9,2,256]{2,1,0:T(2,128)} %copy-done.33, s32[1024,1]{1,0:T(8,128)} %copy-done.12, ...), custom_call_target="tpu_custom_call" | custom-call | flops 3019898880 | bytes 14155776 | tf_op jit(solution)/shard_map/attend_back/pallas_call | solution.py:924
  688.5 7.4 multiply_reduce_fusion.4
  706.3 9.4 convert_reduce_fusion.1
  715.7 9.7 multiply_reduce_fusion.5
  743.4 14.1 %fusion.117 = f32[1604,1088]{0,1:T(8,128)} fusion(bf16[2048,1604]{0,1:T(8,128)(2,1)} %copy-done.52, bf16[2048,1088]{1,0:T(8,128)(2,1)} %bitcast.234), kind=kOutput, calls=%fused_computation.304 | convolution fusion | flops 7148142592 | bytes 18007040 | tf_op jit(solution)/shard_map/dot_general | solution.py:972
  757.5 40.8 %attend_back.3 = (bf16[256,1152]{1,0:T(8,128)(2,1)}, bf16[512,1152]{1,0:T(8,128)(2,1)}) custom-call(bf16[256,1152]{1,0:T(8,128)(2,1)} %copy-done.10, bf16[4,512,1152]{2,1,0:T(8,128)(2,1)} %get-tuple-element.281.kv_ref, bf16[256,1152]{1,0:T(8,128)(2,1)} %pad.45.grad_ref, f32[9,2,256]{2,1,0:T(2,128)} %copy-done.32, s32[1024,1]{1,0:T(8,128)} %copy-done.12, ...), custom_call_target="tpu_custom_call" | custom-call | flops 3019898880 | bytes 14155776 | tf_op jit(solution)/shard_map/attend_back/pallas_call | solution.py:924
  808.0 15.5 %trade_rows.1 = (bf16[3,544,512]{2,1,0:T(8,128)(2,1)S(1)}, bf16[1,544,512]{2,1,0:T(8,128)(2,1)S(1)}, bf16[4,544,512]{2,1,0:T(8,128)(2,1)}, bf16[4,544,512]{2,1,0...) custom-call(bf16[3,2,544,256]{3,2,1,0:T(8,128)(2,1)} %bitcast.229, ...), custom_call_target="tpu_custom_call" | custom-call | tf_op jit(solution)/shard_map/trade_rows/pallas_call | solution.py:655
  824.7 8.8 multiply_reduce_fusion.6
  865.4 208.8 %close_rows.1 = (f32[4,136,1088]{2,1,0:T(8,128)}, bf16[32,32,1088]{2,1,0:T(8,128)(2,1)}, f32[224,128]{1,0:T(8,128)}, bf16[32,24,1088]{2,1,0:T(8,128)(2,1)}) custom-call(bf16[16,136,1088]{2,1,0:T(8,128)(2,1)} %bitcast.216, bf16[16,136,1088]{2,1,0:T(8,128)(2,1)} %bitcast.230, bf16[16,136,1088]{2,1,0:T(8,128)(2,1)} %bitcast.231, ...), custom_call_target="tpu_custom_call" | custom-call | tf_op jit(solution)/shard_map/close_rows/pallas_call | solution.py:168
  1075.4 13.4 %fusion.12 = f32[1604,1088]{0,1:T(8,128)} fusion(f32[1604,1088]{0,1:T(8,128)} %fusion.117, s32[1856]{0:T(1024)S(1)} %copy-done.122, bf16[32,1088]{1,0:T(8,128)(2,1)S(1)} %subtract_convert_fusion, bf16[32,1088]{1,0:T(8,128)(2,1)S(1)} %pad_convert_fusion, bf16[1024,1088]{1,0:T(8,128)(2,1)} %bitcast.263, bf16[768,1088]{1,0:T(8,128)(2,1)} %bitcast.266), kind=kOutput, calls=%fused_computation.44 | convolution fusion | flops 6498880512 | bytes 18007296 | tf_op jit(solution)/shard_map/dot_general | solution.py:978
  1097.8 12.6 %share_norm.1 = f32[8,128]{1,0:T(8,128)S(1)} custom-call(f32[8,128]{1,0:T(8,128)S(1)} %broadcast_in_dim.223.refs_0_), custom_call_target="tpu_custom_call" | custom-call | tf_op jit(solution)/shard_map/share_norm/pallas_call | solution.py:168
  1115.7 6.8 multiply_subtract_fusion.1
  1122.5 19.2 %multiply_subtract_fusion = (f32[1604,1088]{0,1:T(8,128)}, f32[1604,1088]{0,1:T(8,128)}, f32[1604,1088]{0,1:T(8,128)}) fusion(f32[1604,1088]{0,1:T(8,128)} %param.25, f32[1604]{0:T(1024)S(1)} %copy-done.93, f32[]{:T(128)} %bitcast.68, f32[]{:T(128)} %bitcast.67, f32[1604]{0:T(1024)S(1)} %copy-done.94, f32[1604,1088]{0,1:T(8,128)} %get-tuple-element.309, ...), kind=kLoop, calls=%fused_computation.58 | loop fusion | flops 27922432 | bytes 48877100 | tf_op jit(solution)/shard_map/sub | solution.py:1107
  (421 shorter events, 157.3 us)
Async XLA Ops:
  7.2 256.7 %all-gather.5.cloned.1.call-start = ((), (), s32[]{:S(2)}) async-start(), calls=%async_computation.2 | async-start | bytes 31021056 | tf_op jit(solution)/shard_map/all_gather | solution.py:1188
  10.5 413.8 %all-gather.7.cloned.1.call-start = ((), (), s32[]{:S(2)}) async-start(), calls=%async_computation.3 | async-start | bytes 20680704 | tf_op jit(solution)/shard_map/all_gather | solution.py:1191
  11.5 746.0 %reduce-scatter.7.cloned.1.call-start = ((), (), s32[]{:S(2)}) async-start(), calls=%async_computation.4 | async-start | bytes 10340352
  248.7 88.9 %copy-start.12 = (s32[1024,1]{1,0:T(8,128)}, s32[1024,1]{1,0:T(8,128)S(1)}, u32[]{:S(2)}) copy-start(s32[1024,1]{1,0:T(8,128)S(1)} %copy.93.key_ids_ref) | copy-start | bytes 12292
  259.1 55.0 %copy-start.34 = (f32[256,1088]{1,0:T(8,128)}, f32[256,1088]{1,0:T(8,128)S(1)}, u32[]{:S(2)}) copy-start(f32[256,1088]{1,0:T(8,128)S(1)} %copy.94) | copy-start | bytes 3342340
  261.1 76.5 %copy-start.13 = (s32[1,256]{1,0:T(1,128)}, s32[1,256]{1,0:T(1,128)S(1)}, u32[]{:S(2)}) copy-start(s32[1,256]{1,0:T(1,128)S(1)} %constant_dynamic-slice_fusion.query_ids_ref) | copy-start | bytes 3076
  262.5 54.8 %copy-start.83 = (f32[1088]{0:T(1024)}, f32[1088]{0:T(1024)S(1)}, u32[]{:S(2)}) copy-start(f32[1088]{0:T(1024)S(1)} %get-tuple-element.339) | copy-start | bytes 13060
  262.5 161.8 %copy-start.91 = (f32[1088]{0:T(1024)}, f32[1088]{0:T(1024)S(1)}, u32[]{:S(2)}) copy-start(f32[1088]{0:T(1024)S(1)} %get-tuple-element.330) | copy-start | bytes 13060
  270.1 44.0 %copy-start.10 = (bf16[256,1152]{1,0:T(8,128)(2,1)}, bf16[256,1152]{1,0:T(8,128)(2,1)S(1)}, u32[]{:S(2)}) copy-start(bf16[256,1152]{1,0:T(8,128)(2,1)S(1)} %pad.38.q_ref) | copy-start | bytes 1769476
  333.8 64.2 %copy-start.43 = (f32[256,1088]{1,0:T(8,128)}, f32[256,1088]{1,0:T(8,128)S(1)}, u32[]{:S(2)}) copy-start(f32[256,1088]{1,0:T(8,128)S(1)} %get-tuple-element.430) | copy-start | bytes 3342340
  337.4 60.6 %copy-start.11 = (bf16[256,1152]{1,0:T(8,128)(2,1)}, bf16[256,1152]{1,0:T(8,128)(2,1)S(1)}, u32[]{:S(2)}) copy-start(bf16[256,1152]{1,0:T(8,128)(2,1)S(1)} %pad.41.q_ref) | copy-start | bytes 1769476
  337.5 60.5 %copy-start.64 = (bf16[8,136,1088]{2,1,0:T(8,128)(2,1)S(1)}, bf16[8,136,1088]{2,1,0:T(8,128)(2,1)}, u32[]{:S(2)}) copy-start(bf16[8,136,1088]{2,1,0:T(8,128)(2,1)} %slice.255) | copy-start | bytes 7102468
  398.0 26.4 %copy-start.95 = (f32[4352]{0:T(1024)S(1)}, f32[4352]{0:T(1024)}, u32[]{:S(2)}) copy-start(f32[4352]{0:T(1024)} %add.560) | copy-start | bytes 52228
  399.1 230.9 %copy-start.105 = (f32[256]{0:T(256)}, f32[256]{0:T(256)S(1)}, u32[]{:S(2)}) copy-start(f32[256]{0:T(256)S(1)} %broadcast_multiply_fusion.1) | copy-start | bytes 3076
  400.4 229.7 %copy-start.119 = (f32[256]{0:T(256)}, f32[256]{0:T(256)S(1)}, u32[]{:S(2)}) copy-start(f32[256]{0:T(256)S(1)} %fusion.96) | copy-start | bytes 3076
  442.0 48.6 %copy-start.97 = (pred[1604]{0:T(1024)(128)(4,1)S(1)}, pred[1604]{0:T(1024)(128)(4,1)}, u32[]{:S(2)}) copy-start(pred[1604]{0:T(1024)(128)(4,1)} %fusion.87) | copy-start | bytes 4816
  490.5 12.5 %copy-start.89 = (s32[2048]{0:T(1024)S(1)}, s32[2048]{0:T(1024)}, u32[]{:S(2)}) copy-start(s32[2048]{0:T(1024)} %param.20) | copy-start | bytes 24580
  609.1 466.2 %reduce-scatter.9.cloned.1.call-start = ((), (), s32[]{:S(2)}) async-start(), calls=%async_computation.5 | async-start | bytes 10340352
  807.9 15.6 %copy-start.63 = (bf16[512,1152]{1,0:T(8,128)(2,1)S(1)}, bf16[512,1152]{1,0:T(8,128)(2,1)}, u32[]{:S(2)}) copy-start(bf16[512,1152]{1,0:T(8,128)(2,1)} %get-tuple-element.289) | copy-start | bytes 3538948
  807.9 15.6 %copy-start.70 = (bf16[256,1152]{1,0:T(8,128)(2,1)S(1)}, bf16[256,1152]{1,0:T(8,128)(2,1)}, u32[]{:S(2)}) copy-start(bf16[256,1152]{1,0:T(8,128)(2,1)} %get-tuple-element.288) | copy-start | bytes 1769476
  807.9 16.7 %copy-start.35 = (f32[256,1088]{1,0:T(8,128)S(1)}, f32[256,1088]{1,0:T(8,128)}, u32[]{:S(2)}) copy-start(f32[256,1088]{1,0:T(8,128)} %copy-done.34) | copy-start | bytes 3342340
  807.9 16.7 %copy-start.51 = (bf16[256,3264]{1,0:T(8,128)(2,1)S(1)}, bf16[256,3264]{1,0:T(8,128)(2,1)}, u32[]{:S(2)}) copy-start(bf16[256,3264]{1,0:T(8,128)(2,1)} %concatenate.42) | copy-start | bytes 5013508
  807.9 16.7 %copy-start.82 = (f32[1088]{0:T(1024)S(1)}, f32[1088]{0:T(1024)}, u32[]{:S(2)}) copy-start(f32[1088]{0:T(1024)} %copy-done.81) | copy-start | bytes 13060
  808.0 16.7 %copy-start.100 = (f32[256]{0:T(256)S(1)}, f32[256]{0:T(256)}, u32[]{:S(2)}) copy-start(f32[256]{0:T(256)} %copy-done.99) | copy-start | bytes 3076
  808.0 16.7 %copy-start.114 = (f32[256]{0:T(256)S(1)}, f32[256]{0:T(256)}, u32[]{:S(2)}) copy-start(f32[256]{0:T(256)} %copy-done.113) | copy-start | bytes 3076
  824.7 12.8 %copy-start.36 = (f32[256,1088]{1,0:T(8,128)S(1)}, f32[256,1088]{1,0:T(8,128)}, u32[]{:S(2)}) copy-start(f32[256,1088]{1,0:T(8,128)} %copy-done.34) | copy-start | bytes 3342340
  865.4 209.9 %copy-start.122 = (s32[1856]{0:T(1024)S(1)}, s32[1856]{0:T(1024)}, u32[]{:S(2)}) copy-start(s32[1856]{0:T(1024)} %concatenate.48) | copy-start | bytes 22276
  1075.3 13.5 %copy-start.57 = (s32[32,256]{1,0:T(8,128)S(1)}, s32[32,256]{1,0:T(8,128)}, u32[]{:S(2)}) copy-start(s32[32,256]{1,0:T(8,128)} %copy-done.56) | copy-start | bytes 98308
  1075.4 13.5 %copy-start.59 = (s32[32,256]{1,0:T(8,128)S(1)}, s32[32,256]{1,0:T(8,128)}, u32[]{:S(2)}) copy-start(s32[32,256]{1,0:T(8,128)} %copy-done.58) | copy-start | bytes 98308
  1075.4 13.5 %copy-start.74 = (pred[32,256]{1,0:T(32,128)(4,1)S(1)}, pred[32,256]{1,0:T(32,128)(4,1)}, u32[]{:S(2)}) copy-start(pred[32,256]{1,0:T(32,128)(4,1)} %copy-done.73) | copy-start | bytes 24580
  1075.4 13.5 %copy-start.78 = (s32[256]{0:T(256)S(1)}, s32[256]{0:T(256)}, u32[]{:S(2)}) copy-start(s32[256]{0:T(256)} %copy-done.77) | copy-start | bytes 3076
  1075.4 13.5 %copy-start.80 = (s32[256]{0:T(256)S(1)}, s32[256]{0:T(256)}, u32[]{:S(2)}) copy-start(s32[256]{0:T(256)} %copy-done.79) | copy-start | bytes 3076
  (105 other events, 563.1 us)
Sparse Core Ops, SparseCore 0:
  11.6 252.1 all-gather.4
  266.8 157.5 all-gather.6
  609.2 136.6 reduce-scatter.6
  751.9 137.0 reduce-scatter.8
